TPU v7x, 32 devices: a whole 2x2x4 slice. The times are simulated.
32 devices in a mesh: ctx: 8 (over z, y), head: 4 (over x, core).
Axes of the slice: x: 2, y: 2, z: 4, core: 2. Of those that a mesh axis runs over, the one named last changes fastest.
Arguments:
- queries: bfloat16 [2048, 4096], P(('ctx', 'head')), may hold values from -6 to 6
- key_rows: bfloat16 [2048, 512], P(('ctx', 'head')), may hold values from -6 to 6
- value_rows: bfloat16 [2048, 512], P(('ctx', 'head')), may hold values from -6 to 6
- attn_out: bfloat16 [2048, 4096], P(('ctx', 'head')), may hold values from -6 to 6
- out_grad: bfloat16 [2048, 4096], P(('ctx', 'head')), may hold values from -864 to 864
- logsumexp: float32 [32, 2048], P('head', 'ctx'), may hold values from 7.5 to 8.7
Outputs:
- grad_queries: float32 [2048, 4096], P(('ctx', 'head'))
- grad_keys: float32 [2048, 512], P(('ctx', 'head'))
- grad_values: float32 [2048, 512], P(('ctx', 'head'))
All inputs are finite; a program needn't handle non-finite values.
Results may differ from a plain program's by a relative error of at most 0.0051.
Values may be sent and summed in bfloat16 or wider, within the bound.
No kernel may reach another device: no remote copies, remote signals or barrier semaphores. Data moves between devices by JAX's collectives and lax.ppermute only.
A program may use at most 64 MiB of HBM per device.

v0:
```python
import math

import jax
import jax.numpy as jnp
from jax import lax
from jax.sharding import PartitionSpec as P

HEAD_DIM = 128
GROUP = 8
BLOCK = 256


def from_partner(value, axis, distance):
    return lax.ppermute(value, axis, [(i, i ^ 1 << distance) for i in range(lax.axis_size(axis))])


def block_grads(query_blk, grad_blk, lse_rows, dot_rows, key_blk, value_blk):
    score_scale = 1.0 / math.sqrt(query_blk.shape[-1])
    scores = (
        jnp.einsum("nbhgd,nkhd->nhgbk", query_blk, key_blk, preferred_element_type=jnp.float32)
        * score_scale
    )
    attn_probs = jnp.exp(scores - lse_rows[..., None])
    dprobs = jnp.einsum(
        "nbhgd,nkhd->nhgbk", grad_blk, value_blk, preferred_element_type=jnp.float32
    )
    dscores = (attn_probs * (dprobs - dot_rows[..., None])).astype(jnp.bfloat16)
    weights = attn_probs.astype(jnp.bfloat16)
    d_values = jnp.einsum(
        "nhgbk,nbhgd->nkhd", weights, grad_blk, preferred_element_type=jnp.float32
    )
    d_query = (
        jnp.einsum("nhgbk,nkhd->nbhgd", dscores, key_blk, preferred_element_type=jnp.float32)
        * score_scale
    )
    d_keys = (
        jnp.einsum("nhgbk,nbhgd->nkhd", dscores, query_blk, preferred_element_type=jnp.float32)
        * score_scale
    )
    return (d_query, d_keys, d_values)


def on_device(queries, key_rows, value_rows, attn_out, out_grad, logsumexp):
    rows_before = queries.shape[0]
    dot_before = jnp.sum(
        (out_grad.astype(jnp.float32) * attn_out.astype(jnp.float32)).reshape(
            rows_before, -1, HEAD_DIM
        ),
        axis=2,
    )
    q_local, k_local, v_local, g_local = (
        lax.all_to_all(queries, "head", split_axis=1, concat_axis=0, tiled=True),
        lax.all_to_all(key_rows, "head", split_axis=1, concat_axis=0, tiled=True),
        lax.all_to_all(value_rows, "head", split_axis=1, concat_axis=0, tiled=True),
        lax.all_to_all(out_grad, "head", split_axis=1, concat_axis=0, tiled=True),
    )
    dot_local = lax.all_to_all(dot_before, "head", split_axis=1, concat_axis=0, tiled=True)
    row_count = q_local.shape[0]
    blocks = row_count // BLOCK
    kv_heads = k_local.shape[1] // HEAD_DIM
    query_blk = q_local.reshape(blocks, BLOCK, kv_heads, GROUP, HEAD_DIM)
    grad_blk = g_local.reshape(blocks, BLOCK, kv_heads, GROUP, HEAD_DIM)
    key_blk = k_local.reshape(blocks, BLOCK, kv_heads, HEAD_DIM)
    value_blk = v_local.reshape(blocks, BLOCK, kv_heads, HEAD_DIM)
    lse_rows = logsumexp.reshape(kv_heads, GROUP, blocks, BLOCK).transpose(2, 0, 1, 3)
    dot_rows = dot_local.reshape(blocks, BLOCK, kv_heads, GROUP).transpose(0, 2, 3, 1)
    grad_q, grad_k, grad_v = block_grads(
        query_blk, grad_blk, lse_rows, dot_rows, key_blk, value_blk
    )
    ctx_levels = lax.axis_size("ctx").bit_length() - 1
    plan = list(range(ctx_levels))
    for bit_level in plan:
        far_k, far_v = from_partner((key_blk, value_blk), "ctx", bit_level)
        part_q, part_k, part_v = block_grads(query_blk, grad_blk, lse_rows, dot_rows, far_k, far_v)
        back_k, back_v = from_partner((part_k, part_v), "ctx", bit_level)
        grad_q = grad_q + part_q
        grad_k = grad_k + back_k
        grad_v = grad_v + back_v
    result_q, result_k, result_v = (
        lax.all_to_all(
            grad_q.reshape(row_count, -1), "head", split_axis=0, concat_axis=1, tiled=True
        ),
        lax.all_to_all(
            grad_k.reshape(row_count, -1), "head", split_axis=0, concat_axis=1, tiled=True
        ),
        lax.all_to_all(
            grad_v.reshape(row_count, -1), "head", split_axis=0, concat_axis=1, tiled=True
        ),
    )
    return (result_q, result_k, result_v)


def solution(mesh):
    placed = (
        P(("ctx", "head"), None),
        P(("ctx", "head"), None),
        P(("ctx", "head"), None),
        P(("ctx", "head"), None),
        P(("ctx", "head"), None),
        P("head", "ctx"),
    )
    return jax.shard_map(
        on_device,
        mesh=mesh,
        in_specs=placed,
        out_specs=(P(("ctx", "head"), None), P(("ctx", "head"), None), P(("ctx", "head"), None)),
        check_vma=False,
    )
```

profile of v0, /device:TPU:0, one launch (start us, length us, event | category | flops | bytes accessed | tf_op | source)
XLA Modules:
  0.0 108.8 jit_solution(2686458098232040991)
XLA Ops:
  0.6 1.3 %multiply_bitcast_fusion = f32[8,8,32,128]{3,1,2,0:T(8,128)S(1)} fusion(bf16[64,4096]{1,0:T(8,128)(2,1)} %param.9, bf16[64,4096]{1,0:T(8,128)(2,1)} %param.10), kind=kLoop, calls=%fused_computation.59 | loop fusion | flops 786432 | bytes 2097152
  3.3 4.2 %all-to-all-start.4 = ((f32[4,1,512]{2,1,0:T(1,128)}), f32[4,1,512]{2,1,0:T(1,128)S(1)}, u32[]{:S(2)}, u32[]{:S(2)}) async-start(f32[4,1,512]{2,1,0:T(1,128)} %reshape.241), calls=%async_computation.4 | async-start | bytes 16384 | tf_op jit(solution)/shard_map/all_to_all | solution.py:57
  8.2 3.2 %all-to-all-done.4 = f32[4,1,512]{2,1,0:T(1,128)S(1)} async-done(((f32[4,1,512]{2,1,0:T(1,128)}), f32[4,1,512]{2,1,0:T(1,128)S(1)}, u32[]{:S(2)}, u32[]{:S(2)}) %all-to-all-start.4) | async-done | bytes 8224 | tf_op jit(solution)/shard_map/all_to_all | solution.py:57
  11.4 3.3 %all-to-all-start = ((bf16[64,4,128]{2,0,1:T(8,128)(2,1)}), bf16[64,4,128]{2,0,1:T(8,128)(2,1)S(1)}, u32[]{:S(2)}, u32[]{:S(2)}) async-start(bf16[64,4,128]{2,0,1:T(8,128)(2,1)} %copy_bitcast_fusion.5), calls=%async_computation | async-start | bytes 131072 | tf_op jit(solution)/shard_map/all_to_all | solution.py:53
  15.3 3.4 %all-to-all-done = bf16[64,4,128]{2,0,1:T(8,128)(2,1)S(1)} async-done(((bf16[64,4,128]{2,0,1:T(8,128)(2,1)}), bf16[64,4,128]{2,0,1:T(8,128)(2,1)S(1)}, u32[]{:S(2)}, u32[]{:S(2)}) %all-to-all-start) | async-done | bytes 65568 | tf_op jit(solution)/shard_map/all_to_all | solution.py:53
  18.8 3.3 %all-to-all-start.2 = ((bf16[64,4,128]{2,0,1:T(8,128)(2,1)}), bf16[64,4,128]{2,0,1:T(8,128)(2,1)S(1)}, u32[]{:S(2)}, u32[]{:S(2)}) async-start(bf16[64,4,128]{2,0,1:T(8,128)(2,1)} %copy_bitcast_fusion.4), calls=%async_computation.2 | async-start | bytes 131072 | tf_op jit(solution)/shard_map/all_to_all | solution.py:54
  22.9 3.2 %all-to-all-done.2 = bf16[64,4,128]{2,0,1:T(8,128)(2,1)S(1)} async-done(((bf16[64,4,128]{2,0,1:T(8,128)(2,1)}), bf16[64,4,128]{2,0,1:T(8,128)(2,1)S(1)}, u32[]{:S(2)}, u32[]{:S(2)}) %all-to-all-start.2) | async-done | bytes 65568 | tf_op jit(solution)/shard_map/all_to_all | solution.py:54
  26.1 3.5 %all-to-all-start.1 = ((bf16[64,4,1024]{2,0,1:T(8,128)(2,1)}), bf16[64,4,1024]{2,0,1:T(8,128)(2,1)S(1)}, u32[]{:S(2)}, u32[]{:S(2)}) async-start(bf16[64,4,1024]{2,0,1:T(8,128)(2,1)} %bitcast.347), calls=%async_computation.1 | async-start | bytes 1048576 | tf_op jit(solution)/shard_map/all_to_all | solution.py:52
  30.5 7.9 %all-to-all-done.1 = bf16[64,4,1024]{2,0,1:T(8,128)(2,1)S(1)} async-done(((bf16[64,4,1024]{2,0,1:T(8,128)(2,1)}), bf16[64,4,1024]{2,0,1:T(8,128)(2,1)S(1)}, u32[]{:S(2)}, u32[]{:S(2)}) %all-to-all-start.1) | async-done | bytes 524320 | tf_op jit(solution)/shard_map/all_to_all | solution.py:52
  38.4 3.5 %all-to-all-start.3 = ((bf16[64,4,1024]{2,0,1:T(8,128)(2,1)}), bf16[64,4,1024]{2,0,1:T(8,128)(2,1)S(1)}, u32[]{:S(2)}, u32[]{:S(2)}) async-start(bf16[64,4,1024]{2,0,1:T(8,128)(2,1)} %bitcast.346), calls=%async_computation.3 | async-start | bytes 1048576 | tf_op jit(solution)/shard_map/all_to_all | solution.py:55
  43.1 2.0 %collective-permute-start = (bf16[1,256,1,128]{3,1,2,0:T(8,128)(2,1)S(1)}, bf16[1,256,1,128]{3,1,2,0:T(8,128)(2,1)S(1)}, u32[]{:S(2)}, u32[]{:S(2)}) collective-permute-start(bf16[1,256,1,128]{3,1,2,0:T(8,128)(2,1)S(1)} %bitcast.370), channel_id=1, source_target_pairs={{0,4},{4,0},{8,12},{12,8},{16,20},{20,16},{24,28},{28,24},{1,5},{5... | collective-permute-start | bytes 196616 | tf_op jit(solution)/shard_map/ppermute | solution.py:14
  45.2 2.6 %collective-permute-start.5 = (bf16[1,256,1,128]{3,1,2,0:T(8,128)(2,1)S(1)}, bf16[1,256,1,128]{3,1,2,0:T(8,128)(2,1)S(1)}, u32[]{:S(2)}, u32[]{:S(2)}) collective-permute-start(bf16[1,256,1,128]{3,1,2,0:T(8,128)(2,1)S(1)} %bitcast.376), channel_id=1, source_target_pairs={{0,16},{4,20},{8,24},{12,28},{16,0},{20,4},{24,8},{28,12},{1,17},{... | collective-permute-start | bytes 196616 | tf_op jit(solution)/shard_map/ppermute | solution.py:14
  47.8 1.6 %collective-permute-start.3 = (bf16[1,256,1,128]{3,1,2,0:T(8,128)(2,1)S(1)}, bf16[1,256,1,128]{3,1,2,0:T(8,128)(2,1)S(1)}, u32[]{:S(2)}, u32[]{:S(2)}) collective-permute-start(bf16[1,256,1,128]{3,1,2,0:T(8,128)(2,1)S(1)} %bitcast.377), channel_id=1, source_target_pairs={{0,8},{4,12},{8,0},{12,4},{16,24},{20,28},{24,16},{28,20},{1,9},{5... | collective-permute-start | bytes 196616 | tf_op jit(solution)/shard_map/ppermute | solution.py:14
  50.8 2.1 %collective-permute-start.2 = (bf16[1,256,1,128]{3,1,2,0:T(8,128)(2,1)S(1)}, bf16[1,256,1,128]{3,1,2,0:T(8,128)(2,1)S(1)}, u32[]{:S(2)}, u32[]{:S(2)}) collective-permute-start(bf16[1,256,1,128]{3,1,2,0:T(8,128)(2,1)S(1)} %bitcast.372), channel_id=1, source_target_pairs={{0,8},{4,12},{8,0},{12,4},{16,24},{20,28},{24,16},{28,20},{1,9},{5... | collective-permute-start | bytes 196616 | tf_op jit(solution)/shard_map/ppermute | solution.py:14
  55.0 1.6 %collective-permute-start.6 = (f32[1,256,1,128]{3,1,2,0:T(8,128)S(1)}, f32[1,256,1,128]{3,1,2,0:T(8,128)S(1)}, u32[]{:S(2)}, u32[]{:S(2)}) collective-permute-start(f32[1,256,1,128]{3,1,2,0:T(8,128)S(1)} %fusion.28), channel_id=1, source_target_pairs={{0,4},{4,0},{8,12},{12,8},{16,20},{20,16},{24,28},{28,24},{1,5},{5... | collective-permute-start | bytes 393224 | tf_op jit(solution)/shard_map/ppermute | solution.py:14
  57.6 1.1 fusion.26
  61.4 1.6 %collective-permute-start.9 = (f32[1,256,1,128]{3,1,2,0:T(8,128)S(1)}, f32[1,256,1,128]{3,1,2,0:T(8,128)S(1)}, u32[]{:S(2)}, u32[]{:S(2)}) collective-permute-start(f32[1,256,1,128]{3,1,2,0:T(8,128)S(1)} %convolution_bitcast_fusion.2), channel_id=1, source_target_pairs={{0,4},{4,0},{8,12},{12,8},{16,20},{20,16},{24,28},{28,24},{1,5},{5... | collective-permute-start | bytes 393224 | tf_op jit(solution)/shard_map/ppermute | solution.py:14
  63.0 1.1 %collective-permute-start.10 = (f32[1,256,1,128]{3,1,2,0:T(8,128)S(1)}, f32[1,256,1,128]{3,1,2,0:T(8,128)S(1)}, u32[]{:S(2)}, u32[]{:S(2)}) collective-permute-start(f32[1,256,1,128]{3,1,2,0:T(8,128)S(1)} %convolution_bitcast_fusion.1), channel_id=1, source_target_pairs={{0,8},{4,12},{8,0},{12,4},{16,24},{20,28},{24,16},{28,20},{1,9},{5... | collective-permute-start | bytes 393224 | tf_op jit(solution)/shard_map/ppermute | solution.py:14
  65.1 2.0 %collective-permute-start.11 = (f32[1,256,1,128]{3,1,2,0:T(8,128)S(1)}, f32[1,256,1,128]{3,1,2,0:T(8,128)S(1)}, u32[]{:S(2)}, u32[]{:S(2)}) collective-permute-start(f32[1,256,1,128]{3,1,2,0:T(8,128)S(1)} %convolution_bitcast_fusion), channel_id=1, source_target_pairs={{0,16},{4,20},{8,24},{12,28},{16,0},{20,4},{24,8},{28,12},{1,17},{... | collective-permute-start | bytes 393224 | tf_op jit(solution)/shard_map/ppermute | solution.py:14
  67.7 1.5 %fusion.74 = f32[8,256,128]{2,1,0:T(8,128)} fusion(bf16[8,256,256]{1,2,0:T(8,128)(2,1)S(1)} %fusion.19, bf16[1,256,1,128]{3,1,2,0:T(8,128)(2,1)S(1)} %collective-permute-done.4), kind=kOutput, calls=%fused_computation.95 | convolution fusion | flops 134217728 | bytes 2162688 | tf_op jit(solution)/shard_map/nhgbk,nkhd->nbhgd/dot_general | solution.py:33
  69.2 1.5 %convolution_add_fusion.1 = f32[8,256,128]{2,1,0:T(8,128)} fusion(f32[8,256,128]{2,1,0:T(8,128)S(1)} %fusion.87, bf16[8,256,256]{1,2,0:T(8,128)(2,1)S(1)} %fusion.17, bf16[1,256,1,128]{3,1,2,0:T(8,128)(2,1)S(1)} %collective-permute-done), kind=kOutput, calls=%fused_computation.30 | convolution fusion | flops 134479872 | bytes 3211264 | tf_op jit(solution)/shard_map/nhgbk,nkhd->nbhgd/dot_general | solution.py:33
  70.7 1.1 fusion.24
  72.8 1.2 %fusion.36 = f32[1,256,1,128]{3,1,2,0:T(8,128)} fusion(f32[1,256,1,128]{3,1,2,0:T(8,128)S(1)} %collective-permute-done.11, f32[1,256,1,128]{3,1,2,0:T(8,128)S(1)} %collective-permute-done.10, f32[1,256,1,128]{3,1,2,0:T(8,128)S(1)} %collective-permute-done.9, f32[256,256,8]{1,0,2:T(8,128)S(1)} %fusion.71, f32[8,256]{1,0:T(8,128)S(1)} %copy-done.2, ...), kind=kOutput, calls=%fused_computation.54 | convolution fusion | flops 135888896 | bytes 3153920 | tf_op jit(solution)/shard_map/nhgbk,nbhgd->nkhd/dot_general | solution.py:29
  74.0 3.3 %all-to-all-start.7 = ((f32[4,64,128]{2,1,0:T(8,128)}), f32[4,64,128]{2,1,0:T(8,128)S(1)}, u32[]{:S(2)}, u32[]{:S(2)}) async-start(f32[4,64,128]{2,1,0:T(8,128)} %bitcast.90), calls=%async_computation.7 | async-start | bytes 262144 | tf_op jit(solution)/shard_map/all_to_all | solution.py:86
  77.4 1.9 %collective-permute-done.8 = f32[1,256,1,128]{3,1,2,0:T(8,128)S(1)} collective-permute-done((f32[1,256,1,128]{3,1,2,0:T(8,128)}, f32[1,256,1,128]{3,1,2,0:T(8,128)S(1)}, u32[]{:S(2)}, u32[]{:S(2)}) %collective-permute-start.8) | collective-permute-done | bytes 131104 | tf_op jit(solution)/shard_map/ppermute | solution.py:14
  79.3 1.1 %fusion.33 = f32[1,256,1,128]{3,1,2,0:T(8,128)} fusion(f32[1,256,1,128]{3,1,2,0:T(8,128)S(1)} %collective-permute-done.8, f32[1,256,1,128]{3,1,2,0:T(8,128)S(1)} %collective-permute-done.7, f32[1,256,1,128]{3,1,2,0:T(8,128)S(1)} %collective-permute-done.6, bf16[8,256,256]{1,2,0:T(8,128)(2,1)S(1)} %fusion.16, bf16[256,8,128]{2,1,0:T(8,128)(2,1)S(1)} %bitcast.363), kind=kOutput, calls=%fused_computation.51 | convolution fusion | flops 134348800 | bytes 2097152 | tf_op jit(solution)/shard_map/nhgbk,nbhgd->nkhd/dot_general | solution.py:37
  80.4 1.6 %all-to-all-done.7 = f32[4,64,128]{2,1,0:T(8,128)S(1)} async-done(((f32[4,64,128]{2,1,0:T(8,128)}), f32[4,64,128]{2,1,0:T(8,128)S(1)}, u32[]{:S(2)}, u32[]{:S(2)}) %all-to-all-start.7) | async-done | bytes 131104 | tf_op jit(solution)/shard_map/all_to_all | solution.py:86
  81.9 3.3 %all-to-all-start.6 = ((f32[4,64,128]{2,1,0:T(8,128)}), f32[4,64,128]{2,1,0:T(8,128)S(1)}, u32[]{:S(2)}, u32[]{:S(2)}) async-start(f32[4,64,128]{2,1,0:T(8,128)} %bitcast.68), calls=%async_computation.6 | async-start | bytes 262144 | tf_op jit(solution)/shard_map/all_to_all | solution.py:83
  85.3 2.0 %fusion.22 = f32[1,256,1,8,128]{4,1,3,2,0:T(8,128)S(1)} fusion(f32[8,256,128]{2,1,0:T(8,128)} %fusion.74, f32[8,256,128]{2,1,0:T(8,128)} %convolution_add_fusion.1, bf16[8,256,256]{1,2,0:T(8,128)(2,1)S(1)} %fusion.18, bf16[1,256,1,128]{3,1,2,0:T(8,128)(2,1)S(1)} %collective-permute-done.2), kind=kOutput, calls=%fused_computation.32 | convolution fusion | flops 135004160 | bytes 4259840 | tf_op jit(solution)/shard_map/nhgbk,nkhd->nbhgd/dot_general | solution.py:33
  87.9 1.1 %all_to_all.117 = f32[4,64,1024]{2,1,0:T(8,128)} reshape(f32[1,256,1,8,128]{4,3,1,2,0:T(8,128)S(1)} %copy.91) | data formatting | bytes 2097152 | tf_op jit(solution)/shard_map/all_to_all | solution.py:80
  89.8 3.5 %all-to-all-start.5 = ((f32[4,64,1024]{2,1,0:T(8,128)}), f32[4,64,1024]{2,1,0:T(8,128)S(1)}, u32[]{:S(2)}, u32[]{:S(2)}) async-start(f32[4,64,1024]{2,1,0:T(8,128)} %all_to_all.117), calls=%async_computation.5 | async-start | bytes 2097152 | tf_op jit(solution)/shard_map/all_to_all | solution.py:80
  94.7 13.1 %all-to-all-done.5 = f32[4,64,1024]{2,1,0:T(8,128)S(1)} async-done(((f32[4,64,1024]{2,1,0:T(8,128)}), f32[4,64,1024]{2,1,0:T(8,128)S(1)}, u32[]{:S(2)}, u32[]{:S(2)}) %all-to-all-start.5) | async-done | bytes 1048608 | tf_op jit(solution)/shard_map/all_to_all | solution.py:80
  (61 shorter events, 19.2 us)
Async XLA Ops:
  0.6 6.9 %copy-start = (bf16[64,512]{1,0:T(8,128)(2,1)S(1)}, bf16[64,512]{1,0:T(8,128)(2,1)}, u32[]{:S(2)}) copy-start(bf16[64,512]{1,0:T(8,128)(2,1)} %param.7) | copy-start | bytes 196612
  2.0 12.7 %copy-start.4 = (bf16[64,512]{1,0:T(8,128)(2,1)S(1)}, bf16[64,512]{1,0:T(8,128)(2,1)}, u32[]{:S(2)}) copy-start(bf16[64,512]{1,0:T(8,128)(2,1)} %param.8) | copy-start | bytes 196612
  2.0 20.1 %copy-start.3 = (bf16[64,4096]{1,0:T(8,128)(2,1)S(1)}, bf16[64,4096]{1,0:T(8,128)(2,1)}, u32[]{:S(2)}) copy-start(bf16[64,4096]{1,0:T(8,128)(2,1)} %param.6) | copy-start | bytes 1572868
  2.2 27.4 %copy-start.1 = (bf16[64,4096]{1,0:T(8,128)(2,1)S(1)}, bf16[64,4096]{1,0:T(8,128)(2,1)}, u32[]{:S(2)}) copy-start(bf16[64,4096]{1,0:T(8,128)(2,1)} %param.10) | copy-start | bytes 1572868
  3.3 8.1 %all-to-all-start.4 = ((f32[4,1,512]{2,1,0:T(1,128)}), f32[4,1,512]{2,1,0:T(1,128)S(1)}, u32[]{:S(2)}, u32[]{:S(2)}) async-start(f32[4,1,512]{2,1,0:T(1,128)} %reshape.241), calls=%async_computation.4 | async-start | bytes 16384 | tf_op jit(solution)/shard_map/all_to_all | solution.py:57
  11.4 7.4 %all-to-all-start = ((bf16[64,4,128]{2,0,1:T(8,128)(2,1)}), bf16[64,4,128]{2,0,1:T(8,128)(2,1)S(1)}, u32[]{:S(2)}, u32[]{:S(2)}) async-start(bf16[64,4,128]{2,0,1:T(8,128)(2,1)} %copy_bitcast_fusion.5), calls=%async_computation | async-start | bytes 131072 | tf_op jit(solution)/shard_map/all_to_all | solution.py:53
  18.8 7.4 %all-to-all-start.2 = ((bf16[64,4,128]{2,0,1:T(8,128)(2,1)}), bf16[64,4,128]{2,0,1:T(8,128)(2,1)S(1)}, u32[]{:S(2)}, u32[]{:S(2)}) async-start(bf16[64,4,128]{2,0,1:T(8,128)(2,1)} %copy_bitcast_fusion.4), calls=%async_computation.2 | async-start | bytes 131072 | tf_op jit(solution)/shard_map/all_to_all | solution.py:54
  26.1 12.3 %all-to-all-start.1 = ((bf16[64,4,1024]{2,0,1:T(8,128)(2,1)}), bf16[64,4,1024]{2,0,1:T(8,128)(2,1)S(1)}, u32[]{:S(2)}, u32[]{:S(2)}) async-start(bf16[64,4,1024]{2,0,1:T(8,128)(2,1)} %bitcast.347), calls=%async_computation.1 | async-start | bytes 1048576 | tf_op jit(solution)/shard_map/all_to_all | solution.py:52
  38.4 12.3 %all-to-all-start.3 = ((bf16[64,4,1024]{2,0,1:T(8,128)(2,1)}), bf16[64,4,1024]{2,0,1:T(8,128)(2,1)S(1)}, u32[]{:S(2)}, u32[]{:S(2)}) async-start(bf16[64,4,1024]{2,0,1:T(8,128)(2,1)} %bitcast.346), calls=%async_computation.3 | async-start | bytes 1048576 | tf_op jit(solution)/shard_map/all_to_all | solution.py:55
  43.1 7.6 %collective-permute-start = (bf16[1,256,1,128]{3,1,2,0:T(8,128)(2,1)S(1)}, bf16[1,256,1,128]{3,1,2,0:T(8,128)(2,1)S(1)}, u32[]{:S(2)}, u32[]{:S(2)}) collective-permute-start(bf16[1,256,1,128]{3,1,2,0:T(8,128)(2,1)S(1)} %bitcast.370), channel_id=1, source_target_pairs={{0,4},{4,0},{8,12},{12,8},{16,20},{20,16},{24,28},{28,24},{1,5},{5... | collective-permute-start | bytes 196616 | tf_op jit(solution)/shard_map/ppermute | solution.py:14
  45.2 19.9 %collective-permute-start.5 = (bf16[1,256,1,128]{3,1,2,0:T(8,128)(2,1)S(1)}, bf16[1,256,1,128]{3,1,2,0:T(8,128)(2,1)S(1)}, u32[]{:S(2)}, u32[]{:S(2)}) collective-permute-start(bf16[1,256,1,128]{3,1,2,0:T(8,128)(2,1)S(1)} %bitcast.376), channel_id=1, source_target_pairs={{0,16},{4,20},{8,24},{12,28},{16,0},{20,4},{24,8},{28,12},{1,17},{... | collective-permute-start | bytes 196616 | tf_op jit(solution)/shard_map/ppermute | solution.py:14
  47.8 9.2 %collective-permute-start.3 = (bf16[1,256,1,128]{3,1,2,0:T(8,128)(2,1)S(1)}, bf16[1,256,1,128]{3,1,2,0:T(8,128)(2,1)S(1)}, u32[]{:S(2)}, u32[]{:S(2)}) collective-permute-start(bf16[1,256,1,128]{3,1,2,0:T(8,128)(2,1)S(1)} %bitcast.377), channel_id=1, source_target_pairs={{0,8},{4,12},{8,0},{12,4},{16,24},{20,28},{24,16},{28,20},{1,9},{5... | collective-permute-start | bytes 196616 | tf_op jit(solution)/shard_map/ppermute | solution.py:14
  49.4 4.5 %collective-permute-start.1 = (bf16[1,256,1,128]{3,1,2,0:T(8,128)(2,1)S(1)}, bf16[1,256,1,128]{3,1,2,0:T(8,128)(2,1)S(1)}, u32[]{:S(2)}, u32[]{:S(2)}) collective-permute-start(bf16[1,256,1,128]{3,1,2,0:T(8,128)(2,1)S(1)} %bitcast.378), channel_id=1, source_target_pairs={{0,4},{4,0},{8,12},{12,8},{16,20},{20,16},{24,28},{28,24},{1,5},{5... | collective-permute-start | bytes 196616 | tf_op jit(solution)/shard_map/ppermute | solution.py:14
  49.9 13.1 %collective-permute-start.4 = (bf16[1,256,1,128]{3,1,2,0:T(8,128)(2,1)S(1)}, bf16[1,256,1,128]{3,1,2,0:T(8,128)(2,1)S(1)}, u32[]{:S(2)}, u32[]{:S(2)}) collective-permute-start(bf16[1,256,1,128]{3,1,2,0:T(8,128)(2,1)S(1)} %bitcast.371), channel_id=1, source_target_pairs={{0,16},{4,20},{8,24},{12,28},{16,0},{20,4},{24,8},{28,12},{1,17},{... | collective-permute-start | bytes 196616 | tf_op jit(solution)/shard_map/ppermute | solution.py:14
  50.3 3.0 %copy-start.2 = (f32[8,256]{1,0:T(8,128)S(1)}, f32[8,256]{1,0:T(8,128)}, u32[]{:S(2)}) copy-start(f32[8,256]{1,0:T(8,128)} %param.11) | copy-start | bytes 24580
  50.8 5.8 %collective-permute-start.2 = (bf16[1,256,1,128]{3,1,2,0:T(8,128)(2,1)S(1)}, bf16[1,256,1,128]{3,1,2,0:T(8,128)(2,1)S(1)}, u32[]{:S(2)}, u32[]{:S(2)}) collective-permute-start(bf16[1,256,1,128]{3,1,2,0:T(8,128)(2,1)S(1)} %bitcast.372), channel_id=1, source_target_pairs={{0,8},{4,12},{8,0},{12,4},{16,24},{20,28},{24,16},{28,20},{1,9},{5... | collective-permute-start | bytes 196616 | tf_op jit(solution)/shard_map/ppermute | solution.py:14
  55.0 22.4 %collective-permute-start.6 = (f32[1,256,1,128]{3,1,2,0:T(8,128)S(1)}, f32[1,256,1,128]{3,1,2,0:T(8,128)S(1)}, u32[]{:S(2)}, u32[]{:S(2)}) collective-permute-start(f32[1,256,1,128]{3,1,2,0:T(8,128)S(1)} %fusion.28), channel_id=1, source_target_pairs={{0,4},{4,0},{8,12},{12,8},{16,20},{20,16},{24,28},{28,24},{1,5},{5... | collective-permute-start | bytes 393224 | tf_op jit(solution)/shard_map/ppermute | solution.py:14
  58.7 18.7 %collective-permute-start.7 = (f32[1,256,1,128]{3,1,2,0:T(8,128)}, f32[1,256,1,128]{3,1,2,0:T(8,128)S(1)}, u32[]{:S(2)}, u32[]{:S(2)}) collective-permute-start(f32[1,256,1,128]{3,1,2,0:T(8,128)} %fusion.26), channel_id=1, source_target_pairs={{0,8},{4,12},{8,0},{12,4},{16,24},{20,28},{24,16},{28,20},{1,9},{5... | collective-permute-start | bytes 393224 | tf_op jit(solution)/shard_map/ppermute | solution.py:14
  61.4 10.4 %collective-permute-start.9 = (f32[1,256,1,128]{3,1,2,0:T(8,128)S(1)}, f32[1,256,1,128]{3,1,2,0:T(8,128)S(1)}, u32[]{:S(2)}, u32[]{:S(2)}) collective-permute-start(f32[1,256,1,128]{3,1,2,0:T(8,128)S(1)} %convolution_bitcast_fusion.2), channel_id=1, source_target_pairs={{0,4},{4,0},{8,12},{12,8},{16,20},{20,16},{24,28},{28,24},{1,5},{5... | collective-permute-start | bytes 393224 | tf_op jit(solution)/shard_map/ppermute | solution.py:14
  63.0 9.8 %collective-permute-start.10 = (f32[1,256,1,128]{3,1,2,0:T(8,128)S(1)}, f32[1,256,1,128]{3,1,2,0:T(8,128)S(1)}, u32[]{:S(2)}, u32[]{:S(2)}) collective-permute-start(f32[1,256,1,128]{3,1,2,0:T(8,128)S(1)} %convolution_bitcast_fusion.1), channel_id=1, source_target_pairs={{0,8},{4,12},{8,0},{12,4},{16,24},{20,28},{24,16},{28,20},{1,9},{5... | collective-permute-start | bytes 393224 | tf_op jit(solution)/shard_map/ppermute | solution.py:14
  65.1 7.7 %collective-permute-start.11 = (f32[1,256,1,128]{3,1,2,0:T(8,128)S(1)}, f32[1,256,1,128]{3,1,2,0:T(8,128)S(1)}, u32[]{:S(2)}, u32[]{:S(2)}) collective-permute-start(f32[1,256,1,128]{3,1,2,0:T(8,128)S(1)} %convolution_bitcast_fusion), channel_id=1, source_target_pairs={{0,16},{4,20},{8,24},{12,28},{16,0},{20,4},{24,8},{28,12},{1,17},{... | collective-permute-start | bytes 393224 | tf_op jit(solution)/shard_map/ppermute | solution.py:14
  71.8 7.5 %collective-permute-start.8 = (f32[1,256,1,128]{3,1,2,0:T(8,128)}, f32[1,256,1,128]{3,1,2,0:T(8,128)S(1)}, u32[]{:S(2)}, u32[]{:S(2)}) collective-permute-start(f32[1,256,1,128]{3,1,2,0:T(8,128)} %fusion.24), channel_id=1, source_target_pairs={{0,16},{4,20},{8,24},{12,28},{16,0},{20,4},{24,8},{28,12},{1,17},{... | collective-permute-start | bytes 393224 | tf_op jit(solution)/shard_map/ppermute | solution.py:14
  74.0 7.9 %all-to-all-start.7 = ((f32[4,64,128]{2,1,0:T(8,128)}), f32[4,64,128]{2,1,0:T(8,128)S(1)}, u32[]{:S(2)}, u32[]{:S(2)}) async-start(f32[4,64,128]{2,1,0:T(8,128)} %bitcast.90), calls=%async_computation.7 | async-start | bytes 262144 | tf_op jit(solution)/shard_map/all_to_all | solution.py:86
  81.9 7.9 %all-to-all-start.6 = ((f32[4,64,128]{2,1,0:T(8,128)}), f32[4,64,128]{2,1,0:T(8,128)S(1)}, u32[]{:S(2)}, u32[]{:S(2)}) async-start(f32[4,64,128]{2,1,0:T(8,128)} %bitcast.68), calls=%async_computation.6 | async-start | bytes 262144 | tf_op jit(solution)/shard_map/all_to_all | solution.py:83
  89.8 17.9 %all-to-all-start.5 = ((f32[4,64,1024]{2,1,0:T(8,128)}), f32[4,64,1024]{2,1,0:T(8,128)S(1)}, u32[]{:S(2)}, u32[]{:S(2)}) async-start(f32[4,64,1024]{2,1,0:T(8,128)} %all_to_all.117), calls=%async_computation.5 | async-start | bytes 2097152 | tf_op jit(solution)/shard_map/all_to_all | solution.py:80
where the time goes:
time: 110 us; the launch traced here: 109 us
  starting transfers between devices  44.9 us (41%)
  waiting for transfers between devices  35.4 us (32%)
  matrix products  16.3 us (15%)
  local copies, waits for them, and re-layouts  8.94 us (8%)
  other arithmetic  2.35 us (2%)
    ppermute x12, starting transfers between devices, from_partner(): lax.ppermute(value, axis, [(i, i ^ 1 << distance) for i in range(lax.axis...  17 us
    all_to_all x1, waiting for transfers between devices, on_device(): lax.all_to_all(grad_q.reshape(row_count, -1), 'head', split_axis=0, conca...  13.1 us
    all_to_all x1, waiting for transfers between devices, on_device(): lax.all_to_all(queries, 'head', split_axis=1, concat_axis=0, tiled=True)  7.92 us
    dot_general x4, matrix products, block_grads(): jnp.einsum('nhgbk,nkhd->nbhgd', dscores, key_blk, preferred_element_type=...  5.48 us
    all_to_all x1, starting transfers between devices, on_device(): lax.all_to_all(dot_before, 'head', split_axis=1, concat_axis=0, tiled=True)  4.24 us
    dot_general x4, matrix products, block_grads(): jnp.einsum('nhgbk,nbhgd->nkhd', dscores, query_blk, preferred_element_typ...  3.69 us
    all_to_all x1, starting transfers between devices, on_device(): lax.all_to_all(grad_q.reshape(row_count, -1), 'head', split_axis=0, conca...  3.52 us
    all_to_all x1, starting transfers between devices, on_device(): lax.all_to_all(queries, 'head', split_axis=1, concat_axis=0, tiled=True)  3.47 us
  transfers between devices with their start and end apart: 20, of which 9 were waited for; matrix products, arithmetic and copies ran while one was open for 21% of the time, Pallas kernels for 0%

commit v1 on v0

v1 whole, which is shorter than its diff:
```python
import functools
import math

import jax
import jax.numpy as jnp
from jax import lax
from jax.experimental import pallas as pl
from jax.experimental.pallas import tpu as pltpu
from jax.sharding import PartitionSpec as P

HEAD_DIM = 128
GROUP = 8
DOT_ROWS = 32

F32 = jnp.float32
BF16 = jnp.bfloat16


def dot_nt(a, b):
    return lax.dot_general(a, b, (((1,), (1,)), ((), ())), preferred_element_type=F32)


def dot_nn(a, b):
    return lax.dot_general(a, b, (((1,), (0,)), ((), ())), preferred_element_type=F32)


def dot_tn(a, b):
    return lax.dot_general(a, b, (((0,), (0,)), ((), ())), preferred_element_type=F32)


def vmem_specs(count):
    return [pl.BlockSpec(memory_space=pltpu.VMEM) for _ in range(count)]


def call(kernel, out_shapes, place, *args):
    return pl.pallas_call(
        kernel,
        out_shape=out_shapes,
        in_specs=[pl.BlockSpec(memory_space=pltpu.SMEM)] + vmem_specs(len(args)),
        out_specs=vmem_specs(len(out_shapes)),
    )(place, *args)


def pack_kernel(parts, place, q_ref, g_ref, o_ref, k_ref, v_ref, *outs):
    qg_refs, kv_refs = outs[:parts], outs[parts:]
    own = place[0]
    rows = q_ref.shape[0]
    width = GROUP * HEAD_DIM
    lane = lax.broadcasted_iota(jnp.int32, (2 * rows, HEAD_DIM), 1)
    dots = jnp.zeros((2 * rows, HEAD_DIM), F32)
    for m in range(parts):
        peer = own ^ m
        col = pl.multiple_of(peer * HEAD_DIM, HEAD_DIM)
        kv_refs[m][:rows, :] = k_ref[:, pl.ds(col, HEAD_DIM)]
        kv_refs[m][rows:, :] = v_ref[:, pl.ds(col, HEAD_DIM)]
        sums = []
        for j in range(GROUP):
            col = pl.multiple_of(peer * width + j * HEAD_DIM, HEAD_DIM)
            qg_refs[m][j * rows : (j + 1) * rows, :] = q_ref[:, pl.ds(col, HEAD_DIM)]
            grad = g_ref[:, pl.ds(col, HEAD_DIM)]
            qg_refs[m][(GROUP + j) * rows : (GROUP + j + 1) * rows, :] = grad
            prod = grad.astype(F32) * o_ref[:, pl.ds(col, HEAD_DIM)].astype(F32)
            sums.append(jnp.sum(prod, axis=1, keepdims=True))
        for j in range(GROUP // 2):
            pair = jnp.concatenate([sums[2 * j], sums[2 * j + 1]], axis=0)
            dots = jnp.where(lane == 8 * m + j, pair, dots)
    turned = dots.T
    for m in range(parts):
        full = turned[8 * m : 8 * m + 8, :]
        high = full.astype(BF16).astype(F32)
        mid = (full - high).astype(BF16).astype(F32)
        low = (full - high) - mid
        qg_refs[m][2 * GROUP * rows :, :] = jnp.concatenate(
            [high, mid, low, jnp.zeros_like(high)], axis=0
        ).astype(BF16)


def join_kernel(parts, place, *refs):
    pieces, out = refs[:parts], refs[parts]
    rows = pieces[0].shape[0] // 2
    for m in range(parts):
        out[m * rows : (m + 1) * rows, :] = pieces[m][:rows, :]
        out[(parts + m) * rows : (parts + m + 1) * rows, :] = pieces[m][rows:, :]


def row_of(stack):
    return jnp.concatenate([stack[j : j + 1, :] for j in range(GROUP // 2)], axis=1)


def chunk_kernel(pieces, levels, has_acc, last, place, *refs):
    count = len(pieces)
    qg_refs, refs = refs[:count], refs[count:]
    lse_ref, refs = refs[0], refs[1:]
    kv_refs, refs = refs[:levels], refs[levels:]
    if has_acc:
        acc_refs, refs = refs[:levels], refs[levels:]
    dq_refs, dkv_refs = refs[:count], refs[count:]
    scale = 1.0 / math.sqrt(HEAD_DIM)
    span = (qg_refs[0].shape[0] - DOT_ROWS) // 2
    block = kv_refs[0].shape[0] // 2
    dk = [acc_refs[b][:block, :] if has_acc else None for b in range(levels)]
    dv = [acc_refs[b][block:, :] if has_acc else None for b in range(levels)]
    for i, m in enumerate(pieces):
        query = qg_refs[i][:span, :]
        grad = qg_refs[i][span : 2 * span, :]
        split = qg_refs[i][2 * span :, :].astype(F32)
        dots = row_of((split[:8] + split[8:16]) + split[16:24])
        lse = row_of(lse_ref[place[0] ^ m])
        dq = None
        for b in range(levels):
            keys = kv_refs[b][:block, :]
            values = kv_refs[b][block:, :]
            probs = jnp.exp(dot_nt(keys, query) * scale - lse)
            dprobs = dot_nt(values, grad)
            dscores = (probs * (dprobs - dots)).astype(BF16)
            part_v = dot_nn(probs.astype(BF16), grad)
            part_k = dot_nn(dscores, query)
            part_q = dot_tn(keys, dscores)
            dv[b] = part_v if dv[b] is None else dv[b] + part_v
            dk[b] = part_k if dk[b] is None else dk[b] + part_k
            dq = part_q if dq is None else dq + part_q
        dq_refs[i][...] = (dq.T * scale).astype(dq_refs[i].dtype)
    for b in range(levels):
        dkv_refs[b][:block, :] = (dk[b] * scale if last else dk[b]).astype(dkv_refs[b].dtype)
        dkv_refs[b][block:, :] = dv[b].astype(dkv_refs[b].dtype)


def total_kernel(parts, levels, place, *refs):
    terms, outs = refs[:levels], refs[levels:]
    total = terms[0][...]
    for term in terms[1:]:
        total = total + term[...].astype(F32)
    rows = total.shape[0] // (2 * parts)
    for m in range(parts):
        outs[m][:rows, :] = total[m * rows : (m + 1) * rows].astype(outs[m].dtype)
        outs[m][rows:, :] = total[(parts + m) * rows : (parts + m + 1) * rows].astype(
            outs[m].dtype
        )


def unpack_q_kernel(parts, place, *refs):
    pieces, out = refs[:parts], refs[parts]
    rows = out.shape[0]
    width = GROUP * HEAD_DIM
    for m in range(parts):
        for j in range(GROUP):
            col = pl.multiple_of((place[0] ^ m) * width + j * HEAD_DIM, HEAD_DIM)
            out[:, pl.ds(col, HEAD_DIM)] = pieces[m][j * rows : (j + 1) * rows, :].astype(F32)


def unpack_kv_kernel(parts, place, *refs):
    pieces, out_k, out_v = refs[:parts], refs[parts], refs[parts + 1]
    rows = out_k.shape[0]
    for m in range(parts):
        col = pl.multiple_of((place[0] ^ m) * HEAD_DIM, HEAD_DIM)
        out_k[:, pl.ds(col, HEAD_DIM)] = pieces[m][:rows, :].astype(F32)
        out_v[:, pl.ds(col, HEAD_DIM)] = pieces[m][rows:, :].astype(F32)


def swap(value, axis, distance):
    return lax.ppermute(value, axis, [(i, i ^ distance) for i in range(lax.axis_size(axis))])


def on_device(queries, key_rows, value_rows, attn_out, out_grad, logsumexp):
    parts = lax.axis_size("head")
    levels = lax.axis_size("ctx").bit_length()
    rows = queries.shape[0]
    block = rows * parts
    span = rows * GROUP
    place = lax.axis_index("head").astype(jnp.int32).reshape(1)
    shape = jax.ShapeDtypeStruct

    packed = call(
        functools.partial(pack_kernel, parts),
        [shape((2 * span + DOT_ROWS, HEAD_DIM), BF16)] * parts
        + [shape((2 * rows, HEAD_DIM), BF16)] * parts,
        place,
        queries,
        out_grad,
        attn_out,
        key_rows,
        value_rows,
    )
    qg, kv = list(packed[:parts]), list(packed[parts:])
    kv = [kv[0]] + [swap(kv[m], "head", m) for m in range(1, parts)]
    qg = [qg[0]] + [swap(qg[m], "head", m) for m in range(1, parts)]
    lse = (
        logsumexp.reshape(GROUP // 2, 2, parts, rows)
        .transpose(2, 0, 1, 3)
        .reshape(parts, GROUP // 2, 2 * rows)
    )
    (kv_own,) = call(
        functools.partial(join_kernel, parts), [shape((2 * block, HEAD_DIM), BF16)], place, *kv
    )
    kv_all = [kv_own] + [swap(kv_own, "ctx", 1 << b) for b in range(levels - 1)]

    groups = [(0, 1)] + [(m,) for m in range(2, parts)]
    dq = []
    acc = []
    for step, pieces in enumerate(groups):
        last = step == len(groups) - 1
        outs = [shape((span, HEAD_DIM), F32 if m == 0 else BF16) for m in pieces]
        outs += [
            shape((2 * block, HEAD_DIM), BF16 if last and b > 0 else F32) for b in range(levels)
        ]
        result = call(
            functools.partial(chunk_kernel, pieces, levels, step > 0, last),
            outs,
            place,
            *[qg[m] for m in pieces],
            lse,
            *kv_all,
            *acc,
        )
        for i, m in enumerate(pieces):
            dq.append(result[i] if m == 0 else swap(result[i], "head", m))
        acc = list(result[len(pieces) :])

    terms = [acc[0]] + [swap(acc[b + 1], "ctx", 1 << b) for b in range(levels - 1)]
    dkv = call(
        functools.partial(total_kernel, parts, levels),
        [shape((2 * rows, HEAD_DIM), F32 if m == 0 else BF16) for m in range(parts)],
        place,
        *terms,
    )
    dkv = [dkv[0]] + [swap(dkv[m], "head", m) for m in range(1, parts)]
    (grad_q,) = call(
        functools.partial(unpack_q_kernel, parts), [shape(queries.shape, F32)], place, *dq
    )
    grad_k, grad_v = call(
        functools.partial(unpack_kv_kernel, parts),
        [shape(key_rows.shape, F32), shape(value_rows.shape, F32)],
        place,
        *dkv,
    )
    return (grad_q, grad_k, grad_v)


def solution(mesh):
    rows = P(("ctx", "head"), None)
    return jax.shard_map(
        on_device,
        mesh=mesh,
        in_specs=(rows, rows, rows, rows, rows, P("head", "ctx")),
        out_specs=(rows, rows, rows),
        check_vma=False,
    )
```

time: 110 us -> 63.6 us (0.58)
  starting transfers between devices: 44.9 us -> 20.8 us
  Pallas kernels: 0 us -> 22.9 us
  waiting for transfers between devices: 35.4 us -> 13.3 us
  matrix products: 16.3 us -> 0 us
  local copies, waits for them, and re-layouts: 8.94 us -> 5.46 us
  other arithmetic: 2.35 us -> 0 us
    all_to_all x8 -> x0, waiting for transfers between devices: 33.5 us -> none  [the longest x1 13.1 us: on_device(): lax.all_to_all(grad_q.reshape(row_count, -1), 'head', split_axis=0, conca...]
    all_to_all x8 -> x0, starting transfers between devices: 27.9 us -> none  [the longest x1 4.24 us: on_device(): lax.all_to_all(dot_before, 'head', split_axis=1, concat_axis=0, tiled=True)]
    pallas_call x0 -> x8, Pallas kernels: none -> 22.9 us  [call(): pl.pallas_call(kernel, out_shape=out_shapes, in_specs=[pl.BlockSpec(memor...]
    dot_general x20 -> x0, matrix products: 16.3 us -> none  [the longest x4 5.48 us: block_grads(): jnp.einsum('nhgbk,nkhd->nbhgd', dscores, key_blk, preferred_element_type=...]
    ppermute x12 -> x18, waiting for transfers between devices: 1.93 us -> 13.3 us  [swap(): lax.ppermute(value, axis, [(i, i ^ distance) for i in range(lax.axis_size...]
    all_to_all x11 -> x0, local copies, waits for them, and re-layouts: 6.99 us -> none  [the longest x2 2.17 us: on_device(): lax.all_to_all(grad_q.reshape(row_count, -1), 'head', split_axis=0, conca...]
    ppermute x12 -> x18, starting transfers between devices: 17 us -> 20.8 us  [swap(): lax.ppermute(value, axis, [(i, i ^ distance) for i in range(lax.axis_size...]
    unnamed x16 -> x42, local copies, waits for them, and re-layouts: 1.18 us -> 4.69 us
  transfers between devices with their start and end apart: 20 -> 18, of which waited for: 9 -> 5; matrix products, arithmetic and copies ran while one was open for 21% -> 1% of each run, Pallas kernels for 0% -> 23%
where the time goes in v1:
time: 63.6 us; the launch traced here: 63.2 us
  Pallas kernels  22.9 us (36%)
  starting transfers between devices  20.8 us (33%)
  waiting for transfers between devices  13.3 us (21%)
  local copies, waits for them, and re-layouts  5.46 us (9%)
  between operations  0.75 us (1%)
    pallas_call x8, Pallas kernels, call(): pl.pallas_call(kernel, out_shape=out_shapes, in_specs=[pl.BlockSpec(memor...  22.9 us
    ppermute x18, starting transfers between devices, swap(): lax.ppermute(value, axis, [(i, i ^ distance) for i in range(lax.axis_size...  20.8 us
    ppermute x18, waiting for transfers between devices, swap(): lax.ppermute(value, axis, [(i, i ^ distance) for i in range(lax.axis_size...  13.3 us
    unnamed x42, local copies, waits for them, and re-layouts  4.69 us
  transfers between devices with their start and end apart: 18, of which 5 were waited for; matrix products, arithmetic and copies ran while one was open for 1% of the time, Pallas kernels for 23%

profile of v1, /device:TPU:0, one launch (start us, length us, event | category | flops | bytes accessed | tf_op | source)
XLA Modules:
  0.0 63.2 jit_solution(8391770113236862264)
XLA Ops:
  0.6 3.3 %shard_map.85 = (bf16[1056,128]{1,0:T(8,128)(2,1)}, bf16[1056,128]{1,0:T(8,128)(2,1)}, bf16[1056,128]{1,0:T(8,128)(2,1)}, bf16[1056,128]{1,0:T(8,128)(2,1)}, bf1...) custom-call(s32[1]{0:T(128)} %bitcast.place, ...), custom_call_target="tpu_custom_call" | custom-call | tf_op jit(solution)/shard_map/pallas_call | solution.py:36
  4.4 2.5 %collective-permute-start.2 = (bf16[128,128]{1,0:T(8,128)(2,1)}, bf16[128,128]{1,0:T(8,128)(2,1)S(1)}, u32[]{:S(2)}, u32[]{:S(2)}) collective-permute-start(bf16[128,128]{1,0:T(8,128)(2,1)} %get-tuple-element.37), channel_id=1, source_target_pairs={{0,2},{1,3},{2,0},{3,1},{4,6},{5,7},{6,4},{7,5},{8,10},{9,11},{10,... | collective-permute-start | bytes 98312 | tf_op jit(solution)/shard_map/ppermute | solution.py:161
  7.2 1.9 %collective-permute-start.8 = (bf16[1056,128]{1,0:T(8,128)(2,1)}, bf16[1056,128]{1,0:T(8,128)(2,1)S(1)}, u32[]{:S(2)}, u32[]{:S(2)}) collective-permute-start(bf16[1056,128]{1,0:T(8,128)(2,1)} %get-tuple-element.41), channel_id=1, source_target_pairs={{0,2},{1,3},{2,0},{3,1},{4,6},{5,7},{6,4},{7,5},{8,10},{9,11},{10,... | collective-permute-start | bytes 811016 | tf_op jit(solution)/shard_map/ppermute | solution.py:161
  9.2 1.4 %collective-permute-done.3.refs_3_ = bf16[128,128]{1,0:T(8,128)(2,1)S(1)} collective-permute-done((bf16[128,128]{1,0:T(8,128)(2,1)}, bf16[128,128]{1,0:T(8,128)(2,1)S(1)}, u32[]{:S(2)}, u32[]{:S(2)}) %collective-permute-start.3) | collective-permute-done | bytes 32800 | tf_op jit(solution)/shard_map/ppermute | solution.py:161
  10.6 0.6 copy-done.17
  11.1 1.5 %shard_map.86.refs_3_.refs_2_ = bf16[512,128]{1,0:T(8,128)(2,1)} custom-call(s32[1]{0:T(128)} %bitcast.place, bf16[128,128]{1,0:T(8,128)(2,1)} %get-tuple-element.35.refs_0_, bf16[128,128]{1,0:T(8,128)(2,1)} %copy-done.15, bf16[128,128]{1,0:T(8,128)(2,1)} %copy-done.16, bf16[128,128]{1,0:T(8,128)(2,1)} %copy-done.17), custom_call_target="tpu_custom_call" | custom-call | tf_op jit(solution)/shard_map/pallas_call | solution.py:36
  12.6 2.6 %collective-permute-start.6 = (bf16[512,128]{1,0:T(8,128)(2,1)}, bf16[512,128]{1,0:T(8,128)(2,1)S(1)}, u32[]{:S(2)}, u32[]{:S(2)}) collective-permute-start(bf16[512,128]{1,0:T(8,128)(2,1)} %shard_map.86.refs_3_.refs_2_), channel_id=1, source_target_pairs={{0,16},{4,20},{8,24},{12,28},{16,0},{20,4},{24,8},{28,12},{1,17},{... | collective-permute-start | bytes 393224 | tf_op jit(solution)/shard_map/ppermute | solution.py:161
  15.2 1.6 %collective-permute-start.5 = (bf16[512,128]{1,0:T(8,128)(2,1)}, bf16[512,128]{1,0:T(8,128)(2,1)S(1)}, u32[]{:S(2)}, u32[]{:S(2)}) collective-permute-start(bf16[512,128]{1,0:T(8,128)(2,1)} %shard_map.86.refs_3_.refs_2_), channel_id=1, source_target_pairs={{0,8},{4,12},{8,0},{12,4},{16,24},{20,28},{24,16},{28,20},{1,9},{5... | collective-permute-start | bytes 393224 | tf_op jit(solution)/shard_map/ppermute | solution.py:161
  16.8 5.7 %collective-permute-done.6.refs_6_.refs_5_ = bf16[512,128]{1,0:T(8,128)(2,1)S(1)} collective-permute-done((bf16[512,128]{1,0:T(8,128)(2,1)}, bf16[512,128]{1,0:T(8,128)(2,1)S(1)}, u32[]{:S(2)}, u32[]{:S(2)}) %collective-permute-start.6) | collective-permute-done | bytes 131104 | tf_op jit(solution)/shard_map/ppermute | solution.py:161
  22.5 1.5 %collective-permute-start.4 = (bf16[512,128]{1,0:T(8,128)(2,1)}, bf16[512,128]{1,0:T(8,128)(2,1)S(1)}, u32[]{:S(2)}, u32[]{:S(2)}) collective-permute-start(bf16[512,128]{1,0:T(8,128)(2,1)} %shard_map.86.refs_3_.refs_2_), channel_id=1, source_target_pairs={{0,4},{4,0},{8,12},{12,8},{16,20},{20,16},{24,28},{28,24},{1,5},{5... | collective-permute-start | bytes 393224 | tf_op jit(solution)/shard_map/ppermute | solution.py:161
  24.1 0.7 %reshape.17.refs_2_.refs_1_ = f32[4,4,128]{2,1,0:T(4,128)} reshape(f32[4,4,2,64]{3,2,1,0:T(2,128)S(1)} %bitcast.4) | data formatting | bytes 16384 | tf_op jit(solution)/shard_map/reshape | solution.py:190
  24.8 2.9 %collective-permute-done.4.refs_4_.refs_3_ = bf16[512,128]{1,0:T(8,128)(2,1)S(1)} collective-permute-done((bf16[512,128]{1,0:T(8,128)(2,1)}, bf16[512,128]{1,0:T(8,128)(2,1)S(1)}, u32[]{:S(2)}, u32[]{:S(2)}) %collective-permute-start.4) | collective-permute-done | bytes 131104 | tf_op jit(solution)/shard_map/ppermute | solution.py:161
  27.7 0.6 %copy-done.2 = bf16[512,128]{1,0:T(8,128)(2,1)} copy-done((bf16[512,128]{1,0:T(8,128)(2,1)}, bf16[512,128]{1,0:T(8,128)(2,1)S(1)}, u32[]{:S(2)}) %copy-start.2) | copy-done | bytes 131096
  28.5 5.2 %shard_map.87 = (f32[512,128]{1,0:T(8,128)}, bf16[512,128]{1,0:T(8,128)(2,1)}, f32[512,128]{1,0:T(8,128)}, f32[512,128]{1,0:T(8,128)}, f32[512,128]{1,0:T(8,128)}, /*index=5*/f32[512,128]{1,0:T(8,128)}) custom-call(s32[1]{0:T(128)} %bitcast.place, bf16[1056,128]{1,0:T(8,128)(2,1)} %get-tuple-element.33.refs_0_, bf16[1056,128]{1,0:T(8,128)(2,1)} %copy-done.5, ...), custom_call_target="tpu_custom_call" | custom-call | tf_op jit(solution)/shard_map/pallas_call | solution.py:36
  33.7 0.7 %copy-done.4 = bf16[1056,128]{1,0:T(8,128)(2,1)} copy-done((bf16[1056,128]{1,0:T(8,128)(2,1)}, bf16[1056,128]{1,0:T(8,128)(2,1)S(1)}, u32[]{:S(2)}) %copy-start.4) | copy-done | bytes 270360
  34.4 3.7 %shard_map.88 = (bf16[512,128]{1,0:T(8,128)(2,1)}, f32[512,128]{1,0:T(8,128)}, f32[512,128]{1,0:T(8,128)}, f32[512,128]{1,0:T(8,128)}, f32[512,128]{1,0:T(8,128)}) custom-call(s32[1]{0:T(128)} %bitcast.place, bf16[1056,128]{1,0:T(8,128)(2,1)} %copy-done.4, f32[4,4,128]{2,1,0:T(4,128)} %reshape.17.refs_2_.refs_1_, ...), custom_call_target="tpu_custom_call" | custom-call | tf_op jit(solution)/shard_map/pallas_call | solution.py:36
  38.1 0.7 %copy-done.3 = bf16[1056,128]{1,0:T(8,128)(2,1)} copy-done((bf16[1056,128]{1,0:T(8,128)(2,1)}, bf16[1056,128]{1,0:T(8,128)(2,1)S(1)}, u32[]{:S(2)}) %copy-start.3) | copy-done | bytes 270360
  38.8 3.7 %shard_map.89 = (bf16[512,128]{1,0:T(8,128)(2,1)}, f32[512,128]{1,0:T(8,128)}, bf16[512,128]{1,0:T(8,128)(2,1)}, bf16[512,128]{1,0:T(8,128)(2,1)}, bf16[512,128]{1,0:T(8,128)(2,1)}) custom-call(s32[1]{0:T(128)} %bitcast.place, bf16[1056,128]{1,0:T(8,128)(2,1)} %copy-done.3, f32[4,4,128]{2,1,0:T(4,128)} %reshape.17.refs_2_.refs_1_, ...), custom_call_target="tpu_custom_call" | custom-call | tf_op jit(solution)/shard_map/pallas_call | solution.py:36
  42.5 1.5 %collective-permute-start.12 = (bf16[512,128]{1,0:T(8,128)(2,1)}, bf16[512,128]{1,0:T(8,128)(2,1)S(1)}, u32[]{:S(2)}, u32[]{:S(2)}) collective-permute-start(bf16[512,128]{1,0:T(8,128)(2,1)} %get-tuple-element.54), channel_id=1, source_target_pairs={{0,4},{4,0},{8,12},{12,8},{16,20},{20,16},{24,28},{28,24},{1,5},{5... | collective-permute-start | bytes 393224 | tf_op jit(solution)/shard_map/ppermute | solution.py:161
  44.0 1.2 %collective-permute-start.13 = (bf16[512,128]{1,0:T(8,128)(2,1)}, bf16[512,128]{1,0:T(8,128)(2,1)S(1)}, u32[]{:S(2)}, u32[]{:S(2)}) collective-permute-start(bf16[512,128]{1,0:T(8,128)(2,1)} %get-tuple-element.55), channel_id=1, source_target_pairs={{0,8},{4,12},{8,0},{12,4},{16,24},{20,28},{24,16},{28,20},{1,9},{5... | collective-permute-start | bytes 393224 | tf_op jit(solution)/shard_map/ppermute | solution.py:161
  45.1 3.3 %collective-permute-start.14 = (bf16[512,128]{1,0:T(8,128)(2,1)}, bf16[512,128]{1,0:T(8,128)(2,1)S(1)}, u32[]{:S(2)}, u32[]{:S(2)}) collective-permute-start(bf16[512,128]{1,0:T(8,128)(2,1)} %get-tuple-element.56), channel_id=1, source_target_pairs={{0,16},{4,20},{8,24},{12,28},{16,0},{20,4},{24,8},{28,12},{1,17},{... | collective-permute-start | bytes 393224 | tf_op jit(solution)/shard_map/ppermute | solution.py:161
  48.4 0.7 %collective-permute-start.11 = (bf16[512,128]{1,0:T(8,128)(2,1)}, bf16[512,128]{1,0:T(8,128)(2,1)S(1)}, u32[]{:S(2)}, u32[]{:S(2)}) collective-permute-start(bf16[512,128]{1,0:T(8,128)(2,1)} %get-tuple-element.52), channel_id=1, source_target_pairs={{0,3},{1,2},{2,1},{3,0},{4,7},{5,6},{6,5},{7,4},{8,11},{9,10},{10,... | collective-permute-start | bytes 393224 | tf_op jit(solution)/shard_map/ppermute | solution.py:161
  49.1 1.5 %collective-permute-start.9 = (bf16[512,128]{1,0:T(8,128)(2,1)S(1)}, bf16[512,128]{1,0:T(8,128)(2,1)S(1)}, u32[]{:S(2)}, u32[]{:S(2)}) collective-permute-start(bf16[512,128]{1,0:T(8,128)(2,1)S(1)} %copy-done.20), channel_id=1, source_target_pairs={{0,2},{1,3},{2,0},{3,1},{4,6},{5,7},{6,4},{7,5},{8,10},{9,11},{10,... | collective-permute-start | bytes 393224 | tf_op jit(solution)/shard_map/ppermute | solution.py:161
  50.8 3.0 %collective-permute-done.14.refs_3_ = bf16[512,128]{1,0:T(8,128)(2,1)S(1)} collective-permute-done((bf16[512,128]{1,0:T(8,128)(2,1)}, bf16[512,128]{1,0:T(8,128)(2,1)S(1)}, u32[]{:S(2)}, u32[]{:S(2)}) %collective-permute-start.14) | collective-permute-done | bytes 131104 | tf_op jit(solution)/shard_map/ppermute | solution.py:161
  53.8 0.6 %copy-done.11 = bf16[512,128]{1,0:T(8,128)(2,1)} copy-done((bf16[512,128]{1,0:T(8,128)(2,1)}, bf16[512,128]{1,0:T(8,128)(2,1)S(1)}, u32[]{:S(2)}) %copy-start.11) | copy-done | bytes 131096
  54.5 1.8 %shard_map.91 = (f32[128,128]{1,0:T(8,128)}, bf16[128,128]{1,0:T(8,128)(2,1)}, bf16[128,128]{1,0:T(8,128)(2,1)}, bf16[128,128]{1,0:T(8,128)(2,1)}) custom-call(s32[1]{0:T(128)} %bitcast.place, f32[512,128]{1,0:T(8,128)} %get-tuple-element.53.refs_0_, bf16[512,128]{1,0:T(8,128)(2,1)} %copy-done.9, bf16[512,128]{1,0:T(8,128)(2,1)} %copy-done.10, ...), custom_call_target="tpu_custom_call" | custom-call | tf_op jit(solution)/shard_map/pallas_call | solution.py:36
  56.2 0.6 collective-permute-start.16
  56.8 1.3 %collective-permute-start.17 = (bf16[128,128]{1,0:T(8,128)(2,1)}, bf16[128,128]{1,0:T(8,128)(2,1)S(1)}, u32[]{:S(2)}, u32[]{:S(2)}) collective-permute-start(bf16[128,128]{1,0:T(8,128)(2,1)} %get-tuple-element.60), channel_id=1, source_target_pairs={{0,3},{1,2},{2,1},{3,0},{4,7},{5,6},{6,5},{7,4},{8,11},{9,10},{10,... | collective-permute-start | bytes 98312 | tf_op jit(solution)/shard_map/ppermute | solution.py:161
  58.1 0.6 copy-done.7
  58.8 2.2 %shard_map.90 = f32[64,4096]{1,0:T(8,128)} custom-call(s32[1]{0:T(128)} %bitcast.place, f32[512,128]{1,0:T(8,128)} %get-tuple-element.39.refs_0_, bf16[512,128]{1,0:T(8,128)(2,1)} %copy-done.6, bf16[512,128]{1,0:T(8,128)(2,1)} %copy-done.8, bf16[512,128]{1,0:T(8,128)(2,1)} %copy-done.7), custom_call_target="tpu_custom_call" | custom-call | tf_op jit(solution)/shard_map/pallas_call | solution.py:36
  61.0 0.6 copy-done.12
  61.6 1.6 %shard_map.92 = (f32[64,512]{1,0:T(8,128)}, f32[64,512]{1,0:T(8,128)}) custom-call(s32[1]{0:T(128)} %bitcast.place, f32[128,128]{1,0:T(8,128)} %get-tuple-element.57.refs_0_, bf16[128,128]{1,0:T(8,128)(2,1)} %copy-done.12, bf16[128,128]{1,0:T(8,128)(2,1)} %copy-done.13, bf16[128,128]{1,0:T(8,128)(2,1)} %copy-done.14), custom_call_target="tpu_custom_call" | custom-call | tf_op jit(solution)/shard_map/pallas_call | solution.py:36
  (57 shorter events, 1.3 us)
Async XLA Ops:
  3.9 5.2 %collective-permute-start.1 = (bf16[128,128]{1,0:T(8,128)(2,1)}, bf16[128,128]{1,0:T(8,128)(2,1)S(1)}, u32[]{:S(2)}, u32[]{:S(2)}) collective-permute-start(bf16[128,128]{1,0:T(8,128)(2,1)} %get-tuple-element.36), channel_id=1, source_target_pairs={{0,1},{1,0},{2,3},{3,2},{4,5},{5,4},{6,7},{7,6},{8,9},{9,8},{10,11... | collective-permute-start | bytes 98312 | tf_op jit(solution)/shard_map/ppermute | solution.py:161
  4.4 4.7 %collective-permute-start.2 = (bf16[128,128]{1,0:T(8,128)(2,1)}, bf16[128,128]{1,0:T(8,128)(2,1)S(1)}, u32[]{:S(2)}, u32[]{:S(2)}) collective-permute-start(bf16[128,128]{1,0:T(8,128)(2,1)} %get-tuple-element.37), channel_id=1, source_target_pairs={{0,2},{1,3},{2,0},{3,1},{4,6},{5,7},{6,4},{7,5},{8,10},{9,11},{10,... | collective-permute-start | bytes 98312 | tf_op jit(solution)/shard_map/ppermute | solution.py:161
  7.0 3.6 %collective-permute-start.3 = (bf16[128,128]{1,0:T(8,128)(2,1)}, bf16[128,128]{1,0:T(8,128)(2,1)S(1)}, u32[]{:S(2)}, u32[]{:S(2)}) collective-permute-start(bf16[128,128]{1,0:T(8,128)(2,1)} %get-tuple-element.38), channel_id=1, source_target_pairs={{0,3},{1,2},{2,1},{3,0},{4,7},{5,6},{6,5},{7,4},{8,11},{9,10},{10,... | collective-permute-start | bytes 98312 | tf_op jit(solution)/shard_map/ppermute | solution.py:161
  7.0 20.7 %collective-permute-start = (bf16[1056,128]{1,0:T(8,128)(2,1)}, bf16[1056,128]{1,0:T(8,128)(2,1)S(1)}, u32[]{:S(2)}, u32[]{:S(2)}) collective-permute-start(bf16[1056,128]{1,0:T(8,128)(2,1)} %get-tuple-element.34), channel_id=1, source_target_pairs={{0,1},{1,0},{2,3},{3,2},{4,5},{5,4},{6,7},{7,6},{8,9},{9,8},{10,11... | collective-permute-start | bytes 811016 | tf_op jit(solution)/shard_map/ppermute | solution.py:161
  7.2 26.5 %collective-permute-start.8 = (bf16[1056,128]{1,0:T(8,128)(2,1)}, bf16[1056,128]{1,0:T(8,128)(2,1)S(1)}, u32[]{:S(2)}, u32[]{:S(2)}) collective-permute-start(bf16[1056,128]{1,0:T(8,128)(2,1)} %get-tuple-element.41), channel_id=1, source_target_pairs={{0,2},{1,3},{2,0},{3,1},{4,6},{5,7},{6,4},{7,5},{8,10},{9,11},{10,... | collective-permute-start | bytes 811016 | tf_op jit(solution)/shard_map/ppermute | solution.py:161
  9.1 1.4 %copy-start.15 = (bf16[128,128]{1,0:T(8,128)(2,1)}, bf16[128,128]{1,0:T(8,128)(2,1)S(1)}, u32[]{:S(2)}) copy-start(bf16[128,128]{1,0:T(8,128)(2,1)S(1)} %collective-permute-done.1.refs_1_) | copy-start | bytes 98308
  9.1 28.9 %collective-permute-start.10 = (bf16[1056,128]{1,0:T(8,128)(2,1)}, bf16[1056,128]{1,0:T(8,128)(2,1)S(1)}, u32[]{:S(2)}, u32[]{:S(2)}) collective-permute-start(bf16[1056,128]{1,0:T(8,128)(2,1)} %get-tuple-element.47), channel_id=1, source_target_pairs={{0,3},{1,2},{2,1},{3,0},{4,7},{5,6},{6,5},{7,4},{8,11},{9,10},{10,... | collective-permute-start | bytes 811016 | tf_op jit(solution)/shard_map/ppermute | solution.py:161
  9.2 1.4 %copy-start.16 = (bf16[128,128]{1,0:T(8,128)(2,1)}, bf16[128,128]{1,0:T(8,128)(2,1)S(1)}, u32[]{:S(2)}) copy-start(bf16[128,128]{1,0:T(8,128)(2,1)S(1)} %collective-permute-done.2.refs_2_) | copy-start | bytes 98308
  11.1 12.9 %copy-start.18 = (f32[8,256]{1,0:T(8,128)S(1)}, f32[8,256]{1,0:T(8,128)}, u32[]{:S(2)}) copy-start(f32[8,256]{1,0:T(8,128)} %param.11) | copy-start | bytes 24580
  12.6 9.9 %collective-permute-start.6 = (bf16[512,128]{1,0:T(8,128)(2,1)}, bf16[512,128]{1,0:T(8,128)(2,1)S(1)}, u32[]{:S(2)}, u32[]{:S(2)}) collective-permute-start(bf16[512,128]{1,0:T(8,128)(2,1)} %shard_map.86.refs_3_.refs_2_), channel_id=1, source_target_pairs={{0,16},{4,20},{8,24},{12,28},{16,0},{20,4},{24,8},{28,12},{1,17},{... | collective-permute-start | bytes 393224 | tf_op jit(solution)/shard_map/ppermute | solution.py:161
  15.2 9.6 %collective-permute-start.5 = (bf16[512,128]{1,0:T(8,128)(2,1)}, bf16[512,128]{1,0:T(8,128)(2,1)S(1)}, u32[]{:S(2)}, u32[]{:S(2)}) collective-permute-start(bf16[512,128]{1,0:T(8,128)(2,1)} %shard_map.86.refs_3_.refs_2_), channel_id=1, source_target_pairs={{0,8},{4,12},{8,0},{12,4},{16,24},{20,28},{24,16},{28,20},{1,9},{5... | collective-permute-start | bytes 393224 | tf_op jit(solution)/shard_map/ppermute | solution.py:161
  22.5 5.2 %copy-start = (bf16[512,128]{1,0:T(8,128)(2,1)}, bf16[512,128]{1,0:T(8,128)(2,1)S(1)}, u32[]{:S(2)}) copy-start(bf16[512,128]{1,0:T(8,128)(2,1)S(1)} %collective-permute-done.6.refs_6_.refs_5_) | copy-start | bytes 393220
  22.5 5.2 %collective-permute-start.4 = (bf16[512,128]{1,0:T(8,128)(2,1)}, bf16[512,128]{1,0:T(8,128)(2,1)S(1)}, u32[]{:S(2)}, u32[]{:S(2)}) collective-permute-start(bf16[512,128]{1,0:T(8,128)(2,1)} %shard_map.86.refs_3_.refs_2_), channel_id=1, source_target_pairs={{0,4},{4,0},{8,12},{12,8},{16,20},{20,16},{24,28},{28,24},{1,5},{5... | collective-permute-start | bytes 393224 | tf_op jit(solution)/shard_map/ppermute | solution.py:161
  24.8 2.9 %copy-start.1 = (bf16[512,128]{1,0:T(8,128)(2,1)}, bf16[512,128]{1,0:T(8,128)(2,1)S(1)}, u32[]{:S(2)}) copy-start(bf16[512,128]{1,0:T(8,128)(2,1)S(1)} %collective-permute-done.5.refs_5_.refs_4_) | copy-start | bytes 393220
  27.7 0.8 %copy-start.5 = (bf16[1056,128]{1,0:T(8,128)(2,1)}, bf16[1056,128]{1,0:T(8,128)(2,1)S(1)}, u32[]{:S(2)}) copy-start(bf16[1056,128]{1,0:T(8,128)(2,1)S(1)} %collective-permute-done.refs_1_) | copy-start | bytes 811012
  33.7 0.7 %copy-start.4 = (bf16[1056,128]{1,0:T(8,128)(2,1)}, bf16[1056,128]{1,0:T(8,128)(2,1)S(1)}, u32[]{:S(2)}) copy-start(bf16[1056,128]{1,0:T(8,128)(2,1)S(1)} %collective-permute-done.8.refs_0_) | copy-start | bytes 811012
  38.1 0.7 %copy-start.3 = (bf16[1056,128]{1,0:T(8,128)(2,1)}, bf16[1056,128]{1,0:T(8,128)(2,1)S(1)}, u32[]{:S(2)}) copy-start(bf16[1056,128]{1,0:T(8,128)(2,1)S(1)} %collective-permute-done.10.refs_0_) | copy-start | bytes 811012
  38.8 9.7 %copy-start.19 = (bf16[512,128]{1,0:T(8,128)(2,1)S(1)}, bf16[512,128]{1,0:T(8,128)(2,1)}, u32[]{:S(2)}) copy-start(bf16[512,128]{1,0:T(8,128)(2,1)} %get-tuple-element.40) | copy-start | bytes 393220
  38.8 10.3 %copy-start.20 = (bf16[512,128]{1,0:T(8,128)(2,1)S(1)}, bf16[512,128]{1,0:T(8,128)(2,1)}, u32[]{:S(2)}) copy-start(bf16[512,128]{1,0:T(8,128)(2,1)} %get-tuple-element.46) | copy-start | bytes 393220
  42.5 6.6 %collective-permute-start.12 = (bf16[512,128]{1,0:T(8,128)(2,1)}, bf16[512,128]{1,0:T(8,128)(2,1)S(1)}, u32[]{:S(2)}, u32[]{:S(2)}) collective-permute-start(bf16[512,128]{1,0:T(8,128)(2,1)} %get-tuple-element.54), channel_id=1, source_target_pairs={{0,4},{4,0},{8,12},{12,8},{16,20},{20,16},{24,28},{28,24},{1,5},{5... | collective-permute-start | bytes 393224 | tf_op jit(solution)/shard_map/ppermute | solution.py:161
  44.0 6.9 %collective-permute-start.13 = (bf16[512,128]{1,0:T(8,128)(2,1)}, bf16[512,128]{1,0:T(8,128)(2,1)S(1)}, u32[]{:S(2)}, u32[]{:S(2)}) collective-permute-start(bf16[512,128]{1,0:T(8,128)(2,1)} %get-tuple-element.55), channel_id=1, source_target_pairs={{0,8},{4,12},{8,0},{12,4},{16,24},{20,28},{24,16},{28,20},{1,9},{5... | collective-permute-start | bytes 393224 | tf_op jit(solution)/shard_map/ppermute | solution.py:161
  45.1 8.7 %collective-permute-start.14 = (bf16[512,128]{1,0:T(8,128)(2,1)}, bf16[512,128]{1,0:T(8,128)(2,1)S(1)}, u32[]{:S(2)}, u32[]{:S(2)}) collective-permute-start(bf16[512,128]{1,0:T(8,128)(2,1)} %get-tuple-element.56), channel_id=1, source_target_pairs={{0,16},{4,20},{8,24},{12,28},{16,0},{20,4},{24,8},{28,12},{1,17},{... | collective-permute-start | bytes 393224 | tf_op jit(solution)/shard_map/ppermute | solution.py:161
  48.4 8.4 %collective-permute-start.7 = (bf16[512,128]{1,0:T(8,128)(2,1)S(1)}, bf16[512,128]{1,0:T(8,128)(2,1)S(1)}, u32[]{:S(2)}, u32[]{:S(2)}) collective-permute-start(bf16[512,128]{1,0:T(8,128)(2,1)S(1)} %copy-done.19), channel_id=1, source_target_pairs={{0,1},{1,0},{2,3},{3,2},{4,5},{5,4},{6,7},{7,6},{8,9},{9,8},{10,11... | collective-permute-start | bytes 393224 | tf_op jit(solution)/shard_map/ppermute | solution.py:161
  48.4 9.7 %collective-permute-start.11 = (bf16[512,128]{1,0:T(8,128)(2,1)}, bf16[512,128]{1,0:T(8,128)(2,1)S(1)}, u32[]{:S(2)}, u32[]{:S(2)}) collective-permute-start(bf16[512,128]{1,0:T(8,128)(2,1)} %get-tuple-element.52), channel_id=1, source_target_pairs={{0,3},{1,2},{2,1},{3,0},{4,7},{5,6},{6,5},{7,4},{8,11},{9,10},{10,... | collective-permute-start | bytes 393224 | tf_op jit(solution)/shard_map/ppermute | solution.py:161
  49.1 4.7 %copy-start.9 = (bf16[512,128]{1,0:T(8,128)(2,1)}, bf16[512,128]{1,0:T(8,128)(2,1)S(1)}, u32[]{:S(2)}) copy-start(bf16[512,128]{1,0:T(8,128)(2,1)S(1)} %collective-permute-done.12.refs_1_) | copy-start | bytes 393220
  49.1 9.0 %collective-permute-start.9 = (bf16[512,128]{1,0:T(8,128)(2,1)S(1)}, bf16[512,128]{1,0:T(8,128)(2,1)S(1)}, u32[]{:S(2)}, u32[]{:S(2)}) collective-permute-start(bf16[512,128]{1,0:T(8,128)(2,1)S(1)} %copy-done.20), channel_id=1, source_target_pairs={{0,2},{1,3},{2,0},{3,1},{4,6},{5,7},{6,4},{7,5},{8,10},{9,11},{10,... | collective-permute-start | bytes 393224 | tf_op jit(solution)/shard_map/ppermute | solution.py:161
  50.8 3.0 %copy-start.10 = (bf16[512,128]{1,0:T(8,128)(2,1)}, bf16[512,128]{1,0:T(8,128)(2,1)S(1)}, u32[]{:S(2)}) copy-start(bf16[512,128]{1,0:T(8,128)(2,1)S(1)} %collective-permute-done.13.refs_2_) | copy-start | bytes 393220
  56.2 4.7 %collective-permute-start.15 = (bf16[128,128]{1,0:T(8,128)(2,1)}, bf16[128,128]{1,0:T(8,128)(2,1)S(1)}, u32[]{:S(2)}, u32[]{:S(2)}) collective-permute-start(bf16[128,128]{1,0:T(8,128)(2,1)} %get-tuple-element.58), channel_id=1, source_target_pairs={{0,1},{1,0},{2,3},{3,2},{4,5},{5,4},{6,7},{7,6},{8,9},{9,8},{10,11... | collective-permute-start | bytes 98312 | tf_op jit(solution)/shard_map/ppermute | solution.py:161
  56.2 4.7 %collective-permute-start.16 = (bf16[128,128]{1,0:T(8,128)(2,1)}, bf16[128,128]{1,0:T(8,128)(2,1)S(1)}, u32[]{:S(2)}, u32[]{:S(2)}) collective-permute-start(bf16[128,128]{1,0:T(8,128)(2,1)} %get-tuple-element.59), channel_id=1, source_target_pairs={{0,2},{1,3},{2,0},{3,1},{4,6},{5,7},{6,4},{7,5},{8,10},{9,11},{10,... | collective-permute-start | bytes 98312 | tf_op jit(solution)/shard_map/ppermute | solution.py:161
  56.8 1.3 %copy-start.6 = (bf16[512,128]{1,0:T(8,128)(2,1)}, bf16[512,128]{1,0:T(8,128)(2,1)S(1)}, u32[]{:S(2)}) copy-start(bf16[512,128]{1,0:T(8,128)(2,1)S(1)} %collective-permute-done.7.refs_1_) | copy-start | bytes 393220
  56.8 4.2 %collective-permute-start.17 = (bf16[128,128]{1,0:T(8,128)(2,1)}, bf16[128,128]{1,0:T(8,128)(2,1)S(1)}, u32[]{:S(2)}, u32[]{:S(2)}) collective-permute-start(bf16[128,128]{1,0:T(8,128)(2,1)} %get-tuple-element.60), channel_id=1, source_target_pairs={{0,3},{1,2},{2,1},{3,0},{4,7},{5,6},{6,5},{7,4},{8,11},{9,10},{10,... | collective-permute-start | bytes 98312 | tf_op jit(solution)/shard_map/ppermute | solution.py:161
  58.1 0.7 %copy-start.8 = (bf16[512,128]{1,0:T(8,128)(2,1)}, bf16[512,128]{1,0:T(8,128)(2,1)S(1)}, u32[]{:S(2)}) copy-start(bf16[512,128]{1,0:T(8,128)(2,1)S(1)} %collective-permute-done.9.refs_2_) | copy-start | bytes 393220
  (7 other events, 4.4 us)

commit v2 on v1

v2 whole, which is shorter than its diff:
```python
import functools
import math

import jax
import jax.numpy as jnp
from jax import lax
from jax.experimental import pallas as pl
from jax.experimental.pallas import tpu as pltpu
from jax.sharding import PartitionSpec as P

HEAD_DIM = 128
GROUP = 8
PAIRS = GROUP // 2
DOT_ROWS = 32
VMEM_BYTES = 16 * 1024 * 1024

F32 = jnp.float32
BF16 = jnp.bfloat16

HEAD_ORDER = [j + half * PAIRS for j in range(PAIRS) for half in range(2)]


def dot_nt(a, b):
    return lax.dot_general(a, b, (((1,), (1,)), ((), ())), preferred_element_type=F32)


def dot_nn(a, b):
    return lax.dot_general(a, b, (((1,), (0,)), ((), ())), preferred_element_type=F32)


def dot_tn(a, b):
    return lax.dot_general(a, b, (((0,), (0,)), ((), ())), preferred_element_type=F32)


def vmem(shape, dtype):
    return pltpu.VMEM(shape, dtype)


def hbm(shape, dtype):
    return jax.ShapeDtypeStruct(shape, dtype)


def call(kernel, out_shapes, place, *args, inside=True):
    if inside:
        args = [pltpu.with_memory_space_constraint(a, pltpu.VMEM) for a in args]
    return pl.pallas_call(
        kernel,
        out_shape=out_shapes,
        in_specs=[pl.BlockSpec(memory_space=pltpu.SMEM)]
        + [pl.BlockSpec(memory_space=pltpu.VMEM) for _ in args],
        out_specs=[pl.BlockSpec(memory_space=pltpu.VMEM) for _ in out_shapes],
        compiler_params=pltpu.CompilerParams(vmem_limit_bytes=VMEM_BYTES),
    )(place, *args)


def pack_kernel(parts, place, q_ref, g_ref, o_ref, k_ref, v_ref, l_ref, *outs):
    qg_refs, kv_refs, lse_ref = outs[:parts], outs[parts : 2 * parts - 1], outs[2 * parts - 1]
    own = place[0]
    rows = q_ref.shape[0]
    width = GROUP * HEAD_DIM
    lane = lax.broadcasted_iota(jnp.int32, (2 * rows, HEAD_DIM), 1)
    dots = jnp.zeros((2 * rows, HEAD_DIM), F32)
    start = 2 * GROUP * rows + DOT_ROWS
    for m in range(parts):
        peer = own ^ m
        col = pl.multiple_of(peer * HEAD_DIM, HEAD_DIM)
        if m == 1:
            target = qg_refs[1].at[start : start + 2 * rows]
        else:
            target = kv_refs[max(m - 1, 0)]
        target[:rows, :] = k_ref[:, pl.ds(col, HEAD_DIM)]
        target[rows:, :] = v_ref[:, pl.ds(col, HEAD_DIM)]
        sums = []
        for i, h in enumerate(HEAD_ORDER):
            col = pl.multiple_of(peer * width + h * HEAD_DIM, HEAD_DIM)
            qg_refs[m][i * rows : (i + 1) * rows, :] = q_ref[:, pl.ds(col, HEAD_DIM)]
            grad = g_ref[:, pl.ds(col, HEAD_DIM)]
            qg_refs[m][(GROUP + i) * rows : (GROUP + i + 1) * rows, :] = grad
            prod = grad.astype(F32) * o_ref[:, pl.ds(col, HEAD_DIM)].astype(F32)
            sums.append(jnp.sum(prod, axis=1, keepdims=True))
        for j in range(PAIRS):
            pair = jnp.concatenate([sums[2 * j], sums[2 * j + 1]], axis=0)
            dots = jnp.where(lane == 8 * m + j, pair, dots)
    turned = dots.T
    for m in range(parts):
        full = turned[8 * m : 8 * m + 8, :]
        high = full.astype(BF16).astype(F32)
        mid = (full - high).astype(BF16).astype(F32)
        low = (full - high) - mid
        first = 2 * GROUP * rows
        qg_refs[m][first : first + DOT_ROWS, :] = jnp.concatenate(
            [high, mid, low, jnp.zeros_like(high)], axis=0
        ).astype(BF16)
    for m in range(parts):
        piece = l_ref[:, :rows]
        for c in range(1, parts):
            piece = jnp.where((own ^ m) == c, l_ref[:, c * rows : (c + 1) * rows], piece)
        piece = piece * math.log2(math.e)
        lse_ref[8 * m : 8 * m + PAIRS, :] = jnp.concatenate([piece[:PAIRS], piece[PAIRS:]], axis=1)
        lse_ref[8 * m + PAIRS : 8 * m + 8, :] = jnp.zeros((8 - PAIRS, 2 * rows), F32)


def join_kernel(parts, place, *refs):
    pieces, out = refs[:parts], refs[parts]
    rows = out.shape[0] // (2 * parts)
    for m in range(parts):
        start = pieces[m].shape[0] - 2 * rows
        out[m * rows : (m + 1) * rows, :] = pieces[m][start : start + rows, :]
        out[(parts + m) * rows : (parts + m + 1) * rows, :] = pieces[m][start + rows :, :]


def row_of(stack):
    return jnp.concatenate([stack[j : j + 1, :] for j in range(PAIRS)], axis=1)


def step_kernel(pieces, blocks, span, has_dq, has_acc, dq_done, acc_done, place, *refs):
    refs = list(refs)

    def take(count):
        out = refs[:count]
        del refs[:count]
        return out

    qg_refs = take(len(pieces))
    (lse_ref,) = take(1)
    kv_refs = take(blocks)
    dq_in = take(len(pieces)) if has_dq else None
    acc_in = take(blocks) if has_acc else None
    dq_out = take(len(pieces))
    acc_out = take(blocks)
    scale = 1.0 / math.sqrt(HEAD_DIM)
    block = kv_refs[0].shape[0] // 2
    dk = [acc_in[b][:block, :] if has_acc else None for b in range(blocks)]
    dv = [acc_in[b][block:, :] if has_acc else None for b in range(blocks)]
    for i, m in enumerate(pieces):
        query = qg_refs[i][:span, :]
        grad = qg_refs[i][span : 2 * span, :]
        split = qg_refs[i][2 * span : 2 * span + DOT_ROWS, :].astype(F32)
        dots = row_of((split[:8] + split[8:16]) + split[16:24])
        lse = row_of(lse_ref[8 * m : 8 * m + 8, :])
        dq = dq_in[i][...] if has_dq else None
        for b in range(blocks):
            keys = kv_refs[b][:block, :]
            values = kv_refs[b][block:, :]
            probs = jnp.exp2(dot_nt(keys, query) * (scale * math.log2(math.e)) - lse)
            dprobs = dot_nt(values, grad)
            dscores = (probs * (dprobs - dots)).astype(BF16)
            part_v = dot_nn(probs.astype(BF16), grad)
            part_k = dot_nn(dscores, query)
            part_q = dot_tn(keys, dscores)
            dv[b] = part_v if dv[b] is None else dv[b] + part_v
            dk[b] = part_k if dk[b] is None else dk[b] + part_k
            dq = part_q if dq is None else dq + part_q
        if dq_done:
            dq_out[i][...] = (dq.T * scale).astype(dq_out[i].dtype)
        else:
            dq_out[i][...] = dq
    for b in range(blocks):
        acc_out[b][:block, :] = (dk[b] * scale if acc_done else dk[b]).astype(acc_out[b].dtype)
        acc_out[b][block:, :] = dv[b].astype(acc_out[b].dtype)


def total_kernel(parts, levels, place, *refs):
    terms, outs = refs[:levels], refs[levels:]
    total = terms[0][...]
    for term in terms[1:]:
        total = total + term[...].astype(F32)
    rows = total.shape[0] // (2 * parts)
    for m in range(parts):
        outs[m][:rows, :] = total[m * rows : (m + 1) * rows].astype(outs[m].dtype)
        outs[m][rows:, :] = total[(parts + m) * rows : (parts + m + 1) * rows].astype(
            outs[m].dtype
        )


def unpack_q_kernel(parts, place, *refs):
    pieces, out = refs[:parts], refs[parts]
    rows = out.shape[0]
    width = GROUP * HEAD_DIM
    for m in range(parts):
        for i, h in enumerate(HEAD_ORDER):
            col = pl.multiple_of((place[0] ^ m) * width + h * HEAD_DIM, HEAD_DIM)
            out[:, pl.ds(col, HEAD_DIM)] = pieces[m][i * rows : (i + 1) * rows, :].astype(F32)


def unpack_kv_kernel(parts, place, *refs):
    pieces, out_k, out_v = refs[:parts], refs[parts], refs[parts + 1]
    rows = out_k.shape[0]
    for m in range(parts):
        col = pl.multiple_of((place[0] ^ m) * HEAD_DIM, HEAD_DIM)
        out_k[:, pl.ds(col, HEAD_DIM)] = pieces[m][:rows, :].astype(F32)
        out_v[:, pl.ds(col, HEAD_DIM)] = pieces[m][rows:, :].astype(F32)


def swap(value, axis, distance):
    return lax.ppermute(value, axis, [(i, i ^ distance) for i in range(lax.axis_size(axis))])


def on_device(queries, key_rows, value_rows, attn_out, out_grad, logsumexp):
    parts = lax.axis_size("head")
    levels = lax.axis_size("ctx").bit_length()
    rows = queries.shape[0]
    block = rows * parts
    span = rows * GROUP
    place = lax.axis_index("head").astype(jnp.int32).reshape(1)

    sizes = [2 * span + DOT_ROWS + (2 * rows if m == 1 else 0) for m in range(parts)]
    packed = call(
        functools.partial(pack_kernel, parts),
        [vmem((size, HEAD_DIM), BF16) for size in sizes]
        + [vmem((2 * rows, HEAD_DIM), BF16)] * (parts - 1)
        + [vmem((8 * parts, 2 * rows), F32)],
        place,
        queries,
        out_grad,
        attn_out,
        key_rows,
        value_rows,
        logsumexp,
        inside=False,
    )
    qg, kv, lse = list(packed[:parts]), list(packed[parts:-1]), packed[-1]
    kv = [kv[0], None] + [swap(kv[m - 1], "head", m) for m in range(2, parts)]
    qg = [qg[0]] + [swap(qg[m], "head", m) for m in range(1, parts)]
    kv[1] = qg[1]
    (kv_own,) = call(
        functools.partial(join_kernel, parts), [vmem((2 * block, HEAD_DIM), BF16)], place, *kv
    )
    kv_all = [kv_own] + [swap(kv_own, "ctx", 1 << b) for b in range(levels - 1)]

    dq = [None] * parts
    acc = [None] * levels

    def step(pieces, blocks, dq_done, acc_done):
        has_dq = dq[pieces[0]] is not None
        has_acc = acc[blocks[0]] is not None
        outs = []
        for m in pieces:
            if dq_done:
                outs.append(vmem((span, HEAD_DIM), F32 if m == 0 else BF16))
            else:
                outs.append(vmem((HEAD_DIM, span), F32))
        for b in blocks:
            outs.append(vmem((2 * block, HEAD_DIM), BF16 if acc_done and b > 0 else F32))
        result = call(
            functools.partial(
                step_kernel, pieces, len(blocks), span, has_dq, has_acc, dq_done, acc_done
            ),
            outs,
            place,
            *[qg[m] for m in pieces],
            lse,
            *[kv_all[b] for b in blocks],
            *([dq[m] for m in pieces] if has_dq else []),
            *([acc[b] for b in blocks] if has_acc else []),
        )
        for i, m in enumerate(pieces):
            dq[m] = result[i]
            if dq_done and m > 0:
                dq[m] = swap(dq[m], "head", m)
        for i, b in enumerate(blocks):
            acc[b] = result[len(pieces) + i]
            if acc_done and b > 0:
                acc[b] = swap(acc[b], "ctx", 1 << (b - 1))

    for b in range(levels):
        step((0, 1), (b,), b == levels - 1, False)
    for m in range(2, parts - 1):
        step((m,), tuple(range(levels)), True, False)
    for b in reversed(range(levels)):
        step((parts - 1,), (b,), b == 0, True)

    dkv = call(
        functools.partial(total_kernel, parts, levels),
        [vmem((2 * rows, HEAD_DIM), F32 if m == 0 else BF16) for m in range(parts)],
        place,
        *acc,
    )
    dkv = [dkv[0]] + [swap(dkv[m], "head", m) for m in range(1, parts)]
    (grad_q,) = call(
        functools.partial(unpack_q_kernel, parts), [hbm(queries.shape, F32)], place, *dq
    )
    grad_k, grad_v = call(
        functools.partial(unpack_kv_kernel, parts),
        [hbm(key_rows.shape, F32), hbm(value_rows.shape, F32)],
        place,
        *dkv,
    )
    return (grad_q, grad_k, grad_v)


def solution(mesh):
    rows = P(("ctx", "head"), None)
    return jax.shard_map(
        on_device,
        mesh=mesh,
        in_specs=(rows, rows, rows, rows, rows, P("head", "ctx")),
        out_specs=(rows, rows, rows),
        check_vma=False,
    )
```

time: 63.6 us -> 55.1 us (0.87)
  Pallas kernels: 22.9 us -> 10.1 us
  waiting for transfers between devices: 13.3 us -> 19.8 us
  starting transfers between devices: 20.8 us -> 18.5 us
    pallas_call x8 -> x14, Pallas kernels: 22.9 us -> 10.1 us  [call(): pl.pallas_call(kernel, out_shape=out_shapes, in_specs=[pl.BlockSpec(memor...]
    ppermute x18 -> x17, waiting for transfers between devices: 13.3 us -> 19.8 us  [swap(): lax.ppermute(value, axis, [(i, i ^ distance) for i in range(lax.axis_size...]
    ppermute x18 -> x17, starting transfers between devices: 20.8 us -> 18.5 us  [swap(): lax.ppermute(value, axis, [(i, i ^ distance) for i in range(lax.axis_size...]
    unnamed x42 -> x12, local copies, waits for them, and re-layouts: 4.69 us -> 5.49 us
    reshape x3 -> x0, local copies, waits for them, and re-layouts: 0.77 us -> none  [the longest x1 0.68 us: on_device(): lse = logsumexp.reshape(GROUP // 2, 2, parts, rows).transpose(2, 0, 1, 3)...]
  transfers between devices with their start and end apart: 18 -> 17, of which waited for: 5 -> 8; matrix products, arithmetic and copies ran while one was open for 1% -> 0% of each run, Pallas kernels for 23% -> 13%
where the time goes in v2:
time: 55.1 us; the launch traced here: 54.8 us
  waiting for transfers between devices  19.8 us (36%)
  starting transfers between devices  18.5 us (34%)
  Pallas kernels  10.1 us (18%)
  local copies, waits for them, and re-layouts  5.49 us (10%)
  between operations  0.78 us (1%)
    ppermute x17, waiting for transfers between devices, swap(): lax.ppermute(value, axis, [(i, i ^ distance) for i in range(lax.axis_size...  19.8 us
    ppermute x17, starting transfers between devices, swap(): lax.ppermute(value, axis, [(i, i ^ distance) for i in range(lax.axis_size...  18.5 us
    pallas_call x14, Pallas kernels, call(): pl.pallas_call(kernel, out_shape=out_shapes, in_specs=[pl.BlockSpec(memor...  10.1 us
    unnamed x12, local copies, waits for them, and re-layouts  5.49 us
  transfers between devices with their start and end apart: 17, of which 8 were waited for; matrix products, arithmetic and copies ran while one was open for 0% of the time, Pallas kernels for 13%

profile of v2, /device:TPU:0, one launch (start us, length us, event | category | flops | bytes accessed | tf_op | source)
XLA Modules:
  0.0 54.8 jit_solution(8576966540261058992)
XLA Ops:
  0.6 1.0 %copy-done = bf16[64,4096]{1,0:T(8,128)(2,1)S(1)} copy-done((bf16[64,4096]{1,0:T(8,128)(2,1)S(1)}, bf16[64,4096]{1,0:T(8,128)(2,1)}, u32[]{:S(2)}) %copy-start) | copy-done | bytes 524312
  1.7 1.0 %copy-done.1 = bf16[64,4096]{1,0:T(8,128)(2,1)S(1)} copy-done((bf16[64,4096]{1,0:T(8,128)(2,1)S(1)}, bf16[64,4096]{1,0:T(8,128)(2,1)}, u32[]{:S(2)}) %copy-start.1) | copy-done | bytes 524312
  2.7 1.0 %copy-done.2 = bf16[64,4096]{1,0:T(8,128)(2,1)S(1)} copy-done((bf16[64,4096]{1,0:T(8,128)(2,1)S(1)}, bf16[64,4096]{1,0:T(8,128)(2,1)}, u32[]{:S(2)}) %copy-start.2) | copy-done | bytes 524312
  3.8 0.8 %copy-done.3 = bf16[64,512]{1,0:T(8,128)(2,1)S(1)} copy-done((bf16[64,512]{1,0:T(8,128)(2,1)S(1)}, bf16[64,512]{1,0:T(8,128)(2,1)}, u32[]{:S(2)}) %copy-start.3) | copy-done | bytes 65560
  4.6 0.8 %copy-done.4 = bf16[64,512]{1,0:T(8,128)(2,1)S(1)} copy-done((bf16[64,512]{1,0:T(8,128)(2,1)S(1)}, bf16[64,512]{1,0:T(8,128)(2,1)}, u32[]{:S(2)}) %copy-start.4) | copy-done | bytes 65560
  5.4 0.7 %copy-done.5 = f32[8,256]{1,0:T(8,128)S(1)} copy-done((f32[8,256]{1,0:T(8,128)S(1)}, f32[8,256]{1,0:T(8,128)}, u32[]{:S(2)}) %copy-start.5) | copy-done | bytes 8216
  6.1 1.0 %shard_map.85 = (bf16[1056,128]{1,0:T(8,128)(2,1)S(1)}, bf16[1184,128]{1,0:T(8,128)(2,1)S(1)}, bf16[1056,128]{1,0:T(8,128)(2,1)S(1)}, bf16[1056,128]{1,0:T(8,128...) custom-call(s32[1]{0:T(128)} %bitcast.place, ...), custom_call_target="tpu_custom_call" | custom-call | tf_op jit(solution)/shard_map/pallas_call | solution.py:46
  7.2 0.6 %collective-permute-start = (bf16[1184,128]{1,0:T(8,128)(2,1)S(1)}, bf16[1184,128]{1,0:T(8,128)(2,1)S(1)}, u32[]{:S(2)}, u32[]{:S(2)}) collective-permute-start(bf16[1184,128]{1,0:T(8,128)(2,1)S(1)} %get-tuple-element.43), channel_id=1, source_target_pairs={{0,1},{1,0},{2,3},{3,2},{4,5},{5,4},{6,7},{7,6},{8,9},{9,8},{10,11... | collective-permute-start | bytes 909320 | tf_op jit(solution)/shard_map/ppermute | solution.py:196
  7.7 2.6 %collective-permute-start.7 = (bf16[1056,128]{1,0:T(8,128)(2,1)S(1)}, bf16[1056,128]{1,0:T(8,128)(2,1)S(1)}, u32[]{:S(2)}, u32[]{:S(2)}) collective-permute-start(bf16[1056,128]{1,0:T(8,128)(2,1)S(1)} %get-tuple-element.56), channel_id=1, source_target_pairs={{0,2},{1,3},{2,0},{3,1},{4,6},{5,7},{6,4},{7,5},{8,10},{9,11},{10,... | collective-permute-start | bytes 811016 | tf_op jit(solution)/shard_map/ppermute | solution.py:196
  10.3 1.7 %collective-permute-start.1 = (bf16[128,128]{1,0:T(8,128)(2,1)S(1)}, bf16[128,128]{1,0:T(8,128)(2,1)S(1)}, u32[]{:S(2)}, u32[]{:S(2)}) collective-permute-start(bf16[128,128]{1,0:T(8,128)(2,1)S(1)} %get-tuple-element.46), channel_id=1, source_target_pairs={{0,2},{1,3},{2,0},{3,1},{4,6},{5,7},{6,4},{7,5},{8,10},{9,11},{10,... | collective-permute-start | bytes 98312 | tf_op jit(solution)/shard_map/ppermute | solution.py:196
  12.1 12.0 %collective-permute-done.1.refs_2_ = bf16[128,128]{1,0:T(8,128)(2,1)S(1)} collective-permute-done((bf16[128,128]{1,0:T(8,128)(2,1)S(1)}, bf16[128,128]{1,0:T(8,128)(2,1)S(1)}, u32[]{:S(2)}, u32[]{:S(2)}) %collective-permute-start.1) | collective-permute-done | bytes 32800 | tf_op jit(solution)/shard_map/ppermute | solution.py:196
  24.3 1.8 %collective-permute-start.5 = (bf16[512,128]{1,0:T(8,128)(2,1)S(1)}, bf16[512,128]{1,0:T(8,128)(2,1)S(1)}, u32[]{:S(2)}, u32[]{:S(2)}) collective-permute-start(bf16[512,128]{1,0:T(8,128)(2,1)S(1)} %shard_map.86.refs_3_.refs_2_), channel_id=1, source_target_pairs={{0,4},{4,0},{8,12},{12,8},{16,20},{20,16},{24,28},{28,24},{1,5},{5... | collective-permute-start | bytes 393224 | tf_op jit(solution)/shard_map/ppermute | solution.py:196
  26.1 1.6 %collective-permute-start.4 = (bf16[512,128]{1,0:T(8,128)(2,1)S(1)}, bf16[512,128]{1,0:T(8,128)(2,1)S(1)}, u32[]{:S(2)}, u32[]{:S(2)}) collective-permute-start(bf16[512,128]{1,0:T(8,128)(2,1)S(1)} %shard_map.86.refs_3_.refs_2_), channel_id=1, source_target_pairs={{0,8},{4,12},{8,0},{12,4},{16,24},{20,28},{24,16},{28,20},{1,9},{5... | collective-permute-start | bytes 393224 | tf_op jit(solution)/shard_map/ppermute | solution.py:196
  27.7 2.6 %collective-permute-start.3 = (bf16[512,128]{1,0:T(8,128)(2,1)S(1)}, bf16[512,128]{1,0:T(8,128)(2,1)S(1)}, u32[]{:S(2)}, u32[]{:S(2)}) collective-permute-start(bf16[512,128]{1,0:T(8,128)(2,1)S(1)} %shard_map.86.refs_3_.refs_2_), channel_id=1, source_target_pairs={{0,16},{4,20},{8,24},{12,28},{16,0},{20,4},{24,8},{28,12},{1,17},{... | collective-permute-start | bytes 393224 | tf_op jit(solution)/shard_map/ppermute | solution.py:196
  30.2 0.9 %shard_map.87 = (f32[128,512]{1,0:T(8,128)S(1)}, f32[128,512]{1,0:T(8,128)S(1)}, f32[512,128]{1,0:T(8,128)S(1)}) custom-call(s32[1]{0:T(128)} %bitcast.place, bf16[1056,128]{1,0:T(8,128)(2,1)S(1)} %get-tuple-element.42.refs_0_, bf16[1184,128]{1,0:T(8,128)(2,1)S(1)} %collective-permute-done.refs_1_, f32[32,128]{1,0:T(8,128)S(1)} %get-tuple-element.44.refs_2_.refs_1_, ...), custom_call_target="tpu_custom_call" | custom-call | tf_op jit(solution)/shard_map/pallas_call | solution.py:46
  31.2 0.9 %shard_map.88 = (f32[128,512]{1,0:T(8,128)S(1)}, f32[128,512]{1,0:T(8,128)S(1)}, f32[512,128]{1,0:T(8,128)S(1)}) custom-call(s32[1]{0:T(128)} %bitcast.place, bf16[1056,128]{1,0:T(8,128)(2,1)S(1)} %get-tuple-element.42.refs_0_, bf16[1184,128]{1,0:T(8,128)(2,1)S(1)} %collective-permute-done.refs_1_, f32[32,128]{1,0:T(8,128)S(1)} %get-tuple-element.44.refs_2_.refs_1_, ...), custom_call_target="tpu_custom_call" | custom-call | tf_op jit(solution)/shard_map/pallas_call | solution.py:46
  32.1 1.3 %collective-permute-done.4.refs_3_.refs_4_.refs_2_ = bf16[512,128]{1,0:T(8,128)(2,1)S(1)} collective-permute-done((bf16[512,128]{1,0:T(8,128)(2,1)S(1)}, bf16[512,128]{1,0:T(8,128)(2,1)S(1)}, u32[]{:S(2)}, u32[]{:S(2)}) %collective-permute-start.4) | collective-permute-done | bytes 131104 | tf_op jit(solution)/shard_map/ppermute | solution.py:196
  33.4 0.9 %shard_map.89 = (f32[128,512]{1,0:T(8,128)S(1)}, f32[128,512]{1,0:T(8,128)S(1)}, f32[512,128]{1,0:T(8,128)S(1)}) custom-call(s32[1]{0:T(128)} %bitcast.place, bf16[1056,128]{1,0:T(8,128)(2,1)S(1)} %get-tuple-element.42.refs_0_, bf16[1184,128]{1,0:T(8,128)(2,1)S(1)} %collective-permute-done.refs_1_, f32[32,128]{1,0:T(8,128)S(1)} %get-tuple-element.44.refs_2_.refs_1_, ...), custom_call_target="tpu_custom_call" | custom-call | tf_op jit(solution)/shard_map/pallas_call | solution.py:46
  34.4 2.1 %collective-permute-done.3.refs_3_.refs_5_.refs_2_ = bf16[512,128]{1,0:T(8,128)(2,1)S(1)} collective-permute-done((bf16[512,128]{1,0:T(8,128)(2,1)S(1)}, bf16[512,128]{1,0:T(8,128)(2,1)S(1)}, u32[]{:S(2)}, u32[]{:S(2)}) %collective-permute-start.3) | collective-permute-done | bytes 131104 | tf_op jit(solution)/shard_map/ppermute | solution.py:196
  36.4 0.9 %shard_map.90 = (f32[512,128]{1,0:T(8,128)S(1)}, bf16[512,128]{1,0:T(8,128)(2,1)S(1)}, f32[512,128]{1,0:T(8,128)S(1)}) custom-call(s32[1]{0:T(128)} %bitcast.place, bf16[1056,128]{1,0:T(8,128)(2,1)S(1)} %get-tuple-element.42.refs_0_, bf16[1184,128]{1,0:T(8,128)(2,1)S(1)} %collective-permute-done.refs_1_, f32[32,128]{1,0:T(8,128)S(1)} %get-tuple-element.44.refs_2_.refs_1_, ...), custom_call_target="tpu_custom_call" | custom-call | tf_op jit(solution)/shard_map/pallas_call | solution.py:46
  37.4 1.5 %shard_map.91 = (bf16[512,128]{1,0:T(8,128)(2,1)S(1)}, f32[512,128]{1,0:T(8,128)S(1)}, f32[512,128]{1,0:T(8,128)S(1)}, f32[512,128]{1,0:T(8,128)S(1)}, f32[512,128]{1,0:T(8,128)S(1)}) custom-call(s32[1]{0:T(128)} %bitcast.place, bf16[1056,128]{1,0:T(8,128)(2,1)S(1)} %collective-permute-done.7.refs_0_, f32[32,128]{1,0:T(8,128)S(1)} %get-tuple-element.44.refs_2_.refs_1_, ...), custom_call_target="tpu_custom_call" | custom-call | tf_op jit(solution)/shard_map/pallas_call | solution.py:46
  40.3 0.6 %collective-permute-start.11 = (bf16[512,128]{1,0:T(8,128)(2,1)S(1)}, bf16[512,128]{1,0:T(8,128)(2,1)S(1)}, u32[]{:S(2)}, u32[]{:S(2)}) collective-permute-start(bf16[512,128]{1,0:T(8,128)(2,1)S(1)} %get-tuple-element.72), channel_id=1, source_target_pairs={{0,4},{4,0},{8,12},{12,8},{16,20},{20,16},{24,28},{28,24},{1,5},{5... | collective-permute-start | bytes 393224 | tf_op jit(solution)/shard_map/ppermute | solution.py:196
  41.3 2.6 %collective-permute-start.13 = (bf16[512,128]{1,0:T(8,128)(2,1)S(1)}, bf16[512,128]{1,0:T(8,128)(2,1)S(1)}, u32[]{:S(2)}, u32[]{:S(2)}) collective-permute-start(bf16[512,128]{1,0:T(8,128)(2,1)S(1)} %get-tuple-element.74), channel_id=1, source_target_pairs={{0,16},{4,20},{8,24},{12,28},{16,0},{20,4},{24,8},{28,12},{1,17},{... | collective-permute-start | bytes 393224 | tf_op jit(solution)/shard_map/ppermute | solution.py:196
  43.9 1.5 %collective-permute-start.8 = (bf16[512,128]{1,0:T(8,128)(2,1)S(1)}, bf16[512,128]{1,0:T(8,128)(2,1)S(1)}, u32[]{:S(2)}, u32[]{:S(2)}) collective-permute-start(bf16[512,128]{1,0:T(8,128)(2,1)S(1)} %get-tuple-element.61), channel_id=1, source_target_pairs={{0,2},{1,3},{2,0},{3,1},{4,6},{5,7},{6,4},{7,5},{8,10},{9,11},{10,... | collective-permute-start | bytes 393224 | tf_op jit(solution)/shard_map/ppermute | solution.py:196
  45.4 0.6 %shard_map.95 = (bf16[512,128]{1,0:T(8,128)(2,1)S(1)}, f32[512,128]{1,0:T(8,128)S(1)}) custom-call(s32[1]{0:T(128)} %bitcast.place, bf16[1056,128]{1,0:T(8,128)(2,1)S(1)} %collective-permute-done.9.refs_0_, f32[32,128]{1,0:T(8,128)S(1)} %get-tuple-element.44.refs_2_.refs_1_, bf16[512,128]{1,0:T(8,128)(2,1)S(1)} %shard_map.86.refs_3_.refs_2_, ...), custom_call_target="tpu_custom_call" | custom-call | tf_op jit(solution)/shard_map/pallas_call | solution.py:46
  46.0 0.7 %collective-permute-start.10 = (bf16[512,128]{1,0:T(8,128)(2,1)S(1)}, bf16[512,128]{1,0:T(8,128)(2,1)S(1)}, u32[]{:S(2)}, u32[]{:S(2)}) collective-permute-start(bf16[512,128]{1,0:T(8,128)(2,1)S(1)} %get-tuple-element.70), channel_id=1, source_target_pairs={{0,3},{1,2},{2,1},{3,0},{4,7},{5,6},{6,5},{7,4},{8,11},{9,10},{10,... | collective-permute-start | bytes 393224 | tf_op jit(solution)/shard_map/ppermute | solution.py:196
  46.7 2.2 %collective-permute-done.13.refs_3_ = bf16[512,128]{1,0:T(8,128)(2,1)S(1)} collective-permute-done((bf16[512,128]{1,0:T(8,128)(2,1)S(1)}, bf16[512,128]{1,0:T(8,128)(2,1)S(1)}, u32[]{:S(2)}, u32[]{:S(2)}) %collective-permute-start.13) | collective-permute-done | bytes 131104 | tf_op jit(solution)/shard_map/ppermute | solution.py:196
  49.1 1.6 %collective-permute-start.15 = (bf16[128,128]{1,0:T(8,128)(2,1)S(1)}, bf16[128,128]{1,0:T(8,128)(2,1)S(1)}, u32[]{:S(2)}, u32[]{:S(2)}) collective-permute-start(bf16[128,128]{1,0:T(8,128)(2,1)S(1)} %get-tuple-element.77), channel_id=1, source_target_pairs={{0,2},{1,3},{2,0},{3,1},{4,6},{5,7},{6,4},{7,5},{8,10},{9,11},{10,... | collective-permute-start | bytes 98312 | tf_op jit(solution)/shard_map/ppermute | solution.py:196
  51.2 1.1 %shard_map.96 = f32[64,4096]{1,0:T(8,128)} custom-call(s32[1]{0:T(128)} %bitcast.place, f32[512,128]{1,0:T(8,128)S(1)} %get-tuple-element.54.refs_0_, bf16[512,128]{1,0:T(8,128)(2,1)S(1)} %collective-permute-done.6.refs_1_, bf16[512,128]{1,0:T(8,128)(2,1)S(1)} %collective-permute-done.8.refs_2_, bf16[512,128]{1,0:T(8,128)(2,1)S(1)} %collective-permute-done.10.refs_3_), custom_call_target="tpu_custom_call" | custom-call | tf_op jit(solution)/shard_map/pallas_call | solution.py:46
  52.3 0.8 %collective-permute-done.15.refs_2_ = bf16[128,128]{1,0:T(8,128)(2,1)S(1)} collective-permute-done((bf16[128,128]{1,0:T(8,128)(2,1)S(1)}, bf16[128,128]{1,0:T(8,128)(2,1)S(1)}, u32[]{:S(2)}, u32[]{:S(2)}) %collective-permute-start.15) | collective-permute-done | bytes 32800 | tf_op jit(solution)/shard_map/ppermute | solution.py:196
  53.1 0.9 %collective-permute-done.16.refs_3_ = bf16[128,128]{1,0:T(8,128)(2,1)S(1)} collective-permute-done((bf16[128,128]{1,0:T(8,128)(2,1)S(1)}, bf16[128,128]{1,0:T(8,128)(2,1)S(1)}, u32[]{:S(2)}, u32[]{:S(2)}) %collective-permute-start.16) | collective-permute-done | bytes 32800 | tf_op jit(solution)/shard_map/ppermute | solution.py:196
  54.0 0.7 %shard_map.98 = (f32[64,512]{1,0:T(8,128)}, f32[64,512]{1,0:T(8,128)}) custom-call(s32[1]{0:T(128)} %bitcast.place, f32[128,128]{1,0:T(8,128)S(1)} %get-tuple-element.75.refs_0_, bf16[128,128]{1,0:T(8,128)(2,1)S(1)} %collective-permute-done.14.refs_1_, bf16[128,128]{1,0:T(8,128)(2,1)S(1)} %collective-permute-done.15.refs_2_, ...), custom_call_target="tpu_custom_call" | custom-call | tf_op jit(solution)/shard_map/pallas_call | solution.py:46
  (28 shorter events, 2.8 us)
Async XLA Ops:
  0.6 1.0 %copy-start = (bf16[64,4096]{1,0:T(8,128)(2,1)S(1)}, bf16[64,4096]{1,0:T(8,128)(2,1)}, u32[]{:S(2)}) copy-start(bf16[64,4096]{1,0:T(8,128)(2,1)} %q_ref.1) | copy-start | bytes 1572868
  1.7 1.0 %copy-start.1 = (bf16[64,4096]{1,0:T(8,128)(2,1)S(1)}, bf16[64,4096]{1,0:T(8,128)(2,1)}, u32[]{:S(2)}) copy-start(bf16[64,4096]{1,0:T(8,128)(2,1)} %g_ref.1) | copy-start | bytes 1572868
  2.7 1.0 %copy-start.2 = (bf16[64,4096]{1,0:T(8,128)(2,1)S(1)}, bf16[64,4096]{1,0:T(8,128)(2,1)}, u32[]{:S(2)}) copy-start(bf16[64,4096]{1,0:T(8,128)(2,1)} %o_ref.1) | copy-start | bytes 1572868
  3.8 0.8 %copy-start.3 = (bf16[64,512]{1,0:T(8,128)(2,1)S(1)}, bf16[64,512]{1,0:T(8,128)(2,1)}, u32[]{:S(2)}) copy-start(bf16[64,512]{1,0:T(8,128)(2,1)} %k_ref.1) | copy-start | bytes 196612
  4.6 0.8 %copy-start.4 = (bf16[64,512]{1,0:T(8,128)(2,1)S(1)}, bf16[64,512]{1,0:T(8,128)(2,1)}, u32[]{:S(2)}) copy-start(bf16[64,512]{1,0:T(8,128)(2,1)} %v_ref.1) | copy-start | bytes 196612
  5.4 0.7 %copy-start.5 = (f32[8,256]{1,0:T(8,128)S(1)}, f32[8,256]{1,0:T(8,128)}, u32[]{:S(2)}) copy-start(f32[8,256]{1,0:T(8,128)} %l_ref.1) | copy-start | bytes 24580
  7.2 17.1 %collective-permute-start = (bf16[1184,128]{1,0:T(8,128)(2,1)S(1)}, bf16[1184,128]{1,0:T(8,128)(2,1)S(1)}, u32[]{:S(2)}, u32[]{:S(2)}) collective-permute-start(bf16[1184,128]{1,0:T(8,128)(2,1)S(1)} %get-tuple-element.43), channel_id=1, source_target_pairs={{0,1},{1,0},{2,3},{3,2},{4,5},{5,4},{6,7},{7,6},{8,9},{9,8},{10,11... | collective-permute-start | bytes 909320 | tf_op jit(solution)/shard_map/ppermute | solution.py:196
  7.7 29.6 %collective-permute-start.7 = (bf16[1056,128]{1,0:T(8,128)(2,1)S(1)}, bf16[1056,128]{1,0:T(8,128)(2,1)S(1)}, u32[]{:S(2)}, u32[]{:S(2)}) collective-permute-start(bf16[1056,128]{1,0:T(8,128)(2,1)S(1)} %get-tuple-element.56), channel_id=1, source_target_pairs={{0,2},{1,3},{2,0},{3,1},{4,6},{5,7},{6,4},{7,5},{8,10},{9,11},{10,... | collective-permute-start | bytes 811016 | tf_op jit(solution)/shard_map/ppermute | solution.py:196
  10.3 28.6 %collective-permute-start.9 = (bf16[1056,128]{1,0:T(8,128)(2,1)S(1)}, bf16[1056,128]{1,0:T(8,128)(2,1)S(1)}, u32[]{:S(2)}, u32[]{:S(2)}) collective-permute-start(bf16[1056,128]{1,0:T(8,128)(2,1)S(1)} %get-tuple-element.62), channel_id=1, source_target_pairs={{0,3},{1,2},{2,1},{3,0},{4,7},{5,6},{6,5},{7,4},{8,11},{9,10},{10,... | collective-permute-start | bytes 811016 | tf_op jit(solution)/shard_map/ppermute | solution.py:196
  10.3 13.8 %collective-permute-start.1 = (bf16[128,128]{1,0:T(8,128)(2,1)S(1)}, bf16[128,128]{1,0:T(8,128)(2,1)S(1)}, u32[]{:S(2)}, u32[]{:S(2)}) collective-permute-start(bf16[128,128]{1,0:T(8,128)(2,1)S(1)} %get-tuple-element.46), channel_id=1, source_target_pairs={{0,2},{1,3},{2,0},{3,1},{4,6},{5,7},{6,4},{7,5},{8,10},{9,11},{10,... | collective-permute-start | bytes 98312 | tf_op jit(solution)/shard_map/ppermute | solution.py:196
  12.1 12.2 %collective-permute-start.2 = (bf16[128,128]{1,0:T(8,128)(2,1)S(1)}, bf16[128,128]{1,0:T(8,128)(2,1)S(1)}, u32[]{:S(2)}, u32[]{:S(2)}) collective-permute-start(bf16[128,128]{1,0:T(8,128)(2,1)S(1)} %get-tuple-element.47), channel_id=1, source_target_pairs={{0,3},{1,2},{2,1},{3,0},{4,7},{5,6},{6,5},{7,4},{8,11},{9,10},{10,... | collective-permute-start | bytes 98312 | tf_op jit(solution)/shard_map/ppermute | solution.py:196
  24.3 6.9 %collective-permute-start.5 = (bf16[512,128]{1,0:T(8,128)(2,1)S(1)}, bf16[512,128]{1,0:T(8,128)(2,1)S(1)}, u32[]{:S(2)}, u32[]{:S(2)}) collective-permute-start(bf16[512,128]{1,0:T(8,128)(2,1)S(1)} %shard_map.86.refs_3_.refs_2_), channel_id=1, source_target_pairs={{0,4},{4,0},{8,12},{12,8},{16,20},{20,16},{24,28},{28,24},{1,5},{5... | collective-permute-start | bytes 393224 | tf_op jit(solution)/shard_map/ppermute | solution.py:196
  26.1 7.4 %collective-permute-start.4 = (bf16[512,128]{1,0:T(8,128)(2,1)S(1)}, bf16[512,128]{1,0:T(8,128)(2,1)S(1)}, u32[]{:S(2)}, u32[]{:S(2)}) collective-permute-start(bf16[512,128]{1,0:T(8,128)(2,1)S(1)} %shard_map.86.refs_3_.refs_2_), channel_id=1, source_target_pairs={{0,8},{4,12},{8,0},{12,4},{16,24},{20,28},{24,16},{28,20},{1,9},{5... | collective-permute-start | bytes 393224 | tf_op jit(solution)/shard_map/ppermute | solution.py:196
  27.7 8.8 %collective-permute-start.3 = (bf16[512,128]{1,0:T(8,128)(2,1)S(1)}, bf16[512,128]{1,0:T(8,128)(2,1)S(1)}, u32[]{:S(2)}, u32[]{:S(2)}) collective-permute-start(bf16[512,128]{1,0:T(8,128)(2,1)S(1)} %shard_map.86.refs_3_.refs_2_), channel_id=1, source_target_pairs={{0,16},{4,20},{8,24},{12,28},{16,0},{20,4},{24,8},{28,12},{1,17},{... | collective-permute-start | bytes 393224 | tf_op jit(solution)/shard_map/ppermute | solution.py:196
  40.3 5.7 %collective-permute-start.11 = (bf16[512,128]{1,0:T(8,128)(2,1)S(1)}, bf16[512,128]{1,0:T(8,128)(2,1)S(1)}, u32[]{:S(2)}, u32[]{:S(2)}) collective-permute-start(bf16[512,128]{1,0:T(8,128)(2,1)S(1)} %get-tuple-element.72), channel_id=1, source_target_pairs={{0,4},{4,0},{8,12},{12,8},{16,20},{20,16},{24,28},{28,24},{1,5},{5... | collective-permute-start | bytes 393224 | tf_op jit(solution)/shard_map/ppermute | solution.py:196
  40.9 5.8 %collective-permute-start.12 = (bf16[512,128]{1,0:T(8,128)(2,1)S(1)}, bf16[512,128]{1,0:T(8,128)(2,1)S(1)}, u32[]{:S(2)}, u32[]{:S(2)}) collective-permute-start(bf16[512,128]{1,0:T(8,128)(2,1)S(1)} %get-tuple-element.73), channel_id=1, source_target_pairs={{0,8},{4,12},{8,0},{12,4},{16,24},{20,28},{24,16},{28,20},{1,9},{5... | collective-permute-start | bytes 393224 | tf_op jit(solution)/shard_map/ppermute | solution.py:196
  41.3 7.6 %collective-permute-start.13 = (bf16[512,128]{1,0:T(8,128)(2,1)S(1)}, bf16[512,128]{1,0:T(8,128)(2,1)S(1)}, u32[]{:S(2)}, u32[]{:S(2)}) collective-permute-start(bf16[512,128]{1,0:T(8,128)(2,1)S(1)} %get-tuple-element.74), channel_id=1, source_target_pairs={{0,16},{4,20},{8,24},{12,28},{16,0},{20,4},{24,8},{28,12},{1,17},{... | collective-permute-start | bytes 393224 | tf_op jit(solution)/shard_map/ppermute | solution.py:196
  43.9 6.7 %collective-permute-start.8 = (bf16[512,128]{1,0:T(8,128)(2,1)S(1)}, bf16[512,128]{1,0:T(8,128)(2,1)S(1)}, u32[]{:S(2)}, u32[]{:S(2)}) collective-permute-start(bf16[512,128]{1,0:T(8,128)(2,1)S(1)} %get-tuple-element.61), channel_id=1, source_target_pairs={{0,2},{1,3},{2,0},{3,1},{4,6},{5,7},{6,4},{7,5},{8,10},{9,11},{10,... | collective-permute-start | bytes 393224 | tf_op jit(solution)/shard_map/ppermute | solution.py:196
  45.4 5.6 %collective-permute-start.6 = (bf16[512,128]{1,0:T(8,128)(2,1)S(1)}, bf16[512,128]{1,0:T(8,128)(2,1)S(1)}, u32[]{:S(2)}, u32[]{:S(2)}) collective-permute-start(bf16[512,128]{1,0:T(8,128)(2,1)S(1)} %get-tuple-element.55), channel_id=1, source_target_pairs={{0,1},{1,0},{2,3},{3,2},{4,5},{5,4},{6,7},{7,6},{8,9},{9,8},{10,11... | collective-permute-start | bytes 393224 | tf_op jit(solution)/shard_map/ppermute | solution.py:196
  46.0 5.2 %collective-permute-start.10 = (bf16[512,128]{1,0:T(8,128)(2,1)S(1)}, bf16[512,128]{1,0:T(8,128)(2,1)S(1)}, u32[]{:S(2)}, u32[]{:S(2)}) collective-permute-start(bf16[512,128]{1,0:T(8,128)(2,1)S(1)} %get-tuple-element.70), channel_id=1, source_target_pairs={{0,3},{1,2},{2,1},{3,0},{4,7},{5,6},{6,5},{7,4},{8,11},{9,10},{10,... | collective-permute-start | bytes 393224 | tf_op jit(solution)/shard_map/ppermute | solution.py:196
  49.0 3.2 %collective-permute-start.14 = (bf16[128,128]{1,0:T(8,128)(2,1)S(1)}, bf16[128,128]{1,0:T(8,128)(2,1)S(1)}, u32[]{:S(2)}, u32[]{:S(2)}) collective-permute-start(bf16[128,128]{1,0:T(8,128)(2,1)S(1)} %get-tuple-element.76), channel_id=1, source_target_pairs={{0,1},{1,0},{2,3},{3,2},{4,5},{5,4},{6,7},{7,6},{8,9},{9,8},{10,11... | collective-permute-start | bytes 98312 | tf_op jit(solution)/shard_map/ppermute | solution.py:196
  49.1 4.0 %collective-permute-start.15 = (bf16[128,128]{1,0:T(8,128)(2,1)S(1)}, bf16[128,128]{1,0:T(8,128)(2,1)S(1)}, u32[]{:S(2)}, u32[]{:S(2)}) collective-permute-start(bf16[128,128]{1,0:T(8,128)(2,1)S(1)} %get-tuple-element.77), channel_id=1, source_target_pairs={{0,2},{1,3},{2,0},{3,1},{4,6},{5,7},{6,4},{7,5},{8,10},{9,11},{10,... | collective-permute-start | bytes 98312 | tf_op jit(solution)/shard_map/ppermute | solution.py:196
  50.7 3.4 %collective-permute-start.16 = (bf16[128,128]{1,0:T(8,128)(2,1)S(1)}, bf16[128,128]{1,0:T(8,128)(2,1)S(1)}, u32[]{:S(2)}, u32[]{:S(2)}) collective-permute-start(bf16[128,128]{1,0:T(8,128)(2,1)S(1)} %get-tuple-element.78), channel_id=1, source_target_pairs={{0,3},{1,2},{2,1},{3,0},{4,7},{5,6},{6,5},{7,4},{8,11},{9,10},{10,... | collective-permute-start | bytes 98312 | tf_op jit(solution)/shard_map/ppermute | solution.py:196

commit v3 on v2

--- a/solution.py
+++ b/solution.py
@@ -8,12 +8,14 @@
 from jax.experimental.pallas import tpu as pltpu
 from jax.sharding import PartitionSpec as P
 
+
 HEAD_DIM = 128
 GROUP = 8
 PAIRS = GROUP // 2
 DOT_ROWS = 32
 VMEM_BYTES = 16 * 1024 * 1024
 
+
 F32 = jnp.float32
 BF16 = jnp.bfloat16
 
@@ -40,36 +42,67 @@
     return jax.ShapeDtypeStruct(shape, dtype)
 
 
-def call(kernel, out_shapes, place, *args, inside=True):
-    if inside:
-        args = [pltpu.with_memory_space_constraint(a, pltpu.VMEM) for a in args]
+def call(kernel, out_shapes, place, *args, space=pltpu.VMEM, scratch=()):
+    args = [pltpu.with_memory_space_constraint(a, space) for a in args]
     return pl.pallas_call(
         kernel,
         out_shape=out_shapes,
         in_specs=[pl.BlockSpec(memory_space=pltpu.SMEM)]
-        + [pl.BlockSpec(memory_space=pltpu.VMEM) for _ in args],
+        + [pl.BlockSpec(memory_space=space) for _ in args],
         out_specs=[pl.BlockSpec(memory_space=pltpu.VMEM) for _ in out_shapes],
+        scratch_shapes=scratch,
         compiler_params=pltpu.CompilerParams(vmem_limit_bytes=VMEM_BYTES),
     )(place, *args)
 
 
-def pack_kernel(parts, place, q_ref, g_ref, o_ref, k_ref, v_ref, l_ref, *outs):
-    qg_refs, kv_refs, lse_ref = outs[:parts], outs[parts : 2 * parts - 1], outs[2 * parts - 1]
+def load_kernel(parts, place, q_any, g_any, o_any, k_any, v_any, l_any, *refs):
+    q_ref, g_ref, o_ref = refs[:3]
+    kv_refs, lse_ref = refs[3 : 3 + parts], refs[3 + parts]
+    k_ref, v_ref, l_ref, sems = refs[4 + parts :]
+    own = place[0]
+    rows = k_ref.shape[0]
+    copies = [
+        pltpu.make_async_copy(source, target, sems.at[i])
+        for i, (source, target) in enumerate(
+            [
+                (k_any, k_ref),
+                (v_any, v_ref),
+                (l_any, l_ref),
+                (q_any, q_ref),
+                (g_any, g_ref),
+                (o_any, o_ref),
+            ]
+        )
+    ]
+    for copy in copies:
+        copy.start()
+    copies[0].wait()
+    copies[1].wait()
+    for m in range(parts):
+        col = pl.multiple_of((own ^ m) * HEAD_DIM, HEAD_DIM)
+        kv_refs[m][:rows, :] = k_ref[:, pl.ds(col, HEAD_DIM)]
+        kv_refs[m][rows:, :] = v_ref[:, pl.ds(col, HEAD_DIM)]
+    copies[2].wait()
+    for m in range(parts):
+        piece = l_ref[:, :rows]
+        for c in range(1, parts):
+            piece = jnp.where((own ^ m) == c, l_ref[:, c * rows : (c + 1) * rows], piece)
+        piece = piece * math.log2(math.e)
+        lse_ref[8 * m : 8 * m + PAIRS, :] = jnp.concatenate([piece[:PAIRS], piece[PAIRS:]], axis=1)
+        lse_ref[8 * m + PAIRS : 8 * m + 8, :] = jnp.zeros((8 - PAIRS, 2 * rows), F32)
+    for copy in copies[3:]:
+        copy.wait()
+
+
+def pack_kernel(parts, place, q_ref, g_ref, o_ref, kv_ref, *qg_refs):
     own = place[0]
     rows = q_ref.shape[0]
     width = GROUP * HEAD_DIM
     lane = lax.broadcasted_iota(jnp.int32, (2 * rows, HEAD_DIM), 1)
     dots = jnp.zeros((2 * rows, HEAD_DIM), F32)
-    start = 2 * GROUP * rows + DOT_ROWS
+    qg_refs[1][2 * GROUP * rows + DOT_ROWS :, :] = kv_ref[...]
     for m in range(parts):
         peer = own ^ m
-        col = pl.multiple_of(peer * HEAD_DIM, HEAD_DIM)
-        if m == 1:
-            target = qg_refs[1].at[start : start + 2 * rows]
-        else:
-            target = kv_refs[max(m - 1, 0)]
-        target[:rows, :] = k_ref[:, pl.ds(col, HEAD_DIM)]
-        target[rows:, :] = v_ref[:, pl.ds(col, HEAD_DIM)]
         sums = []
         for i, h in enumerate(HEAD_ORDER):
             col = pl.multiple_of(peer * width + h * HEAD_DIM, HEAD_DIM)
@@ -91,13 +124,6 @@
         qg_refs[m][first : first + DOT_ROWS, :] = jnp.concatenate(
             [high, mid, low, jnp.zeros_like(high)], axis=0
         ).astype(BF16)
-    for m in range(parts):
-        piece = l_ref[:, :rows]
-        for c in range(1, parts):
-            piece = jnp.where((own ^ m) == c, l_ref[:, c * rows : (c + 1) * rows], piece)
-        piece = piece * math.log2(math.e)
-        lse_ref[8 * m : 8 * m + PAIRS, :] = jnp.concatenate([piece[:PAIRS], piece[PAIRS:]], axis=1)
-        lse_ref[8 * m + PAIRS : 8 * m + 8, :] = jnp.zeros((8 - PAIRS, 2 * rows), F32)
 
 
 def join_kernel(parts, place, *refs):
@@ -204,11 +230,10 @@
     span = rows * GROUP
     place = lax.axis_index("head").astype(jnp.int32).reshape(1)
 
-    sizes = [2 * span + DOT_ROWS + (2 * rows if m == 1 else 0) for m in range(parts)]
-    packed = call(
-        functools.partial(pack_kernel, parts),
-        [vmem((size, HEAD_DIM), BF16) for size in sizes]
-        + [vmem((2 * rows, HEAD_DIM), BF16)] * (parts - 1)
+    loaded = call(
+        functools.partial(load_kernel, parts),
+        [vmem(queries.shape, BF16)] * 3
+        + [vmem((2 * rows, HEAD_DIM), BF16)] * parts
         + [vmem((8 * parts, 2 * rows), F32)],
         place,
         queries,
@@ -217,16 +242,29 @@
         key_rows,
         value_rows,
         logsumexp,
-        inside=False,
-    )
-    qg, kv, lse = list(packed[:parts]), list(packed[parts:-1]), packed[-1]
-    kv = [kv[0], None] + [swap(kv[m - 1], "head", m) for m in range(2, parts)]
+        space=pltpu.HBM,
+        scratch=[
+            vmem(key_rows.shape, BF16),
+            vmem(value_rows.shape, BF16),
+            vmem(logsumexp.shape, F32),
+            pltpu.SemaphoreType.DMA((6,)),
+        ],
+    )
+    kv, lse = list(loaded[3:-1]), loaded[-1]
+    sizes = [2 * span + DOT_ROWS + (2 * rows if m == 1 else 0) for m in range(parts)]
+    qg = call(
+        functools.partial(pack_kernel, parts),
+        [vmem((size, HEAD_DIM), BF16) for size in sizes],
+        place,
+        *loaded[:3],
+        kv[1],
+    )
     qg = [qg[0]] + [swap(qg[m], "head", m) for m in range(1, parts)]
-    kv[1] = qg[1]
+    kv = [kv[0], qg[1]] + [swap(kv[m], "head", m) for m in range(2, parts)]
     (kv_own,) = call(
         functools.partial(join_kernel, parts), [vmem((2 * block, HEAD_DIM), BF16)], place, *kv
     )
-    kv_all = [kv_own] + [swap(kv_own, "ctx", 1 << b) for b in range(levels - 1)]
+    kv_all = [kv_own] + [swap(kv_own, "ctx", 1 << (b - 1)) for b in range(1, levels)]
 
     dq = [None] * parts
     acc = [None] * levels

time: 55.1 us -> 50.8 us (0.922)
  local copies, waits for them, and re-layouts: 5.49 us -> 0 us
  Pallas kernels: 10.1 us -> 11.5 us
    unnamed x12 -> x0, local copies, waits for them, and re-layouts: 5.49 us -> none
    pallas_call x14 -> x15, Pallas kernels: 10.1 us -> 11.5 us  [call(): pl.pallas_call(kernel, out_shape=out_shapes, in_specs=[pl.BlockSpec(memor...]
  transfers between devices with their start and end apart: 17 -> 17, of which waited for: 8 -> 8; matrix products, arithmetic and copies ran while one was open for 0% -> 0% of each run, Pallas kernels for 13% -> 14%
where the time goes in v3:
time: 50.8 us; the launch traced here: 50.6 us
  waiting for transfers between devices  19.8 us (39%)
  starting transfers between devices  18.6 us (37%)
  Pallas kernels  11.5 us (23%)
  between operations  0.76 us (1%)
    ppermute x17, waiting for transfers between devices, swap(): lax.ppermute(value, axis, [(i, i ^ distance) for i in range(lax.axis_size...  19.8 us
    ppermute x17, starting transfers between devices, swap(): lax.ppermute(value, axis, [(i, i ^ distance) for i in range(lax.axis_size...  18.6 us
    pallas_call x15, Pallas kernels, call(): pl.pallas_call(kernel, out_shape=out_shapes, in_specs=[pl.BlockSpec(memor...  11.5 us
  transfers between devices with their start and end apart: 17, of which 8 were waited for; matrix products, arithmetic and copies ran while one was open for 0% of the time, Pallas kernels for 14%

profile of v3, /device:TPU:0, one launch (start us, length us, event | category | flops | bytes accessed | tf_op | source)
XLA Modules:
  0.0 50.6 jit_solution(13970972217949958596)
XLA Ops:
  0.6 1.5 %shard_map.85 = (bf16[64,4096]{1,0:T(8,128)(2,1)S(1)}, bf16[64,4096]{1,0:T(8,128)(2,1)S(1)}, bf16[64,4096]{1,0:T(8,128)(2,1)S(1)}, bf16[128,128]{1,0:T(8,128)(2,...) custom-call(s32[1]{0:T(128)} %bitcast.place, ...), custom_call_target="tpu_custom_call" | custom-call | tf_op jit(solution)/shard_map/pallas_call | solution.py:47
  2.1 0.9 %shard_map.86 = (bf16[1056,128]{1,0:T(8,128)(2,1)S(1)}, bf16[1184,128]{1,0:T(8,128)(2,1)S(1)}, bf16[1056,128]{1,0:T(8,128)(2,1)S(1)}, bf16[1056,128]{1,0:T(8,128)(2,1)S(1)}) custom-call(s32[1]{0:T(128)} %bitcast.place, bf16[64,4096]{1,0:T(8,128)(2,1)S(1)} %get-tuple-element.46.q_ref, bf16[64,4096]{1,0:T(8,128)(2,1)S(1)} %get-tuple-element.47.g_ref, ...), custom_call_target="tpu_custom_call" | custom-call | tf_op jit(solution)/shard_map/pallas_call | solution.py:47
  3.1 0.6 %collective-permute-start = (bf16[1184,128]{1,0:T(8,128)(2,1)S(1)}, bf16[1184,128]{1,0:T(8,128)(2,1)S(1)}, u32[]{:S(2)}, u32[]{:S(2)}) collective-permute-start(bf16[1184,128]{1,0:T(8,128)(2,1)S(1)} %get-tuple-element.51), channel_id=1, source_target_pairs={{0,1},{1,0},{2,3},{3,2},{4,5},{5,4},{6,7},{7,6},{8,9},{9,8},{10,11... | collective-permute-start | bytes 909320 | tf_op jit(solution)/shard_map/ppermute | solution.py:222
  3.6 2.6 %collective-permute-start.7 = (bf16[1056,128]{1,0:T(8,128)(2,1)S(1)}, bf16[1056,128]{1,0:T(8,128)(2,1)S(1)}, u32[]{:S(2)}, u32[]{:S(2)}) collective-permute-start(bf16[1056,128]{1,0:T(8,128)(2,1)S(1)} %get-tuple-element.64), channel_id=1, source_target_pairs={{0,2},{1,3},{2,0},{3,1},{4,6},{5,7},{6,4},{7,5},{8,10},{9,11},{10,... | collective-permute-start | bytes 811016 | tf_op jit(solution)/shard_map/ppermute | solution.py:222
  6.2 1.7 %collective-permute-start.1 = (bf16[128,128]{1,0:T(8,128)(2,1)S(1)}, bf16[128,128]{1,0:T(8,128)(2,1)S(1)}, u32[]{:S(2)}, u32[]{:S(2)}) collective-permute-start(bf16[128,128]{1,0:T(8,128)(2,1)S(1)} %get-tuple-element.54), channel_id=1, source_target_pairs={{0,2},{1,3},{2,0},{3,1},{4,6},{5,7},{6,4},{7,5},{8,10},{9,11},{10,... | collective-permute-start | bytes 98312 | tf_op jit(solution)/shard_map/ppermute | solution.py:222
  8.0 12.0 %collective-permute-done.1.refs_2_ = bf16[128,128]{1,0:T(8,128)(2,1)S(1)} collective-permute-done((bf16[128,128]{1,0:T(8,128)(2,1)S(1)}, bf16[128,128]{1,0:T(8,128)(2,1)S(1)}, u32[]{:S(2)}, u32[]{:S(2)}) %collective-permute-start.1) | collective-permute-done | bytes 32800 | tf_op jit(solution)/shard_map/ppermute | solution.py:222
  20.2 1.8 %collective-permute-start.5 = (bf16[512,128]{1,0:T(8,128)(2,1)S(1)}, bf16[512,128]{1,0:T(8,128)(2,1)S(1)}, u32[]{:S(2)}, u32[]{:S(2)}) collective-permute-start(bf16[512,128]{1,0:T(8,128)(2,1)S(1)} %shard_map.87.refs_3_.refs_2_), channel_id=1, source_target_pairs={{0,4},{4,0},{8,12},{12,8},{16,20},{20,16},{24,28},{28,24},{1,5},{5... | collective-permute-start | bytes 393224 | tf_op jit(solution)/shard_map/ppermute | solution.py:222
  22.0 1.6 %collective-permute-start.4 = (bf16[512,128]{1,0:T(8,128)(2,1)S(1)}, bf16[512,128]{1,0:T(8,128)(2,1)S(1)}, u32[]{:S(2)}, u32[]{:S(2)}) collective-permute-start(bf16[512,128]{1,0:T(8,128)(2,1)S(1)} %shard_map.87.refs_3_.refs_2_), channel_id=1, source_target_pairs={{0,8},{4,12},{8,0},{12,4},{16,24},{20,28},{24,16},{28,20},{1,9},{5... | collective-permute-start | bytes 393224 | tf_op jit(solution)/shard_map/ppermute | solution.py:222
  23.5 2.6 %collective-permute-start.3 = (bf16[512,128]{1,0:T(8,128)(2,1)S(1)}, bf16[512,128]{1,0:T(8,128)(2,1)S(1)}, u32[]{:S(2)}, u32[]{:S(2)}) collective-permute-start(bf16[512,128]{1,0:T(8,128)(2,1)S(1)} %shard_map.87.refs_3_.refs_2_), channel_id=1, source_target_pairs={{0,16},{4,20},{8,24},{12,28},{16,0},{20,4},{24,8},{28,12},{1,17},{... | collective-permute-start | bytes 393224 | tf_op jit(solution)/shard_map/ppermute | solution.py:222
  26.1 0.9 %shard_map.88 = (f32[128,512]{1,0:T(8,128)S(1)}, f32[128,512]{1,0:T(8,128)S(1)}, f32[512,128]{1,0:T(8,128)S(1)}) custom-call(s32[1]{0:T(128)} %bitcast.place, bf16[1056,128]{1,0:T(8,128)(2,1)S(1)} %get-tuple-element.50.refs_0_, bf16[1184,128]{1,0:T(8,128)(2,1)S(1)} %collective-permute-done.refs_1_, f32[32,128]{1,0:T(8,128)S(1)} %get-tuple-element.52.refs_2_.refs_1_, ...), custom_call_target="tpu_custom_call" | custom-call | tf_op jit(solution)/shard_map/pallas_call | solution.py:47
  27.1 0.9 %shard_map.89 = (f32[128,512]{1,0:T(8,128)S(1)}, f32[128,512]{1,0:T(8,128)S(1)}, f32[512,128]{1,0:T(8,128)S(1)}) custom-call(s32[1]{0:T(128)} %bitcast.place, bf16[1056,128]{1,0:T(8,128)(2,1)S(1)} %get-tuple-element.50.refs_0_, bf16[1184,128]{1,0:T(8,128)(2,1)S(1)} %collective-permute-done.refs_1_, f32[32,128]{1,0:T(8,128)S(1)} %get-tuple-element.52.refs_2_.refs_1_, ...), custom_call_target="tpu_custom_call" | custom-call | tf_op jit(solution)/shard_map/pallas_call | solution.py:47
  28.0 1.3 %collective-permute-done.4.refs_3_.refs_4_.refs_2_ = bf16[512,128]{1,0:T(8,128)(2,1)S(1)} collective-permute-done((bf16[512,128]{1,0:T(8,128)(2,1)S(1)}, bf16[512,128]{1,0:T(8,128)(2,1)S(1)}, u32[]{:S(2)}, u32[]{:S(2)}) %collective-permute-start.4) | collective-permute-done | bytes 131104 | tf_op jit(solution)/shard_map/ppermute | solution.py:222
  29.3 0.9 %shard_map.90 = (f32[128,512]{1,0:T(8,128)S(1)}, f32[128,512]{1,0:T(8,128)S(1)}, f32[512,128]{1,0:T(8,128)S(1)}) custom-call(s32[1]{0:T(128)} %bitcast.place, bf16[1056,128]{1,0:T(8,128)(2,1)S(1)} %get-tuple-element.50.refs_0_, bf16[1184,128]{1,0:T(8,128)(2,1)S(1)} %collective-permute-done.refs_1_, f32[32,128]{1,0:T(8,128)S(1)} %get-tuple-element.52.refs_2_.refs_1_, ...), custom_call_target="tpu_custom_call" | custom-call | tf_op jit(solution)/shard_map/pallas_call | solution.py:47
  30.3 2.0 %collective-permute-done.3.refs_3_.refs_5_.refs_2_ = bf16[512,128]{1,0:T(8,128)(2,1)S(1)} collective-permute-done((bf16[512,128]{1,0:T(8,128)(2,1)S(1)}, bf16[512,128]{1,0:T(8,128)(2,1)S(1)}, u32[]{:S(2)}, u32[]{:S(2)}) %collective-permute-start.3) | collective-permute-done | bytes 131104 | tf_op jit(solution)/shard_map/ppermute | solution.py:222
  32.3 0.9 %shard_map.91 = (f32[512,128]{1,0:T(8,128)S(1)}, bf16[512,128]{1,0:T(8,128)(2,1)S(1)}, f32[512,128]{1,0:T(8,128)S(1)}) custom-call(s32[1]{0:T(128)} %bitcast.place, bf16[1056,128]{1,0:T(8,128)(2,1)S(1)} %get-tuple-element.50.refs_0_, bf16[1184,128]{1,0:T(8,128)(2,1)S(1)} %collective-permute-done.refs_1_, f32[32,128]{1,0:T(8,128)S(1)} %get-tuple-element.52.refs_2_.refs_1_, ...), custom_call_target="tpu_custom_call" | custom-call | tf_op jit(solution)/shard_map/pallas_call | solution.py:47
  33.2 1.5 %shard_map.92 = (bf16[512,128]{1,0:T(8,128)(2,1)S(1)}, f32[512,128]{1,0:T(8,128)S(1)}, f32[512,128]{1,0:T(8,128)S(1)}, f32[512,128]{1,0:T(8,128)S(1)}, f32[512,128]{1,0:T(8,128)S(1)}) custom-call(s32[1]{0:T(128)} %bitcast.place, bf16[1056,128]{1,0:T(8,128)(2,1)S(1)} %collective-permute-done.7.refs_0_, f32[32,128]{1,0:T(8,128)S(1)} %get-tuple-element.52.refs_2_.refs_1_, ...), custom_call_target="tpu_custom_call" | custom-call | tf_op jit(solution)/shard_map/pallas_call | solution.py:47
  34.8 0.5 shard_map.93
  35.2 0.5 shard_map.94
  35.7 0.5 shard_map.95
  36.2 0.6 %collective-permute-start.11 = (bf16[512,128]{1,0:T(8,128)(2,1)S(1)}, bf16[512,128]{1,0:T(8,128)(2,1)S(1)}, u32[]{:S(2)}, u32[]{:S(2)}) collective-permute-start(bf16[512,128]{1,0:T(8,128)(2,1)S(1)} %get-tuple-element.80), channel_id=1, source_target_pairs={{0,4},{4,0},{8,12},{12,8},{16,20},{20,16},{24,28},{28,24},{1,5},{5... | collective-permute-start | bytes 393224 | tf_op jit(solution)/shard_map/ppermute | solution.py:222
  36.8 0.4 collective-permute-start.12
  37.2 2.6 %collective-permute-start.13 = (bf16[512,128]{1,0:T(8,128)(2,1)S(1)}, bf16[512,128]{1,0:T(8,128)(2,1)S(1)}, u32[]{:S(2)}, u32[]{:S(2)}) collective-permute-start(bf16[512,128]{1,0:T(8,128)(2,1)S(1)} %get-tuple-element.82), channel_id=1, source_target_pairs={{0,16},{4,20},{8,24},{12,28},{16,0},{20,4},{24,8},{28,12},{1,17},{... | collective-permute-start | bytes 393224 | tf_op jit(solution)/shard_map/ppermute | solution.py:222
  39.8 1.5 %collective-permute-start.8 = (bf16[512,128]{1,0:T(8,128)(2,1)S(1)}, bf16[512,128]{1,0:T(8,128)(2,1)S(1)}, u32[]{:S(2)}, u32[]{:S(2)}) collective-permute-start(bf16[512,128]{1,0:T(8,128)(2,1)S(1)} %get-tuple-element.69), channel_id=1, source_target_pairs={{0,2},{1,3},{2,0},{3,1},{4,6},{5,7},{6,4},{7,5},{8,10},{9,11},{10,... | collective-permute-start | bytes 393224 | tf_op jit(solution)/shard_map/ppermute | solution.py:222
  41.3 0.6 %shard_map.96 = (bf16[512,128]{1,0:T(8,128)(2,1)S(1)}, f32[512,128]{1,0:T(8,128)S(1)}) custom-call(s32[1]{0:T(128)} %bitcast.place, bf16[1056,128]{1,0:T(8,128)(2,1)S(1)} %collective-permute-done.9.refs_0_, f32[32,128]{1,0:T(8,128)S(1)} %get-tuple-element.52.refs_2_.refs_1_, bf16[512,128]{1,0:T(8,128)(2,1)S(1)} %shard_map.87.refs_3_.refs_2_, ...), custom_call_target="tpu_custom_call" | custom-call | tf_op jit(solution)/shard_map/pallas_call | solution.py:47
  41.9 0.7 %collective-permute-start.10 = (bf16[512,128]{1,0:T(8,128)(2,1)S(1)}, bf16[512,128]{1,0:T(8,128)(2,1)S(1)}, u32[]{:S(2)}, u32[]{:S(2)}) collective-permute-start(bf16[512,128]{1,0:T(8,128)(2,1)S(1)} %get-tuple-element.78), channel_id=1, source_target_pairs={{0,3},{1,2},{2,1},{3,0},{4,7},{5,6},{6,5},{7,4},{8,11},{9,10},{10,... | collective-permute-start | bytes 393224 | tf_op jit(solution)/shard_map/ppermute | solution.py:222
  42.6 2.2 %collective-permute-done.13.refs_3_ = bf16[512,128]{1,0:T(8,128)(2,1)S(1)} collective-permute-done((bf16[512,128]{1,0:T(8,128)(2,1)S(1)}, bf16[512,128]{1,0:T(8,128)(2,1)S(1)}, u32[]{:S(2)}, u32[]{:S(2)}) %collective-permute-start.13) | collective-permute-done | bytes 131104 | tf_op jit(solution)/shard_map/ppermute | solution.py:222
  45.0 1.6 %collective-permute-start.15 = (bf16[128,128]{1,0:T(8,128)(2,1)S(1)}, bf16[128,128]{1,0:T(8,128)(2,1)S(1)}, u32[]{:S(2)}, u32[]{:S(2)}) collective-permute-start(bf16[128,128]{1,0:T(8,128)(2,1)S(1)} %get-tuple-element.85), channel_id=1, source_target_pairs={{0,2},{1,3},{2,0},{3,1},{4,6},{5,7},{6,4},{7,5},{8,10},{9,11},{10,... | collective-permute-start | bytes 98312 | tf_op jit(solution)/shard_map/ppermute | solution.py:222
  46.6 0.3 collective-permute-start.16
  47.1 1.1 %shard_map.97 = f32[64,4096]{1,0:T(8,128)} custom-call(s32[1]{0:T(128)} %bitcast.place, f32[512,128]{1,0:T(8,128)S(1)} %get-tuple-element.62.refs_0_, bf16[512,128]{1,0:T(8,128)(2,1)S(1)} %collective-permute-done.6.refs_1_, bf16[512,128]{1,0:T(8,128)(2,1)S(1)} %collective-permute-done.8.refs_2_, bf16[512,128]{1,0:T(8,128)(2,1)S(1)} %collective-permute-done.10.refs_3_), custom_call_target="tpu_custom_call" | custom-call | tf_op jit(solution)/shard_map/pallas_call | solution.py:47
  48.2 0.8 %collective-permute-done.15.refs_2_ = bf16[128,128]{1,0:T(8,128)(2,1)S(1)} collective-permute-done((bf16[128,128]{1,0:T(8,128)(2,1)S(1)}, bf16[128,128]{1,0:T(8,128)(2,1)S(1)}, u32[]{:S(2)}, u32[]{:S(2)}) %collective-permute-start.15) | collective-permute-done | bytes 32800 | tf_op jit(solution)/shard_map/ppermute | solution.py:222
  49.0 0.9 %collective-permute-done.16.refs_3_ = bf16[128,128]{1,0:T(8,128)(2,1)S(1)} collective-permute-done((bf16[128,128]{1,0:T(8,128)(2,1)S(1)}, bf16[128,128]{1,0:T(8,128)(2,1)S(1)}, u32[]{:S(2)}, u32[]{:S(2)}) %collective-permute-start.16) | collective-permute-done | bytes 32800 | tf_op jit(solution)/shard_map/ppermute | solution.py:222
  49.9 0.7 %shard_map.99 = (f32[64,512]{1,0:T(8,128)}, f32[64,512]{1,0:T(8,128)}) custom-call(s32[1]{0:T(128)} %bitcast.place, f32[128,128]{1,0:T(8,128)S(1)} %get-tuple-element.83.refs_0_, bf16[128,128]{1,0:T(8,128)(2,1)S(1)} %collective-permute-done.14.refs_1_, bf16[128,128]{1,0:T(8,128)(2,1)S(1)} %collective-permute-done.15.refs_2_, ...), custom_call_target="tpu_custom_call" | custom-call | tf_op jit(solution)/shard_map/pallas_call | solution.py:47
  (17 shorter events, 0.6 us)
Async XLA Ops:
  3.1 17.1 %collective-permute-start = (bf16[1184,128]{1,0:T(8,128)(2,1)S(1)}, bf16[1184,128]{1,0:T(8,128)(2,1)S(1)}, u32[]{:S(2)}, u32[]{:S(2)}) collective-permute-start(bf16[1184,128]{1,0:T(8,128)(2,1)S(1)} %get-tuple-element.51), channel_id=1, source_target_pairs={{0,1},{1,0},{2,3},{3,2},{4,5},{5,4},{6,7},{7,6},{8,9},{9,8},{10,11... | collective-permute-start | bytes 909320 | tf_op jit(solution)/shard_map/ppermute | solution.py:222
  3.6 29.6 %collective-permute-start.7 = (bf16[1056,128]{1,0:T(8,128)(2,1)S(1)}, bf16[1056,128]{1,0:T(8,128)(2,1)S(1)}, u32[]{:S(2)}, u32[]{:S(2)}) collective-permute-start(bf16[1056,128]{1,0:T(8,128)(2,1)S(1)} %get-tuple-element.64), channel_id=1, source_target_pairs={{0,2},{1,3},{2,0},{3,1},{4,6},{5,7},{6,4},{7,5},{8,10},{9,11},{10,... | collective-permute-start | bytes 811016 | tf_op jit(solution)/shard_map/ppermute | solution.py:222
  6.2 28.6 %collective-permute-start.9 = (bf16[1056,128]{1,0:T(8,128)(2,1)S(1)}, bf16[1056,128]{1,0:T(8,128)(2,1)S(1)}, u32[]{:S(2)}, u32[]{:S(2)}) collective-permute-start(bf16[1056,128]{1,0:T(8,128)(2,1)S(1)} %get-tuple-element.70), channel_id=1, source_target_pairs={{0,3},{1,2},{2,1},{3,0},{4,7},{5,6},{6,5},{7,4},{8,11},{9,10},{10,... | collective-permute-start | bytes 811016 | tf_op jit(solution)/shard_map/ppermute | solution.py:222
  6.2 13.8 %collective-permute-start.1 = (bf16[128,128]{1,0:T(8,128)(2,1)S(1)}, bf16[128,128]{1,0:T(8,128)(2,1)S(1)}, u32[]{:S(2)}, u32[]{:S(2)}) collective-permute-start(bf16[128,128]{1,0:T(8,128)(2,1)S(1)} %get-tuple-element.54), channel_id=1, source_target_pairs={{0,2},{1,3},{2,0},{3,1},{4,6},{5,7},{6,4},{7,5},{8,10},{9,11},{10,... | collective-permute-start | bytes 98312 | tf_op jit(solution)/shard_map/ppermute | solution.py:222
  8.0 12.2 %collective-permute-start.2 = (bf16[128,128]{1,0:T(8,128)(2,1)S(1)}, bf16[128,128]{1,0:T(8,128)(2,1)S(1)}, u32[]{:S(2)}, u32[]{:S(2)}) collective-permute-start(bf16[128,128]{1,0:T(8,128)(2,1)S(1)} %get-tuple-element.55), channel_id=1, source_target_pairs={{0,3},{1,2},{2,1},{3,0},{4,7},{5,6},{6,5},{7,4},{8,11},{9,10},{10,... | collective-permute-start | bytes 98312 | tf_op jit(solution)/shard_map/ppermute | solution.py:222
  20.2 6.8 %collective-permute-start.5 = (bf16[512,128]{1,0:T(8,128)(2,1)S(1)}, bf16[512,128]{1,0:T(8,128)(2,1)S(1)}, u32[]{:S(2)}, u32[]{:S(2)}) collective-permute-start(bf16[512,128]{1,0:T(8,128)(2,1)S(1)} %shard_map.87.refs_3_.refs_2_), channel_id=1, source_target_pairs={{0,4},{4,0},{8,12},{12,8},{16,20},{20,16},{24,28},{28,24},{1,5},{5... | collective-permute-start | bytes 393224 | tf_op jit(solution)/shard_map/ppermute | solution.py:222
  22.0 7.4 %collective-permute-start.4 = (bf16[512,128]{1,0:T(8,128)(2,1)S(1)}, bf16[512,128]{1,0:T(8,128)(2,1)S(1)}, u32[]{:S(2)}, u32[]{:S(2)}) collective-permute-start(bf16[512,128]{1,0:T(8,128)(2,1)S(1)} %shard_map.87.refs_3_.refs_2_), channel_id=1, source_target_pairs={{0,8},{4,12},{8,0},{12,4},{16,24},{20,28},{24,16},{28,20},{1,9},{5... | collective-permute-start | bytes 393224 | tf_op jit(solution)/shard_map/ppermute | solution.py:222
  23.5 8.8 %collective-permute-start.3 = (bf16[512,128]{1,0:T(8,128)(2,1)S(1)}, bf16[512,128]{1,0:T(8,128)(2,1)S(1)}, u32[]{:S(2)}, u32[]{:S(2)}) collective-permute-start(bf16[512,128]{1,0:T(8,128)(2,1)S(1)} %shard_map.87.refs_3_.refs_2_), channel_id=1, source_target_pairs={{0,16},{4,20},{8,24},{12,28},{16,0},{20,4},{24,8},{28,12},{1,17},{... | collective-permute-start | bytes 393224 | tf_op jit(solution)/shard_map/ppermute | solution.py:222
  36.2 5.7 %collective-permute-start.11 = (bf16[512,128]{1,0:T(8,128)(2,1)S(1)}, bf16[512,128]{1,0:T(8,128)(2,1)S(1)}, u32[]{:S(2)}, u32[]{:S(2)}) collective-permute-start(bf16[512,128]{1,0:T(8,128)(2,1)S(1)} %get-tuple-element.80), channel_id=1, source_target_pairs={{0,4},{4,0},{8,12},{12,8},{16,20},{20,16},{24,28},{28,24},{1,5},{5... | collective-permute-start | bytes 393224 | tf_op jit(solution)/shard_map/ppermute | solution.py:222
  36.8 5.8 %collective-permute-start.12 = (bf16[512,128]{1,0:T(8,128)(2,1)S(1)}, bf16[512,128]{1,0:T(8,128)(2,1)S(1)}, u32[]{:S(2)}, u32[]{:S(2)}) collective-permute-start(bf16[512,128]{1,0:T(8,128)(2,1)S(1)} %get-tuple-element.81), channel_id=1, source_target_pairs={{0,8},{4,12},{8,0},{12,4},{16,24},{20,28},{24,16},{28,20},{1,9},{5... | collective-permute-start | bytes 393224 | tf_op jit(solution)/shard_map/ppermute | solution.py:222
  37.2 7.6 %collective-permute-start.13 = (bf16[512,128]{1,0:T(8,128)(2,1)S(1)}, bf16[512,128]{1,0:T(8,128)(2,1)S(1)}, u32[]{:S(2)}, u32[]{:S(2)}) collective-permute-start(bf16[512,128]{1,0:T(8,128)(2,1)S(1)} %get-tuple-element.82), channel_id=1, source_target_pairs={{0,16},{4,20},{8,24},{12,28},{16,0},{20,4},{24,8},{28,12},{1,17},{... | collective-permute-start | bytes 393224 | tf_op jit(solution)/shard_map/ppermute | solution.py:222
  39.8 6.7 %collective-permute-start.8 = (bf16[512,128]{1,0:T(8,128)(2,1)S(1)}, bf16[512,128]{1,0:T(8,128)(2,1)S(1)}, u32[]{:S(2)}, u32[]{:S(2)}) collective-permute-start(bf16[512,128]{1,0:T(8,128)(2,1)S(1)} %get-tuple-element.69), channel_id=1, source_target_pairs={{0,2},{1,3},{2,0},{3,1},{4,6},{5,7},{6,4},{7,5},{8,10},{9,11},{10,... | collective-permute-start | bytes 393224 | tf_op jit(solution)/shard_map/ppermute | solution.py:222
  41.3 5.5 %collective-permute-start.6 = (bf16[512,128]{1,0:T(8,128)(2,1)S(1)}, bf16[512,128]{1,0:T(8,128)(2,1)S(1)}, u32[]{:S(2)}, u32[]{:S(2)}) collective-permute-start(bf16[512,128]{1,0:T(8,128)(2,1)S(1)} %get-tuple-element.63), channel_id=1, source_target_pairs={{0,1},{1,0},{2,3},{3,2},{4,5},{5,4},{6,7},{7,6},{8,9},{9,8},{10,11... | collective-permute-start | bytes 393224 | tf_op jit(solution)/shard_map/ppermute | solution.py:222
  41.9 5.2 %collective-permute-start.10 = (bf16[512,128]{1,0:T(8,128)(2,1)S(1)}, bf16[512,128]{1,0:T(8,128)(2,1)S(1)}, u32[]{:S(2)}, u32[]{:S(2)}) collective-permute-start(bf16[512,128]{1,0:T(8,128)(2,1)S(1)} %get-tuple-element.78), channel_id=1, source_target_pairs={{0,3},{1,2},{2,1},{3,0},{4,7},{5,6},{6,5},{7,4},{8,11},{9,10},{10,... | collective-permute-start | bytes 393224 | tf_op jit(solution)/shard_map/ppermute | solution.py:222
  44.9 3.2 %collective-permute-start.14 = (bf16[128,128]{1,0:T(8,128)(2,1)S(1)}, bf16[128,128]{1,0:T(8,128)(2,1)S(1)}, u32[]{:S(2)}, u32[]{:S(2)}) collective-permute-start(bf16[128,128]{1,0:T(8,128)(2,1)S(1)} %get-tuple-element.84), channel_id=1, source_target_pairs={{0,1},{1,0},{2,3},{3,2},{4,5},{5,4},{6,7},{7,6},{8,9},{9,8},{10,11... | collective-permute-start | bytes 98312 | tf_op jit(solution)/shard_map/ppermute | solution.py:222
  45.0 4.0 %collective-permute-start.15 = (bf16[128,128]{1,0:T(8,128)(2,1)S(1)}, bf16[128,128]{1,0:T(8,128)(2,1)S(1)}, u32[]{:S(2)}, u32[]{:S(2)}) collective-permute-start(bf16[128,128]{1,0:T(8,128)(2,1)S(1)} %get-tuple-element.85), channel_id=1, source_target_pairs={{0,2},{1,3},{2,0},{3,1},{4,6},{5,7},{6,4},{7,5},{8,10},{9,11},{10,... | collective-permute-start | bytes 98312 | tf_op jit(solution)/shard_map/ppermute | solution.py:222
  46.6 3.4 %collective-permute-start.16 = (bf16[128,128]{1,0:T(8,128)(2,1)S(1)}, bf16[128,128]{1,0:T(8,128)(2,1)S(1)}, u32[]{:S(2)}, u32[]{:S(2)}) collective-permute-start(bf16[128,128]{1,0:T(8,128)(2,1)S(1)} %get-tuple-element.86), channel_id=1, source_target_pairs={{0,3},{1,2},{2,1},{3,0},{4,7},{5,6},{6,5},{7,4},{8,11},{9,10},{10,... | collective-permute-start | bytes 98312 | tf_op jit(solution)/shard_map/ppermute | solution.py:222

commit v4 on v3

--- a/solution.py
+++ b/solution.py
@@ -61,28 +61,20 @@
     k_ref, v_ref, l_ref, sems = refs[4 + parts :]
     own = place[0]
     rows = k_ref.shape[0]
+    pairs = [(k_any, k_ref), (v_any, v_ref), (l_any, l_ref)]
+    pairs += [(q_any, q_ref), (g_any, g_ref), (o_any, o_ref)]
     copies = [
         pltpu.make_async_copy(source, target, sems.at[i])
-        for i, (source, target) in enumerate(
-            [
-                (k_any, k_ref),
-                (v_any, v_ref),
-                (l_any, l_ref),
-                (q_any, q_ref),
-                (g_any, g_ref),
-                (o_any, o_ref),
-            ]
-        )
+        for i, (source, target) in enumerate(pairs)
     ]
     for copy in copies:
         copy.start()
-    copies[0].wait()
-    copies[1].wait()
+    for copy in copies[:3]:
+        copy.wait()
     for m in range(parts):
         col = pl.multiple_of((own ^ m) * HEAD_DIM, HEAD_DIM)
         kv_refs[m][:rows, :] = k_ref[:, pl.ds(col, HEAD_DIM)]
         kv_refs[m][rows:, :] = v_ref[:, pl.ds(col, HEAD_DIM)]
-    copies[2].wait()
     for m in range(parts):
         piece = l_ref[:, :rows]
         for c in range(1, parts):
@@ -94,45 +86,38 @@
         copy.wait()
 
 
-def pack_kernel(parts, place, q_ref, g_ref, o_ref, kv_ref, *qg_refs):
-    own = place[0]
+def pack_kernel(m, place, q_ref, g_ref, o_ref, qg_ref):
     rows = q_ref.shape[0]
-    width = GROUP * HEAD_DIM
+    span = GROUP * rows
+    base = (place[0] ^ m) * (GROUP * HEAD_DIM)
     lane = lax.broadcasted_iota(jnp.int32, (2 * rows, HEAD_DIM), 1)
     dots = jnp.zeros((2 * rows, HEAD_DIM), F32)
-    qg_refs[1][2 * GROUP * rows + DOT_ROWS :, :] = kv_ref[...]
-    for m in range(parts):
-        peer = own ^ m
-        sums = []
-        for i, h in enumerate(HEAD_ORDER):
-            col = pl.multiple_of(peer * width + h * HEAD_DIM, HEAD_DIM)
-            qg_refs[m][i * rows : (i + 1) * rows, :] = q_ref[:, pl.ds(col, HEAD_DIM)]
-            grad = g_ref[:, pl.ds(col, HEAD_DIM)]
-            qg_refs[m][(GROUP + i) * rows : (GROUP + i + 1) * rows, :] = grad
-            prod = grad.astype(F32) * o_ref[:, pl.ds(col, HEAD_DIM)].astype(F32)
-            sums.append(jnp.sum(prod, axis=1, keepdims=True))
-        for j in range(PAIRS):
-            pair = jnp.concatenate([sums[2 * j], sums[2 * j + 1]], axis=0)
-            dots = jnp.where(lane == 8 * m + j, pair, dots)
-    turned = dots.T
-    for m in range(parts):
-        full = turned[8 * m : 8 * m + 8, :]
-        high = full.astype(BF16).astype(F32)
-        mid = (full - high).astype(BF16).astype(F32)
-        low = (full - high) - mid
-        first = 2 * GROUP * rows
-        qg_refs[m][first : first + DOT_ROWS, :] = jnp.concatenate(
-            [high, mid, low, jnp.zeros_like(high)], axis=0
-        ).astype(BF16)
+    sums = []
+    for i, h in enumerate(HEAD_ORDER):
+        col = pl.multiple_of(base + h * HEAD_DIM, HEAD_DIM)
+        qg_ref[i * rows : (i + 1) * rows, :] = q_ref[:, pl.ds(col, HEAD_DIM)]
+        grad = g_ref[:, pl.ds(col, HEAD_DIM)]
+        qg_ref[span + i * rows : span + (i + 1) * rows, :] = grad
+        prod = grad.astype(F32) * o_ref[:, pl.ds(col, HEAD_DIM)].astype(F32)
+        sums.append(jnp.sum(prod, axis=1, keepdims=True))
+    for j in range(PAIRS):
+        pair = jnp.concatenate([sums[2 * j], sums[2 * j + 1]], axis=0)
+        dots = jnp.where(lane == j, pair, dots)
+    full = dots.T[:8, :]
+    high = full.astype(BF16).astype(F32)
+    mid = (full - high).astype(BF16).astype(F32)
+    low = (full - high) - mid
+    qg_ref[2 * span :, :] = jnp.concatenate([high, mid, low, jnp.zeros_like(high)], axis=0).astype(
+        BF16
+    )
 
 
 def join_kernel(parts, place, *refs):
     pieces, out = refs[:parts], refs[parts]
     rows = out.shape[0] // (2 * parts)
     for m in range(parts):
-        start = pieces[m].shape[0] - 2 * rows
-        out[m * rows : (m + 1) * rows, :] = pieces[m][start : start + rows, :]
-        out[(parts + m) * rows : (parts + m + 1) * rows, :] = pieces[m][start + rows :, :]
+        out[m * rows : (m + 1) * rows, :] = pieces[m][:rows, :]
+        out[(parts + m) * rows : (parts + m + 1) * rows, :] = pieces[m][rows:, :]
 
 
 def row_of(stack):
@@ -187,16 +172,17 @@
 
 
 def total_kernel(parts, levels, place, *refs):
-    terms, outs = refs[:levels], refs[levels:]
+    terms, near_dq, outs = refs[:levels], refs[levels], refs[levels + 1 :]
     total = terms[0][...]
     for term in terms[1:]:
         total = total + term[...].astype(F32)
     rows = total.shape[0] // (2 * parts)
     for m in range(parts):
         outs[m][:rows, :] = total[m * rows : (m + 1) * rows].astype(outs[m].dtype)
-        outs[m][rows:, :] = total[(parts + m) * rows : (parts + m + 1) * rows].astype(
+        outs[m][rows : 2 * rows, :] = total[(parts + m) * rows : (parts + m + 1) * rows].astype(
             outs[m].dtype
         )
+    outs[1][2 * rows :, :] = near_dq[...]
 
 
 def unpack_q_kernel(parts, place, *refs):
@@ -206,7 +192,8 @@
     for m in range(parts):
         for i, h in enumerate(HEAD_ORDER):
             col = pl.multiple_of((place[0] ^ m) * width + h * HEAD_DIM, HEAD_DIM)
-            out[:, pl.ds(col, HEAD_DIM)] = pieces[m][i * rows : (i + 1) * rows, :].astype(F32)
+            first = pieces[m].shape[0] - GROUP * rows + i * rows
+            out[:, pl.ds(col, HEAD_DIM)] = pieces[m][first : first + rows, :].astype(F32)
 
 
 def unpack_kv_kernel(parts, place, *refs):
@@ -215,7 +202,7 @@
     for m in range(parts):
         col = pl.multiple_of((place[0] ^ m) * HEAD_DIM, HEAD_DIM)
         out_k[:, pl.ds(col, HEAD_DIM)] = pieces[m][:rows, :].astype(F32)
-        out_v[:, pl.ds(col, HEAD_DIM)] = pieces[m][rows:, :].astype(F32)
+        out_v[:, pl.ds(col, HEAD_DIM)] = pieces[m][rows : 2 * rows, :].astype(F32)
 
 
 def swap(value, axis, distance):
@@ -230,7 +217,7 @@
     span = rows * GROUP
     place = lax.axis_index("head").astype(jnp.int32).reshape(1)
 
-    loaded = call(
+    *rows_in, lse = call(
         functools.partial(load_kernel, parts),
         [vmem(queries.shape, BF16)] * 3
         + [vmem((2 * rows, HEAD_DIM), BF16)] * parts
@@ -250,17 +237,17 @@
             pltpu.SemaphoreType.DMA((6,)),
         ],
     )
-    kv, lse = list(loaded[3:-1]), loaded[-1]
-    sizes = [2 * span + DOT_ROWS + (2 * rows if m == 1 else 0) for m in range(parts)]
-    qg = call(
-        functools.partial(pack_kernel, parts),
-        [vmem((size, HEAD_DIM), BF16) for size in sizes],
-        place,
-        *loaded[:3],
-        kv[1],
-    )
-    qg = [qg[0]] + [swap(qg[m], "head", m) for m in range(1, parts)]
-    kv = [kv[0], qg[1]] + [swap(kv[m], "head", m) for m in range(2, parts)]
+    kv = rows_in[3:]
+    qg = []
+    for m in range(parts):
+        (packed,) = call(
+            functools.partial(pack_kernel, m),
+            [vmem((2 * span + DOT_ROWS, HEAD_DIM), BF16)],
+            place,
+            *rows_in[:3],
+        )
+        qg.append(packed if m == 0 else swap(packed, "head", m))
+    kv = [kv[0]] + [swap(kv[m], "head", m) for m in range(1, parts)]
     (kv_own,) = call(
         functools.partial(join_kernel, parts), [vmem((2 * block, HEAD_DIM), BF16)], place, *kv
     )
@@ -294,27 +281,33 @@
         )
         for i, m in enumerate(pieces):
             dq[m] = result[i]
-            if dq_done and m > 0:
+            if dq_done and m > 1:
                 dq[m] = swap(dq[m], "head", m)
         for i, b in enumerate(blocks):
             acc[b] = result[len(pieces) + i]
             if acc_done and b > 0:
                 acc[b] = swap(acc[b], "ctx", 1 << (b - 1))
 
-    for b in range(levels):
-        step((0, 1), (b,), b == levels - 1, False)
-    for m in range(2, parts - 1):
-        step((m,), tuple(range(levels)), True, False)
+    early = tuple(range(parts - 1))
+    step((0,), (0,), False, False)
+    step(early[1:], (0,), False, False)
+    for b in range(1, levels):
+        step(early, (b,), b == levels - 1, False)
     for b in reversed(range(levels)):
         step((parts - 1,), (b,), b == 0, True)
 
     dkv = call(
         functools.partial(total_kernel, parts, levels),
-        [vmem((2 * rows, HEAD_DIM), F32 if m == 0 else BF16) for m in range(parts)],
+        [
+            vmem((2 * rows + (span if m == 1 else 0), HEAD_DIM), F32 if m == 0 else BF16)
+            for m in range(parts)
+        ],
         place,
         *acc,
+        dq[1],
     )
     dkv = [dkv[0]] + [swap(dkv[m], "head", m) for m in range(1, parts)]
+    dq[1] = dkv[1]
     (grad_q,) = call(
         functools.partial(unpack_q_kernel, parts), [hbm(queries.shape, F32)], place, *dq
     )

time: 50.8 us -> 55.4 us (1.091)
  waiting for transfers between devices: 19.8 us -> 23.6 us
    ppermute x17, waiting for transfers between devices: 19.8 us -> 23.6 us  [swap(): lax.ppermute(value, axis, [(i, i ^ distance) for i in range(lax.axis_size...]
    ppermute x17, starting transfers between devices: 18.6 us -> 19.1 us  [swap(): lax.ppermute(value, axis, [(i, i ^ distance) for i in range(lax.axis_size...]
    pallas_call x15 -> x18, Pallas kernels: 11.5 us -> 11.8 us  [call(): pl.pallas_call(kernel, out_shape=out_shapes, in_specs=[pl.BlockSpec(memor...]
  transfers between devices with their start and end apart: 17 -> 17, of which waited for: 8 -> 8; matrix products, arithmetic and copies ran while one was open for 0% -> 0% of each run, Pallas kernels for 14% -> 13%
where the time goes in v4:
time: 55.4 us; the launch traced here: 55.2 us
  waiting for transfers between devices  23.6 us (43%)
  starting transfers between devices  19.1 us (34%)
  Pallas kernels  11.8 us (21%)
  between operations  0.75 us (1%)
    ppermute x17, waiting for transfers between devices, swap(): lax.ppermute(value, axis, [(i, i ^ distance) for i in range(lax.axis_size...  23.6 us
    ppermute x17, starting transfers between devices, swap(): lax.ppermute(value, axis, [(i, i ^ distance) for i in range(lax.axis_size...  19.1 us
    pallas_call x18, Pallas kernels, call(): pl.pallas_call(kernel, out_shape=out_shapes, in_specs=[pl.BlockSpec(memor...  11.8 us
  transfers between devices with their start and end apart: 17, of which 8 were waited for; matrix products, arithmetic and copies ran while one was open for 0% of the time, Pallas kernels for 13%

profile of v4, /device:TPU:0, one launch (start us, length us, event | category | flops | bytes accessed | tf_op | source)
XLA Modules:
  0.0 55.2 jit_solution(6142195670532658549)
XLA Ops:
  0.6 1.5 %shard_map.85 = (bf16[64,4096]{1,0:T(8,128)(2,1)S(1)}, bf16[64,4096]{1,0:T(8,128)(2,1)S(1)}, bf16[64,4096]{1,0:T(8,128)(2,1)S(1)}, bf16[128,128]{1,0:T(8,128)(2,...) custom-call(s32[1]{0:T(128)} %bitcast.place, ...), custom_call_target="tpu_custom_call" | custom-call | tf_op jit(solution)/shard_map/pallas_call | solution.py:47
  2.1 0.3 shard_map.87
  2.5 0.5 collective-permute-start
  3.3 2.5 %collective-permute-start.1 = (bf16[1056,128]{1,0:T(8,128)(2,1)S(1)}, bf16[1056,128]{1,0:T(8,128)(2,1)S(1)}, u32[]{:S(2)}, u32[]{:S(2)}) collective-permute-start(bf16[1056,128]{1,0:T(8,128)(2,1)S(1)} %shard_map.88), channel_id=1, source_target_pairs={{0,2},{1,3},{2,0},{3,1},{4,6},{5,7},{6,4},{7,5},{8,10},{9,11},{10,... | collective-permute-start | bytes 811016 | tf_op jit(solution)/shard_map/ppermute | solution.py:209
  6.5 1.9 %collective-permute-start.3 = (bf16[128,128]{1,0:T(8,128)(2,1)S(1)}, bf16[128,128]{1,0:T(8,128)(2,1)S(1)}, u32[]{:S(2)}, u32[]{:S(2)}) collective-permute-start(bf16[128,128]{1,0:T(8,128)(2,1)S(1)} %get-tuple-element.48), channel_id=1, source_target_pairs={{0,2},{1,3},{2,0},{3,1},{4,6},{5,7},{6,4},{7,5},{8,10},{9,11},{10,... | collective-permute-start | bytes 98312 | tf_op jit(solution)/shard_map/ppermute | solution.py:209
  8.4 0.8 %collective-permute-start.4 = (bf16[128,128]{1,0:T(8,128)(2,1)S(1)}, bf16[128,128]{1,0:T(8,128)(2,1)S(1)}, u32[]{:S(2)}, u32[]{:S(2)}) collective-permute-start(bf16[128,128]{1,0:T(8,128)(2,1)S(1)} %get-tuple-element.49), channel_id=1, source_target_pairs={{0,3},{1,2},{2,1},{3,0},{4,7},{5,6},{6,5},{7,4},{8,11},{9,10},{10,... | collective-permute-start | bytes 98312 | tf_op jit(solution)/shard_map/ppermute | solution.py:209
  9.2 10.5 %collective-permute-done.3.refs_2_ = bf16[128,128]{1,0:T(8,128)(2,1)S(1)} collective-permute-done((bf16[128,128]{1,0:T(8,128)(2,1)S(1)}, bf16[128,128]{1,0:T(8,128)(2,1)S(1)}, u32[]{:S(2)}, u32[]{:S(2)}) %collective-permute-start.3) | collective-permute-done | bytes 32800 | tf_op jit(solution)/shard_map/ppermute | solution.py:209
  20.0 1.7 %collective-permute-start.7 = (bf16[512,128]{1,0:T(8,128)(2,1)S(1)}, bf16[512,128]{1,0:T(8,128)(2,1)S(1)}, u32[]{:S(2)}, u32[]{:S(2)}) collective-permute-start(bf16[512,128]{1,0:T(8,128)(2,1)S(1)} %shard_map.89.refs_2_.refs_3_), channel_id=1, source_target_pairs={{0,4},{4,0},{8,12},{12,8},{16,20},{20,16},{24,28},{28,24},{1,5},{5... | collective-permute-start | bytes 393224 | tf_op jit(solution)/shard_map/ppermute | solution.py:209
  21.7 1.6 %collective-permute-start.6 = (bf16[512,128]{1,0:T(8,128)(2,1)S(1)}, bf16[512,128]{1,0:T(8,128)(2,1)S(1)}, u32[]{:S(2)}, u32[]{:S(2)}) collective-permute-start(bf16[512,128]{1,0:T(8,128)(2,1)S(1)} %shard_map.89.refs_2_.refs_3_), channel_id=1, source_target_pairs={{0,8},{4,12},{8,0},{12,4},{16,24},{20,28},{24,16},{28,20},{1,9},{5... | collective-permute-start | bytes 393224 | tf_op jit(solution)/shard_map/ppermute | solution.py:209
  23.3 2.6 %collective-permute-start.5 = (bf16[512,128]{1,0:T(8,128)(2,1)S(1)}, bf16[512,128]{1,0:T(8,128)(2,1)S(1)}, u32[]{:S(2)}, u32[]{:S(2)}) collective-permute-start(bf16[512,128]{1,0:T(8,128)(2,1)S(1)} %shard_map.89.refs_2_.refs_3_), channel_id=1, source_target_pairs={{0,16},{4,20},{8,24},{12,28},{16,0},{20,4},{24,8},{28,12},{1,17},{... | collective-permute-start | bytes 393224 | tf_op jit(solution)/shard_map/ppermute | solution.py:209
  26.2 0.5 shard_map.90
  26.7 0.8 %shard_map.91 = (f32[128,512]{1,0:T(8,128)S(1)}, f32[128,512]{1,0:T(8,128)S(1)}, f32[512,128]{1,0:T(8,128)S(1)}) custom-call(s32[1]{0:T(128)} %bitcast.place, bf16[1056,128]{1,0:T(8,128)(2,1)S(1)} %collective-permute-done.refs_0_.refs_1_, bf16[1056,128]{1,0:T(8,128)(2,1)S(1)} %collective-permute-done.1.refs_1_.refs_2_, ...), custom_call_target="tpu_custom_call" | custom-call | tf_op jit(solution)/shard_map/pallas_call | solution.py:47
  27.5 1.2 %shard_map.92 = (f32[128,512]{1,0:T(8,128)S(1)}, f32[128,512]{1,0:T(8,128)S(1)}, f32[128,512]{1,0:T(8,128)S(1)}, f32[512,128]{1,0:T(8,128)S(1)}) custom-call(s32[1]{0:T(128)} %bitcast.place, bf16[1056,128]{1,0:T(8,128)(2,1)S(1)} %shard_map.86.refs_0_, bf16[1056,128]{1,0:T(8,128)(2,1)S(1)} %collective-permute-done.refs_0_.refs_1_, ...), custom_call_target="tpu_custom_call" | custom-call | tf_op jit(solution)/shard_map/pallas_call | solution.py:47
  28.7 0.3 collective-permute-done.6.refs_4_.refs_2_
  29.1 1.2 %shard_map.93 = (f32[128,512]{1,0:T(8,128)S(1)}, f32[128,512]{1,0:T(8,128)S(1)}, f32[128,512]{1,0:T(8,128)S(1)}, f32[512,128]{1,0:T(8,128)S(1)}) custom-call(s32[1]{0:T(128)} %bitcast.place, bf16[1056,128]{1,0:T(8,128)(2,1)S(1)} %shard_map.86.refs_0_, bf16[1056,128]{1,0:T(8,128)(2,1)S(1)} %collective-permute-done.refs_0_.refs_1_, ...), custom_call_target="tpu_custom_call" | custom-call | tf_op jit(solution)/shard_map/pallas_call | solution.py:47
  30.3 1.7 %collective-permute-done.5.refs_4_.refs_2_ = bf16[512,128]{1,0:T(8,128)(2,1)S(1)} collective-permute-done((bf16[512,128]{1,0:T(8,128)(2,1)S(1)}, bf16[512,128]{1,0:T(8,128)(2,1)S(1)}, u32[]{:S(2)}, u32[]{:S(2)}) %collective-permute-start.5) | collective-permute-done | bytes 131104 | tf_op jit(solution)/shard_map/ppermute | solution.py:209
  32.1 1.3 %shard_map.94 = (f32[512,128]{1,0:T(8,128)S(1)}, bf16[512,128]{1,0:T(8,128)(2,1)S(1)}, bf16[512,128]{1,0:T(8,128)(2,1)S(1)}, f32[512,128]{1,0:T(8,128)S(1)}) custom-call(s32[1]{0:T(128)} %bitcast.place, bf16[1056,128]{1,0:T(8,128)(2,1)S(1)} %shard_map.86.refs_0_, bf16[1056,128]{1,0:T(8,128)(2,1)S(1)} %collective-permute-done.refs_0_.refs_1_, ...), custom_call_target="tpu_custom_call" | custom-call | tf_op jit(solution)/shard_map/pallas_call | solution.py:47
  33.4 0.5 shard_map.96
  33.9 0.5 shard_map.97
  34.4 0.5 shard_map.98
  34.8 0.6 %collective-permute-start.9 = (bf16[512,128]{1,0:T(8,128)(2,1)S(1)}, bf16[512,128]{1,0:T(8,128)(2,1)S(1)}, u32[]{:S(2)}, u32[]{:S(2)}) collective-permute-start(bf16[512,128]{1,0:T(8,128)(2,1)S(1)} %get-tuple-element.69), channel_id=1, source_target_pairs={{0,4},{4,0},{8,12},{12,8},{16,20},{20,16},{24,28},{28,24},{1,5},{5... | collective-permute-start | bytes 393224 | tf_op jit(solution)/shard_map/ppermute | solution.py:209
  35.4 0.4 collective-permute-start.10
  35.9 2.6 %collective-permute-start.11 = (bf16[512,128]{1,0:T(8,128)(2,1)S(1)}, bf16[512,128]{1,0:T(8,128)(2,1)S(1)}, u32[]{:S(2)}, u32[]{:S(2)}) collective-permute-start(bf16[512,128]{1,0:T(8,128)(2,1)S(1)} %get-tuple-element.71), channel_id=1, source_target_pairs={{0,16},{4,20},{8,24},{12,28},{16,0},{20,4},{24,8},{28,12},{1,17},{... | collective-permute-start | bytes 393224 | tf_op jit(solution)/shard_map/ppermute | solution.py:209
  38.5 0.6 %shard_map.99 = (bf16[512,128]{1,0:T(8,128)(2,1)S(1)}, f32[512,128]{1,0:T(8,128)S(1)}) custom-call(s32[1]{0:T(128)} %bitcast.place, bf16[1056,128]{1,0:T(8,128)(2,1)S(1)} %collective-permute-done.8.refs_0_, f32[32,128]{1,0:T(8,128)S(1)} %get-tuple-element.45.refs_1_.refs_2_.refs_3_, bf16[512,128]{1,0:T(8,128)(2,1)S(1)} %shard_map.89.refs_2_.refs_3_, ...), custom_call_target="tpu_custom_call" | custom-call | tf_op jit(solution)/shard_map/pallas_call | solution.py:47
  39.0 0.8 %collective-permute-done.9.refs_1_ = bf16[512,128]{1,0:T(8,128)(2,1)S(1)} collective-permute-done((bf16[512,128]{1,0:T(8,128)(2,1)S(1)}, bf16[512,128]{1,0:T(8,128)(2,1)S(1)}, u32[]{:S(2)}, u32[]{:S(2)}) %collective-permute-start.9) | collective-permute-done | bytes 131104 | tf_op jit(solution)/shard_map/ppermute | solution.py:209
  39.9 0.9 %collective-permute-done.10.refs_2_ = bf16[512,128]{1,0:T(8,128)(2,1)S(1)} collective-permute-done((bf16[512,128]{1,0:T(8,128)(2,1)S(1)}, bf16[512,128]{1,0:T(8,128)(2,1)S(1)}, u32[]{:S(2)}, u32[]{:S(2)}) %collective-permute-start.10) | collective-permute-done | bytes 131104 | tf_op jit(solution)/shard_map/ppermute | solution.py:209
  40.8 2.7 %collective-permute-done.11.refs_3_ = bf16[512,128]{1,0:T(8,128)(2,1)S(1)} collective-permute-done((bf16[512,128]{1,0:T(8,128)(2,1)S(1)}, bf16[512,128]{1,0:T(8,128)(2,1)S(1)}, u32[]{:S(2)}, u32[]{:S(2)}) %collective-permute-start.11) | collective-permute-done | bytes 131104 | tf_op jit(solution)/shard_map/ppermute | solution.py:209
  43.6 1.6 %collective-permute-start.13 = (bf16[512,128]{1,0:T(8,128)(2,1)S(1)}, bf16[512,128]{1,0:T(8,128)(2,1)S(1)}, u32[]{:S(2)}, u32[]{:S(2)}) collective-permute-start(bf16[512,128]{1,0:T(8,128)(2,1)S(1)} %get-tuple-element.74), channel_id=1, source_target_pairs={{0,2},{1,3},{2,0},{3,1},{4,6},{5,7},{6,4},{7,5},{8,10},{9,11},{10,... | collective-permute-start | bytes 393224 | tf_op jit(solution)/shard_map/ppermute | solution.py:209
  45.5 1.5 %collective-permute-start.15 = (bf16[128,128]{1,0:T(8,128)(2,1)S(1)}, bf16[128,128]{1,0:T(8,128)(2,1)S(1)}, u32[]{:S(2)}, u32[]{:S(2)}) collective-permute-start(bf16[128,128]{1,0:T(8,128)(2,1)S(1)} %get-tuple-element.77), channel_id=1, source_target_pairs={{0,2},{1,3},{2,0},{3,1},{4,6},{5,7},{6,4},{7,5},{8,10},{9,11},{10,... | collective-permute-start | bytes 98312 | tf_op jit(solution)/shard_map/ppermute | solution.py:209
  47.2 6.2 %collective-permute-done.15.refs_2_ = bf16[128,128]{1,0:T(8,128)(2,1)S(1)} collective-permute-done((bf16[128,128]{1,0:T(8,128)(2,1)S(1)}, bf16[128,128]{1,0:T(8,128)(2,1)S(1)}, u32[]{:S(2)}, u32[]{:S(2)}) %collective-permute-start.15) | collective-permute-done | bytes 32800 | tf_op jit(solution)/shard_map/ppermute | solution.py:209
  53.4 0.7 %shard_map.102 = (f32[64,512]{1,0:T(8,128)}, f32[64,512]{1,0:T(8,128)}) custom-call(s32[1]{0:T(128)} %bitcast.place, f32[128,128]{1,0:T(8,128)S(1)} %get-tuple-element.76.refs_0_, bf16[640,128]{1,0:T(8,128)(2,1)S(1)} %collective-permute-done.12.refs_1_, bf16[128,128]{1,0:T(8,128)(2,1)S(1)} %collective-permute-done.15.refs_2_, ...), custom_call_target="tpu_custom_call" | custom-call | tf_op jit(solution)/shard_map/pallas_call | solution.py:47
  54.1 1.1 %shard_map.101 = f32[64,4096]{1,0:T(8,128)} custom-call(s32[1]{0:T(128)} %bitcast.place, f32[512,128]{1,0:T(8,128)S(1)} %get-tuple-element.60.refs_0_, bf16[640,128]{1,0:T(8,128)(2,1)S(1)} %collective-permute-done.12.refs_1_, bf16[512,128]{1,0:T(8,128)(2,1)S(1)} %collective-permute-done.13.refs_2_, bf16[512,128]{1,0:T(8,128)(2,1)S(1)} %collective-permute-done.14.refs_3_), custom_call_target="tpu_custom_call" | custom-call | tf_op jit(solution)/shard_map/pallas_call | solution.py:47
  (20 shorter events, 2.3 us)
Async XLA Ops:
  2.5 20.8 %collective-permute-start = (bf16[1056,128]{1,0:T(8,128)(2,1)S(1)}, bf16[1056,128]{1,0:T(8,128)(2,1)S(1)}, u32[]{:S(2)}, u32[]{:S(2)}) collective-permute-start(bf16[1056,128]{1,0:T(8,128)(2,1)S(1)} %shard_map.87), channel_id=1, source_target_pairs={{0,1},{1,0},{2,3},{3,2},{4,5},{5,4},{6,7},{7,6},{8,9},{9,8},{10,11... | collective-permute-start | bytes 811016 | tf_op jit(solution)/shard_map/ppermute | solution.py:209
  3.3 23.3 %collective-permute-start.1 = (bf16[1056,128]{1,0:T(8,128)(2,1)S(1)}, bf16[1056,128]{1,0:T(8,128)(2,1)S(1)}, u32[]{:S(2)}, u32[]{:S(2)}) collective-permute-start(bf16[1056,128]{1,0:T(8,128)(2,1)S(1)} %shard_map.88), channel_id=1, source_target_pairs={{0,2},{1,3},{2,0},{3,1},{4,6},{5,7},{6,4},{7,5},{8,10},{9,11},{10,... | collective-permute-start | bytes 811016 | tf_op jit(solution)/shard_map/ppermute | solution.py:209
  6.2 27.2 %collective-permute-start.8 = (bf16[1056,128]{1,0:T(8,128)(2,1)S(1)}, bf16[1056,128]{1,0:T(8,128)(2,1)S(1)}, u32[]{:S(2)}, u32[]{:S(2)}) collective-permute-start(bf16[1056,128]{1,0:T(8,128)(2,1)S(1)} %shard_map.95), channel_id=1, source_target_pairs={{0,3},{1,2},{2,1},{3,0},{4,7},{5,6},{6,5},{7,4},{8,11},{9,10},{10,... | collective-permute-start | bytes 811016 | tf_op jit(solution)/shard_map/ppermute | solution.py:209
  6.4 2.0 %collective-permute-start.2 = (bf16[128,128]{1,0:T(8,128)(2,1)S(1)}, bf16[128,128]{1,0:T(8,128)(2,1)S(1)}, u32[]{:S(2)}, u32[]{:S(2)}) collective-permute-start(bf16[128,128]{1,0:T(8,128)(2,1)S(1)} %get-tuple-element.47), channel_id=1, source_target_pairs={{0,1},{1,0},{2,3},{3,2},{4,5},{5,4},{6,7},{7,6},{8,9},{9,8},{10,11... | collective-permute-start | bytes 98312 | tf_op jit(solution)/shard_map/ppermute | solution.py:209
  6.5 13.2 %collective-permute-start.3 = (bf16[128,128]{1,0:T(8,128)(2,1)S(1)}, bf16[128,128]{1,0:T(8,128)(2,1)S(1)}, u32[]{:S(2)}, u32[]{:S(2)}) collective-permute-start(bf16[128,128]{1,0:T(8,128)(2,1)S(1)} %get-tuple-element.48), channel_id=1, source_target_pairs={{0,2},{1,3},{2,0},{3,1},{4,6},{5,7},{6,4},{7,5},{8,10},{9,11},{10,... | collective-permute-start | bytes 98312 | tf_op jit(solution)/shard_map/ppermute | solution.py:209
  8.4 11.6 %collective-permute-start.4 = (bf16[128,128]{1,0:T(8,128)(2,1)S(1)}, bf16[128,128]{1,0:T(8,128)(2,1)S(1)}, u32[]{:S(2)}, u32[]{:S(2)}) collective-permute-start(bf16[128,128]{1,0:T(8,128)(2,1)S(1)} %get-tuple-element.49), channel_id=1, source_target_pairs={{0,3},{1,2},{2,1},{3,0},{4,7},{5,6},{6,5},{7,4},{8,11},{9,10},{10,... | collective-permute-start | bytes 98312 | tf_op jit(solution)/shard_map/ppermute | solution.py:209
  20.0 7.5 %collective-permute-start.7 = (bf16[512,128]{1,0:T(8,128)(2,1)S(1)}, bf16[512,128]{1,0:T(8,128)(2,1)S(1)}, u32[]{:S(2)}, u32[]{:S(2)}) collective-permute-start(bf16[512,128]{1,0:T(8,128)(2,1)S(1)} %shard_map.89.refs_2_.refs_3_), channel_id=1, source_target_pairs={{0,4},{4,0},{8,12},{12,8},{16,20},{20,16},{24,28},{28,24},{1,5},{5... | collective-permute-start | bytes 393224 | tf_op jit(solution)/shard_map/ppermute | solution.py:209
  21.7 7.4 %collective-permute-start.6 = (bf16[512,128]{1,0:T(8,128)(2,1)S(1)}, bf16[512,128]{1,0:T(8,128)(2,1)S(1)}, u32[]{:S(2)}, u32[]{:S(2)}) collective-permute-start(bf16[512,128]{1,0:T(8,128)(2,1)S(1)} %shard_map.89.refs_2_.refs_3_), channel_id=1, source_target_pairs={{0,8},{4,12},{8,0},{12,4},{16,24},{20,28},{24,16},{28,20},{1,9},{5... | collective-permute-start | bytes 393224 | tf_op jit(solution)/shard_map/ppermute | solution.py:209
  23.3 8.8 %collective-permute-start.5 = (bf16[512,128]{1,0:T(8,128)(2,1)S(1)}, bf16[512,128]{1,0:T(8,128)(2,1)S(1)}, u32[]{:S(2)}, u32[]{:S(2)}) collective-permute-start(bf16[512,128]{1,0:T(8,128)(2,1)S(1)} %shard_map.89.refs_2_.refs_3_), channel_id=1, source_target_pairs={{0,16},{4,20},{8,24},{12,28},{16,0},{20,4},{24,8},{28,12},{1,17},{... | collective-permute-start | bytes 393224 | tf_op jit(solution)/shard_map/ppermute | solution.py:209
  34.8 5.0 %collective-permute-start.9 = (bf16[512,128]{1,0:T(8,128)(2,1)S(1)}, bf16[512,128]{1,0:T(8,128)(2,1)S(1)}, u32[]{:S(2)}, u32[]{:S(2)}) collective-permute-start(bf16[512,128]{1,0:T(8,128)(2,1)S(1)} %get-tuple-element.69), channel_id=1, source_target_pairs={{0,4},{4,0},{8,12},{12,8},{16,20},{20,16},{24,28},{28,24},{1,5},{5... | collective-permute-start | bytes 393224 | tf_op jit(solution)/shard_map/ppermute | solution.py:209
  35.4 5.4 %collective-permute-start.10 = (bf16[512,128]{1,0:T(8,128)(2,1)S(1)}, bf16[512,128]{1,0:T(8,128)(2,1)S(1)}, u32[]{:S(2)}, u32[]{:S(2)}) collective-permute-start(bf16[512,128]{1,0:T(8,128)(2,1)S(1)} %get-tuple-element.70), channel_id=1, source_target_pairs={{0,8},{4,12},{8,0},{12,4},{16,24},{20,28},{24,16},{28,20},{1,9},{5... | collective-permute-start | bytes 393224 | tf_op jit(solution)/shard_map/ppermute | solution.py:209
  35.9 7.6 %collective-permute-start.11 = (bf16[512,128]{1,0:T(8,128)(2,1)S(1)}, bf16[512,128]{1,0:T(8,128)(2,1)S(1)}, u32[]{:S(2)}, u32[]{:S(2)}) collective-permute-start(bf16[512,128]{1,0:T(8,128)(2,1)S(1)} %get-tuple-element.71), channel_id=1, source_target_pairs={{0,16},{4,20},{8,24},{12,28},{16,0},{20,4},{24,8},{28,12},{1,17},{... | collective-permute-start | bytes 393224 | tf_op jit(solution)/shard_map/ppermute | solution.py:209
  43.6 9.8 %collective-permute-start.12 = (bf16[640,128]{1,0:T(8,128)(2,1)S(1)}, bf16[640,128]{1,0:T(8,128)(2,1)S(1)}, u32[]{:S(2)}, u32[]{:S(2)}) collective-permute-start(bf16[640,128]{1,0:T(8,128)(2,1)S(1)} %get-tuple-element.73), channel_id=1, source_target_pairs={{0,1},{1,0},{2,3},{3,2},{4,5},{5,4},{6,7},{7,6},{8,9},{9,8},{10,11... | collective-permute-start | bytes 491528 | tf_op jit(solution)/shard_map/ppermute | solution.py:209
  43.6 10.5 %collective-permute-start.13 = (bf16[512,128]{1,0:T(8,128)(2,1)S(1)}, bf16[512,128]{1,0:T(8,128)(2,1)S(1)}, u32[]{:S(2)}, u32[]{:S(2)}) collective-permute-start(bf16[512,128]{1,0:T(8,128)(2,1)S(1)} %get-tuple-element.74), channel_id=1, source_target_pairs={{0,2},{1,3},{2,0},{3,1},{4,6},{5,7},{6,4},{7,5},{8,10},{9,11},{10,... | collective-permute-start | bytes 393224 | tf_op jit(solution)/shard_map/ppermute | solution.py:209
  45.2 8.9 %collective-permute-start.14 = (bf16[512,128]{1,0:T(8,128)(2,1)S(1)}, bf16[512,128]{1,0:T(8,128)(2,1)S(1)}, u32[]{:S(2)}, u32[]{:S(2)}) collective-permute-start(bf16[512,128]{1,0:T(8,128)(2,1)S(1)} %get-tuple-element.75), channel_id=1, source_target_pairs={{0,3},{1,2},{2,1},{3,0},{4,7},{5,6},{6,5},{7,4},{8,11},{9,10},{10,... | collective-permute-start | bytes 393224 | tf_op jit(solution)/shard_map/ppermute | solution.py:209
  45.5 7.9 %collective-permute-start.15 = (bf16[128,128]{1,0:T(8,128)(2,1)S(1)}, bf16[128,128]{1,0:T(8,128)(2,1)S(1)}, u32[]{:S(2)}, u32[]{:S(2)}) collective-permute-start(bf16[128,128]{1,0:T(8,128)(2,1)S(1)} %get-tuple-element.77), channel_id=1, source_target_pairs={{0,2},{1,3},{2,0},{3,1},{4,6},{5,7},{6,4},{7,5},{8,10},{9,11},{10,... | collective-permute-start | bytes 98312 | tf_op jit(solution)/shard_map/ppermute | solution.py:209
  47.0 6.4 %collective-permute-start.16 = (bf16[128,128]{1,0:T(8,128)(2,1)S(1)}, bf16[128,128]{1,0:T(8,128)(2,1)S(1)}, u32[]{:S(2)}, u32[]{:S(2)}) collective-permute-start(bf16[128,128]{1,0:T(8,128)(2,1)S(1)} %get-tuple-element.78), channel_id=1, source_target_pairs={{0,3},{1,2},{2,1},{3,0},{4,7},{5,6},{6,5},{7,4},{8,11},{9,10},{10,... | collective-permute-start | bytes 98312 | tf_op jit(solution)/shard_map/ppermute | solution.py:209

commit v5 on v4

--- a/solution.py
+++ b/solution.py
@@ -42,23 +42,31 @@
     return jax.ShapeDtypeStruct(shape, dtype)
 
 
-def call(kernel, out_shapes, place, *args, space=pltpu.VMEM, scratch=()):
+def call(
+    kernel, out_shapes, place, *args, space=pltpu.VMEM, out_space=pltpu.VMEM, filled=None, scratch=()
+):
     args = [pltpu.with_memory_space_constraint(a, space) for a in args]
+    specs = [pl.BlockSpec(memory_space=pltpu.SMEM)]
+    if filled is not None:
+        args = [pltpu.with_memory_space_constraint(filled, pltpu.HBM)] + args
+        specs += [pl.BlockSpec(memory_space=pltpu.HBM)]
+    specs += [pl.BlockSpec(memory_space=space)] * (len(args) + 1 - len(specs))
     return pl.pallas_call(
         kernel,
         out_shape=out_shapes,
-        in_specs=[pl.BlockSpec(memory_space=pltpu.SMEM)]
-        + [pl.BlockSpec(memory_space=space) for _ in args],
-        out_specs=[pl.BlockSpec(memory_space=pltpu.VMEM) for _ in out_shapes],
+        in_specs=specs,
+        out_specs=[pl.BlockSpec(memory_space=out_space) for _ in out_shapes],
         scratch_shapes=scratch,
+        input_output_aliases={} if filled is None else {1: 0},
         compiler_params=pltpu.CompilerParams(vmem_limit_bytes=VMEM_BYTES),
     )(place, *args)
 
 
 def load_kernel(parts, place, q_any, g_any, o_any, k_any, v_any, l_any, *refs):
     q_ref, g_ref, o_ref = refs[:3]
-    kv_refs, lse_ref = refs[3 : 3 + parts], refs[3 + parts]
-    k_ref, v_ref, l_ref, sems = refs[4 + parts :]
+    count = 2 + (parts - 2) // 2
+    kv_refs, lse_ref = refs[3 : 3 + count], refs[3 + count]
+    k_ref, v_ref, l_ref, sems = refs[4 + count :]
     own = place[0]
     rows = k_ref.shape[0]
     pairs = [(k_any, k_ref), (v_any, v_ref), (l_any, l_ref)]
@@ -73,8 +81,9 @@
         copy.wait()
     for m in range(parts):
         col = pl.multiple_of((own ^ m) * HEAD_DIM, HEAD_DIM)
-        kv_refs[m][:rows, :] = k_ref[:, pl.ds(col, HEAD_DIM)]
-        kv_refs[m][rows:, :] = v_ref[:, pl.ds(col, HEAD_DIM)]
+        target, first = (kv_refs[m], 0) if m < 2 else (kv_refs[1 + m // 2], m % 2 * 2 * rows)
+        target[first : first + rows, :] = k_ref[:, pl.ds(col, HEAD_DIM)]
+        target[first + rows : first + 2 * rows, :] = v_ref[:, pl.ds(col, HEAD_DIM)]
     for m in range(parts):
         piece = l_ref[:, :rows]
         for c in range(1, parts):
@@ -112,12 +121,26 @@
     )
 
 
+def forward_kernel(parts, place, *refs):
+    out = refs[-1]
+    size = refs[0].shape[0]
+    out[:size, :] = refs[0][...]
+    for i in range(1, parts // 2):
+        out[i * size : (i + 1) * size, :] = refs[i][size:, :]
+
+
 def join_kernel(parts, place, *refs):
-    pieces, out = refs[:parts], refs[parts]
+    near, far, passed, out = refs[0], refs[1 : parts // 2], refs[-2], refs[-1]
     rows = out.shape[0] // (2 * parts)
     for m in range(parts):
-        out[m * rows : (m + 1) * rows, :] = pieces[m][:rows, :]
-        out[(parts + m) * rows : (parts + m + 1) * rows, :] = pieces[m][rows:, :]
+        if m % 2:
+            source, first = passed, m // 2 * 2 * rows
+        else:
+            source, first = (far[m // 2 - 1], 0) if m else (near, 0)
+        out[m * rows : (m + 1) * rows, :] = source[first : first + rows, :]
+        out[(parts + m) * rows : (parts + m + 1) * rows, :] = source[
+            first + rows : first + 2 * rows, :
+        ]
 
 
 def row_of(stack):
@@ -185,28 +208,59 @@
     outs[1][2 * rows :, :] = near_dq[...]
 
 
-def unpack_q_kernel(parts, place, *refs):
-    pieces, out = refs[:parts], refs[parts]
+def put_queries(pieces, sources, place, out, stage, sems):
     rows = out.shape[0]
     width = GROUP * HEAD_DIM
-    for m in range(parts):
+    copies = []
+    for slot, (m, source) in enumerate(zip(pieces, sources)):
         for i, h in enumerate(HEAD_ORDER):
-            col = pl.multiple_of((place[0] ^ m) * width + h * HEAD_DIM, HEAD_DIM)
-            first = pieces[m].shape[0] - GROUP * rows + i * rows
-            out[:, pl.ds(col, HEAD_DIM)] = pieces[m][first : first + rows, :].astype(F32)
-
-
-def unpack_kv_kernel(parts, place, *refs):
-    pieces, out_k, out_v = refs[:parts], refs[parts], refs[parts + 1]
-    rows = out_k.shape[0]
+            first = source.shape[0] - GROUP * rows + i * rows
+            stage[slot, :, h * HEAD_DIM : (h + 1) * HEAD_DIM] = source[
+                first : first + rows, :
+            ].astype(F32)
+        col = pl.multiple_of((place[0] ^ m) * width, width)
+        copies.append(
+            pltpu.make_async_copy(stage.at[slot], out.at[:, pl.ds(col, width)], sems.at[slot])
+        )
+        copies[-1].start()
+    return copies
+
+
+def first_kernel(pieces, place, *refs):
+    out, stage, sems = refs[-3:]
+    for copy in put_queries(pieces, refs[: len(pieces)], place, out, stage, sems):
+        copy.wait()
+
+
+def more_kernel(pieces, place, filled, *refs):
+    out, stage, sems = refs[-3:]
+    for copy in put_queries(pieces, refs[: len(pieces)], place, out, stage, sems):
+        copy.wait()
+
+
+def finish_kernel(parts, place, filled, *refs):
+    pieces, refs = refs[:parts], refs[parts:]
+    out, out_k, out_v, stage, stage_k, stage_v, sems = refs
+    rows = out.shape[0]
+    copies = put_queries((1,), (pieces[1],), place, out, stage, sems)
     for m in range(parts):
         col = pl.multiple_of((place[0] ^ m) * HEAD_DIM, HEAD_DIM)
-        out_k[:, pl.ds(col, HEAD_DIM)] = pieces[m][:rows, :].astype(F32)
-        out_v[:, pl.ds(col, HEAD_DIM)] = pieces[m][rows : 2 * rows, :].astype(F32)
+        stage_k[:, pl.ds(col, HEAD_DIM)] = pieces[m][:rows, :].astype(F32)
+        stage_v[:, pl.ds(col, HEAD_DIM)] = pieces[m][rows : 2 * rows, :].astype(F32)
+    copies.append(pltpu.make_async_copy(stage_k, out_k, sems.at[1]))
+    copies.append(pltpu.make_async_copy(stage_v, out_v, sems.at[2]))
+    for copy in copies[1:]:
+        copy.start()
+    for copy in copies:
+        copy.wait()
 
 
 def swap(value, axis, distance):
     return lax.ppermute(value, axis, [(i, i ^ distance) for i in range(lax.axis_size(axis))])
+
+
+def far_order(levels):
+    return [b for b in (2, 3, 1) if b < levels] + list(range(4, levels))
 
 
 def on_device(queries, key_rows, value_rows, attn_out, out_grad, logsumexp):
@@ -220,7 +274,8 @@
     *rows_in, lse = call(
         functools.partial(load_kernel, parts),
         [vmem(queries.shape, BF16)] * 3
-        + [vmem((2 * rows, HEAD_DIM), BF16)] * parts
+        + [vmem((2 * rows, HEAD_DIM), BF16)] * 2
+        + [vmem((4 * rows, HEAD_DIM), BF16)] * (parts // 2 - 1)
         + [vmem((8 * parts, 2 * rows), F32)],
         place,
         queries,
@@ -247,9 +302,22 @@
             *rows_in[:3],
         )
         qg.append(packed if m == 0 else swap(packed, "head", m))
-    kv = [kv[0]] + [swap(kv[m], "head", m) for m in range(1, parts)]
+    kv_far = [swap(kv[1 + i], "head", 2 * i) for i in range(1, parts // 2)]
+    (passed,) = call(
+        functools.partial(forward_kernel, parts),
+        [vmem((parts * rows, HEAD_DIM), BF16)],
+        place,
+        kv[1],
+        *kv_far,
+    )
+    passed = swap(passed, "head", 1)
     (kv_own,) = call(
-        functools.partial(join_kernel, parts), [vmem((2 * block, HEAD_DIM), BF16)], place, *kv
+        functools.partial(join_kernel, parts),
+        [vmem((2 * block, HEAD_DIM), BF16)],
+        place,
+        kv[0],
+        *kv_far,
+        passed,
     )
     kv_all = [kv_own] + [swap(kv_own, "ctx", 1 << (b - 1)) for b in range(1, levels)]
 
@@ -293,7 +361,7 @@
     step(early[1:], (0,), False, False)
     for b in range(1, levels):
         step(early, (b,), b == levels - 1, False)
-    for b in reversed(range(levels)):
+    for b in far_order(levels) + [0]:
         step((parts - 1,), (b,), b == 0, True)
 
     dkv = call(
@@ -307,15 +375,42 @@
         dq[1],
     )
     dkv = [dkv[0]] + [swap(dkv[m], "head", m) for m in range(1, parts)]
-    dq[1] = dkv[1]
+    width = GROUP * HEAD_DIM
+
+    def stage(count):
+        return vmem((count, rows, width), F32)
+
+    early = (0,) + tuple(range(2, parts - 1))
     (grad_q,) = call(
-        functools.partial(unpack_q_kernel, parts), [hbm(queries.shape, F32)], place, *dq
-    )
-    grad_k, grad_v = call(
-        functools.partial(unpack_kv_kernel, parts),
-        [hbm(key_rows.shape, F32), hbm(value_rows.shape, F32)],
+        functools.partial(first_kernel, early),
+        [hbm(queries.shape, F32)],
+        place,
+        *[dq[m] for m in early],
+        out_space=pltpu.HBM,
+        scratch=[stage(len(early)), pltpu.SemaphoreType.DMA((len(early),))],
+    )
+    (grad_q,) = call(
+        functools.partial(more_kernel, (parts - 1,)),
+        [hbm(queries.shape, F32)],
+        place,
+        dq[parts - 1],
+        out_space=pltpu.HBM,
+        filled=grad_q,
+        scratch=[stage(1), pltpu.SemaphoreType.DMA((1,))],
+    )
+    grad_q, grad_k, grad_v = call(
+        functools.partial(finish_kernel, parts),
+        [hbm(queries.shape, F32), hbm(key_rows.shape, F32), hbm(value_rows.shape, F32)],
         place,
         *dkv,
+        out_space=pltpu.HBM,
+        filled=grad_q,
+        scratch=[
+            stage(1),
+            vmem(key_rows.shape, F32),
+            vmem(value_rows.shape, F32),
+            pltpu.SemaphoreType.DMA((3,)),
+        ],
     )
     return (grad_q, grad_k, grad_v)
 

time: 55.4 us -> 54.8 us (0.989)
  starting transfers between devices: 19.1 us -> 18.2 us
  Pallas kernels: 11.8 us -> 12.4 us
    ppermute x17 -> x16, starting transfers between devices: 19.1 us -> 18.2 us  [swap(): lax.ppermute(value, axis, [(i, i ^ distance) for i in range(lax.axis_size...]
    pallas_call x18 -> x20, Pallas kernels: 11.8 us -> 12.4 us  [call(): pl.pallas_call(kernel, out_shape=out_shapes, in_specs=specs, out_specs=[p...]
    ppermute x17 -> x16, waiting for transfers between devices: 23.6 us -> 23.3 us  [swap(): lax.ppermute(value, axis, [(i, i ^ distance) for i in range(lax.axis_size...]
  transfers between devices with their start and end apart: 17 -> 16, of which waited for: 8 -> 9; matrix products, arithmetic and copies ran while one was open for 0% -> 0% of each run, Pallas kernels for 13% -> 13%
where the time goes in v5:
time: 54.8 us; the launch traced here: 54.6 us
  waiting for transfers between devices  23.3 us (43%)
  starting transfers between devices  18.2 us (33%)
  Pallas kernels  12.4 us (23%)
  between operations  0.77 us (1%)
    ppermute x16, waiting for transfers between devices, swap(): lax.ppermute(value, axis, [(i, i ^ distance) for i in range(lax.axis_size...  23.3 us
    ppermute x16, starting transfers between devices, swap(): lax.ppermute(value, axis, [(i, i ^ distance) for i in range(lax.axis_size...  18.2 us
    pallas_call x20, Pallas kernels, call(): pl.pallas_call(kernel, out_shape=out_shapes, in_specs=specs, out_specs=[p...  12.4 us
  transfers between devices with their start and end apart: 16, of which 9 were waited for; matrix products, arithmetic and copies ran while one was open for 0% of the time, Pallas kernels for 13%

profile of v5, /device:TPU:0, one launch (start us, length us, event | category | flops | bytes accessed | tf_op | source)
XLA Modules:
  0.0 54.6 jit_solution(3403419452777033288)
XLA Ops:
  0.6 1.5 %shard_map.85 = (bf16[64,4096]{1,0:T(8,128)(2,1)S(1)}, bf16[64,4096]{1,0:T(8,128)(2,1)S(1)}, bf16[64,4096]{1,0:T(8,128)(2,1)S(1)}, bf16[128,128]{1,0:T(8,128)(2,...) custom-call(s32[1]{0:T(128)} %bitcast.place, bf16[64,4096]{1,0:T(8,128)(2,1)} %q_any.1, ...), custom_call_target="tpu_custom_call" | custom-call | tf_op jit(solution)/shard_map/pallas_call | solution.py:54
  2.5 0.5 collective-permute-start
  3.3 2.5 %collective-permute-start.1 = (bf16[1056,128]{1,0:T(8,128)(2,1)S(1)}, bf16[1056,128]{1,0:T(8,128)(2,1)S(1)}, u32[]{:S(2)}, u32[]{:S(2)}) collective-permute-start(bf16[1056,128]{1,0:T(8,128)(2,1)S(1)} %shard_map.88), channel_id=1, source_target_pairs={{0,2},{1,3},{2,0},{3,1},{4,6},{5,7},{6,4},{7,5},{8,10},{9,11},{10,... | collective-permute-start | bytes 811016 | tf_op jit(solution)/shard_map/ppermute | solution.py:259
  6.4 1.7 %collective-permute-start.2 = (bf16[256,128]{1,0:T(8,128)(2,1)S(1)}, bf16[256,128]{1,0:T(8,128)(2,1)S(1)}, u32[]{:S(2)}, u32[]{:S(2)}) collective-permute-start(bf16[256,128]{1,0:T(8,128)(2,1)S(1)} %get-tuple-element.44), channel_id=1, source_target_pairs={{0,2},{1,3},{2,0},{3,1},{4,6},{5,7},{6,4},{7,5},{8,10},{9,11},{10,... | collective-permute-start | bytes 196616 | tf_op jit(solution)/shard_map/ppermute | solution.py:259
  8.1 12.1 %collective-permute-done.2.refs_1_ = bf16[256,128]{1,0:T(8,128)(2,1)S(1)} collective-permute-done((bf16[256,128]{1,0:T(8,128)(2,1)S(1)}, bf16[256,128]{1,0:T(8,128)(2,1)S(1)}, u32[]{:S(2)}, u32[]{:S(2)}) %collective-permute-start.2) | collective-permute-done | bytes 65568 | tf_op jit(solution)/shard_map/ppermute | solution.py:259
  20.2 1.2 %collective-permute-done.3.refs_2_ = bf16[256,128]{1,0:T(8,128)(2,1)S(1)} collective-permute-done((bf16[256,128]{1,0:T(8,128)(2,1)S(1)}, bf16[256,128]{1,0:T(8,128)(2,1)S(1)}, u32[]{:S(2)}, u32[]{:S(2)}) %collective-permute-start.3) | collective-permute-done | bytes 65568 | tf_op jit(solution)/shard_map/ppermute | solution.py:259
  21.5 1.8 %collective-permute-start.6 = (bf16[512,128]{1,0:T(8,128)(2,1)S(1)}, bf16[512,128]{1,0:T(8,128)(2,1)S(1)}, u32[]{:S(2)}, u32[]{:S(2)}) collective-permute-start(bf16[512,128]{1,0:T(8,128)(2,1)S(1)} %shard_map.90.refs_2_.refs_3_), channel_id=1, source_target_pairs={{0,4},{4,0},{8,12},{12,8},{16,20},{20,16},{24,28},{28,24},{1,5},{5... | collective-permute-start | bytes 393224 | tf_op jit(solution)/shard_map/ppermute | solution.py:259
  23.3 1.6 %collective-permute-start.5 = (bf16[512,128]{1,0:T(8,128)(2,1)S(1)}, bf16[512,128]{1,0:T(8,128)(2,1)S(1)}, u32[]{:S(2)}, u32[]{:S(2)}) collective-permute-start(bf16[512,128]{1,0:T(8,128)(2,1)S(1)} %shard_map.90.refs_2_.refs_3_), channel_id=1, source_target_pairs={{0,8},{4,12},{8,0},{12,4},{16,24},{20,28},{24,16},{28,20},{1,9},{5... | collective-permute-start | bytes 393224 | tf_op jit(solution)/shard_map/ppermute | solution.py:259
  24.9 2.6 %collective-permute-start.4 = (bf16[512,128]{1,0:T(8,128)(2,1)S(1)}, bf16[512,128]{1,0:T(8,128)(2,1)S(1)}, u32[]{:S(2)}, u32[]{:S(2)}) collective-permute-start(bf16[512,128]{1,0:T(8,128)(2,1)S(1)} %shard_map.90.refs_2_.refs_3_), channel_id=1, source_target_pairs={{0,16},{4,20},{8,24},{12,28},{16,0},{20,4},{24,8},{28,12},{1,17},{... | collective-permute-start | bytes 393224 | tf_op jit(solution)/shard_map/ppermute | solution.py:259
  27.8 0.5 shard_map.91
  28.3 0.8 %shard_map.92 = (f32[128,512]{1,0:T(8,128)S(1)}, f32[128,512]{1,0:T(8,128)S(1)}, f32[512,128]{1,0:T(8,128)S(1)}) custom-call(s32[1]{0:T(128)} %bitcast.place, bf16[1056,128]{1,0:T(8,128)(2,1)S(1)} %collective-permute-done.refs_0_.refs_1_, bf16[1056,128]{1,0:T(8,128)(2,1)S(1)} %collective-permute-done.1.refs_1_.refs_2_, ...), custom_call_target="tpu_custom_call" | custom-call | tf_op jit(solution)/shard_map/pallas_call | solution.py:54
  29.1 1.2 %shard_map.93 = (f32[128,512]{1,0:T(8,128)S(1)}, f32[128,512]{1,0:T(8,128)S(1)}, f32[128,512]{1,0:T(8,128)S(1)}, f32[512,128]{1,0:T(8,128)S(1)}) custom-call(s32[1]{0:T(128)} %bitcast.place, bf16[1056,128]{1,0:T(8,128)(2,1)S(1)} %shard_map.86.refs_0_, bf16[1056,128]{1,0:T(8,128)(2,1)S(1)} %collective-permute-done.refs_0_.refs_1_, ...), custom_call_target="tpu_custom_call" | custom-call | tf_op jit(solution)/shard_map/pallas_call | solution.py:54
  30.7 1.2 %shard_map.94 = (f32[128,512]{1,0:T(8,128)S(1)}, f32[128,512]{1,0:T(8,128)S(1)}, f32[128,512]{1,0:T(8,128)S(1)}, f32[512,128]{1,0:T(8,128)S(1)}) custom-call(s32[1]{0:T(128)} %bitcast.place, bf16[1056,128]{1,0:T(8,128)(2,1)S(1)} %shard_map.86.refs_0_, bf16[1056,128]{1,0:T(8,128)(2,1)S(1)} %collective-permute-done.refs_0_.refs_1_, ...), custom_call_target="tpu_custom_call" | custom-call | tf_op jit(solution)/shard_map/pallas_call | solution.py:54
  31.9 0.5 shard_map.98
  32.4 1.3 %collective-permute-done.4.refs_4_.refs_2_ = bf16[512,128]{1,0:T(8,128)(2,1)S(1)} collective-permute-done((bf16[512,128]{1,0:T(8,128)(2,1)S(1)}, bf16[512,128]{1,0:T(8,128)(2,1)S(1)}, u32[]{:S(2)}, u32[]{:S(2)}) %collective-permute-start.4) | collective-permute-done | bytes 131104 | tf_op jit(solution)/shard_map/ppermute | solution.py:259
  33.7 1.3 %shard_map.95 = (f32[512,128]{1,0:T(8,128)S(1)}, bf16[512,128]{1,0:T(8,128)(2,1)S(1)}, bf16[512,128]{1,0:T(8,128)(2,1)S(1)}, f32[512,128]{1,0:T(8,128)S(1)}) custom-call(s32[1]{0:T(128)} %bitcast.place, bf16[1056,128]{1,0:T(8,128)(2,1)S(1)} %shard_map.86.refs_0_, bf16[1056,128]{1,0:T(8,128)(2,1)S(1)} %collective-permute-done.refs_0_.refs_1_, ...), custom_call_target="tpu_custom_call" | custom-call | tf_op jit(solution)/shard_map/pallas_call | solution.py:54
  35.0 0.5 shard_map.99
  35.5 0.5 shard_map.100
  36.0 0.6 %collective-permute-start.10 = (bf16[512,128]{1,0:T(8,128)(2,1)S(1)}, bf16[512,128]{1,0:T(8,128)(2,1)S(1)}, u32[]{:S(2)}, u32[]{:S(2)}) collective-permute-start(bf16[512,128]{1,0:T(8,128)(2,1)S(1)} %get-tuple-element.67), channel_id=1, source_target_pairs={{0,4},{4,0},{8,12},{12,8},{16,20},{20,16},{24,28},{28,24},{1,5},{5... | collective-permute-start | bytes 393224 | tf_op jit(solution)/shard_map/ppermute | solution.py:259
  36.5 0.4 collective-permute-start.12
  36.9 2.7 %collective-permute-start.11 = (bf16[512,128]{1,0:T(8,128)(2,1)S(1)}, bf16[512,128]{1,0:T(8,128)(2,1)S(1)}, u32[]{:S(2)}, u32[]{:S(2)}) collective-permute-start(bf16[512,128]{1,0:T(8,128)(2,1)S(1)} %get-tuple-element.68), channel_id=1, source_target_pairs={{0,8},{4,12},{8,0},{12,4},{16,24},{20,28},{24,16},{28,20},{1,9},{5... | collective-permute-start | bytes 393224 | tf_op jit(solution)/shard_map/ppermute | solution.py:259
  39.6 0.6 %shard_map.101 = (bf16[512,128]{1,0:T(8,128)(2,1)S(1)}, f32[512,128]{1,0:T(8,128)S(1)}) custom-call(s32[1]{0:T(128)} %bitcast.place, bf16[1056,128]{1,0:T(8,128)(2,1)S(1)} %collective-permute-done.8.refs_0_, f32[32,128]{1,0:T(8,128)S(1)} %get-tuple-element.42.refs_1_.refs_2_.refs_3_, bf16[512,128]{1,0:T(8,128)(2,1)S(1)} %shard_map.90.refs_2_.refs_3_, ...), custom_call_target="tpu_custom_call" | custom-call | tf_op jit(solution)/shard_map/pallas_call | solution.py:54
  40.2 0.8 %collective-permute-done.10.refs_1_ = bf16[512,128]{1,0:T(8,128)(2,1)S(1)} collective-permute-done((bf16[512,128]{1,0:T(8,128)(2,1)S(1)}, bf16[512,128]{1,0:T(8,128)(2,1)S(1)}, u32[]{:S(2)}, u32[]{:S(2)}) %collective-permute-start.10) | collective-permute-done | bytes 131104 | tf_op jit(solution)/shard_map/ppermute | solution.py:259
  41.0 2.8 %collective-permute-done.12.refs_3_ = bf16[512,128]{1,0:T(8,128)(2,1)S(1)} collective-permute-done((bf16[512,128]{1,0:T(8,128)(2,1)S(1)}, bf16[512,128]{1,0:T(8,128)(2,1)S(1)}, u32[]{:S(2)}, u32[]{:S(2)}) %collective-permute-start.12) | collective-permute-done | bytes 131104 | tf_op jit(solution)/shard_map/ppermute | solution.py:259
  44.0 1.6 %collective-permute-start.7 = (bf16[512,128]{1,0:T(8,128)(2,1)S(1)}, bf16[512,128]{1,0:T(8,128)(2,1)S(1)}, u32[]{:S(2)}, u32[]{:S(2)}) collective-permute-start(bf16[512,128]{1,0:T(8,128)(2,1)S(1)} %get-tuple-element.57), channel_id=1, source_target_pairs={{0,2},{1,3},{2,0},{3,1},{4,6},{5,7},{6,4},{7,5},{8,10},{9,11},{10,... | collective-permute-start | bytes 393224 | tf_op jit(solution)/shard_map/ppermute | solution.py:259
  45.9 1.5 %collective-permute-start.14 = (bf16[128,128]{1,0:T(8,128)(2,1)S(1)}, bf16[128,128]{1,0:T(8,128)(2,1)S(1)}, u32[]{:S(2)}, u32[]{:S(2)}) collective-permute-start(bf16[128,128]{1,0:T(8,128)(2,1)S(1)} %get-tuple-element.73), channel_id=1, source_target_pairs={{0,2},{1,3},{2,0},{3,1},{4,6},{5,7},{6,4},{7,5},{8,10},{9,11},{10,... | collective-permute-start | bytes 98312 | tf_op jit(solution)/shard_map/ppermute | solution.py:259
  47.6 2.9 %collective-permute-done.7.refs_1_ = bf16[512,128]{1,0:T(8,128)(2,1)S(1)} collective-permute-done((bf16[512,128]{1,0:T(8,128)(2,1)S(1)}, bf16[512,128]{1,0:T(8,128)(2,1)S(1)}, u32[]{:S(2)}, u32[]{:S(2)}) %collective-permute-start.7) | collective-permute-done | bytes 131104 | tf_op jit(solution)/shard_map/ppermute | solution.py:259
  50.4 0.8 %shard_map.96.filled = f32[64,4096]{1,0:T(8,128)} custom-call(s32[1]{0:T(128)} %bitcast.place, f32[512,128]{1,0:T(8,128)S(1)} %get-tuple-element.56.refs_0_, bf16[512,128]{1,0:T(8,128)(2,1)S(1)} %collective-permute-done.7.refs_1_), custom_call_target="tpu_custom_call" | custom-call | tf_op jit(solution)/shard_map/pallas_call | solution.py:54
  51.3 1.0 %collective-permute-done.9.refs_0_ = bf16[512,128]{1,0:T(8,128)(2,1)S(1)} collective-permute-done((bf16[512,128]{1,0:T(8,128)(2,1)S(1)}, bf16[512,128]{1,0:T(8,128)(2,1)S(1)}, u32[]{:S(2)}, u32[]{:S(2)}) %collective-permute-start.9) | collective-permute-done | bytes 131104 | tf_op jit(solution)/shard_map/ppermute | solution.py:259
  52.3 0.7 %shard_map.102.filled = f32[64,4096]{1,0:T(8,128)} custom-call(s32[1]{0:T(128)} %bitcast.place, f32[64,4096]{1,0:T(8,128)} %shard_map.96.filled, bf16[512,128]{1,0:T(8,128)(2,1)S(1)} %collective-permute-done.9.refs_0_), custom_call_target="tpu_custom_call", output_to_operand_aliasing={{}: (1, {})} | custom-call | tf_op jit(solution)/shard_map/pallas_call | solution.py:54
  53.0 0.8 %collective-permute-done.14.refs_2_ = bf16[128,128]{1,0:T(8,128)(2,1)S(1)} collective-permute-done((bf16[128,128]{1,0:T(8,128)(2,1)S(1)}, bf16[128,128]{1,0:T(8,128)(2,1)S(1)}, u32[]{:S(2)}, u32[]{:S(2)}) %collective-permute-start.14) | collective-permute-done | bytes 32800 | tf_op jit(solution)/shard_map/ppermute | solution.py:259
  53.8 0.9 %shard_map.104 = (f32[64,4096]{1,0:T(8,128)}, f32[64,512]{1,0:T(8,128)}, f32[64,512]{1,0:T(8,128)}) custom-call(s32[1]{0:T(128)} %bitcast.place, f32[64,4096]{1,0:T(8,128)} %shard_map.102.filled, f32[128,128]{1,0:T(8,128)S(1)} %get-tuple-element.71.refs_0_, bf16[640,128]{1,0:T(8,128)(2,1)S(1)} %collective-permute-done.13.refs_1_, ...), custom_call_target="tpu_custom_call", output_to_operand_aliasing={{0}: (1, {})} | custom-call | tf_op jit(solution)/shard_map/pallas_call | solution.py:54
  (20 shorter events, 2.5 us)
Async XLA Ops:
  2.5 22.4 %collective-permute-start = (bf16[1056,128]{1,0:T(8,128)(2,1)S(1)}, bf16[1056,128]{1,0:T(8,128)(2,1)S(1)}, u32[]{:S(2)}, u32[]{:S(2)}) collective-permute-start(bf16[1056,128]{1,0:T(8,128)(2,1)S(1)} %shard_map.87), channel_id=1, source_target_pairs={{0,1},{1,0},{2,3},{3,2},{4,5},{5,4},{6,7},{7,6},{8,9},{9,8},{10,11... | collective-permute-start | bytes 811016 | tf_op jit(solution)/shard_map/ppermute | solution.py:259
  3.3 25.0 %collective-permute-start.1 = (bf16[1056,128]{1,0:T(8,128)(2,1)S(1)}, bf16[1056,128]{1,0:T(8,128)(2,1)S(1)}, u32[]{:S(2)}, u32[]{:S(2)}) collective-permute-start(bf16[1056,128]{1,0:T(8,128)(2,1)S(1)} %shard_map.88), channel_id=1, source_target_pairs={{0,2},{1,3},{2,0},{3,1},{4,6},{5,7},{6,4},{7,5},{8,10},{9,11},{10,... | collective-permute-start | bytes 811016 | tf_op jit(solution)/shard_map/ppermute | solution.py:259
  6.2 25.7 %collective-permute-start.8 = (bf16[1056,128]{1,0:T(8,128)(2,1)S(1)}, bf16[1056,128]{1,0:T(8,128)(2,1)S(1)}, u32[]{:S(2)}, u32[]{:S(2)}) collective-permute-start(bf16[1056,128]{1,0:T(8,128)(2,1)S(1)} %shard_map.97), channel_id=1, source_target_pairs={{0,3},{1,2},{2,1},{3,0},{4,7},{5,6},{6,5},{7,4},{8,11},{9,10},{10,... | collective-permute-start | bytes 811016 | tf_op jit(solution)/shard_map/ppermute | solution.py:259
  6.4 13.9 %collective-permute-start.2 = (bf16[256,128]{1,0:T(8,128)(2,1)S(1)}, bf16[256,128]{1,0:T(8,128)(2,1)S(1)}, u32[]{:S(2)}, u32[]{:S(2)}) collective-permute-start(bf16[256,128]{1,0:T(8,128)(2,1)S(1)} %get-tuple-element.44), channel_id=1, source_target_pairs={{0,2},{1,3},{2,0},{3,1},{4,6},{5,7},{6,4},{7,5},{8,10},{9,11},{10,... | collective-permute-start | bytes 196616 | tf_op jit(solution)/shard_map/ppermute | solution.py:259
  20.2 1.3 %collective-permute-start.3 = (bf16[256,128]{1,0:T(8,128)(2,1)S(1)}, bf16[256,128]{1,0:T(8,128)(2,1)S(1)}, u32[]{:S(2)}, u32[]{:S(2)}) collective-permute-start(bf16[256,128]{1,0:T(8,128)(2,1)S(1)} %shard_map.89), channel_id=1, source_target_pairs={{0,1},{1,0},{2,3},{3,2},{4,5},{5,4},{6,7},{7,6},{8,9},{9,8},{10,11... | collective-permute-start | bytes 196616 | tf_op jit(solution)/shard_map/ppermute | solution.py:259
  21.5 7.6 %collective-permute-start.6 = (bf16[512,128]{1,0:T(8,128)(2,1)S(1)}, bf16[512,128]{1,0:T(8,128)(2,1)S(1)}, u32[]{:S(2)}, u32[]{:S(2)}) collective-permute-start(bf16[512,128]{1,0:T(8,128)(2,1)S(1)} %shard_map.90.refs_2_.refs_3_), channel_id=1, source_target_pairs={{0,4},{4,0},{8,12},{12,8},{16,20},{20,16},{24,28},{28,24},{1,5},{5... | collective-permute-start | bytes 393224 | tf_op jit(solution)/shard_map/ppermute | solution.py:259
  23.3 7.3 %collective-permute-start.5 = (bf16[512,128]{1,0:T(8,128)(2,1)S(1)}, bf16[512,128]{1,0:T(8,128)(2,1)S(1)}, u32[]{:S(2)}, u32[]{:S(2)}) collective-permute-start(bf16[512,128]{1,0:T(8,128)(2,1)S(1)} %shard_map.90.refs_2_.refs_3_), channel_id=1, source_target_pairs={{0,8},{4,12},{8,0},{12,4},{16,24},{20,28},{24,16},{28,20},{1,9},{5... | collective-permute-start | bytes 393224 | tf_op jit(solution)/shard_map/ppermute | solution.py:259
  24.9 8.8 %collective-permute-start.4 = (bf16[512,128]{1,0:T(8,128)(2,1)S(1)}, bf16[512,128]{1,0:T(8,128)(2,1)S(1)}, u32[]{:S(2)}, u32[]{:S(2)}) collective-permute-start(bf16[512,128]{1,0:T(8,128)(2,1)S(1)} %shard_map.90.refs_2_.refs_3_), channel_id=1, source_target_pairs={{0,16},{4,20},{8,24},{12,28},{16,0},{20,4},{24,8},{28,12},{1,17},{... | collective-permute-start | bytes 393224 | tf_op jit(solution)/shard_map/ppermute | solution.py:259
  36.0 5.0 %collective-permute-start.10 = (bf16[512,128]{1,0:T(8,128)(2,1)S(1)}, bf16[512,128]{1,0:T(8,128)(2,1)S(1)}, u32[]{:S(2)}, u32[]{:S(2)}) collective-permute-start(bf16[512,128]{1,0:T(8,128)(2,1)S(1)} %get-tuple-element.67), channel_id=1, source_target_pairs={{0,4},{4,0},{8,12},{12,8},{16,20},{20,16},{24,28},{28,24},{1,5},{5... | collective-permute-start | bytes 393224 | tf_op jit(solution)/shard_map/ppermute | solution.py:259
  36.5 7.3 %collective-permute-start.12 = (bf16[512,128]{1,0:T(8,128)(2,1)S(1)}, bf16[512,128]{1,0:T(8,128)(2,1)S(1)}, u32[]{:S(2)}, u32[]{:S(2)}) collective-permute-start(bf16[512,128]{1,0:T(8,128)(2,1)S(1)} %get-tuple-element.69), channel_id=1, source_target_pairs={{0,16},{4,20},{8,24},{12,28},{16,0},{20,4},{24,8},{28,12},{1,17},{... | collective-permute-start | bytes 393224 | tf_op jit(solution)/shard_map/ppermute | solution.py:259
  36.9 7.0 %collective-permute-start.11 = (bf16[512,128]{1,0:T(8,128)(2,1)S(1)}, bf16[512,128]{1,0:T(8,128)(2,1)S(1)}, u32[]{:S(2)}, u32[]{:S(2)}) collective-permute-start(bf16[512,128]{1,0:T(8,128)(2,1)S(1)} %get-tuple-element.68), channel_id=1, source_target_pairs={{0,8},{4,12},{8,0},{12,4},{16,24},{20,28},{24,16},{28,20},{1,9},{5... | collective-permute-start | bytes 393224 | tf_op jit(solution)/shard_map/ppermute | solution.py:259
  43.9 9.8 %collective-permute-start.13 = (bf16[640,128]{1,0:T(8,128)(2,1)S(1)}, bf16[640,128]{1,0:T(8,128)(2,1)S(1)}, u32[]{:S(2)}, u32[]{:S(2)}) collective-permute-start(bf16[640,128]{1,0:T(8,128)(2,1)S(1)} %get-tuple-element.72), channel_id=1, source_target_pairs={{0,1},{1,0},{2,3},{3,2},{4,5},{5,4},{6,7},{7,6},{8,9},{9,8},{10,11... | collective-permute-start | bytes 491528 | tf_op jit(solution)/shard_map/ppermute | solution.py:259
  44.0 6.4 %collective-permute-start.7 = (bf16[512,128]{1,0:T(8,128)(2,1)S(1)}, bf16[512,128]{1,0:T(8,128)(2,1)S(1)}, u32[]{:S(2)}, u32[]{:S(2)}) collective-permute-start(bf16[512,128]{1,0:T(8,128)(2,1)S(1)} %get-tuple-element.57), channel_id=1, source_target_pairs={{0,2},{1,3},{2,0},{3,1},{4,6},{5,7},{6,4},{7,5},{8,10},{9,11},{10,... | collective-permute-start | bytes 393224 | tf_op jit(solution)/shard_map/ppermute | solution.py:259
  45.6 6.7 %collective-permute-start.9 = (bf16[512,128]{1,0:T(8,128)(2,1)S(1)}, bf16[512,128]{1,0:T(8,128)(2,1)S(1)}, u32[]{:S(2)}, u32[]{:S(2)}) collective-permute-start(bf16[512,128]{1,0:T(8,128)(2,1)S(1)} %get-tuple-element.65), channel_id=1, source_target_pairs={{0,3},{1,2},{2,1},{3,0},{4,7},{5,6},{6,5},{7,4},{8,11},{9,10},{10,... | collective-permute-start | bytes 393224 | tf_op jit(solution)/shard_map/ppermute | solution.py:259
  45.9 7.9 %collective-permute-start.14 = (bf16[128,128]{1,0:T(8,128)(2,1)S(1)}, bf16[128,128]{1,0:T(8,128)(2,1)S(1)}, u32[]{:S(2)}, u32[]{:S(2)}) collective-permute-start(bf16[128,128]{1,0:T(8,128)(2,1)S(1)} %get-tuple-element.73), channel_id=1, source_target_pairs={{0,2},{1,3},{2,0},{3,1},{4,6},{5,7},{6,4},{7,5},{8,10},{9,11},{10,... | collective-permute-start | bytes 98312 | tf_op jit(solution)/shard_map/ppermute | solution.py:259
  47.4 6.4 %collective-permute-start.15 = (bf16[128,128]{1,0:T(8,128)(2,1)S(1)}, bf16[128,128]{1,0:T(8,128)(2,1)S(1)}, u32[]{:S(2)}, u32[]{:S(2)}) collective-permute-start(bf16[128,128]{1,0:T(8,128)(2,1)S(1)} %get-tuple-element.74), channel_id=1, source_target_pairs={{0,3},{1,2},{2,1},{3,0},{4,7},{5,6},{6,5},{7,4},{8,11},{9,10},{10,... | collective-permute-start | bytes 98312 | tf_op jit(solution)/shard_map/ppermute | solution.py:259

commit v6 on v5

--- a/solution.py
+++ b/solution.py
@@ -64,9 +64,8 @@
 
 def load_kernel(parts, place, q_any, g_any, o_any, k_any, v_any, l_any, *refs):
     q_ref, g_ref, o_ref = refs[:3]
-    count = 2 + (parts - 2) // 2
-    kv_refs, lse_ref = refs[3 : 3 + count], refs[3 + count]
-    k_ref, v_ref, l_ref, sems = refs[4 + count :]
+    kv_refs, lse_ref = refs[3 : 3 + parts], refs[3 + parts]
+    k_ref, v_ref, l_ref, sems = refs[4 + parts :]
     own = place[0]
     rows = k_ref.shape[0]
     pairs = [(k_any, k_ref), (v_any, v_ref), (l_any, l_ref)]
@@ -81,9 +80,8 @@
         copy.wait()
     for m in range(parts):
         col = pl.multiple_of((own ^ m) * HEAD_DIM, HEAD_DIM)
-        target, first = (kv_refs[m], 0) if m < 2 else (kv_refs[1 + m // 2], m % 2 * 2 * rows)
-        target[first : first + rows, :] = k_ref[:, pl.ds(col, HEAD_DIM)]
-        target[first + rows : first + 2 * rows, :] = v_ref[:, pl.ds(col, HEAD_DIM)]
+        kv_refs[m][:rows, :] = k_ref[:, pl.ds(col, HEAD_DIM)]
+        kv_refs[m][rows:, :] = v_ref[:, pl.ds(col, HEAD_DIM)]
     for m in range(parts):
         piece = l_ref[:, :rows]
         for c in range(1, parts):
@@ -121,26 +119,12 @@
     )
 
 
-def forward_kernel(parts, place, *refs):
-    out = refs[-1]
-    size = refs[0].shape[0]
-    out[:size, :] = refs[0][...]
-    for i in range(1, parts // 2):
-        out[i * size : (i + 1) * size, :] = refs[i][size:, :]
-
-
 def join_kernel(parts, place, *refs):
-    near, far, passed, out = refs[0], refs[1 : parts // 2], refs[-2], refs[-1]
+    pieces, out = refs[:parts], refs[parts]
     rows = out.shape[0] // (2 * parts)
     for m in range(parts):
-        if m % 2:
-            source, first = passed, m // 2 * 2 * rows
-        else:
-            source, first = (far[m // 2 - 1], 0) if m else (near, 0)
-        out[m * rows : (m + 1) * rows, :] = source[first : first + rows, :]
-        out[(parts + m) * rows : (parts + m + 1) * rows, :] = source[
-            first + rows : first + 2 * rows, :
-        ]
+        out[m * rows : (m + 1) * rows, :] = pieces[m][:rows, :]
+        out[(parts + m) * rows : (parts + m + 1) * rows, :] = pieces[m][rows:, :]
 
 
 def row_of(stack):
@@ -263,6 +247,10 @@
     return [b for b in (2, 3, 1) if b < levels] + list(range(4, levels))
 
 
+def use_order(levels):
+    return [b for b in (2, 1, 3) if b < levels] + list(range(4, levels))
+
+
 def on_device(queries, key_rows, value_rows, attn_out, out_grad, logsumexp):
     parts = lax.axis_size("head")
     levels = lax.axis_size("ctx").bit_length()
@@ -274,8 +262,7 @@
     *rows_in, lse = call(
         functools.partial(load_kernel, parts),
         [vmem(queries.shape, BF16)] * 3
-        + [vmem((2 * rows, HEAD_DIM), BF16)] * 2
-        + [vmem((4 * rows, HEAD_DIM), BF16)] * (parts // 2 - 1)
+        + [vmem((2 * rows, HEAD_DIM), BF16)] * parts
         + [vmem((8 * parts, 2 * rows), F32)],
         place,
         queries,
@@ -302,22 +289,9 @@
             *rows_in[:3],
         )
         qg.append(packed if m == 0 else swap(packed, "head", m))
-    kv_far = [swap(kv[1 + i], "head", 2 * i) for i in range(1, parts // 2)]
-    (passed,) = call(
-        functools.partial(forward_kernel, parts),
-        [vmem((parts * rows, HEAD_DIM), BF16)],
-        place,
-        kv[1],
-        *kv_far,
-    )
-    passed = swap(passed, "head", 1)
+    kv = [kv[0]] + [swap(kv[m], "head", m) for m in range(1, parts)]
     (kv_own,) = call(
-        functools.partial(join_kernel, parts),
-        [vmem((2 * block, HEAD_DIM), BF16)],
-        place,
-        kv[0],
-        *kv_far,
-        passed,
+        functools.partial(join_kernel, parts), [vmem((2 * block, HEAD_DIM), BF16)], place, *kv
     )
     kv_all = [kv_own] + [swap(kv_own, "ctx", 1 << (b - 1)) for b in range(1, levels)]
 
@@ -359,8 +333,8 @@
     early = tuple(range(parts - 1))
     step((0,), (0,), False, False)
     step(early[1:], (0,), False, False)
-    for b in range(1, levels):
-        step(early, (b,), b == levels - 1, False)
+    for b in use_order(levels):
+        step(early, (b,), b == use_order(levels)[-1], False)
     for b in far_order(levels) + [0]:
         step((parts - 1,), (b,), b == 0, True)
 

time: 54.8 us -> 53.9 us (0.984)
  waiting for transfers between devices: 23.3 us -> 21.2 us
  starting transfers between devices: 18.2 us -> 19.4 us
    ppermute x16 -> x17, waiting for transfers between devices: 23.3 us -> 21.2 us  [swap(): lax.ppermute(value, axis, [(i, i ^ distance) for i in range(lax.axis_size...]
    ppermute x16 -> x17, starting transfers between devices: 18.2 us -> 19.4 us  [swap(): lax.ppermute(value, axis, [(i, i ^ distance) for i in range(lax.axis_size...]
    pallas_call x20 -> x19, Pallas kernels: 12.4 us -> 12.4 us  [call(): pl.pallas_call(kernel, out_shape=out_shapes, in_specs=specs, out_specs=[p...]
  transfers between devices with their start and end apart: 16 -> 17, of which waited for: 9 -> 9; matrix products, arithmetic and copies ran while one was open for 0% -> 0% of each run, Pallas kernels for 13% -> 14%
where the time goes in v6:
time: 53.9 us; the launch traced here: 53.8 us
  waiting for transfers between devices  21.2 us (39%)
  starting transfers between devices  19.4 us (36%)
  Pallas kernels  12.4 us (23%)
  between operations  0.78 us (1%)
    ppermute x17, waiting for transfers between devices, swap(): lax.ppermute(value, axis, [(i, i ^ distance) for i in range(lax.axis_size...  21.2 us
    ppermute x17, starting transfers between devices, swap(): lax.ppermute(value, axis, [(i, i ^ distance) for i in range(lax.axis_size...  19.4 us
    pallas_call x19, Pallas kernels, call(): pl.pallas_call(kernel, out_shape=out_shapes, in_specs=specs, out_specs=[p...  12.4 us
  transfers between devices with their start and end apart: 17, of which 9 were waited for; matrix products, arithmetic and copies ran while one was open for 0% of the time, Pallas kernels for 14%

profile of v6, /device:TPU:0, one launch (start us, length us, event | category | flops | bytes accessed | tf_op | source)
XLA Modules:
  0.0 53.8 jit_solution(7429152509960887317)
XLA Ops:
  0.6 1.5 %shard_map.85 = (bf16[64,4096]{1,0:T(8,128)(2,1)S(1)}, bf16[64,4096]{1,0:T(8,128)(2,1)S(1)}, bf16[64,4096]{1,0:T(8,128)(2,1)S(1)}, bf16[128,128]{1,0:T(8,128)(2,...) custom-call(s32[1]{0:T(128)} %bitcast.place, ...), custom_call_target="tpu_custom_call" | custom-call | tf_op jit(solution)/shard_map/pallas_call | solution.py:54
  2.5 0.5 collective-permute-start
  3.3 2.5 %collective-permute-start.1 = (bf16[1056,128]{1,0:T(8,128)(2,1)S(1)}, bf16[1056,128]{1,0:T(8,128)(2,1)S(1)}, u32[]{:S(2)}, u32[]{:S(2)}) collective-permute-start(bf16[1056,128]{1,0:T(8,128)(2,1)S(1)} %shard_map.88), channel_id=1, source_target_pairs={{0,2},{1,3},{2,0},{3,1},{4,6},{5,7},{6,4},{7,5},{8,10},{9,11},{10,... | collective-permute-start | bytes 811016 | tf_op jit(solution)/shard_map/ppermute | solution.py:243
  6.5 1.9 %collective-permute-start.3 = (bf16[128,128]{1,0:T(8,128)(2,1)S(1)}, bf16[128,128]{1,0:T(8,128)(2,1)S(1)}, u32[]{:S(2)}, u32[]{:S(2)}) collective-permute-start(bf16[128,128]{1,0:T(8,128)(2,1)S(1)} %get-tuple-element.46), channel_id=1, source_target_pairs={{0,2},{1,3},{2,0},{3,1},{4,6},{5,7},{6,4},{7,5},{8,10},{9,11},{10,... | collective-permute-start | bytes 98312 | tf_op jit(solution)/shard_map/ppermute | solution.py:243
  8.4 0.8 %collective-permute-start.4 = (bf16[128,128]{1,0:T(8,128)(2,1)S(1)}, bf16[128,128]{1,0:T(8,128)(2,1)S(1)}, u32[]{:S(2)}, u32[]{:S(2)}) collective-permute-start(bf16[128,128]{1,0:T(8,128)(2,1)S(1)} %get-tuple-element.47), channel_id=1, source_target_pairs={{0,3},{1,2},{2,1},{3,0},{4,7},{5,6},{6,5},{7,4},{8,11},{9,10},{10,... | collective-permute-start | bytes 98312 | tf_op jit(solution)/shard_map/ppermute | solution.py:243
  9.2 10.5 %collective-permute-done.3.refs_2_ = bf16[128,128]{1,0:T(8,128)(2,1)S(1)} collective-permute-done((bf16[128,128]{1,0:T(8,128)(2,1)S(1)}, bf16[128,128]{1,0:T(8,128)(2,1)S(1)}, u32[]{:S(2)}, u32[]{:S(2)}) %collective-permute-start.3) | collective-permute-done | bytes 32800 | tf_op jit(solution)/shard_map/ppermute | solution.py:243
  20.0 1.7 %collective-permute-start.7 = (bf16[512,128]{1,0:T(8,128)(2,1)S(1)}, bf16[512,128]{1,0:T(8,128)(2,1)S(1)}, u32[]{:S(2)}, u32[]{:S(2)}) collective-permute-start(bf16[512,128]{1,0:T(8,128)(2,1)S(1)} %shard_map.89.refs_2_.refs_3_), channel_id=1, source_target_pairs={{0,8},{4,12},{8,0},{12,4},{16,24},{20,28},{24,16},{28,20},{1,9},{5... | collective-permute-start | bytes 393224 | tf_op jit(solution)/shard_map/ppermute | solution.py:243
  21.8 1.5 %collective-permute-start.6 = (bf16[512,128]{1,0:T(8,128)(2,1)S(1)}, bf16[512,128]{1,0:T(8,128)(2,1)S(1)}, u32[]{:S(2)}, u32[]{:S(2)}) collective-permute-start(bf16[512,128]{1,0:T(8,128)(2,1)S(1)} %shard_map.89.refs_2_.refs_3_), channel_id=1, source_target_pairs={{0,4},{4,0},{8,12},{12,8},{16,20},{20,16},{24,28},{28,24},{1,5},{5... | collective-permute-start | bytes 393224 | tf_op jit(solution)/shard_map/ppermute | solution.py:243
  23.3 2.6 %collective-permute-start.5 = (bf16[512,128]{1,0:T(8,128)(2,1)S(1)}, bf16[512,128]{1,0:T(8,128)(2,1)S(1)}, u32[]{:S(2)}, u32[]{:S(2)}) collective-permute-start(bf16[512,128]{1,0:T(8,128)(2,1)S(1)} %shard_map.89.refs_2_.refs_3_), channel_id=1, source_target_pairs={{0,16},{4,20},{8,24},{12,28},{16,0},{20,4},{24,8},{28,12},{1,17},{... | collective-permute-start | bytes 393224 | tf_op jit(solution)/shard_map/ppermute | solution.py:243
  26.2 0.5 shard_map.90
  26.7 0.8 %shard_map.91 = (f32[128,512]{1,0:T(8,128)S(1)}, f32[128,512]{1,0:T(8,128)S(1)}, f32[512,128]{1,0:T(8,128)S(1)}) custom-call(s32[1]{0:T(128)} %bitcast.place, bf16[1056,128]{1,0:T(8,128)(2,1)S(1)} %collective-permute-done.refs_0_.refs_1_, bf16[1056,128]{1,0:T(8,128)(2,1)S(1)} %collective-permute-done.1.refs_1_.refs_2_, ...), custom_call_target="tpu_custom_call" | custom-call | tf_op jit(solution)/shard_map/pallas_call | solution.py:54
  27.5 1.2 %shard_map.92 = (f32[128,512]{1,0:T(8,128)S(1)}, f32[128,512]{1,0:T(8,128)S(1)}, f32[128,512]{1,0:T(8,128)S(1)}, f32[512,128]{1,0:T(8,128)S(1)}) custom-call(s32[1]{0:T(128)} %bitcast.place, bf16[1056,128]{1,0:T(8,128)(2,1)S(1)} %shard_map.86.refs_0_, bf16[1056,128]{1,0:T(8,128)(2,1)S(1)} %collective-permute-done.refs_0_.refs_1_, ...), custom_call_target="tpu_custom_call" | custom-call | tf_op jit(solution)/shard_map/pallas_call | solution.py:54
  28.8 0.5 shard_map.97
  29.2 1.2 %shard_map.93 = (f32[128,512]{1,0:T(8,128)S(1)}, f32[128,512]{1,0:T(8,128)S(1)}, f32[128,512]{1,0:T(8,128)S(1)}, f32[512,128]{1,0:T(8,128)S(1)}) custom-call(s32[1]{0:T(128)} %bitcast.place, bf16[1056,128]{1,0:T(8,128)(2,1)S(1)} %shard_map.86.refs_0_, bf16[1056,128]{1,0:T(8,128)(2,1)S(1)} %collective-permute-done.refs_0_.refs_1_, ...), custom_call_target="tpu_custom_call" | custom-call | tf_op jit(solution)/shard_map/pallas_call | solution.py:54
  30.5 1.5 %collective-permute-done.5.refs_4_.refs_2_ = bf16[512,128]{1,0:T(8,128)(2,1)S(1)} collective-permute-done((bf16[512,128]{1,0:T(8,128)(2,1)S(1)}, bf16[512,128]{1,0:T(8,128)(2,1)S(1)}, u32[]{:S(2)}, u32[]{:S(2)}) %collective-permute-start.5) | collective-permute-done | bytes 131104 | tf_op jit(solution)/shard_map/ppermute | solution.py:243
  32.0 1.3 %shard_map.94 = (f32[512,128]{1,0:T(8,128)S(1)}, bf16[512,128]{1,0:T(8,128)(2,1)S(1)}, bf16[512,128]{1,0:T(8,128)(2,1)S(1)}, f32[512,128]{1,0:T(8,128)S(1)}) custom-call(s32[1]{0:T(128)} %bitcast.place, bf16[1056,128]{1,0:T(8,128)(2,1)S(1)} %shard_map.86.refs_0_, bf16[1056,128]{1,0:T(8,128)(2,1)S(1)} %collective-permute-done.refs_0_.refs_1_, ...), custom_call_target="tpu_custom_call" | custom-call | tf_op jit(solution)/shard_map/pallas_call | solution.py:54
  33.4 0.5 shard_map.98
  33.8 0.5 shard_map.99
  34.3 0.6 %collective-permute-start.11 = (bf16[512,128]{1,0:T(8,128)(2,1)S(1)}, bf16[512,128]{1,0:T(8,128)(2,1)S(1)}, u32[]{:S(2)}, u32[]{:S(2)}) collective-permute-start(bf16[512,128]{1,0:T(8,128)(2,1)S(1)} %get-tuple-element.69), channel_id=1, source_target_pairs={{0,4},{4,0},{8,12},{12,8},{16,20},{20,16},{24,28},{28,24},{1,5},{5... | collective-permute-start | bytes 393224 | tf_op jit(solution)/shard_map/ppermute | solution.py:243
  34.9 1.1 %collective-permute-start.13 = (bf16[512,128]{1,0:T(8,128)(2,1)S(1)}, bf16[512,128]{1,0:T(8,128)(2,1)S(1)}, u32[]{:S(2)}, u32[]{:S(2)}) collective-permute-start(bf16[512,128]{1,0:T(8,128)(2,1)S(1)} %get-tuple-element.71), channel_id=1, source_target_pairs={{0,16},{4,20},{8,24},{12,28},{16,0},{20,4},{24,8},{28,12},{1,17},{... | collective-permute-start | bytes 393224 | tf_op jit(solution)/shard_map/ppermute | solution.py:243
  36.1 2.1 %collective-permute-start.12 = (bf16[512,128]{1,0:T(8,128)(2,1)S(1)}, bf16[512,128]{1,0:T(8,128)(2,1)S(1)}, u32[]{:S(2)}, u32[]{:S(2)}) collective-permute-start(bf16[512,128]{1,0:T(8,128)(2,1)S(1)} %get-tuple-element.70), channel_id=1, source_target_pairs={{0,8},{4,12},{8,0},{12,4},{16,24},{20,28},{24,16},{28,20},{1,9},{5... | collective-permute-start | bytes 393224 | tf_op jit(solution)/shard_map/ppermute | solution.py:243
  38.2 0.6 %shard_map.100 = (bf16[512,128]{1,0:T(8,128)(2,1)S(1)}, f32[512,128]{1,0:T(8,128)S(1)}) custom-call(s32[1]{0:T(128)} %bitcast.place, bf16[1056,128]{1,0:T(8,128)(2,1)S(1)} %collective-permute-done.9.refs_0_, f32[32,128]{1,0:T(8,128)S(1)} %get-tuple-element.43.refs_1_.refs_2_.refs_3_, bf16[512,128]{1,0:T(8,128)(2,1)S(1)} %shard_map.89.refs_2_.refs_3_, ...), custom_call_target="tpu_custom_call" | custom-call | tf_op jit(solution)/shard_map/pallas_call | solution.py:54
  38.8 0.6 %collective-permute-done.11.refs_1_ = bf16[512,128]{1,0:T(8,128)(2,1)S(1)} collective-permute-done((bf16[512,128]{1,0:T(8,128)(2,1)S(1)}, bf16[512,128]{1,0:T(8,128)(2,1)S(1)}, u32[]{:S(2)}, u32[]{:S(2)}) %collective-permute-start.11) | collective-permute-done | bytes 131104 | tf_op jit(solution)/shard_map/ppermute | solution.py:243
  39.4 3.4 %collective-permute-done.13.refs_3_ = bf16[512,128]{1,0:T(8,128)(2,1)S(1)} collective-permute-done((bf16[512,128]{1,0:T(8,128)(2,1)S(1)}, bf16[512,128]{1,0:T(8,128)(2,1)S(1)}, u32[]{:S(2)}, u32[]{:S(2)}) %collective-permute-start.13) | collective-permute-done | bytes 131104 | tf_op jit(solution)/shard_map/ppermute | solution.py:243
  43.1 1.6 %collective-permute-start.8 = (bf16[512,128]{1,0:T(8,128)(2,1)S(1)}, bf16[512,128]{1,0:T(8,128)(2,1)S(1)}, u32[]{:S(2)}, u32[]{:S(2)}) collective-permute-start(bf16[512,128]{1,0:T(8,128)(2,1)S(1)} %get-tuple-element.59), channel_id=1, source_target_pairs={{0,2},{1,3},{2,0},{3,1},{4,6},{5,7},{6,4},{7,5},{8,10},{9,11},{10,... | collective-permute-start | bytes 393224 | tf_op jit(solution)/shard_map/ppermute | solution.py:243
  45.0 1.5 %collective-permute-start.15 = (bf16[128,128]{1,0:T(8,128)(2,1)S(1)}, bf16[128,128]{1,0:T(8,128)(2,1)S(1)}, u32[]{:S(2)}, u32[]{:S(2)}) collective-permute-start(bf16[128,128]{1,0:T(8,128)(2,1)S(1)} %get-tuple-element.75), channel_id=1, source_target_pairs={{0,2},{1,3},{2,0},{3,1},{4,6},{5,7},{6,4},{7,5},{8,10},{9,11},{10,... | collective-permute-start | bytes 98312 | tf_op jit(solution)/shard_map/ppermute | solution.py:243
  46.7 2.9 %collective-permute-done.8.refs_1_ = bf16[512,128]{1,0:T(8,128)(2,1)S(1)} collective-permute-done((bf16[512,128]{1,0:T(8,128)(2,1)S(1)}, bf16[512,128]{1,0:T(8,128)(2,1)S(1)}, u32[]{:S(2)}, u32[]{:S(2)}) %collective-permute-start.8) | collective-permute-done | bytes 131104 | tf_op jit(solution)/shard_map/ppermute | solution.py:243
  49.6 0.8 %shard_map.95.filled = f32[64,4096]{1,0:T(8,128)} custom-call(s32[1]{0:T(128)} %bitcast.place, f32[512,128]{1,0:T(8,128)S(1)} %get-tuple-element.58.refs_0_, bf16[512,128]{1,0:T(8,128)(2,1)S(1)} %collective-permute-done.8.refs_1_), custom_call_target="tpu_custom_call" | custom-call | tf_op jit(solution)/shard_map/pallas_call | solution.py:54
  50.4 1.0 %collective-permute-done.10.refs_0_ = bf16[512,128]{1,0:T(8,128)(2,1)S(1)} collective-permute-done((bf16[512,128]{1,0:T(8,128)(2,1)S(1)}, bf16[512,128]{1,0:T(8,128)(2,1)S(1)}, u32[]{:S(2)}, u32[]{:S(2)}) %collective-permute-start.10) | collective-permute-done | bytes 131104 | tf_op jit(solution)/shard_map/ppermute | solution.py:243
  51.4 0.7 %shard_map.101.filled = f32[64,4096]{1,0:T(8,128)} custom-call(s32[1]{0:T(128)} %bitcast.place, f32[64,4096]{1,0:T(8,128)} %shard_map.95.filled, bf16[512,128]{1,0:T(8,128)(2,1)S(1)} %collective-permute-done.10.refs_0_), custom_call_target="tpu_custom_call", output_to_operand_aliasing={{}: (1, {})} | custom-call | tf_op jit(solution)/shard_map/pallas_call | solution.py:54
  52.1 0.8 %collective-permute-done.15.refs_2_ = bf16[128,128]{1,0:T(8,128)(2,1)S(1)} collective-permute-done((bf16[128,128]{1,0:T(8,128)(2,1)S(1)}, bf16[128,128]{1,0:T(8,128)(2,1)S(1)}, u32[]{:S(2)}, u32[]{:S(2)}) %collective-permute-start.15) | collective-permute-done | bytes 32800 | tf_op jit(solution)/shard_map/ppermute | solution.py:243
  52.9 0.9 %shard_map.103 = (f32[64,4096]{1,0:T(8,128)}, f32[64,512]{1,0:T(8,128)}, f32[64,512]{1,0:T(8,128)}) custom-call(s32[1]{0:T(128)} %bitcast.place, f32[64,4096]{1,0:T(8,128)} %shard_map.101.filled, f32[128,128]{1,0:T(8,128)S(1)} %get-tuple-element.73.refs_0_, bf16[640,128]{1,0:T(8,128)(2,1)S(1)} %collective-permute-done.14.refs_1_, ...), custom_call_target="tpu_custom_call", output_to_operand_aliasing={{0}: (1, {})} | custom-call | tf_op jit(solution)/shard_map/pallas_call | solution.py:54
  (21 shorter events, 2.9 us)
Async XLA Ops:
  2.5 20.8 %collective-permute-start = (bf16[1056,128]{1,0:T(8,128)(2,1)S(1)}, bf16[1056,128]{1,0:T(8,128)(2,1)S(1)}, u32[]{:S(2)}, u32[]{:S(2)}) collective-permute-start(bf16[1056,128]{1,0:T(8,128)(2,1)S(1)} %shard_map.87), channel_id=1, source_target_pairs={{0,1},{1,0},{2,3},{3,2},{4,5},{5,4},{6,7},{7,6},{8,9},{9,8},{10,11... | collective-permute-start | bytes 811016 | tf_op jit(solution)/shard_map/ppermute | solution.py:243
  3.3 23.3 %collective-permute-start.1 = (bf16[1056,128]{1,0:T(8,128)(2,1)S(1)}, bf16[1056,128]{1,0:T(8,128)(2,1)S(1)}, u32[]{:S(2)}, u32[]{:S(2)}) collective-permute-start(bf16[1056,128]{1,0:T(8,128)(2,1)S(1)} %shard_map.88), channel_id=1, source_target_pairs={{0,2},{1,3},{2,0},{3,1},{4,6},{5,7},{6,4},{7,5},{8,10},{9,11},{10,... | collective-permute-start | bytes 811016 | tf_op jit(solution)/shard_map/ppermute | solution.py:243
  6.2 22.5 %collective-permute-start.9 = (bf16[1056,128]{1,0:T(8,128)(2,1)S(1)}, bf16[1056,128]{1,0:T(8,128)(2,1)S(1)}, u32[]{:S(2)}, u32[]{:S(2)}) collective-permute-start(bf16[1056,128]{1,0:T(8,128)(2,1)S(1)} %shard_map.96), channel_id=1, source_target_pairs={{0,3},{1,2},{2,1},{3,0},{4,7},{5,6},{6,5},{7,4},{8,11},{9,10},{10,... | collective-permute-start | bytes 811016 | tf_op jit(solution)/shard_map/ppermute | solution.py:243
  6.4 2.0 %collective-permute-start.2 = (bf16[128,128]{1,0:T(8,128)(2,1)S(1)}, bf16[128,128]{1,0:T(8,128)(2,1)S(1)}, u32[]{:S(2)}, u32[]{:S(2)}) collective-permute-start(bf16[128,128]{1,0:T(8,128)(2,1)S(1)} %get-tuple-element.45), channel_id=1, source_target_pairs={{0,1},{1,0},{2,3},{3,2},{4,5},{5,4},{6,7},{7,6},{8,9},{9,8},{10,11... | collective-permute-start | bytes 98312 | tf_op jit(solution)/shard_map/ppermute | solution.py:243
  6.5 13.2 %collective-permute-start.3 = (bf16[128,128]{1,0:T(8,128)(2,1)S(1)}, bf16[128,128]{1,0:T(8,128)(2,1)S(1)}, u32[]{:S(2)}, u32[]{:S(2)}) collective-permute-start(bf16[128,128]{1,0:T(8,128)(2,1)S(1)} %get-tuple-element.46), channel_id=1, source_target_pairs={{0,2},{1,3},{2,0},{3,1},{4,6},{5,7},{6,4},{7,5},{8,10},{9,11},{10,... | collective-permute-start | bytes 98312 | tf_op jit(solution)/shard_map/ppermute | solution.py:243
  8.4 11.6 %collective-permute-start.4 = (bf16[128,128]{1,0:T(8,128)(2,1)S(1)}, bf16[128,128]{1,0:T(8,128)(2,1)S(1)}, u32[]{:S(2)}, u32[]{:S(2)}) collective-permute-start(bf16[128,128]{1,0:T(8,128)(2,1)S(1)} %get-tuple-element.47), channel_id=1, source_target_pairs={{0,3},{1,2},{2,1},{3,0},{4,7},{5,6},{6,5},{7,4},{8,11},{9,10},{10,... | collective-permute-start | bytes 98312 | tf_op jit(solution)/shard_map/ppermute | solution.py:243
  20.0 7.5 %collective-permute-start.7 = (bf16[512,128]{1,0:T(8,128)(2,1)S(1)}, bf16[512,128]{1,0:T(8,128)(2,1)S(1)}, u32[]{:S(2)}, u32[]{:S(2)}) collective-permute-start(bf16[512,128]{1,0:T(8,128)(2,1)S(1)} %shard_map.89.refs_2_.refs_3_), channel_id=1, source_target_pairs={{0,8},{4,12},{8,0},{12,4},{16,24},{20,28},{24,16},{28,20},{1,9},{5... | collective-permute-start | bytes 393224 | tf_op jit(solution)/shard_map/ppermute | solution.py:243
  21.8 7.5 %collective-permute-start.6 = (bf16[512,128]{1,0:T(8,128)(2,1)S(1)}, bf16[512,128]{1,0:T(8,128)(2,1)S(1)}, u32[]{:S(2)}, u32[]{:S(2)}) collective-permute-start(bf16[512,128]{1,0:T(8,128)(2,1)S(1)} %shard_map.89.refs_2_.refs_3_), channel_id=1, source_target_pairs={{0,4},{4,0},{8,12},{12,8},{16,20},{20,16},{24,28},{28,24},{1,5},{5... | collective-permute-start | bytes 393224 | tf_op jit(solution)/shard_map/ppermute | solution.py:243
  23.3 8.7 %collective-permute-start.5 = (bf16[512,128]{1,0:T(8,128)(2,1)S(1)}, bf16[512,128]{1,0:T(8,128)(2,1)S(1)}, u32[]{:S(2)}, u32[]{:S(2)}) collective-permute-start(bf16[512,128]{1,0:T(8,128)(2,1)S(1)} %shard_map.89.refs_2_.refs_3_), channel_id=1, source_target_pairs={{0,16},{4,20},{8,24},{12,28},{16,0},{20,4},{24,8},{28,12},{1,17},{... | collective-permute-start | bytes 393224 | tf_op jit(solution)/shard_map/ppermute | solution.py:243
  34.3 5.0 %collective-permute-start.11 = (bf16[512,128]{1,0:T(8,128)(2,1)S(1)}, bf16[512,128]{1,0:T(8,128)(2,1)S(1)}, u32[]{:S(2)}, u32[]{:S(2)}) collective-permute-start(bf16[512,128]{1,0:T(8,128)(2,1)S(1)} %get-tuple-element.69), channel_id=1, source_target_pairs={{0,4},{4,0},{8,12},{12,8},{16,20},{20,16},{24,28},{28,24},{1,5},{5... | collective-permute-start | bytes 393224 | tf_op jit(solution)/shard_map/ppermute | solution.py:243
  34.9 7.8 %collective-permute-start.13 = (bf16[512,128]{1,0:T(8,128)(2,1)S(1)}, bf16[512,128]{1,0:T(8,128)(2,1)S(1)}, u32[]{:S(2)}, u32[]{:S(2)}) collective-permute-start(bf16[512,128]{1,0:T(8,128)(2,1)S(1)} %get-tuple-element.71), channel_id=1, source_target_pairs={{0,16},{4,20},{8,24},{12,28},{16,0},{20,4},{24,8},{28,12},{1,17},{... | collective-permute-start | bytes 393224 | tf_op jit(solution)/shard_map/ppermute | solution.py:243
  36.1 6.9 %collective-permute-start.12 = (bf16[512,128]{1,0:T(8,128)(2,1)S(1)}, bf16[512,128]{1,0:T(8,128)(2,1)S(1)}, u32[]{:S(2)}, u32[]{:S(2)}) collective-permute-start(bf16[512,128]{1,0:T(8,128)(2,1)S(1)} %get-tuple-element.70), channel_id=1, source_target_pairs={{0,8},{4,12},{8,0},{12,4},{16,24},{20,28},{24,16},{28,20},{1,9},{5... | collective-permute-start | bytes 393224 | tf_op jit(solution)/shard_map/ppermute | solution.py:243
  43.1 9.8 %collective-permute-start.14 = (bf16[640,128]{1,0:T(8,128)(2,1)S(1)}, bf16[640,128]{1,0:T(8,128)(2,1)S(1)}, u32[]{:S(2)}, u32[]{:S(2)}) collective-permute-start(bf16[640,128]{1,0:T(8,128)(2,1)S(1)} %get-tuple-element.74), channel_id=1, source_target_pairs={{0,1},{1,0},{2,3},{3,2},{4,5},{5,4},{6,7},{7,6},{8,9},{9,8},{10,11... | collective-permute-start | bytes 491528 | tf_op jit(solution)/shard_map/ppermute | solution.py:243
  43.1 6.4 %collective-permute-start.8 = (bf16[512,128]{1,0:T(8,128)(2,1)S(1)}, bf16[512,128]{1,0:T(8,128)(2,1)S(1)}, u32[]{:S(2)}, u32[]{:S(2)}) collective-permute-start(bf16[512,128]{1,0:T(8,128)(2,1)S(1)} %get-tuple-element.59), channel_id=1, source_target_pairs={{0,2},{1,3},{2,0},{3,1},{4,6},{5,7},{6,4},{7,5},{8,10},{9,11},{10,... | collective-permute-start | bytes 393224 | tf_op jit(solution)/shard_map/ppermute | solution.py:243
  44.7 6.7 %collective-permute-start.10 = (bf16[512,128]{1,0:T(8,128)(2,1)S(1)}, bf16[512,128]{1,0:T(8,128)(2,1)S(1)}, u32[]{:S(2)}, u32[]{:S(2)}) collective-permute-start(bf16[512,128]{1,0:T(8,128)(2,1)S(1)} %get-tuple-element.67), channel_id=1, source_target_pairs={{0,3},{1,2},{2,1},{3,0},{4,7},{5,6},{6,5},{7,4},{8,11},{9,10},{10,... | collective-permute-start | bytes 393224 | tf_op jit(solution)/shard_map/ppermute | solution.py:243
  45.0 7.9 %collective-permute-start.15 = (bf16[128,128]{1,0:T(8,128)(2,1)S(1)}, bf16[128,128]{1,0:T(8,128)(2,1)S(1)}, u32[]{:S(2)}, u32[]{:S(2)}) collective-permute-start(bf16[128,128]{1,0:T(8,128)(2,1)S(1)} %get-tuple-element.75), channel_id=1, source_target_pairs={{0,2},{1,3},{2,0},{3,1},{4,6},{5,7},{6,4},{7,5},{8,10},{9,11},{10,... | collective-permute-start | bytes 98312 | tf_op jit(solution)/shard_map/ppermute | solution.py:243
  46.5 6.4 %collective-permute-start.16 = (bf16[128,128]{1,0:T(8,128)(2,1)S(1)}, bf16[128,128]{1,0:T(8,128)(2,1)S(1)}, u32[]{:S(2)}, u32[]{:S(2)}) collective-permute-start(bf16[128,128]{1,0:T(8,128)(2,1)S(1)} %get-tuple-element.76), channel_id=1, source_target_pairs={{0,3},{1,2},{2,1},{3,0},{4,7},{5,6},{6,5},{7,4},{8,11},{9,10},{10,... | collective-permute-start | bytes 98312 | tf_op jit(solution)/shard_map/ppermute | solution.py:243

commit v7 on v6

--- a/solution.py
+++ b/solution.py
@@ -331,10 +331,13 @@
                 acc[b] = swap(acc[b], "ctx", 1 << (b - 1))
 
     early = tuple(range(parts - 1))
+    hops = use_order(levels)
     step((0,), (0,), False, False)
-    step(early[1:], (0,), False, False)
-    for b in use_order(levels):
-        step(early, (b,), b == use_order(levels)[-1], False)
+    step((1,), (0,), False, False)
+    for b in hops[:-1]:
+        step((0, 1), (b,), False, False)
+    step(early[2:], (0, *hops[:-1]), False, False)
+    step(early, (hops[-1],), True, False)
     for b in far_order(levels) + [0]:
         step((parts - 1,), (b,), b == 0, True)
 

time: 53.9 us -> 53.9 us (level)
  waiting for transfers between devices: 21.2 us -> 20.6 us
    ppermute x17, waiting for transfers between devices: 21.2 us -> 20.6 us  [swap(): lax.ppermute(value, axis, [(i, i ^ distance) for i in range(lax.axis_size...]
    pallas_call x19 -> x20, Pallas kernels: 12.4 us -> 12.5 us  [call(): pl.pallas_call(kernel, out_shape=out_shapes, in_specs=specs, out_specs=[p...]
where the time goes in v7:
time: 53.9 us; the launch traced here: 53.8 us
  waiting for transfers between devices  20.6 us (38%)
  starting transfers between devices  19.8 us (37%)
  Pallas kernels  12.5 us (23%)
  between operations  0.78 us (1%)
    ppermute x17, waiting for transfers between devices, swap(): lax.ppermute(value, axis, [(i, i ^ distance) for i in range(lax.axis_size...  20.6 us
    ppermute x17, starting transfers between devices, swap(): lax.ppermute(value, axis, [(i, i ^ distance) for i in range(lax.axis_size...  19.8 us
    pallas_call x20, Pallas kernels, call(): pl.pallas_call(kernel, out_shape=out_shapes, in_specs=specs, out_specs=[p...  12.5 us
  transfers between devices with their start and end apart: 17, of which 9 were waited for; matrix products, arithmetic and copies ran while one was open for 0% of the time, Pallas kernels for 14%

profile of v7, /device:TPU:0, one launch (start us, length us, event | category | flops | bytes accessed | tf_op | source)
XLA Modules:
  0.0 53.8 jit_solution(16184939813991389345)
XLA Ops:
  0.6 1.5 %shard_map.85 = (bf16[64,4096]{1,0:T(8,128)(2,1)S(1)}, bf16[64,4096]{1,0:T(8,128)(2,1)S(1)}, bf16[64,4096]{1,0:T(8,128)(2,1)S(1)}, bf16[128,128]{1,0:T(8,128)(2,...) custom-call(s32[1]{0:T(128)} %bitcast.place, ...), custom_call_target="tpu_custom_call" | custom-call | tf_op jit(solution)/shard_map/pallas_call | solution.py:54
  2.5 0.5 collective-permute-start
  3.3 2.5 %collective-permute-start.1 = (bf16[1056,128]{1,0:T(8,128)(2,1)S(1)}, bf16[1056,128]{1,0:T(8,128)(2,1)S(1)}, u32[]{:S(2)}, u32[]{:S(2)}) collective-permute-start(bf16[1056,128]{1,0:T(8,128)(2,1)S(1)} %shard_map.88), channel_id=1, source_target_pairs={{0,2},{1,3},{2,0},{3,1},{4,6},{5,7},{6,4},{7,5},{8,10},{9,11},{10,... | collective-permute-start | bytes 811016 | tf_op jit(solution)/shard_map/ppermute | solution.py:243
  6.5 1.9 %collective-permute-start.3 = (bf16[128,128]{1,0:T(8,128)(2,1)S(1)}, bf16[128,128]{1,0:T(8,128)(2,1)S(1)}, u32[]{:S(2)}, u32[]{:S(2)}) collective-permute-start(bf16[128,128]{1,0:T(8,128)(2,1)S(1)} %get-tuple-element.47), channel_id=1, source_target_pairs={{0,2},{1,3},{2,0},{3,1},{4,6},{5,7},{6,4},{7,5},{8,10},{9,11},{10,... | collective-permute-start | bytes 98312 | tf_op jit(solution)/shard_map/ppermute | solution.py:243
  8.4 0.8 %collective-permute-start.4 = (bf16[128,128]{1,0:T(8,128)(2,1)S(1)}, bf16[128,128]{1,0:T(8,128)(2,1)S(1)}, u32[]{:S(2)}, u32[]{:S(2)}) collective-permute-start(bf16[128,128]{1,0:T(8,128)(2,1)S(1)} %get-tuple-element.48), channel_id=1, source_target_pairs={{0,3},{1,2},{2,1},{3,0},{4,7},{5,6},{6,5},{7,4},{8,11},{9,10},{10,... | collective-permute-start | bytes 98312 | tf_op jit(solution)/shard_map/ppermute | solution.py:243
  9.2 10.5 %collective-permute-done.3.refs_2_ = bf16[128,128]{1,0:T(8,128)(2,1)S(1)} collective-permute-done((bf16[128,128]{1,0:T(8,128)(2,1)S(1)}, bf16[128,128]{1,0:T(8,128)(2,1)S(1)}, u32[]{:S(2)}, u32[]{:S(2)}) %collective-permute-start.3) | collective-permute-done | bytes 32800 | tf_op jit(solution)/shard_map/ppermute | solution.py:243
  20.0 1.7 %collective-permute-start.7 = (bf16[512,128]{1,0:T(8,128)(2,1)S(1)}, bf16[512,128]{1,0:T(8,128)(2,1)S(1)}, u32[]{:S(2)}, u32[]{:S(2)}) collective-permute-start(bf16[512,128]{1,0:T(8,128)(2,1)S(1)} %shard_map.89.refs_2_), channel_id=1, source_target_pairs={{0,8},{4,12},{8,0},{12,4},{16,24},{20,28},{24,16},{28,20},{1,9},{5... | collective-permute-start | bytes 393224 | tf_op jit(solution)/shard_map/ppermute | solution.py:243
  21.8 1.5 %collective-permute-start.6 = (bf16[512,128]{1,0:T(8,128)(2,1)S(1)}, bf16[512,128]{1,0:T(8,128)(2,1)S(1)}, u32[]{:S(2)}, u32[]{:S(2)}) collective-permute-start(bf16[512,128]{1,0:T(8,128)(2,1)S(1)} %shard_map.89.refs_2_), channel_id=1, source_target_pairs={{0,4},{4,0},{8,12},{12,8},{16,20},{20,16},{24,28},{28,24},{1,5},{5... | collective-permute-start | bytes 393224 | tf_op jit(solution)/shard_map/ppermute | solution.py:243
  23.3 2.6 %collective-permute-start.5 = (bf16[512,128]{1,0:T(8,128)(2,1)S(1)}, bf16[512,128]{1,0:T(8,128)(2,1)S(1)}, u32[]{:S(2)}, u32[]{:S(2)}) collective-permute-start(bf16[512,128]{1,0:T(8,128)(2,1)S(1)} %shard_map.89.refs_2_), channel_id=1, source_target_pairs={{0,16},{4,20},{8,24},{12,28},{16,0},{20,4},{24,8},{28,12},{1,17},{... | collective-permute-start | bytes 393224 | tf_op jit(solution)/shard_map/ppermute | solution.py:243
  26.2 0.5 shard_map.90
  26.7 0.5 shard_map.91
  27.2 0.9 %shard_map.92 = (f32[128,512]{1,0:T(8,128)S(1)}, f32[128,512]{1,0:T(8,128)S(1)}, f32[512,128]{1,0:T(8,128)S(1)}) custom-call(s32[1]{0:T(128)} %bitcast.place, bf16[1056,128]{1,0:T(8,128)(2,1)S(1)} %shard_map.86.refs_0_, bf16[1056,128]{1,0:T(8,128)(2,1)S(1)} %collective-permute-done.refs_0_.refs_1_, f32[32,128]{1,0:T(8,128)S(1)} %get-tuple-element.44.refs_1_.refs_2_.refs_3_, ...), custom_call_target="tpu_custom_call" | custom-call | tf_op jit(solution)/shard_map/pallas_call | solution.py:54
  28.1 0.9 %shard_map.93 = (f32[128,512]{1,0:T(8,128)S(1)}, f32[128,512]{1,0:T(8,128)S(1)}, f32[512,128]{1,0:T(8,128)S(1)}) custom-call(s32[1]{0:T(128)} %bitcast.place, bf16[1056,128]{1,0:T(8,128)(2,1)S(1)} %shard_map.86.refs_0_, bf16[1056,128]{1,0:T(8,128)(2,1)S(1)} %collective-permute-done.refs_0_.refs_1_, f32[32,128]{1,0:T(8,128)S(1)} %get-tuple-element.44.refs_1_.refs_2_.refs_3_, ...), custom_call_target="tpu_custom_call" | custom-call | tf_op jit(solution)/shard_map/pallas_call | solution.py:54
  29.1 1.1 %shard_map.94 = (f32[128,512]{1,0:T(8,128)S(1)}, f32[512,128]{1,0:T(8,128)S(1)}, f32[512,128]{1,0:T(8,128)S(1)}, f32[512,128]{1,0:T(8,128)S(1)}) custom-call(s32[1]{0:T(128)} %bitcast.place, bf16[1056,128]{1,0:T(8,128)(2,1)S(1)} %collective-permute-done.1.refs_0_.refs_2_, f32[32,128]{1,0:T(8,128)S(1)} %get-tuple-element.44.refs_1_.refs_2_.refs_3_, ...), custom_call_target="tpu_custom_call" | custom-call | tf_op jit(solution)/shard_map/pallas_call | solution.py:54
  30.2 0.5 shard_map.98
  30.6 1.4 %collective-permute-done.5.refs_4_.refs_2_ = bf16[512,128]{1,0:T(8,128)(2,1)S(1)} collective-permute-done((bf16[512,128]{1,0:T(8,128)(2,1)S(1)}, bf16[512,128]{1,0:T(8,128)(2,1)S(1)}, u32[]{:S(2)}, u32[]{:S(2)}) %collective-permute-start.5) | collective-permute-done | bytes 131104 | tf_op jit(solution)/shard_map/ppermute | solution.py:243
  32.0 1.3 %shard_map.95 = (f32[512,128]{1,0:T(8,128)S(1)}, bf16[512,128]{1,0:T(8,128)(2,1)S(1)}, bf16[512,128]{1,0:T(8,128)(2,1)S(1)}, f32[512,128]{1,0:T(8,128)S(1)}) custom-call(s32[1]{0:T(128)} %bitcast.place, bf16[1056,128]{1,0:T(8,128)(2,1)S(1)} %shard_map.86.refs_0_, bf16[1056,128]{1,0:T(8,128)(2,1)S(1)} %collective-permute-done.refs_0_.refs_1_, ...), custom_call_target="tpu_custom_call" | custom-call | tf_op jit(solution)/shard_map/pallas_call | solution.py:54
  33.4 0.5 shard_map.99
  33.8 0.5 shard_map.100
  34.3 0.7 %collective-permute-start.11 = (bf16[512,128]{1,0:T(8,128)(2,1)S(1)}, bf16[512,128]{1,0:T(8,128)(2,1)S(1)}, u32[]{:S(2)}, u32[]{:S(2)}) collective-permute-start(bf16[512,128]{1,0:T(8,128)(2,1)S(1)} %get-tuple-element.71), channel_id=1, source_target_pairs={{0,4},{4,0},{8,12},{12,8},{16,20},{20,16},{24,28},{28,24},{1,5},{5... | collective-permute-start | bytes 393224 | tf_op jit(solution)/shard_map/ppermute | solution.py:243
  35.0 1.5 %collective-permute-start.13 = (bf16[512,128]{1,0:T(8,128)(2,1)S(1)}, bf16[512,128]{1,0:T(8,128)(2,1)S(1)}, u32[]{:S(2)}, u32[]{:S(2)}) collective-permute-start(bf16[512,128]{1,0:T(8,128)(2,1)S(1)} %get-tuple-element.73), channel_id=1, source_target_pairs={{0,16},{4,20},{8,24},{12,28},{16,0},{20,4},{24,8},{28,12},{1,17},{... | collective-permute-start | bytes 393224 | tf_op jit(solution)/shard_map/ppermute | solution.py:243
  36.5 2.1 %collective-permute-start.12 = (bf16[512,128]{1,0:T(8,128)(2,1)S(1)}, bf16[512,128]{1,0:T(8,128)(2,1)S(1)}, u32[]{:S(2)}, u32[]{:S(2)}) collective-permute-start(bf16[512,128]{1,0:T(8,128)(2,1)S(1)} %get-tuple-element.72), channel_id=1, source_target_pairs={{0,8},{4,12},{8,0},{12,4},{16,24},{20,28},{24,16},{28,20},{1,9},{5... | collective-permute-start | bytes 393224 | tf_op jit(solution)/shard_map/ppermute | solution.py:243
  38.6 0.6 %shard_map.101 = (bf16[512,128]{1,0:T(8,128)(2,1)S(1)}, f32[512,128]{1,0:T(8,128)S(1)}) custom-call(s32[1]{0:T(128)} %bitcast.place, bf16[1056,128]{1,0:T(8,128)(2,1)S(1)} %collective-permute-done.9.refs_0_, f32[32,128]{1,0:T(8,128)S(1)} %get-tuple-element.44.refs_1_.refs_2_.refs_3_, bf16[512,128]{1,0:T(8,128)(2,1)S(1)} %shard_map.89.refs_2_, ...), custom_call_target="tpu_custom_call" | custom-call | tf_op jit(solution)/shard_map/pallas_call | solution.py:54
  39.3 3.4 %collective-permute-done.13.refs_3_ = bf16[512,128]{1,0:T(8,128)(2,1)S(1)} collective-permute-done((bf16[512,128]{1,0:T(8,128)(2,1)S(1)}, bf16[512,128]{1,0:T(8,128)(2,1)S(1)}, u32[]{:S(2)}, u32[]{:S(2)}) %collective-permute-start.13) | collective-permute-done | bytes 131104 | tf_op jit(solution)/shard_map/ppermute | solution.py:243
  43.1 1.6 %collective-permute-start.8 = (bf16[512,128]{1,0:T(8,128)(2,1)S(1)}, bf16[512,128]{1,0:T(8,128)(2,1)S(1)}, u32[]{:S(2)}, u32[]{:S(2)}) collective-permute-start(bf16[512,128]{1,0:T(8,128)(2,1)S(1)} %get-tuple-element.61), channel_id=1, source_target_pairs={{0,2},{1,3},{2,0},{3,1},{4,6},{5,7},{6,4},{7,5},{8,10},{9,11},{10,... | collective-permute-start | bytes 393224 | tf_op jit(solution)/shard_map/ppermute | solution.py:243
  45.0 1.5 %collective-permute-start.15 = (bf16[128,128]{1,0:T(8,128)(2,1)S(1)}, bf16[128,128]{1,0:T(8,128)(2,1)S(1)}, u32[]{:S(2)}, u32[]{:S(2)}) collective-permute-start(bf16[128,128]{1,0:T(8,128)(2,1)S(1)} %get-tuple-element.77), channel_id=1, source_target_pairs={{0,2},{1,3},{2,0},{3,1},{4,6},{5,7},{6,4},{7,5},{8,10},{9,11},{10,... | collective-permute-start | bytes 98312 | tf_op jit(solution)/shard_map/ppermute | solution.py:243
  46.7 2.9 %collective-permute-done.8.refs_1_ = bf16[512,128]{1,0:T(8,128)(2,1)S(1)} collective-permute-done((bf16[512,128]{1,0:T(8,128)(2,1)S(1)}, bf16[512,128]{1,0:T(8,128)(2,1)S(1)}, u32[]{:S(2)}, u32[]{:S(2)}) %collective-permute-start.8) | collective-permute-done | bytes 131104 | tf_op jit(solution)/shard_map/ppermute | solution.py:243
  49.6 0.8 %shard_map.96.filled = f32[64,4096]{1,0:T(8,128)} custom-call(s32[1]{0:T(128)} %bitcast.place, f32[512,128]{1,0:T(8,128)S(1)} %get-tuple-element.60.refs_0_, bf16[512,128]{1,0:T(8,128)(2,1)S(1)} %collective-permute-done.8.refs_1_), custom_call_target="tpu_custom_call" | custom-call | tf_op jit(solution)/shard_map/pallas_call | solution.py:54
  50.4 1.0 %collective-permute-done.10.refs_0_ = bf16[512,128]{1,0:T(8,128)(2,1)S(1)} collective-permute-done((bf16[512,128]{1,0:T(8,128)(2,1)S(1)}, bf16[512,128]{1,0:T(8,128)(2,1)S(1)}, u32[]{:S(2)}, u32[]{:S(2)}) %collective-permute-start.10) | collective-permute-done | bytes 131104 | tf_op jit(solution)/shard_map/ppermute | solution.py:243
  51.4 0.7 %shard_map.102.filled = f32[64,4096]{1,0:T(8,128)} custom-call(s32[1]{0:T(128)} %bitcast.place, f32[64,4096]{1,0:T(8,128)} %shard_map.96.filled, bf16[512,128]{1,0:T(8,128)(2,1)S(1)} %collective-permute-done.10.refs_0_), custom_call_target="tpu_custom_call", output_to_operand_aliasing={{}: (1, {})} | custom-call | tf_op jit(solution)/shard_map/pallas_call | solution.py:54
  52.1 0.8 %collective-permute-done.15.refs_2_ = bf16[128,128]{1,0:T(8,128)(2,1)S(1)} collective-permute-done((bf16[128,128]{1,0:T(8,128)(2,1)S(1)}, bf16[128,128]{1,0:T(8,128)(2,1)S(1)}, u32[]{:S(2)}, u32[]{:S(2)}) %collective-permute-start.15) | collective-permute-done | bytes 32800 | tf_op jit(solution)/shard_map/ppermute | solution.py:243
  52.9 0.9 %shard_map.104 = (f32[64,4096]{1,0:T(8,128)}, f32[64,512]{1,0:T(8,128)}, f32[64,512]{1,0:T(8,128)}) custom-call(s32[1]{0:T(128)} %bitcast.place, f32[64,4096]{1,0:T(8,128)} %shard_map.102.filled, f32[128,128]{1,0:T(8,128)S(1)} %get-tuple-element.75.refs_0_, bf16[640,128]{1,0:T(8,128)(2,1)S(1)} %collective-permute-done.14.refs_1_, ...), custom_call_target="tpu_custom_call", output_to_operand_aliasing={{0}: (1, {})} | custom-call | tf_op jit(solution)/shard_map/pallas_call | solution.py:54
  (22 shorter events, 3.1 us)
Async XLA Ops:
  2.5 20.8 %collective-permute-start = (bf16[1056,128]{1,0:T(8,128)(2,1)S(1)}, bf16[1056,128]{1,0:T(8,128)(2,1)S(1)}, u32[]{:S(2)}, u32[]{:S(2)}) collective-permute-start(bf16[1056,128]{1,0:T(8,128)(2,1)S(1)} %shard_map.87), channel_id=1, source_target_pairs={{0,1},{1,0},{2,3},{3,2},{4,5},{5,4},{6,7},{7,6},{8,9},{9,8},{10,11... | collective-permute-start | bytes 811016 | tf_op jit(solution)/shard_map/ppermute | solution.py:243
  3.3 25.7 %collective-permute-start.1 = (bf16[1056,128]{1,0:T(8,128)(2,1)S(1)}, bf16[1056,128]{1,0:T(8,128)(2,1)S(1)}, u32[]{:S(2)}, u32[]{:S(2)}) collective-permute-start(bf16[1056,128]{1,0:T(8,128)(2,1)S(1)} %shard_map.88), channel_id=1, source_target_pairs={{0,2},{1,3},{2,0},{3,1},{4,6},{5,7},{6,4},{7,5},{8,10},{9,11},{10,... | collective-permute-start | bytes 811016 | tf_op jit(solution)/shard_map/ppermute | solution.py:243
  6.2 24.0 %collective-permute-start.9 = (bf16[1056,128]{1,0:T(8,128)(2,1)S(1)}, bf16[1056,128]{1,0:T(8,128)(2,1)S(1)}, u32[]{:S(2)}, u32[]{:S(2)}) collective-permute-start(bf16[1056,128]{1,0:T(8,128)(2,1)S(1)} %shard_map.97), channel_id=1, source_target_pairs={{0,3},{1,2},{2,1},{3,0},{4,7},{5,6},{6,5},{7,4},{8,11},{9,10},{10,... | collective-permute-start | bytes 811016 | tf_op jit(solution)/shard_map/ppermute | solution.py:243
  6.4 2.0 %collective-permute-start.2 = (bf16[128,128]{1,0:T(8,128)(2,1)S(1)}, bf16[128,128]{1,0:T(8,128)(2,1)S(1)}, u32[]{:S(2)}, u32[]{:S(2)}) collective-permute-start(bf16[128,128]{1,0:T(8,128)(2,1)S(1)} %get-tuple-element.46), channel_id=1, source_target_pairs={{0,1},{1,0},{2,3},{3,2},{4,5},{5,4},{6,7},{7,6},{8,9},{9,8},{10,11... | collective-permute-start | bytes 98312 | tf_op jit(solution)/shard_map/ppermute | solution.py:243
  6.5 13.2 %collective-permute-start.3 = (bf16[128,128]{1,0:T(8,128)(2,1)S(1)}, bf16[128,128]{1,0:T(8,128)(2,1)S(1)}, u32[]{:S(2)}, u32[]{:S(2)}) collective-permute-start(bf16[128,128]{1,0:T(8,128)(2,1)S(1)} %get-tuple-element.47), channel_id=1, source_target_pairs={{0,2},{1,3},{2,0},{3,1},{4,6},{5,7},{6,4},{7,5},{8,10},{9,11},{10,... | collective-permute-start | bytes 98312 | tf_op jit(solution)/shard_map/ppermute | solution.py:243
  8.4 11.6 %collective-permute-start.4 = (bf16[128,128]{1,0:T(8,128)(2,1)S(1)}, bf16[128,128]{1,0:T(8,128)(2,1)S(1)}, u32[]{:S(2)}, u32[]{:S(2)}) collective-permute-start(bf16[128,128]{1,0:T(8,128)(2,1)S(1)} %get-tuple-element.48), channel_id=1, source_target_pairs={{0,3},{1,2},{2,1},{3,0},{4,7},{5,6},{6,5},{7,4},{8,11},{9,10},{10,... | collective-permute-start | bytes 98312 | tf_op jit(solution)/shard_map/ppermute | solution.py:243
  20.0 7.1 %collective-permute-start.7 = (bf16[512,128]{1,0:T(8,128)(2,1)S(1)}, bf16[512,128]{1,0:T(8,128)(2,1)S(1)}, u32[]{:S(2)}, u32[]{:S(2)}) collective-permute-start(bf16[512,128]{1,0:T(8,128)(2,1)S(1)} %shard_map.89.refs_2_), channel_id=1, source_target_pairs={{0,8},{4,12},{8,0},{12,4},{16,24},{20,28},{24,16},{28,20},{1,9},{5... | collective-permute-start | bytes 393224 | tf_op jit(solution)/shard_map/ppermute | solution.py:243
  21.8 6.3 %collective-permute-start.6 = (bf16[512,128]{1,0:T(8,128)(2,1)S(1)}, bf16[512,128]{1,0:T(8,128)(2,1)S(1)}, u32[]{:S(2)}, u32[]{:S(2)}) collective-permute-start(bf16[512,128]{1,0:T(8,128)(2,1)S(1)} %shard_map.89.refs_2_), channel_id=1, source_target_pairs={{0,4},{4,0},{8,12},{12,8},{16,20},{20,16},{24,28},{28,24},{1,5},{5... | collective-permute-start | bytes 393224 | tf_op jit(solution)/shard_map/ppermute | solution.py:243
  23.3 8.7 %collective-permute-start.5 = (bf16[512,128]{1,0:T(8,128)(2,1)S(1)}, bf16[512,128]{1,0:T(8,128)(2,1)S(1)}, u32[]{:S(2)}, u32[]{:S(2)}) collective-permute-start(bf16[512,128]{1,0:T(8,128)(2,1)S(1)} %shard_map.89.refs_2_), channel_id=1, source_target_pairs={{0,16},{4,20},{8,24},{12,28},{16,0},{20,4},{24,8},{28,12},{1,17},{... | collective-permute-start | bytes 393224 | tf_op jit(solution)/shard_map/ppermute | solution.py:243
  34.3 5.0 %collective-permute-start.11 = (bf16[512,128]{1,0:T(8,128)(2,1)S(1)}, bf16[512,128]{1,0:T(8,128)(2,1)S(1)}, u32[]{:S(2)}, u32[]{:S(2)}) collective-permute-start(bf16[512,128]{1,0:T(8,128)(2,1)S(1)} %get-tuple-element.71), channel_id=1, source_target_pairs={{0,4},{4,0},{8,12},{12,8},{16,20},{20,16},{24,28},{28,24},{1,5},{5... | collective-permute-start | bytes 393224 | tf_op jit(solution)/shard_map/ppermute | solution.py:243
  35.0 7.7 %collective-permute-start.13 = (bf16[512,128]{1,0:T(8,128)(2,1)S(1)}, bf16[512,128]{1,0:T(8,128)(2,1)S(1)}, u32[]{:S(2)}, u32[]{:S(2)}) collective-permute-start(bf16[512,128]{1,0:T(8,128)(2,1)S(1)} %get-tuple-element.73), channel_id=1, source_target_pairs={{0,16},{4,20},{8,24},{12,28},{16,0},{20,4},{24,8},{28,12},{1,17},{... | collective-permute-start | bytes 393224 | tf_op jit(solution)/shard_map/ppermute | solution.py:243
  36.5 6.5 %collective-permute-start.12 = (bf16[512,128]{1,0:T(8,128)(2,1)S(1)}, bf16[512,128]{1,0:T(8,128)(2,1)S(1)}, u32[]{:S(2)}, u32[]{:S(2)}) collective-permute-start(bf16[512,128]{1,0:T(8,128)(2,1)S(1)} %get-tuple-element.72), channel_id=1, source_target_pairs={{0,8},{4,12},{8,0},{12,4},{16,24},{20,28},{24,16},{28,20},{1,9},{5... | collective-permute-start | bytes 393224 | tf_op jit(solution)/shard_map/ppermute | solution.py:243
  43.1 9.8 %collective-permute-start.14 = (bf16[640,128]{1,0:T(8,128)(2,1)S(1)}, bf16[640,128]{1,0:T(8,128)(2,1)S(1)}, u32[]{:S(2)}, u32[]{:S(2)}) collective-permute-start(bf16[640,128]{1,0:T(8,128)(2,1)S(1)} %get-tuple-element.76), channel_id=1, source_target_pairs={{0,1},{1,0},{2,3},{3,2},{4,5},{5,4},{6,7},{7,6},{8,9},{9,8},{10,11... | collective-permute-start | bytes 491528 | tf_op jit(solution)/shard_map/ppermute | solution.py:243
  43.1 6.4 %collective-permute-start.8 = (bf16[512,128]{1,0:T(8,128)(2,1)S(1)}, bf16[512,128]{1,0:T(8,128)(2,1)S(1)}, u32[]{:S(2)}, u32[]{:S(2)}) collective-permute-start(bf16[512,128]{1,0:T(8,128)(2,1)S(1)} %get-tuple-element.61), channel_id=1, source_target_pairs={{0,2},{1,3},{2,0},{3,1},{4,6},{5,7},{6,4},{7,5},{8,10},{9,11},{10,... | collective-permute-start | bytes 393224 | tf_op jit(solution)/shard_map/ppermute | solution.py:243
  44.7 6.7 %collective-permute-start.10 = (bf16[512,128]{1,0:T(8,128)(2,1)S(1)}, bf16[512,128]{1,0:T(8,128)(2,1)S(1)}, u32[]{:S(2)}, u32[]{:S(2)}) collective-permute-start(bf16[512,128]{1,0:T(8,128)(2,1)S(1)} %get-tuple-element.69), channel_id=1, source_target_pairs={{0,3},{1,2},{2,1},{3,0},{4,7},{5,6},{6,5},{7,4},{8,11},{9,10},{10,... | collective-permute-start | bytes 393224 | tf_op jit(solution)/shard_map/ppermute | solution.py:243
  45.0 7.9 %collective-permute-start.15 = (bf16[128,128]{1,0:T(8,128)(2,1)S(1)}, bf16[128,128]{1,0:T(8,128)(2,1)S(1)}, u32[]{:S(2)}, u32[]{:S(2)}) collective-permute-start(bf16[128,128]{1,0:T(8,128)(2,1)S(1)} %get-tuple-element.77), channel_id=1, source_target_pairs={{0,2},{1,3},{2,0},{3,1},{4,6},{5,7},{6,4},{7,5},{8,10},{9,11},{10,... | collective-permute-start | bytes 98312 | tf_op jit(solution)/shard_map/ppermute | solution.py:243
  46.5 6.4 %collective-permute-start.16 = (bf16[128,128]{1,0:T(8,128)(2,1)S(1)}, bf16[128,128]{1,0:T(8,128)(2,1)S(1)}, u32[]{:S(2)}, u32[]{:S(2)}) collective-permute-start(bf16[128,128]{1,0:T(8,128)(2,1)S(1)} %get-tuple-element.78), channel_id=1, source_target_pairs={{0,3},{1,2},{2,1},{3,0},{4,7},{5,6},{6,5},{7,4},{8,11},{9,10},{10,... | collective-permute-start | bytes 98312 | tf_op jit(solution)/shard_map/ppermute | solution.py:243

commit v8 on v7

--- a/solution.py
+++ b/solution.py
@@ -357,23 +357,23 @@
     def stage(count):
         return vmem((count, rows, width), F32)
 
-    early = (0,) + tuple(range(2, parts - 1))
     (grad_q,) = call(
-        functools.partial(first_kernel, early),
+        functools.partial(first_kernel, (0,)),
         [hbm(queries.shape, F32)],
         place,
-        *[dq[m] for m in early],
+        dq[0],
         out_space=pltpu.HBM,
-        scratch=[stage(len(early)), pltpu.SemaphoreType.DMA((len(early),))],
-    )
+        scratch=[stage(1), pltpu.SemaphoreType.DMA((1,))],
+    )
+    late = tuple(range(2, parts))
     (grad_q,) = call(
-        functools.partial(more_kernel, (parts - 1,)),
+        functools.partial(more_kernel, late),
         [hbm(queries.shape, F32)],
         place,
-        dq[parts - 1],
+        *[dq[m] for m in late],
         out_space=pltpu.HBM,
         filled=grad_q,
-        scratch=[stage(1), pltpu.SemaphoreType.DMA((1,))],
+        scratch=[stage(len(late)), pltpu.SemaphoreType.DMA((len(late),))],
     )
     grad_q, grad_k, grad_v = call(
         functools.partial(finish_kernel, parts),

time: 53.9 us -> 54.3 us (level)
  transfers between devices with their start and end apart: 17 -> 17, of which waited for: 9 -> 8; matrix products, arithmetic and copies ran while one was open for 0% -> 0% of each run, Pallas kernels for 14% -> 14%
where the time goes in v8:
time: 54.3 us; the launch traced here: 54.1 us
  waiting for transfers between devices  20.9 us (38%)
  starting transfers between devices  19.9 us (37%)
  Pallas kernels  12.6 us (23%)
  between operations  0.8 us (1%)
    ppermute x17, waiting for transfers between devices, swap(): lax.ppermute(value, axis, [(i, i ^ distance) for i in range(lax.axis_size...  20.9 us
    ppermute x17, starting transfers between devices, swap(): lax.ppermute(value, axis, [(i, i ^ distance) for i in range(lax.axis_size...  19.9 us
    pallas_call x20, Pallas kernels, call(): pl.pallas_call(kernel, out_shape=out_shapes, in_specs=specs, out_specs=[p...  12.6 us
  transfers between devices with their start and end apart: 17, of which 8 were waited for; matrix products, arithmetic and copies ran while one was open for 0% of the time, Pallas kernels for 14%

profile of v8, /device:TPU:0, one launch (start us, length us, event | category | flops | bytes accessed | tf_op | source)
XLA Modules:
  0.0 54.1 jit_solution(10106146125362350918)
XLA Ops:
  0.6 1.5 %shard_map.85 = (bf16[64,4096]{1,0:T(8,128)(2,1)S(1)}, bf16[64,4096]{1,0:T(8,128)(2,1)S(1)}, bf16[64,4096]{1,0:T(8,128)(2,1)S(1)}, bf16[128,128]{1,0:T(8,128)(2,...) custom-call(s32[1]{0:T(128)} %bitcast.place, ...), custom_call_target="tpu_custom_call" | custom-call | tf_op jit(solution)/shard_map/pallas_call | solution.py:54
  2.5 0.5 collective-permute-start
  3.3 2.5 %collective-permute-start.1 = (bf16[1056,128]{1,0:T(8,128)(2,1)S(1)}, bf16[1056,128]{1,0:T(8,128)(2,1)S(1)}, u32[]{:S(2)}, u32[]{:S(2)}) collective-permute-start(bf16[1056,128]{1,0:T(8,128)(2,1)S(1)} %shard_map.88), channel_id=1, source_target_pairs={{0,2},{1,3},{2,0},{3,1},{4,6},{5,7},{6,4},{7,5},{8,10},{9,11},{10,... | collective-permute-start | bytes 811016 | tf_op jit(solution)/shard_map/ppermute | solution.py:243
  6.5 1.9 %collective-permute-start.3 = (bf16[128,128]{1,0:T(8,128)(2,1)S(1)}, bf16[128,128]{1,0:T(8,128)(2,1)S(1)}, u32[]{:S(2)}, u32[]{:S(2)}) collective-permute-start(bf16[128,128]{1,0:T(8,128)(2,1)S(1)} %get-tuple-element.47), channel_id=1, source_target_pairs={{0,2},{1,3},{2,0},{3,1},{4,6},{5,7},{6,4},{7,5},{8,10},{9,11},{10,... | collective-permute-start | bytes 98312 | tf_op jit(solution)/shard_map/ppermute | solution.py:243
  8.4 0.8 %collective-permute-start.4 = (bf16[128,128]{1,0:T(8,128)(2,1)S(1)}, bf16[128,128]{1,0:T(8,128)(2,1)S(1)}, u32[]{:S(2)}, u32[]{:S(2)}) collective-permute-start(bf16[128,128]{1,0:T(8,128)(2,1)S(1)} %get-tuple-element.48), channel_id=1, source_target_pairs={{0,3},{1,2},{2,1},{3,0},{4,7},{5,6},{6,5},{7,4},{8,11},{9,10},{10,... | collective-permute-start | bytes 98312 | tf_op jit(solution)/shard_map/ppermute | solution.py:243
  9.2 10.5 %collective-permute-done.3.refs_2_ = bf16[128,128]{1,0:T(8,128)(2,1)S(1)} collective-permute-done((bf16[128,128]{1,0:T(8,128)(2,1)S(1)}, bf16[128,128]{1,0:T(8,128)(2,1)S(1)}, u32[]{:S(2)}, u32[]{:S(2)}) %collective-permute-start.3) | collective-permute-done | bytes 32800 | tf_op jit(solution)/shard_map/ppermute | solution.py:243
  20.0 1.7 %collective-permute-start.7 = (bf16[512,128]{1,0:T(8,128)(2,1)S(1)}, bf16[512,128]{1,0:T(8,128)(2,1)S(1)}, u32[]{:S(2)}, u32[]{:S(2)}) collective-permute-start(bf16[512,128]{1,0:T(8,128)(2,1)S(1)} %shard_map.89.refs_2_), channel_id=1, source_target_pairs={{0,8},{4,12},{8,0},{12,4},{16,24},{20,28},{24,16},{28,20},{1,9},{5... | collective-permute-start | bytes 393224 | tf_op jit(solution)/shard_map/ppermute | solution.py:243
  21.8 1.5 %collective-permute-start.6 = (bf16[512,128]{1,0:T(8,128)(2,1)S(1)}, bf16[512,128]{1,0:T(8,128)(2,1)S(1)}, u32[]{:S(2)}, u32[]{:S(2)}) collective-permute-start(bf16[512,128]{1,0:T(8,128)(2,1)S(1)} %shard_map.89.refs_2_), channel_id=1, source_target_pairs={{0,4},{4,0},{8,12},{12,8},{16,20},{20,16},{24,28},{28,24},{1,5},{5... | collective-permute-start | bytes 393224 | tf_op jit(solution)/shard_map/ppermute | solution.py:243
  23.3 2.6 %collective-permute-start.5 = (bf16[512,128]{1,0:T(8,128)(2,1)S(1)}, bf16[512,128]{1,0:T(8,128)(2,1)S(1)}, u32[]{:S(2)}, u32[]{:S(2)}) collective-permute-start(bf16[512,128]{1,0:T(8,128)(2,1)S(1)} %shard_map.89.refs_2_), channel_id=1, source_target_pairs={{0,16},{4,20},{8,24},{12,28},{16,0},{20,4},{24,8},{28,12},{1,17},{... | collective-permute-start | bytes 393224 | tf_op jit(solution)/shard_map/ppermute | solution.py:243
  26.2 0.5 shard_map.90
  26.7 0.5 shard_map.91
  27.2 0.9 %shard_map.92 = (f32[128,512]{1,0:T(8,128)S(1)}, f32[128,512]{1,0:T(8,128)S(1)}, f32[512,128]{1,0:T(8,128)S(1)}) custom-call(s32[1]{0:T(128)} %bitcast.place, bf16[1056,128]{1,0:T(8,128)(2,1)S(1)} %shard_map.86.refs_0_, bf16[1056,128]{1,0:T(8,128)(2,1)S(1)} %collective-permute-done.refs_0_.refs_1_, f32[32,128]{1,0:T(8,128)S(1)} %get-tuple-element.44.refs_1_.refs_2_.refs_3_, ...), custom_call_target="tpu_custom_call" | custom-call | tf_op jit(solution)/shard_map/pallas_call | solution.py:54
  28.1 0.9 %shard_map.93 = (f32[128,512]{1,0:T(8,128)S(1)}, f32[128,512]{1,0:T(8,128)S(1)}, f32[512,128]{1,0:T(8,128)S(1)}) custom-call(s32[1]{0:T(128)} %bitcast.place, bf16[1056,128]{1,0:T(8,128)(2,1)S(1)} %shard_map.86.refs_0_, bf16[1056,128]{1,0:T(8,128)(2,1)S(1)} %collective-permute-done.refs_0_.refs_1_, f32[32,128]{1,0:T(8,128)S(1)} %get-tuple-element.44.refs_1_.refs_2_.refs_3_, ...), custom_call_target="tpu_custom_call" | custom-call | tf_op jit(solution)/shard_map/pallas_call | solution.py:54
  29.1 1.1 %shard_map.94 = (f32[128,512]{1,0:T(8,128)S(1)}, f32[512,128]{1,0:T(8,128)S(1)}, f32[512,128]{1,0:T(8,128)S(1)}, f32[512,128]{1,0:T(8,128)S(1)}) custom-call(s32[1]{0:T(128)} %bitcast.place, bf16[1056,128]{1,0:T(8,128)(2,1)S(1)} %collective-permute-done.1.refs_0_.refs_2_, f32[32,128]{1,0:T(8,128)S(1)} %get-tuple-element.44.refs_1_.refs_2_.refs_3_, ...), custom_call_target="tpu_custom_call" | custom-call | tf_op jit(solution)/shard_map/pallas_call | solution.py:54
  30.2 0.5 shard_map.98
  30.6 1.4 %collective-permute-done.5.refs_4_.refs_2_ = bf16[512,128]{1,0:T(8,128)(2,1)S(1)} collective-permute-done((bf16[512,128]{1,0:T(8,128)(2,1)S(1)}, bf16[512,128]{1,0:T(8,128)(2,1)S(1)}, u32[]{:S(2)}, u32[]{:S(2)}) %collective-permute-start.5) | collective-permute-done | bytes 131104 | tf_op jit(solution)/shard_map/ppermute | solution.py:243
  32.0 1.3 %shard_map.95 = (f32[512,128]{1,0:T(8,128)S(1)}, bf16[512,128]{1,0:T(8,128)(2,1)S(1)}, bf16[512,128]{1,0:T(8,128)(2,1)S(1)}, f32[512,128]{1,0:T(8,128)S(1)}) custom-call(s32[1]{0:T(128)} %bitcast.place, bf16[1056,128]{1,0:T(8,128)(2,1)S(1)} %shard_map.86.refs_0_, bf16[1056,128]{1,0:T(8,128)(2,1)S(1)} %collective-permute-done.refs_0_.refs_1_, ...), custom_call_target="tpu_custom_call" | custom-call | tf_op jit(solution)/shard_map/pallas_call | solution.py:54
  33.4 0.5 shard_map.99
  33.8 0.5 shard_map.100
  34.3 0.7 %collective-permute-start.11 = (bf16[512,128]{1,0:T(8,128)(2,1)S(1)}, bf16[512,128]{1,0:T(8,128)(2,1)S(1)}, u32[]{:S(2)}, u32[]{:S(2)}) collective-permute-start(bf16[512,128]{1,0:T(8,128)(2,1)S(1)} %get-tuple-element.71), channel_id=1, source_target_pairs={{0,4},{4,0},{8,12},{12,8},{16,20},{20,16},{24,28},{28,24},{1,5},{5... | collective-permute-start | bytes 393224 | tf_op jit(solution)/shard_map/ppermute | solution.py:243
  35.0 1.5 %collective-permute-start.13 = (bf16[512,128]{1,0:T(8,128)(2,1)S(1)}, bf16[512,128]{1,0:T(8,128)(2,1)S(1)}, u32[]{:S(2)}, u32[]{:S(2)}) collective-permute-start(bf16[512,128]{1,0:T(8,128)(2,1)S(1)} %get-tuple-element.73), channel_id=1, source_target_pairs={{0,16},{4,20},{8,24},{12,28},{16,0},{20,4},{24,8},{28,12},{1,17},{... | collective-permute-start | bytes 393224 | tf_op jit(solution)/shard_map/ppermute | solution.py:243
  36.5 2.1 %collective-permute-start.12 = (bf16[512,128]{1,0:T(8,128)(2,1)S(1)}, bf16[512,128]{1,0:T(8,128)(2,1)S(1)}, u32[]{:S(2)}, u32[]{:S(2)}) collective-permute-start(bf16[512,128]{1,0:T(8,128)(2,1)S(1)} %get-tuple-element.72), channel_id=1, source_target_pairs={{0,8},{4,12},{8,0},{12,4},{16,24},{20,28},{24,16},{28,20},{1,9},{5... | collective-permute-start | bytes 393224 | tf_op jit(solution)/shard_map/ppermute | solution.py:243
  38.6 0.6 %shard_map.101 = (bf16[512,128]{1,0:T(8,128)(2,1)S(1)}, f32[512,128]{1,0:T(8,128)S(1)}) custom-call(s32[1]{0:T(128)} %bitcast.place, bf16[1056,128]{1,0:T(8,128)(2,1)S(1)} %collective-permute-done.9.refs_0_, f32[32,128]{1,0:T(8,128)S(1)} %get-tuple-element.44.refs_1_.refs_2_.refs_3_, bf16[512,128]{1,0:T(8,128)(2,1)S(1)} %shard_map.89.refs_2_, ...), custom_call_target="tpu_custom_call" | custom-call | tf_op jit(solution)/shard_map/pallas_call | solution.py:54
  39.3 3.4 %collective-permute-done.13.refs_3_ = bf16[512,128]{1,0:T(8,128)(2,1)S(1)} collective-permute-done((bf16[512,128]{1,0:T(8,128)(2,1)S(1)}, bf16[512,128]{1,0:T(8,128)(2,1)S(1)}, u32[]{:S(2)}, u32[]{:S(2)}) %collective-permute-start.13) | collective-permute-done | bytes 131104 | tf_op jit(solution)/shard_map/ppermute | solution.py:243
  43.1 1.6 %collective-permute-start.10 = (bf16[512,128]{1,0:T(8,128)(2,1)S(1)}, bf16[512,128]{1,0:T(8,128)(2,1)S(1)}, u32[]{:S(2)}, u32[]{:S(2)}) collective-permute-start(bf16[512,128]{1,0:T(8,128)(2,1)S(1)} %get-tuple-element.69), channel_id=1, source_target_pairs={{0,3},{1,2},{2,1},{3,0},{4,7},{5,6},{6,5},{7,4},{8,11},{9,10},{10,... | collective-permute-start | bytes 393224 | tf_op jit(solution)/shard_map/ppermute | solution.py:243
  44.7 0.5 collective-permute-start.8
  45.3 1.5 %collective-permute-start.15 = (bf16[128,128]{1,0:T(8,128)(2,1)S(1)}, bf16[128,128]{1,0:T(8,128)(2,1)S(1)}, u32[]{:S(2)}, u32[]{:S(2)}) collective-permute-start(bf16[128,128]{1,0:T(8,128)(2,1)S(1)} %get-tuple-element.77), channel_id=1, source_target_pairs={{0,2},{1,3},{2,0},{3,1},{4,6},{5,7},{6,4},{7,5},{8,10},{9,11},{10,... | collective-permute-start | bytes 98312 | tf_op jit(solution)/shard_map/ppermute | solution.py:243
  46.8 0.7 %shard_map.96.filled = f32[64,4096]{1,0:T(8,128)} custom-call(s32[1]{0:T(128)} %bitcast.place, f32[512,128]{1,0:T(8,128)S(1)} %get-tuple-element.60.refs_0_), custom_call_target="tpu_custom_call" | custom-call | tf_op jit(solution)/shard_map/pallas_call | solution.py:54
  47.5 1.1 %collective-permute-done.10.refs_1_ = bf16[512,128]{1,0:T(8,128)(2,1)S(1)} collective-permute-done((bf16[512,128]{1,0:T(8,128)(2,1)S(1)}, bf16[512,128]{1,0:T(8,128)(2,1)S(1)}, u32[]{:S(2)}, u32[]{:S(2)}) %collective-permute-start.10) | collective-permute-done | bytes 131104 | tf_op jit(solution)/shard_map/ppermute | solution.py:243
  48.6 3.8 %collective-permute-done.8.refs_0_ = bf16[512,128]{1,0:T(8,128)(2,1)S(1)} collective-permute-done((bf16[512,128]{1,0:T(8,128)(2,1)S(1)}, bf16[512,128]{1,0:T(8,128)(2,1)S(1)}, u32[]{:S(2)}, u32[]{:S(2)}) %collective-permute-start.8) | collective-permute-done | bytes 131104 | tf_op jit(solution)/shard_map/ppermute | solution.py:243
  52.4 0.8 %shard_map.102.filled = f32[64,4096]{1,0:T(8,128)} custom-call(s32[1]{0:T(128)} %bitcast.place, f32[64,4096]{1,0:T(8,128)} %shard_map.96.filled, bf16[512,128]{1,0:T(8,128)(2,1)S(1)} %collective-permute-done.8.refs_0_, bf16[512,128]{1,0:T(8,128)(2,1)S(1)} %collective-permute-done.10.refs_1_), custom_call_target="tpu_custom_call", output_to_operand_aliasing={{}: (1, {})} | custom-call | tf_op jit(solution)/shard_map/pallas_call | solution.py:54
  53.3 0.9 %shard_map.104 = (f32[64,4096]{1,0:T(8,128)}, f32[64,512]{1,0:T(8,128)}, f32[64,512]{1,0:T(8,128)}) custom-call(s32[1]{0:T(128)} %bitcast.place, f32[64,4096]{1,0:T(8,128)} %shard_map.102.filled, f32[128,128]{1,0:T(8,128)S(1)} %get-tuple-element.75.refs_0_, bf16[640,128]{1,0:T(8,128)(2,1)S(1)} %collective-permute-done.14.refs_1_, ...), custom_call_target="tpu_custom_call", output_to_operand_aliasing={{0}: (1, {})} | custom-call | tf_op jit(solution)/shard_map/pallas_call | solution.py:54
  (22 shorter events, 2.5 us)
Async XLA Ops:
  2.5 20.8 %collective-permute-start = (bf16[1056,128]{1,0:T(8,128)(2,1)S(1)}, bf16[1056,128]{1,0:T(8,128)(2,1)S(1)}, u32[]{:S(2)}, u32[]{:S(2)}) collective-permute-start(bf16[1056,128]{1,0:T(8,128)(2,1)S(1)} %shard_map.87), channel_id=1, source_target_pairs={{0,1},{1,0},{2,3},{3,2},{4,5},{5,4},{6,7},{7,6},{8,9},{9,8},{10,11... | collective-permute-start | bytes 811016 | tf_op jit(solution)/shard_map/ppermute | solution.py:243
  3.3 25.7 %collective-permute-start.1 = (bf16[1056,128]{1,0:T(8,128)(2,1)S(1)}, bf16[1056,128]{1,0:T(8,128)(2,1)S(1)}, u32[]{:S(2)}, u32[]{:S(2)}) collective-permute-start(bf16[1056,128]{1,0:T(8,128)(2,1)S(1)} %shard_map.88), channel_id=1, source_target_pairs={{0,2},{1,3},{2,0},{3,1},{4,6},{5,7},{6,4},{7,5},{8,10},{9,11},{10,... | collective-permute-start | bytes 811016 | tf_op jit(solution)/shard_map/ppermute | solution.py:243
  6.2 24.0 %collective-permute-start.9 = (bf16[1056,128]{1,0:T(8,128)(2,1)S(1)}, bf16[1056,128]{1,0:T(8,128)(2,1)S(1)}, u32[]{:S(2)}, u32[]{:S(2)}) collective-permute-start(bf16[1056,128]{1,0:T(8,128)(2,1)S(1)} %shard_map.97), channel_id=1, source_target_pairs={{0,3},{1,2},{2,1},{3,0},{4,7},{5,6},{6,5},{7,4},{8,11},{9,10},{10,... | collective-permute-start | bytes 811016 | tf_op jit(solution)/shard_map/ppermute | solution.py:243
  6.4 2.0 %collective-permute-start.2 = (bf16[128,128]{1,0:T(8,128)(2,1)S(1)}, bf16[128,128]{1,0:T(8,128)(2,1)S(1)}, u32[]{:S(2)}, u32[]{:S(2)}) collective-permute-start(bf16[128,128]{1,0:T(8,128)(2,1)S(1)} %get-tuple-element.46), channel_id=1, source_target_pairs={{0,1},{1,0},{2,3},{3,2},{4,5},{5,4},{6,7},{7,6},{8,9},{9,8},{10,11... | collective-permute-start | bytes 98312 | tf_op jit(solution)/shard_map/ppermute | solution.py:243
  6.5 13.2 %collective-permute-start.3 = (bf16[128,128]{1,0:T(8,128)(2,1)S(1)}, bf16[128,128]{1,0:T(8,128)(2,1)S(1)}, u32[]{:S(2)}, u32[]{:S(2)}) collective-permute-start(bf16[128,128]{1,0:T(8,128)(2,1)S(1)} %get-tuple-element.47), channel_id=1, source_target_pairs={{0,2},{1,3},{2,0},{3,1},{4,6},{5,7},{6,4},{7,5},{8,10},{9,11},{10,... | collective-permute-start | bytes 98312 | tf_op jit(solution)/shard_map/ppermute | solution.py:243
  8.4 11.6 %collective-permute-start.4 = (bf16[128,128]{1,0:T(8,128)(2,1)S(1)}, bf16[128,128]{1,0:T(8,128)(2,1)S(1)}, u32[]{:S(2)}, u32[]{:S(2)}) collective-permute-start(bf16[128,128]{1,0:T(8,128)(2,1)S(1)} %get-tuple-element.48), channel_id=1, source_target_pairs={{0,3},{1,2},{2,1},{3,0},{4,7},{5,6},{6,5},{7,4},{8,11},{9,10},{10,... | collective-permute-start | bytes 98312 | tf_op jit(solution)/shard_map/ppermute | solution.py:243
  20.0 7.1 %collective-permute-start.7 = (bf16[512,128]{1,0:T(8,128)(2,1)S(1)}, bf16[512,128]{1,0:T(8,128)(2,1)S(1)}, u32[]{:S(2)}, u32[]{:S(2)}) collective-permute-start(bf16[512,128]{1,0:T(8,128)(2,1)S(1)} %shard_map.89.refs_2_), channel_id=1, source_target_pairs={{0,8},{4,12},{8,0},{12,4},{16,24},{20,28},{24,16},{28,20},{1,9},{5... | collective-permute-start | bytes 393224 | tf_op jit(solution)/shard_map/ppermute | solution.py:243
  21.8 6.3 %collective-permute-start.6 = (bf16[512,128]{1,0:T(8,128)(2,1)S(1)}, bf16[512,128]{1,0:T(8,128)(2,1)S(1)}, u32[]{:S(2)}, u32[]{:S(2)}) collective-permute-start(bf16[512,128]{1,0:T(8,128)(2,1)S(1)} %shard_map.89.refs_2_), channel_id=1, source_target_pairs={{0,4},{4,0},{8,12},{12,8},{16,20},{20,16},{24,28},{28,24},{1,5},{5... | collective-permute-start | bytes 393224 | tf_op jit(solution)/shard_map/ppermute | solution.py:243
  23.3 8.7 %collective-permute-start.5 = (bf16[512,128]{1,0:T(8,128)(2,1)S(1)}, bf16[512,128]{1,0:T(8,128)(2,1)S(1)}, u32[]{:S(2)}, u32[]{:S(2)}) collective-permute-start(bf16[512,128]{1,0:T(8,128)(2,1)S(1)} %shard_map.89.refs_2_), channel_id=1, source_target_pairs={{0,16},{4,20},{8,24},{12,28},{16,0},{20,4},{24,8},{28,12},{1,17},{... | collective-permute-start | bytes 393224 | tf_op jit(solution)/shard_map/ppermute | solution.py:243
  34.3 5.0 %collective-permute-start.11 = (bf16[512,128]{1,0:T(8,128)(2,1)S(1)}, bf16[512,128]{1,0:T(8,128)(2,1)S(1)}, u32[]{:S(2)}, u32[]{:S(2)}) collective-permute-start(bf16[512,128]{1,0:T(8,128)(2,1)S(1)} %get-tuple-element.71), channel_id=1, source_target_pairs={{0,4},{4,0},{8,12},{12,8},{16,20},{20,16},{24,28},{28,24},{1,5},{5... | collective-permute-start | bytes 393224 | tf_op jit(solution)/shard_map/ppermute | solution.py:243
  35.0 7.7 %collective-permute-start.13 = (bf16[512,128]{1,0:T(8,128)(2,1)S(1)}, bf16[512,128]{1,0:T(8,128)(2,1)S(1)}, u32[]{:S(2)}, u32[]{:S(2)}) collective-permute-start(bf16[512,128]{1,0:T(8,128)(2,1)S(1)} %get-tuple-element.73), channel_id=1, source_target_pairs={{0,16},{4,20},{8,24},{12,28},{16,0},{20,4},{24,8},{28,12},{1,17},{... | collective-permute-start | bytes 393224 | tf_op jit(solution)/shard_map/ppermute | solution.py:243
  36.5 6.5 %collective-permute-start.12 = (bf16[512,128]{1,0:T(8,128)(2,1)S(1)}, bf16[512,128]{1,0:T(8,128)(2,1)S(1)}, u32[]{:S(2)}, u32[]{:S(2)}) collective-permute-start(bf16[512,128]{1,0:T(8,128)(2,1)S(1)} %get-tuple-element.72), channel_id=1, source_target_pairs={{0,8},{4,12},{8,0},{12,4},{16,24},{20,28},{24,16},{28,20},{1,9},{5... | collective-permute-start | bytes 393224 | tf_op jit(solution)/shard_map/ppermute | solution.py:243
  43.1 10.2 %collective-permute-start.14 = (bf16[640,128]{1,0:T(8,128)(2,1)S(1)}, bf16[640,128]{1,0:T(8,128)(2,1)S(1)}, u32[]{:S(2)}, u32[]{:S(2)}) collective-permute-start(bf16[640,128]{1,0:T(8,128)(2,1)S(1)} %get-tuple-element.76), channel_id=1, source_target_pairs={{0,1},{1,0},{2,3},{3,2},{4,5},{5,4},{6,7},{7,6},{8,9},{9,8},{10,11... | collective-permute-start | bytes 491528 | tf_op jit(solution)/shard_map/ppermute | solution.py:243
  43.1 5.5 %collective-permute-start.10 = (bf16[512,128]{1,0:T(8,128)(2,1)S(1)}, bf16[512,128]{1,0:T(8,128)(2,1)S(1)}, u32[]{:S(2)}, u32[]{:S(2)}) collective-permute-start(bf16[512,128]{1,0:T(8,128)(2,1)S(1)} %get-tuple-element.69), channel_id=1, source_target_pairs={{0,3},{1,2},{2,1},{3,0},{4,7},{5,6},{6,5},{7,4},{8,11},{9,10},{10,... | collective-permute-start | bytes 393224 | tf_op jit(solution)/shard_map/ppermute | solution.py:243
  44.7 7.7 %collective-permute-start.8 = (bf16[512,128]{1,0:T(8,128)(2,1)S(1)}, bf16[512,128]{1,0:T(8,128)(2,1)S(1)}, u32[]{:S(2)}, u32[]{:S(2)}) collective-permute-start(bf16[512,128]{1,0:T(8,128)(2,1)S(1)} %get-tuple-element.61), channel_id=1, source_target_pairs={{0,2},{1,3},{2,0},{3,1},{4,6},{5,7},{6,4},{7,5},{8,10},{9,11},{10,... | collective-permute-start | bytes 393224 | tf_op jit(solution)/shard_map/ppermute | solution.py:243
  45.3 8.0 %collective-permute-start.15 = (bf16[128,128]{1,0:T(8,128)(2,1)S(1)}, bf16[128,128]{1,0:T(8,128)(2,1)S(1)}, u32[]{:S(2)}, u32[]{:S(2)}) collective-permute-start(bf16[128,128]{1,0:T(8,128)(2,1)S(1)} %get-tuple-element.77), channel_id=1, source_target_pairs={{0,2},{1,3},{2,0},{3,1},{4,6},{5,7},{6,4},{7,5},{8,10},{9,11},{10,... | collective-permute-start | bytes 98312 | tf_op jit(solution)/shard_map/ppermute | solution.py:243
  46.8 6.5 %collective-permute-start.16 = (bf16[128,128]{1,0:T(8,128)(2,1)S(1)}, bf16[128,128]{1,0:T(8,128)(2,1)S(1)}, u32[]{:S(2)}, u32[]{:S(2)}) collective-permute-start(bf16[128,128]{1,0:T(8,128)(2,1)S(1)} %get-tuple-element.78), channel_id=1, source_target_pairs={{0,3},{1,2},{2,1},{3,0},{4,7},{5,6},{6,5},{7,4},{8,11},{9,10},{10,... | collective-permute-start | bytes 98312 | tf_op jit(solution)/shard_map/ppermute | solution.py:243

commit v9 on v8

--- a/solution.py
+++ b/solution.py
@@ -12,7 +12,7 @@
 HEAD_DIM = 128
 GROUP = 8
 PAIRS = GROUP // 2
-DOT_ROWS = 32
+DOT_ROWS = 16
 VMEM_BYTES = 16 * 1024 * 1024
 
 
@@ -110,7 +110,7 @@
     for j in range(PAIRS):
         pair = jnp.concatenate([sums[2 * j], sums[2 * j + 1]], axis=0)
         dots = jnp.where(lane == j, pair, dots)
-    full = dots.T[:8, :]
+    full = dots.T[:PAIRS, :]
     high = full.astype(BF16).astype(F32)
     mid = (full - high).astype(BF16).astype(F32)
     low = (full - high) - mid
@@ -154,7 +154,7 @@
         query = qg_refs[i][:span, :]
         grad = qg_refs[i][span : 2 * span, :]
         split = qg_refs[i][2 * span : 2 * span + DOT_ROWS, :].astype(F32)
-        dots = row_of((split[:8] + split[8:16]) + split[16:24])
+        dots = row_of((split[:PAIRS] + split[PAIRS : 2 * PAIRS]) + split[2 * PAIRS : 3 * PAIRS])
         lse = row_of(lse_ref[8 * m : 8 * m + 8, :])
         dq = dq_in[i][...] if has_dq else None
         for b in range(blocks):
@@ -179,7 +179,7 @@
 
 
 def total_kernel(parts, levels, place, *refs):
-    terms, near_dq, outs = refs[:levels], refs[levels], refs[levels + 1 :]
+    terms, outs = refs[:levels], refs[levels:]
     total = terms[0][...]
     for term in terms[1:]:
         total = total + term[...].astype(F32)
@@ -189,7 +189,6 @@
         outs[m][rows : 2 * rows, :] = total[(parts + m) * rows : (parts + m + 1) * rows].astype(
             outs[m].dtype
         )
-    outs[1][2 * rows :, :] = near_dq[...]
 
 
 def put_queries(pieces, sources, place, out, stage, sems):
@@ -222,18 +221,18 @@
         copy.wait()
 
 
-def finish_kernel(parts, place, filled, *refs):
-    pieces, refs = refs[:parts], refs[parts:]
-    out, out_k, out_v, stage, stage_k, stage_v, sems = refs
-    rows = out.shape[0]
-    copies = put_queries((1,), (pieces[1],), place, out, stage, sems)
-    for m in range(parts):
+def finish_kernel(parts, place, *refs):
+    pieces, (out_k, out_v, stage_k, stage_v, sems) = refs[:parts], refs[parts:]
+    for m in range(parts):
+        rows = out_k.shape[0]
         col = pl.multiple_of((place[0] ^ m) * HEAD_DIM, HEAD_DIM)
         stage_k[:, pl.ds(col, HEAD_DIM)] = pieces[m][:rows, :].astype(F32)
-        stage_v[:, pl.ds(col, HEAD_DIM)] = pieces[m][rows : 2 * rows, :].astype(F32)
-    copies.append(pltpu.make_async_copy(stage_k, out_k, sems.at[1]))
-    copies.append(pltpu.make_async_copy(stage_v, out_v, sems.at[2]))
-    for copy in copies[1:]:
+        stage_v[:, pl.ds(col, HEAD_DIM)] = pieces[m][rows:, :].astype(F32)
+    copies = [
+        pltpu.make_async_copy(stage_k, out_k, sems.at[0]),
+        pltpu.make_async_copy(stage_v, out_v, sems.at[1]),
+    ]
+    for copy in copies:
         copy.start()
     for copy in copies:
         copy.wait()
@@ -248,7 +247,7 @@
 
 
 def use_order(levels):
-    return [b for b in (2, 1, 3) if b < levels] + list(range(4, levels))
+    return [b for b in (1, 2, 3) if b < levels] + list(range(4, levels))
 
 
 def on_device(queries, key_rows, value_rows, attn_out, out_grad, logsumexp):
@@ -323,7 +322,7 @@
         )
         for i, m in enumerate(pieces):
             dq[m] = result[i]
-            if dq_done and m > 1:
+            if dq_done and m > 0:
                 dq[m] = swap(dq[m], "head", m)
         for i, b in enumerate(blocks):
             acc[b] = result[len(pieces) + i]
@@ -344,12 +343,10 @@
     dkv = call(
         functools.partial(total_kernel, parts, levels),
         [
-            vmem((2 * rows + (span if m == 1 else 0), HEAD_DIM), F32 if m == 0 else BF16)
-            for m in range(parts)
+            vmem((2 * rows, HEAD_DIM), F32 if m == 0 else BF16) for m in range(parts)
         ],
         place,
         *acc,
-        dq[1],
     )
     dkv = [dkv[0]] + [swap(dkv[m], "head", m) for m in range(1, parts)]
     width = GROUP * HEAD_DIM
@@ -365,7 +362,7 @@
         out_space=pltpu.HBM,
         scratch=[stage(1), pltpu.SemaphoreType.DMA((1,))],
     )
-    late = tuple(range(2, parts))
+    late = tuple(range(1, parts))
     (grad_q,) = call(
         functools.partial(more_kernel, late),
         [hbm(queries.shape, F32)],
@@ -375,18 +372,16 @@
         filled=grad_q,
         scratch=[stage(len(late)), pltpu.SemaphoreType.DMA((len(late),))],
     )
-    grad_q, grad_k, grad_v = call(
+    grad_k, grad_v = call(
         functools.partial(finish_kernel, parts),
-        [hbm(queries.shape, F32), hbm(key_rows.shape, F32), hbm(value_rows.shape, F32)],
+        [hbm(key_rows.shape, F32), hbm(value_rows.shape, F32)],
         place,
         *dkv,
         out_space=pltpu.HBM,
-        filled=grad_q,
         scratch=[
-            stage(1),
             vmem(key_rows.shape, F32),
             vmem(value_rows.shape, F32),
-            pltpu.SemaphoreType.DMA((3,)),
+            pltpu.SemaphoreType.DMA((2,)),
         ],
     )
     return (grad_q, grad_k, grad_v)

time: 54.3 us -> 49.5 us (0.912)
  waiting for transfers between devices: 20.9 us -> 16.5 us
    ppermute x17 -> x18, waiting for transfers between devices: 20.9 us -> 16.5 us  [swap(): lax.ppermute(value, axis, [(i, i ^ distance) for i in range(lax.axis_size...]
    ppermute x17 -> x18, starting transfers between devices: 19.9 us -> 19.5 us  [swap(): lax.ppermute(value, axis, [(i, i ^ distance) for i in range(lax.axis_size...]
  transfers between devices with their start and end apart: 17 -> 18, of which waited for: 8 -> 9; matrix products, arithmetic and copies ran while one was open for 0% -> 0% of each run, Pallas kernels for 14% -> 16%
where the time goes in v9:
time: 49.5 us; the launch traced here: 49.3 us
  starting transfers between devices  19.5 us (39%)
  waiting for transfers between devices  16.5 us (33%)
  Pallas kernels  12.5 us (25%)
  between operations  0.8 us (2%)
    ppermute x18, starting transfers between devices, swap(): lax.ppermute(value, axis, [(i, i ^ distance) for i in range(lax.axis_size...  19.5 us
    ppermute x18, waiting for transfers between devices, swap(): lax.ppermute(value, axis, [(i, i ^ distance) for i in range(lax.axis_size...  16.5 us
    pallas_call x20, Pallas kernels, call(): pl.pallas_call(kernel, out_shape=out_shapes, in_specs=specs, out_specs=[p...  12.5 us
  transfers between devices with their start and end apart: 18, of which 9 were waited for; matrix products, arithmetic and copies ran while one was open for 0% of the time, Pallas kernels for 16%

profile of v9, /device:TPU:0, one launch (start us, length us, event | category | flops | bytes accessed | tf_op | source)
XLA Modules:
  0.0 49.3 jit_solution(8323723228774505747)
XLA Ops:
  0.6 1.5 %shard_map.85 = (bf16[64,4096]{1,0:T(8,128)(2,1)S(1)}, bf16[64,4096]{1,0:T(8,128)(2,1)S(1)}, bf16[64,4096]{1,0:T(8,128)(2,1)S(1)}, bf16[128,128]{1,0:T(8,128)(2,...) custom-call(s32[1]{0:T(128)} %bitcast.place, ...), custom_call_target="tpu_custom_call" | custom-call | tf_op jit(solution)/shard_map/pallas_call | solution.py:54
  2.5 0.5 %collective-permute-start = (bf16[1040,128]{1,0:T(8,128)(2,1)S(1)}, bf16[1040,128]{1,0:T(8,128)(2,1)S(1)}, u32[]{:S(2)}, u32[]{:S(2)}) collective-permute-start(bf16[1040,128]{1,0:T(8,128)(2,1)S(1)} %shard_map.87), channel_id=1, source_target_pairs={{0,1},{1,0},{2,3},{3,2},{4,5},{5,4},{6,7},{7,6},{8,9},{9,8},{10,11... | collective-permute-start | bytes 798728 | tf_op jit(solution)/shard_map/ppermute | solution.py:242
  3.4 2.5 %collective-permute-start.1 = (bf16[1040,128]{1,0:T(8,128)(2,1)S(1)}, bf16[1040,128]{1,0:T(8,128)(2,1)S(1)}, u32[]{:S(2)}, u32[]{:S(2)}) collective-permute-start(bf16[1040,128]{1,0:T(8,128)(2,1)S(1)} %shard_map.88), channel_id=1, source_target_pairs={{0,2},{1,3},{2,0},{3,1},{4,6},{5,7},{6,4},{7,5},{8,10},{9,11},{10,... | collective-permute-start | bytes 798728 | tf_op jit(solution)/shard_map/ppermute | solution.py:242
  6.5 1.9 %collective-permute-start.3 = (bf16[128,128]{1,0:T(8,128)(2,1)S(1)}, bf16[128,128]{1,0:T(8,128)(2,1)S(1)}, u32[]{:S(2)}, u32[]{:S(2)}) collective-permute-start(bf16[128,128]{1,0:T(8,128)(2,1)S(1)} %get-tuple-element.49), channel_id=1, source_target_pairs={{0,2},{1,3},{2,0},{3,1},{4,6},{5,7},{6,4},{7,5},{8,10},{9,11},{10,... | collective-permute-start | bytes 98312 | tf_op jit(solution)/shard_map/ppermute | solution.py:242
  8.4 0.8 %collective-permute-start.4 = (bf16[128,128]{1,0:T(8,128)(2,1)S(1)}, bf16[128,128]{1,0:T(8,128)(2,1)S(1)}, u32[]{:S(2)}, u32[]{:S(2)}) collective-permute-start(bf16[128,128]{1,0:T(8,128)(2,1)S(1)} %get-tuple-element.50), channel_id=1, source_target_pairs={{0,3},{1,2},{2,1},{3,0},{4,7},{5,6},{6,5},{7,4},{8,11},{9,10},{10,... | collective-permute-start | bytes 98312 | tf_op jit(solution)/shard_map/ppermute | solution.py:242
  9.2 10.3 %collective-permute-done.3.refs_2_ = bf16[128,128]{1,0:T(8,128)(2,1)S(1)} collective-permute-done((bf16[128,128]{1,0:T(8,128)(2,1)S(1)}, bf16[128,128]{1,0:T(8,128)(2,1)S(1)}, u32[]{:S(2)}, u32[]{:S(2)}) %collective-permute-start.3) | collective-permute-done | bytes 32800 | tf_op jit(solution)/shard_map/ppermute | solution.py:242
  19.9 1.7 %collective-permute-start.7 = (bf16[512,128]{1,0:T(8,128)(2,1)S(1)}, bf16[512,128]{1,0:T(8,128)(2,1)S(1)}, u32[]{:S(2)}, u32[]{:S(2)}) collective-permute-start(bf16[512,128]{1,0:T(8,128)(2,1)S(1)} %shard_map.89.refs_2_), channel_id=1, source_target_pairs={{0,4},{4,0},{8,12},{12,8},{16,20},{20,16},{24,28},{28,24},{1,5},{5... | collective-permute-start | bytes 393224 | tf_op jit(solution)/shard_map/ppermute | solution.py:242
  21.5 1.6 %collective-permute-start.6 = (bf16[512,128]{1,0:T(8,128)(2,1)S(1)}, bf16[512,128]{1,0:T(8,128)(2,1)S(1)}, u32[]{:S(2)}, u32[]{:S(2)}) collective-permute-start(bf16[512,128]{1,0:T(8,128)(2,1)S(1)} %shard_map.89.refs_2_), channel_id=1, source_target_pairs={{0,8},{4,12},{8,0},{12,4},{16,24},{20,28},{24,16},{28,20},{1,9},{5... | collective-permute-start | bytes 393224 | tf_op jit(solution)/shard_map/ppermute | solution.py:242
  23.1 2.6 %collective-permute-start.5 = (bf16[512,128]{1,0:T(8,128)(2,1)S(1)}, bf16[512,128]{1,0:T(8,128)(2,1)S(1)}, u32[]{:S(2)}, u32[]{:S(2)}) collective-permute-start(bf16[512,128]{1,0:T(8,128)(2,1)S(1)} %shard_map.89.refs_2_), channel_id=1, source_target_pairs={{0,16},{4,20},{8,24},{12,28},{16,0},{20,4},{24,8},{28,12},{1,17},{... | collective-permute-start | bytes 393224 | tf_op jit(solution)/shard_map/ppermute | solution.py:242
  26.0 0.5 shard_map.90
  26.5 0.5 shard_map.91
  27.0 0.9 %shard_map.92 = (f32[128,512]{1,0:T(8,128)S(1)}, f32[128,512]{1,0:T(8,128)S(1)}, f32[512,128]{1,0:T(8,128)S(1)}) custom-call(s32[1]{0:T(128)} %bitcast.place, bf16[1040,128]{1,0:T(8,128)(2,1)S(1)} %shard_map.86.refs_0_, bf16[1040,128]{1,0:T(8,128)(2,1)S(1)} %collective-permute-done.refs_0_.refs_1_, f32[32,128]{1,0:T(8,128)S(1)} %get-tuple-element.46.refs_1_.refs_2_.refs_3_, ...), custom_call_target="tpu_custom_call" | custom-call | tf_op jit(solution)/shard_map/pallas_call | solution.py:54
  27.9 1.0 %collective-permute-done.6.refs_3_.refs_4_.refs_2_ = bf16[512,128]{1,0:T(8,128)(2,1)S(1)} collective-permute-done((bf16[512,128]{1,0:T(8,128)(2,1)S(1)}, bf16[512,128]{1,0:T(8,128)(2,1)S(1)}, u32[]{:S(2)}, u32[]{:S(2)}) %collective-permute-start.6) | collective-permute-done | bytes 131104 | tf_op jit(solution)/shard_map/ppermute | solution.py:242
  28.9 0.9 %shard_map.93 = (f32[128,512]{1,0:T(8,128)S(1)}, f32[128,512]{1,0:T(8,128)S(1)}, f32[512,128]{1,0:T(8,128)S(1)}) custom-call(s32[1]{0:T(128)} %bitcast.place, bf16[1040,128]{1,0:T(8,128)(2,1)S(1)} %shard_map.86.refs_0_, bf16[1040,128]{1,0:T(8,128)(2,1)S(1)} %collective-permute-done.refs_0_.refs_1_, f32[32,128]{1,0:T(8,128)S(1)} %get-tuple-element.46.refs_1_.refs_2_.refs_3_, ...), custom_call_target="tpu_custom_call" | custom-call | tf_op jit(solution)/shard_map/pallas_call | solution.py:54
  29.8 1.1 %shard_map.94 = (f32[128,512]{1,0:T(8,128)S(1)}, f32[512,128]{1,0:T(8,128)S(1)}, f32[512,128]{1,0:T(8,128)S(1)}, f32[512,128]{1,0:T(8,128)S(1)}) custom-call(s32[1]{0:T(128)} %bitcast.place, bf16[1040,128]{1,0:T(8,128)(2,1)S(1)} %collective-permute-done.1.refs_0_.refs_2_, f32[32,128]{1,0:T(8,128)S(1)} %get-tuple-element.46.refs_1_.refs_2_.refs_3_, ...), custom_call_target="tpu_custom_call" | custom-call | tf_op jit(solution)/shard_map/pallas_call | solution.py:54
  31.0 0.5 shard_map.98
  31.9 1.3 %shard_map.95 = (f32[512,128]{1,0:T(8,128)S(1)}, bf16[512,128]{1,0:T(8,128)(2,1)S(1)}, bf16[512,128]{1,0:T(8,128)(2,1)S(1)}, f32[512,128]{1,0:T(8,128)S(1)}) custom-call(s32[1]{0:T(128)} %bitcast.place, bf16[1040,128]{1,0:T(8,128)(2,1)S(1)} %shard_map.86.refs_0_, bf16[1040,128]{1,0:T(8,128)(2,1)S(1)} %collective-permute-done.refs_0_.refs_1_, ...), custom_call_target="tpu_custom_call" | custom-call | tf_op jit(solution)/shard_map/pallas_call | solution.py:54
  33.2 0.5 shard_map.99
  33.7 0.5 shard_map.100
  34.2 0.6 %collective-permute-start.12 = (bf16[512,128]{1,0:T(8,128)(2,1)S(1)}, bf16[512,128]{1,0:T(8,128)(2,1)S(1)}, u32[]{:S(2)}, u32[]{:S(2)}) collective-permute-start(bf16[512,128]{1,0:T(8,128)(2,1)S(1)} %get-tuple-element.74), channel_id=1, source_target_pairs={{0,4},{4,0},{8,12},{12,8},{16,20},{20,16},{24,28},{28,24},{1,5},{5... | collective-permute-start | bytes 393224 | tf_op jit(solution)/shard_map/ppermute | solution.py:242
  34.8 1.2 %collective-permute-start.14 = (bf16[512,128]{1,0:T(8,128)(2,1)S(1)}, bf16[512,128]{1,0:T(8,128)(2,1)S(1)}, u32[]{:S(2)}, u32[]{:S(2)}) collective-permute-start(bf16[512,128]{1,0:T(8,128)(2,1)S(1)} %get-tuple-element.76), channel_id=1, source_target_pairs={{0,16},{4,20},{8,24},{12,28},{16,0},{20,4},{24,8},{28,12},{1,17},{... | collective-permute-start | bytes 393224 | tf_op jit(solution)/shard_map/ppermute | solution.py:242
  35.9 2.1 %collective-permute-start.13 = (bf16[512,128]{1,0:T(8,128)(2,1)S(1)}, bf16[512,128]{1,0:T(8,128)(2,1)S(1)}, u32[]{:S(2)}, u32[]{:S(2)}) collective-permute-start(bf16[512,128]{1,0:T(8,128)(2,1)S(1)} %get-tuple-element.75), channel_id=1, source_target_pairs={{0,8},{4,12},{8,0},{12,4},{16,24},{20,28},{24,16},{28,20},{1,9},{5... | collective-permute-start | bytes 393224 | tf_op jit(solution)/shard_map/ppermute | solution.py:242
  38.0 0.6 %shard_map.101 = (bf16[512,128]{1,0:T(8,128)(2,1)S(1)}, f32[512,128]{1,0:T(8,128)S(1)}) custom-call(s32[1]{0:T(128)} %bitcast.place, bf16[1040,128]{1,0:T(8,128)(2,1)S(1)} %collective-permute-done.10.refs_0_, f32[32,128]{1,0:T(8,128)S(1)} %get-tuple-element.46.refs_1_.refs_2_.refs_3_, bf16[512,128]{1,0:T(8,128)(2,1)S(1)} %shard_map.89.refs_2_, ...), custom_call_target="tpu_custom_call" | custom-call | tf_op jit(solution)/shard_map/pallas_call | solution.py:54
  38.6 1.6 %collective-permute-start.8 = (bf16[512,128]{1,0:T(8,128)(2,1)S(1)}, bf16[512,128]{1,0:T(8,128)(2,1)S(1)}, u32[]{:S(2)}, u32[]{:S(2)}) collective-permute-start(bf16[512,128]{1,0:T(8,128)(2,1)S(1)} %get-tuple-element.63), channel_id=1, source_target_pairs={{0,1},{1,0},{2,3},{3,2},{4,5},{5,4},{6,7},{7,6},{8,9},{9,8},{10,11... | collective-permute-start | bytes 393224 | tf_op jit(solution)/shard_map/ppermute | solution.py:242
  40.2 0.5 %collective-permute-start.9 = (bf16[512,128]{1,0:T(8,128)(2,1)S(1)}, bf16[512,128]{1,0:T(8,128)(2,1)S(1)}, u32[]{:S(2)}, u32[]{:S(2)}) collective-permute-start(bf16[512,128]{1,0:T(8,128)(2,1)S(1)} %get-tuple-element.64), channel_id=1, source_target_pairs={{0,2},{1,3},{2,0},{3,1},{4,6},{5,7},{6,4},{7,5},{8,10},{9,11},{10,... | collective-permute-start | bytes 393224 | tf_op jit(solution)/shard_map/ppermute | solution.py:242
  40.8 1.3 %collective-permute-done.14.refs_3_ = bf16[512,128]{1,0:T(8,128)(2,1)S(1)} collective-permute-done((bf16[512,128]{1,0:T(8,128)(2,1)S(1)}, bf16[512,128]{1,0:T(8,128)(2,1)S(1)}, u32[]{:S(2)}, u32[]{:S(2)}) %collective-permute-start.14) | collective-permute-done | bytes 131104 | tf_op jit(solution)/shard_map/ppermute | solution.py:242
  42.3 1.6 %collective-permute-start.16 = (bf16[128,128]{1,0:T(8,128)(2,1)S(1)}, bf16[128,128]{1,0:T(8,128)(2,1)S(1)}, u32[]{:S(2)}, u32[]{:S(2)}) collective-permute-start(bf16[128,128]{1,0:T(8,128)(2,1)S(1)} %get-tuple-element.79), channel_id=1, source_target_pairs={{0,2},{1,3},{2,0},{3,1},{4,6},{5,7},{6,4},{7,5},{8,10},{9,11},{10,... | collective-permute-start | bytes 98312 | tf_op jit(solution)/shard_map/ppermute | solution.py:242
  43.9 0.5 collective-permute-done.11.refs_2_
  44.4 0.7 %shard_map.96.filled = f32[64,4096]{1,0:T(8,128)} custom-call(s32[1]{0:T(128)} %bitcast.place, f32[512,128]{1,0:T(8,128)S(1)} %get-tuple-element.62.refs_0_), custom_call_target="tpu_custom_call" | custom-call | tf_op jit(solution)/shard_map/pallas_call | solution.py:54
  45.1 2.1 %collective-permute-done.9.refs_1_ = bf16[512,128]{1,0:T(8,128)(2,1)S(1)} collective-permute-done((bf16[512,128]{1,0:T(8,128)(2,1)S(1)}, bf16[512,128]{1,0:T(8,128)(2,1)S(1)}, u32[]{:S(2)}, u32[]{:S(2)}) %collective-permute-start.9) | collective-permute-done | bytes 131104 | tf_op jit(solution)/shard_map/ppermute | solution.py:242
  47.3 0.9 %shard_map.102 = f32[64,4096]{1,0:T(8,128)} custom-call(s32[1]{0:T(128)} %bitcast.place, f32[64,4096]{1,0:T(8,128)} %shard_map.96.filled, bf16[512,128]{1,0:T(8,128)(2,1)S(1)} %collective-permute-done.8.refs_0_, bf16[512,128]{1,0:T(8,128)(2,1)S(1)} %collective-permute-done.9.refs_1_, ...), custom_call_target="tpu_custom_call", output_to_operand_aliasing={{}: (1, {})} | custom-call | tf_op jit(solution)/shard_map/pallas_call | solution.py:54
  48.6 0.7 %shard_map.104 = (f32[64,512]{1,0:T(8,128)}, f32[64,512]{1,0:T(8,128)}) custom-call(s32[1]{0:T(128)} %bitcast.place, f32[128,128]{1,0:T(8,128)S(1)} %get-tuple-element.77.refs_0_, bf16[128,128]{1,0:T(8,128)(2,1)S(1)} %collective-permute-done.15.refs_1_, bf16[128,128]{1,0:T(8,128)(2,1)S(1)} %collective-permute-done.16.refs_2_, ...), custom_call_target="tpu_custom_call" | custom-call | tf_op jit(solution)/shard_map/pallas_call | solution.py:54
  (24 shorter events, 3.1 us)
Async XLA Ops:
  2.5 20.6 %collective-permute-start = (bf16[1040,128]{1,0:T(8,128)(2,1)S(1)}, bf16[1040,128]{1,0:T(8,128)(2,1)S(1)}, u32[]{:S(2)}, u32[]{:S(2)}) collective-permute-start(bf16[1040,128]{1,0:T(8,128)(2,1)S(1)} %shard_map.87), channel_id=1, source_target_pairs={{0,1},{1,0},{2,3},{3,2},{4,5},{5,4},{6,7},{7,6},{8,9},{9,8},{10,11... | collective-permute-start | bytes 798728 | tf_op jit(solution)/shard_map/ppermute | solution.py:242
  3.4 26.5 %collective-permute-start.1 = (bf16[1040,128]{1,0:T(8,128)(2,1)S(1)}, bf16[1040,128]{1,0:T(8,128)(2,1)S(1)}, u32[]{:S(2)}, u32[]{:S(2)}) collective-permute-start(bf16[1040,128]{1,0:T(8,128)(2,1)S(1)} %shard_map.88), channel_id=1, source_target_pairs={{0,2},{1,3},{2,0},{3,1},{4,6},{5,7},{6,4},{7,5},{8,10},{9,11},{10,... | collective-permute-start | bytes 798728 | tf_op jit(solution)/shard_map/ppermute | solution.py:242
  6.2 24.7 %collective-permute-start.10 = (bf16[1040,128]{1,0:T(8,128)(2,1)S(1)}, bf16[1040,128]{1,0:T(8,128)(2,1)S(1)}, u32[]{:S(2)}, u32[]{:S(2)}) collective-permute-start(bf16[1040,128]{1,0:T(8,128)(2,1)S(1)} %shard_map.97), channel_id=1, source_target_pairs={{0,3},{1,2},{2,1},{3,0},{4,7},{5,6},{6,5},{7,4},{8,11},{9,10},{10,... | collective-permute-start | bytes 798728 | tf_op jit(solution)/shard_map/ppermute | solution.py:242
  6.4 2.0 %collective-permute-start.2 = (bf16[128,128]{1,0:T(8,128)(2,1)S(1)}, bf16[128,128]{1,0:T(8,128)(2,1)S(1)}, u32[]{:S(2)}, u32[]{:S(2)}) collective-permute-start(bf16[128,128]{1,0:T(8,128)(2,1)S(1)} %get-tuple-element.48), channel_id=1, source_target_pairs={{0,1},{1,0},{2,3},{3,2},{4,5},{5,4},{6,7},{7,6},{8,9},{9,8},{10,11... | collective-permute-start | bytes 98312 | tf_op jit(solution)/shard_map/ppermute | solution.py:242
  6.5 13.0 %collective-permute-start.3 = (bf16[128,128]{1,0:T(8,128)(2,1)S(1)}, bf16[128,128]{1,0:T(8,128)(2,1)S(1)}, u32[]{:S(2)}, u32[]{:S(2)}) collective-permute-start(bf16[128,128]{1,0:T(8,128)(2,1)S(1)} %get-tuple-element.49), channel_id=1, source_target_pairs={{0,2},{1,3},{2,0},{3,1},{4,6},{5,7},{6,4},{7,5},{8,10},{9,11},{10,... | collective-permute-start | bytes 98312 | tf_op jit(solution)/shard_map/ppermute | solution.py:242
  8.4 11.4 %collective-permute-start.4 = (bf16[128,128]{1,0:T(8,128)(2,1)S(1)}, bf16[128,128]{1,0:T(8,128)(2,1)S(1)}, u32[]{:S(2)}, u32[]{:S(2)}) collective-permute-start(bf16[128,128]{1,0:T(8,128)(2,1)S(1)} %get-tuple-element.50), channel_id=1, source_target_pairs={{0,3},{1,2},{2,1},{3,0},{4,7},{5,6},{6,5},{7,4},{8,11},{9,10},{10,... | collective-permute-start | bytes 98312 | tf_op jit(solution)/shard_map/ppermute | solution.py:242
  19.9 7.2 %collective-permute-start.7 = (bf16[512,128]{1,0:T(8,128)(2,1)S(1)}, bf16[512,128]{1,0:T(8,128)(2,1)S(1)}, u32[]{:S(2)}, u32[]{:S(2)}) collective-permute-start(bf16[512,128]{1,0:T(8,128)(2,1)S(1)} %shard_map.89.refs_2_), channel_id=1, source_target_pairs={{0,4},{4,0},{8,12},{12,8},{16,20},{20,16},{24,28},{28,24},{1,5},{5... | collective-permute-start | bytes 393224 | tf_op jit(solution)/shard_map/ppermute | solution.py:242
  21.5 7.4 %collective-permute-start.6 = (bf16[512,128]{1,0:T(8,128)(2,1)S(1)}, bf16[512,128]{1,0:T(8,128)(2,1)S(1)}, u32[]{:S(2)}, u32[]{:S(2)}) collective-permute-start(bf16[512,128]{1,0:T(8,128)(2,1)S(1)} %shard_map.89.refs_2_), channel_id=1, source_target_pairs={{0,8},{4,12},{8,0},{12,4},{16,24},{20,28},{24,16},{28,20},{1,9},{5... | collective-permute-start | bytes 393224 | tf_op jit(solution)/shard_map/ppermute | solution.py:242
  23.1 8.8 %collective-permute-start.5 = (bf16[512,128]{1,0:T(8,128)(2,1)S(1)}, bf16[512,128]{1,0:T(8,128)(2,1)S(1)}, u32[]{:S(2)}, u32[]{:S(2)}) collective-permute-start(bf16[512,128]{1,0:T(8,128)(2,1)S(1)} %shard_map.89.refs_2_), channel_id=1, source_target_pairs={{0,16},{4,20},{8,24},{12,28},{16,0},{20,4},{24,8},{28,12},{1,17},{... | collective-permute-start | bytes 393224 | tf_op jit(solution)/shard_map/ppermute | solution.py:242
  34.2 6.0 %collective-permute-start.12 = (bf16[512,128]{1,0:T(8,128)(2,1)S(1)}, bf16[512,128]{1,0:T(8,128)(2,1)S(1)}, u32[]{:S(2)}, u32[]{:S(2)}) collective-permute-start(bf16[512,128]{1,0:T(8,128)(2,1)S(1)} %get-tuple-element.74), channel_id=1, source_target_pairs={{0,4},{4,0},{8,12},{12,8},{16,20},{20,16},{24,28},{28,24},{1,5},{5... | collective-permute-start | bytes 393224 | tf_op jit(solution)/shard_map/ppermute | solution.py:242
  34.8 7.3 %collective-permute-start.14 = (bf16[512,128]{1,0:T(8,128)(2,1)S(1)}, bf16[512,128]{1,0:T(8,128)(2,1)S(1)}, u32[]{:S(2)}, u32[]{:S(2)}) collective-permute-start(bf16[512,128]{1,0:T(8,128)(2,1)S(1)} %get-tuple-element.76), channel_id=1, source_target_pairs={{0,16},{4,20},{8,24},{12,28},{16,0},{20,4},{24,8},{28,12},{1,17},{... | collective-permute-start | bytes 393224 | tf_op jit(solution)/shard_map/ppermute | solution.py:242
  35.9 6.3 %collective-permute-start.13 = (bf16[512,128]{1,0:T(8,128)(2,1)S(1)}, bf16[512,128]{1,0:T(8,128)(2,1)S(1)}, u32[]{:S(2)}, u32[]{:S(2)}) collective-permute-start(bf16[512,128]{1,0:T(8,128)(2,1)S(1)} %get-tuple-element.75), channel_id=1, source_target_pairs={{0,8},{4,12},{8,0},{12,4},{16,24},{20,28},{24,16},{28,20},{1,9},{5... | collective-permute-start | bytes 393224 | tf_op jit(solution)/shard_map/ppermute | solution.py:242
  38.6 5.8 %collective-permute-start.11 = (bf16[512,128]{1,0:T(8,128)(2,1)S(1)}, bf16[512,128]{1,0:T(8,128)(2,1)S(1)}, u32[]{:S(2)}, u32[]{:S(2)}) collective-permute-start(bf16[512,128]{1,0:T(8,128)(2,1)S(1)} %get-tuple-element.72), channel_id=1, source_target_pairs={{0,3},{1,2},{2,1},{3,0},{4,7},{5,6},{6,5},{7,4},{8,11},{9,10},{10,... | collective-permute-start | bytes 393224 | tf_op jit(solution)/shard_map/ppermute | solution.py:242
  38.6 6.5 %collective-permute-start.8 = (bf16[512,128]{1,0:T(8,128)(2,1)S(1)}, bf16[512,128]{1,0:T(8,128)(2,1)S(1)}, u32[]{:S(2)}, u32[]{:S(2)}) collective-permute-start(bf16[512,128]{1,0:T(8,128)(2,1)S(1)} %get-tuple-element.63), channel_id=1, source_target_pairs={{0,1},{1,0},{2,3},{3,2},{4,5},{5,4},{6,7},{7,6},{8,9},{9,8},{10,11... | collective-permute-start | bytes 393224 | tf_op jit(solution)/shard_map/ppermute | solution.py:242
  40.2 7.0 %collective-permute-start.9 = (bf16[512,128]{1,0:T(8,128)(2,1)S(1)}, bf16[512,128]{1,0:T(8,128)(2,1)S(1)}, u32[]{:S(2)}, u32[]{:S(2)}) collective-permute-start(bf16[512,128]{1,0:T(8,128)(2,1)S(1)} %get-tuple-element.64), channel_id=1, source_target_pairs={{0,2},{1,3},{2,0},{3,1},{4,6},{5,7},{6,4},{7,5},{8,10},{9,11},{10,... | collective-permute-start | bytes 393224 | tf_op jit(solution)/shard_map/ppermute | solution.py:242
  42.2 6.0 %collective-permute-start.15 = (bf16[128,128]{1,0:T(8,128)(2,1)S(1)}, bf16[128,128]{1,0:T(8,128)(2,1)S(1)}, u32[]{:S(2)}, u32[]{:S(2)}) collective-permute-start(bf16[128,128]{1,0:T(8,128)(2,1)S(1)} %get-tuple-element.78), channel_id=1, source_target_pairs={{0,1},{1,0},{2,3},{3,2},{4,5},{5,4},{6,7},{7,6},{8,9},{9,8},{10,11... | collective-permute-start | bytes 98312 | tf_op jit(solution)/shard_map/ppermute | solution.py:242
  42.3 5.9 %collective-permute-start.16 = (bf16[128,128]{1,0:T(8,128)(2,1)S(1)}, bf16[128,128]{1,0:T(8,128)(2,1)S(1)}, u32[]{:S(2)}, u32[]{:S(2)}) collective-permute-start(bf16[128,128]{1,0:T(8,128)(2,1)S(1)} %get-tuple-element.79), channel_id=1, source_target_pairs={{0,2},{1,3},{2,0},{3,1},{4,6},{5,7},{6,4},{7,5},{8,10},{9,11},{10,... | collective-permute-start | bytes 98312 | tf_op jit(solution)/shard_map/ppermute | solution.py:242
  44.4 4.2 %collective-permute-start.17 = (bf16[128,128]{1,0:T(8,128)(2,1)S(1)}, bf16[128,128]{1,0:T(8,128)(2,1)S(1)}, u32[]{:S(2)}, u32[]{:S(2)}) collective-permute-start(bf16[128,128]{1,0:T(8,128)(2,1)S(1)} %get-tuple-element.80), channel_id=1, source_target_pairs={{0,3},{1,2},{2,1},{3,0},{4,7},{5,6},{6,5},{7,4},{8,11},{9,10},{10,... | collective-permute-start | bytes 98312 | tf_op jit(solution)/shard_map/ppermute | solution.py:242

commit v10 on v9

--- a/solution.py
+++ b/solution.py
@@ -238,12 +238,27 @@
         copy.wait()
 
 
+def partner_bit(slot, core, levels):
+    maps = ((0, 1, 2), (1, 2, 0))
+    return maps[core][slot - 1] if slot <= 3 and levels >= 4 else slot - 1
+
+
+def trade(value, slot, levels):
+    ctx, head = lax.axis_size("ctx"), lax.axis_size("head")
+    pairs = [
+        (i * head + h, (i ^ 1 << partner_bit(slot, h % 2, levels)) * head + h)
+        for i in range(ctx)
+        for h in range(head)
+    ]
+    return lax.ppermute(value, ("ctx", "head"), pairs)
+
+
 def swap(value, axis, distance):
     return lax.ppermute(value, axis, [(i, i ^ distance) for i in range(lax.axis_size(axis))])
 
 
 def far_order(levels):
-    return [b for b in (2, 3, 1) if b < levels] + list(range(4, levels))
+    return [b for b in (1, 2, 3) if b < levels] + list(range(4, levels))
 
 
 def use_order(levels):
@@ -292,7 +307,7 @@
     (kv_own,) = call(
         functools.partial(join_kernel, parts), [vmem((2 * block, HEAD_DIM), BF16)], place, *kv
     )
-    kv_all = [kv_own] + [swap(kv_own, "ctx", 1 << (b - 1)) for b in range(1, levels)]
+    kv_all = [kv_own] + [trade(kv_own, b, levels) for b in range(1, levels)]
 
     dq = [None] * parts
     acc = [None] * levels
@@ -327,7 +342,7 @@
         for i, b in enumerate(blocks):
             acc[b] = result[len(pieces) + i]
             if acc_done and b > 0:
-                acc[b] = swap(acc[b], "ctx", 1 << (b - 1))
+                acc[b] = trade(acc[b], b, levels)
 
     early = tuple(range(parts - 1))
     hops = use_order(levels)

time: 49.5 us -> 49.6 us (level)
  starting transfers between devices: 19.5 us -> 21.9 us
  waiting for transfers between devices: 16.5 us -> 14.2 us
    ppermute x0 -> x6, starting transfers between devices: none -> 10.8 us  [trade(): return lax.ppermute(value, ('ctx', 'head'), pairs)]
    ppermute x18 -> x12, starting transfers between devices: 19.5 us -> 11.1 us  [swap(): lax.ppermute(value, axis, [(i, i ^ distance) for i in range(lax.axis_size...]
    ppermute x18 -> x12, waiting for transfers between devices: 16.5 us -> 11.6 us  [swap(): lax.ppermute(value, axis, [(i, i ^ distance) for i in range(lax.axis_size...]
    ppermute x0 -> x6, waiting for transfers between devices: none -> 2.59 us  [trade(): return lax.ppermute(value, ('ctx', 'head'), pairs)]
  transfers between devices with their start and end apart: 18 -> 18, of which waited for: 9 -> 4; matrix products, arithmetic and copies ran while one was open for 0% -> 0% of each run, Pallas kernels for 16% -> 16%
where the time goes in v10:
time: 49.6 us; the launch traced here: 49.4 us
  starting transfers between devices  21.9 us (44%)
  waiting for transfers between devices  14.2 us (29%)
  Pallas kernels  12.6 us (25%)
  between operations  0.81 us (2%)
    pallas_call x20, Pallas kernels, call(): pl.pallas_call(kernel, out_shape=out_shapes, in_specs=specs, out_specs=[p...  12.6 us
    ppermute x12, waiting for transfers between devices, swap(): lax.ppermute(value, axis, [(i, i ^ distance) for i in range(lax.axis_size...  11.6 us
    ppermute x12, starting transfers between devices, swap(): lax.ppermute(value, axis, [(i, i ^ distance) for i in range(lax.axis_size...  11.1 us
    ppermute x6, starting transfers between devices, trade(): return lax.ppermute(value, ('ctx', 'head'), pairs)  10.8 us
    ppermute x6, waiting for transfers between devices, trade(): return lax.ppermute(value, ('ctx', 'head'), pairs)  2.59 us
  transfers between devices with their start and end apart: 18, of which 4 were waited for; matrix products, arithmetic and copies ran while one was open for 0% of the time, Pallas kernels for 16%

profile of v10, /device:TPU:0, one launch (start us, length us, event | category | flops | bytes accessed | tf_op | source)
XLA Modules:
  0.0 49.4 jit_solution(9388389675274482269)
XLA Ops:
  0.6 1.5 %shard_map.85 = (bf16[64,4096]{1,0:T(8,128)(2,1)S(1)}, bf16[64,4096]{1,0:T(8,128)(2,1)S(1)}, bf16[64,4096]{1,0:T(8,128)(2,1)S(1)}, bf16[128,128]{1,0:T(8,128)(2,...) custom-call(s32[1]{0:T(128)} %bitcast.place, ...), custom_call_target="tpu_custom_call" | custom-call | tf_op jit(solution)/shard_map/pallas_call | solution.py:54
  2.1 0.3 shard_map.87
  2.5 0.5 %collective-permute-start = (bf16[1040,128]{1,0:T(8,128)(2,1)S(1)}, bf16[1040,128]{1,0:T(8,128)(2,1)S(1)}, u32[]{:S(2)}, u32[]{:S(2)}) collective-permute-start(bf16[1040,128]{1,0:T(8,128)(2,1)S(1)} %shard_map.87), channel_id=1, source_target_pairs={{0,1},{1,0},{2,3},{3,2},{4,5},{5,4},{6,7},{7,6},{8,9},{9,8},{10,11... | collective-permute-start | bytes 798728 | tf_op jit(solution)/shard_map/ppermute | solution.py:257
  3.4 2.5 %collective-permute-start.1 = (bf16[1040,128]{1,0:T(8,128)(2,1)S(1)}, bf16[1040,128]{1,0:T(8,128)(2,1)S(1)}, u32[]{:S(2)}, u32[]{:S(2)}) collective-permute-start(bf16[1040,128]{1,0:T(8,128)(2,1)S(1)} %shard_map.88), channel_id=1, source_target_pairs={{0,2},{1,3},{2,0},{3,1},{4,6},{5,7},{6,4},{7,5},{8,10},{9,11},{10,... | collective-permute-start | bytes 798728 | tf_op jit(solution)/shard_map/ppermute | solution.py:257
  6.5 1.9 %collective-permute-start.3 = (bf16[128,128]{1,0:T(8,128)(2,1)S(1)}, bf16[128,128]{1,0:T(8,128)(2,1)S(1)}, u32[]{:S(2)}, u32[]{:S(2)}) collective-permute-start(bf16[128,128]{1,0:T(8,128)(2,1)S(1)} %get-tuple-element.49), channel_id=1, source_target_pairs={{0,2},{1,3},{2,0},{3,1},{4,6},{5,7},{6,4},{7,5},{8,10},{9,11},{10,... | collective-permute-start | bytes 98312 | tf_op jit(solution)/shard_map/ppermute | solution.py:257
  8.4 0.8 %collective-permute-start.4 = (bf16[128,128]{1,0:T(8,128)(2,1)S(1)}, bf16[128,128]{1,0:T(8,128)(2,1)S(1)}, u32[]{:S(2)}, u32[]{:S(2)}) collective-permute-start(bf16[128,128]{1,0:T(8,128)(2,1)S(1)} %get-tuple-element.50), channel_id=1, source_target_pairs={{0,3},{1,2},{2,1},{3,0},{4,7},{5,6},{6,5},{7,4},{8,11},{9,10},{10,... | collective-permute-start | bytes 98312 | tf_op jit(solution)/shard_map/ppermute | solution.py:257
  9.2 10.3 %collective-permute-done.3.refs_2_ = bf16[128,128]{1,0:T(8,128)(2,1)S(1)} collective-permute-done((bf16[128,128]{1,0:T(8,128)(2,1)S(1)}, bf16[128,128]{1,0:T(8,128)(2,1)S(1)}, u32[]{:S(2)}, u32[]{:S(2)}) %collective-permute-start.3) | collective-permute-done | bytes 32800 | tf_op jit(solution)/shard_map/ppermute | solution.py:257
  19.9 1.7 %collective-permute-start.7 = (bf16[512,128]{1,0:T(8,128)(2,1)S(1)}, bf16[512,128]{1,0:T(8,128)(2,1)S(1)}, u32[]{:S(2)}, u32[]{:S(2)}) collective-permute-start(bf16[512,128]{1,0:T(8,128)(2,1)S(1)} %shard_map.89.refs_2_), channel_id=1, source_target_pairs={{0,4},{1,9},{2,6},{3,11},{4,0},{5,13},{6,2},{7,15},{8,12},{9,1},{1... | collective-permute-start | bytes 393224 | tf_op jit(solution)/shard_map/ppermute | solution.py:253
  21.5 1.6 %collective-permute-start.6 = (bf16[512,128]{1,0:T(8,128)(2,1)S(1)}, bf16[512,128]{1,0:T(8,128)(2,1)S(1)}, u32[]{:S(2)}, u32[]{:S(2)}) collective-permute-start(bf16[512,128]{1,0:T(8,128)(2,1)S(1)} %shard_map.89.refs_2_), channel_id=1, source_target_pairs={{0,8},{1,17},{2,10},{3,19},{4,12},{5,21},{6,14},{7,23},{8,0},{9,25... | collective-permute-start | bytes 393224 | tf_op jit(solution)/shard_map/ppermute | solution.py:253
  23.1 2.6 %collective-permute-start.5 = (bf16[512,128]{1,0:T(8,128)(2,1)S(1)}, bf16[512,128]{1,0:T(8,128)(2,1)S(1)}, u32[]{:S(2)}, u32[]{:S(2)}) collective-permute-start(bf16[512,128]{1,0:T(8,128)(2,1)S(1)} %shard_map.89.refs_2_), channel_id=1, source_target_pairs={{0,16},{1,5},{2,18},{3,7},{4,20},{5,1},{6,22},{7,3},{8,24},{9,13},... | collective-permute-start | bytes 393224 | tf_op jit(solution)/shard_map/ppermute | solution.py:253
  26.0 0.5 shard_map.90
  26.5 0.5 shard_map.91
  27.0 0.9 %shard_map.92 = (f32[128,512]{1,0:T(8,128)S(1)}, f32[128,512]{1,0:T(8,128)S(1)}, f32[512,128]{1,0:T(8,128)S(1)}) custom-call(s32[1]{0:T(128)} %bitcast.place, bf16[1040,128]{1,0:T(8,128)(2,1)S(1)} %shard_map.86.refs_0_, bf16[1040,128]{1,0:T(8,128)(2,1)S(1)} %collective-permute-done.refs_0_.refs_1_, f32[32,128]{1,0:T(8,128)S(1)} %get-tuple-element.46.refs_1_.refs_2_.refs_3_, ...), custom_call_target="tpu_custom_call" | custom-call | tf_op jit(solution)/shard_map/pallas_call | solution.py:54
  28.0 0.9 %shard_map.93 = (f32[128,512]{1,0:T(8,128)S(1)}, f32[128,512]{1,0:T(8,128)S(1)}, f32[512,128]{1,0:T(8,128)S(1)}) custom-call(s32[1]{0:T(128)} %bitcast.place, bf16[1040,128]{1,0:T(8,128)(2,1)S(1)} %shard_map.86.refs_0_, bf16[1040,128]{1,0:T(8,128)(2,1)S(1)} %collective-permute-done.refs_0_.refs_1_, f32[32,128]{1,0:T(8,128)S(1)} %get-tuple-element.46.refs_1_.refs_2_.refs_3_, ...), custom_call_target="tpu_custom_call" | custom-call | tf_op jit(solution)/shard_map/pallas_call | solution.py:54
  28.9 1.1 %shard_map.94 = (f32[128,512]{1,0:T(8,128)S(1)}, f32[512,128]{1,0:T(8,128)S(1)}, f32[512,128]{1,0:T(8,128)S(1)}, f32[512,128]{1,0:T(8,128)S(1)}) custom-call(s32[1]{0:T(128)} %bitcast.place, bf16[1040,128]{1,0:T(8,128)(2,1)S(1)} %collective-permute-done.1.refs_0_.refs_2_, f32[32,128]{1,0:T(8,128)S(1)} %get-tuple-element.46.refs_1_.refs_2_.refs_3_, ...), custom_call_target="tpu_custom_call" | custom-call | tf_op jit(solution)/shard_map/pallas_call | solution.py:54
  30.0 0.5 shard_map.98
  30.5 0.5 shard_map.99
  31.0 1.4 %shard_map.95 = (f32[512,128]{1,0:T(8,128)S(1)}, bf16[512,128]{1,0:T(8,128)(2,1)S(1)}, bf16[512,128]{1,0:T(8,128)(2,1)S(1)}, f32[512,128]{1,0:T(8,128)S(1)}) custom-call(s32[1]{0:T(128)} %bitcast.place, bf16[1040,128]{1,0:T(8,128)(2,1)S(1)} %shard_map.86.refs_0_, bf16[1040,128]{1,0:T(8,128)(2,1)S(1)} %collective-permute-done.refs_0_.refs_1_, ...), custom_call_target="tpu_custom_call" | custom-call | tf_op jit(solution)/shard_map/pallas_call | solution.py:54
  32.4 0.5 shard_map.100
  32.8 1.7 %collective-permute-start.14 = (bf16[512,128]{1,0:T(8,128)(2,1)S(1)}, bf16[512,128]{1,0:T(8,128)(2,1)S(1)}, u32[]{:S(2)}, u32[]{:S(2)}) collective-permute-start(bf16[512,128]{1,0:T(8,128)(2,1)S(1)} %get-tuple-element.76), channel_id=1, source_target_pairs={{0,16},{1,5},{2,18},{3,7},{4,20},{5,1},{6,22},{7,3},{8,24},{9,13},... | collective-permute-start | bytes 393224 | tf_op jit(solution)/shard_map/ppermute | solution.py:253
  34.5 2.1 %collective-permute-start.13 = (bf16[512,128]{1,0:T(8,128)(2,1)S(1)}, bf16[512,128]{1,0:T(8,128)(2,1)S(1)}, u32[]{:S(2)}, u32[]{:S(2)}) collective-permute-start(bf16[512,128]{1,0:T(8,128)(2,1)S(1)} %get-tuple-element.75), channel_id=1, source_target_pairs={{0,8},{1,17},{2,10},{3,19},{4,12},{5,21},{6,14},{7,23},{8,0},{9,25... | collective-permute-start | bytes 393224 | tf_op jit(solution)/shard_map/ppermute | solution.py:253
  36.6 1.1 %collective-permute-start.12 = (bf16[512,128]{1,0:T(8,128)(2,1)S(1)}, bf16[512,128]{1,0:T(8,128)(2,1)S(1)}, u32[]{:S(2)}, u32[]{:S(2)}) collective-permute-start(bf16[512,128]{1,0:T(8,128)(2,1)S(1)} %get-tuple-element.74), channel_id=1, source_target_pairs={{0,4},{1,9},{2,6},{3,11},{4,0},{5,13},{6,2},{7,15},{8,12},{9,1},{1... | collective-permute-start | bytes 393224 | tf_op jit(solution)/shard_map/ppermute | solution.py:253
  37.8 0.6 %shard_map.101 = (bf16[512,128]{1,0:T(8,128)(2,1)S(1)}, f32[512,128]{1,0:T(8,128)S(1)}) custom-call(s32[1]{0:T(128)} %bitcast.place, bf16[1040,128]{1,0:T(8,128)(2,1)S(1)} %collective-permute-done.10.refs_0_, f32[32,128]{1,0:T(8,128)S(1)} %get-tuple-element.46.refs_1_.refs_2_.refs_3_, bf16[512,128]{1,0:T(8,128)(2,1)S(1)} %shard_map.89.refs_2_, ...), custom_call_target="tpu_custom_call" | custom-call | tf_op jit(solution)/shard_map/pallas_call | solution.py:54
  38.5 1.5 %collective-permute-start.8 = (bf16[512,128]{1,0:T(8,128)(2,1)S(1)}, bf16[512,128]{1,0:T(8,128)(2,1)S(1)}, u32[]{:S(2)}, u32[]{:S(2)}) collective-permute-start(bf16[512,128]{1,0:T(8,128)(2,1)S(1)} %get-tuple-element.63), channel_id=1, source_target_pairs={{0,1},{1,0},{2,3},{3,2},{4,5},{5,4},{6,7},{7,6},{8,9},{9,8},{10,11... | collective-permute-start | bytes 393224 | tf_op jit(solution)/shard_map/ppermute | solution.py:257
  40.0 2.5 %collective-permute-done.14.refs_3_ = bf16[512,128]{1,0:T(8,128)(2,1)S(1)} collective-permute-done((bf16[512,128]{1,0:T(8,128)(2,1)S(1)}, bf16[512,128]{1,0:T(8,128)(2,1)S(1)}, u32[]{:S(2)}, u32[]{:S(2)}) %collective-permute-start.14) | collective-permute-done | bytes 131104 | tf_op jit(solution)/shard_map/ppermute | solution.py:253
  42.6 1.5 %collective-permute-start.9 = (bf16[512,128]{1,0:T(8,128)(2,1)S(1)}, bf16[512,128]{1,0:T(8,128)(2,1)S(1)}, u32[]{:S(2)}, u32[]{:S(2)}) collective-permute-start(bf16[512,128]{1,0:T(8,128)(2,1)S(1)} %get-tuple-element.64), channel_id=1, source_target_pairs={{0,2},{1,3},{2,0},{3,1},{4,6},{5,7},{6,4},{7,5},{8,10},{9,11},{10,... | collective-permute-start | bytes 393224 | tf_op jit(solution)/shard_map/ppermute | solution.py:257
  44.2 0.6 %collective-permute-start.16 = (bf16[128,128]{1,0:T(8,128)(2,1)S(1)}, bf16[128,128]{1,0:T(8,128)(2,1)S(1)}, u32[]{:S(2)}, u32[]{:S(2)}) collective-permute-start(bf16[128,128]{1,0:T(8,128)(2,1)S(1)} %get-tuple-element.79), channel_id=1, source_target_pairs={{0,2},{1,3},{2,0},{3,1},{4,6},{5,7},{6,4},{7,5},{8,10},{9,11},{10,... | collective-permute-start | bytes 98312 | tf_op jit(solution)/shard_map/ppermute | solution.py:257
  44.8 1.3 %collective-permute-start.17 = (bf16[128,128]{1,0:T(8,128)(2,1)S(1)}, bf16[128,128]{1,0:T(8,128)(2,1)S(1)}, u32[]{:S(2)}, u32[]{:S(2)}) collective-permute-start(bf16[128,128]{1,0:T(8,128)(2,1)S(1)} %get-tuple-element.80), channel_id=1, source_target_pairs={{0,3},{1,2},{2,1},{3,0},{4,7},{5,6},{6,5},{7,4},{8,11},{9,10},{10,... | collective-permute-start | bytes 98312 | tf_op jit(solution)/shard_map/ppermute | solution.py:257
  46.1 0.7 %shard_map.96.filled = f32[64,4096]{1,0:T(8,128)} custom-call(s32[1]{0:T(128)} %bitcast.place, f32[512,128]{1,0:T(8,128)S(1)} %get-tuple-element.62.refs_0_), custom_call_target="tpu_custom_call" | custom-call | tf_op jit(solution)/shard_map/pallas_call | solution.py:54
  46.8 0.9 %collective-permute-done.9.refs_1_ = bf16[512,128]{1,0:T(8,128)(2,1)S(1)} collective-permute-done((bf16[512,128]{1,0:T(8,128)(2,1)S(1)}, bf16[512,128]{1,0:T(8,128)(2,1)S(1)}, u32[]{:S(2)}, u32[]{:S(2)}) %collective-permute-start.9) | collective-permute-done | bytes 131104 | tf_op jit(solution)/shard_map/ppermute | solution.py:257
  47.7 0.9 %shard_map.102 = f32[64,4096]{1,0:T(8,128)} custom-call(s32[1]{0:T(128)} %bitcast.place, f32[64,4096]{1,0:T(8,128)} %shard_map.96.filled, bf16[512,128]{1,0:T(8,128)(2,1)S(1)} %collective-permute-done.8.refs_0_, bf16[512,128]{1,0:T(8,128)(2,1)S(1)} %collective-permute-done.9.refs_1_, ...), custom_call_target="tpu_custom_call", output_to_operand_aliasing={{}: (1, {})} | custom-call | tf_op jit(solution)/shard_map/pallas_call | solution.py:54
  48.7 0.7 %shard_map.104 = (f32[64,512]{1,0:T(8,128)}, f32[64,512]{1,0:T(8,128)}) custom-call(s32[1]{0:T(128)} %bitcast.place, f32[128,128]{1,0:T(8,128)S(1)} %get-tuple-element.77.refs_0_, bf16[128,128]{1,0:T(8,128)(2,1)S(1)} %collective-permute-done.15.refs_1_, bf16[128,128]{1,0:T(8,128)(2,1)S(1)} %collective-permute-done.16.refs_2_, ...), custom_call_target="tpu_custom_call" | custom-call | tf_op jit(solution)/shard_map/pallas_call | solution.py:54
  (24 shorter events, 2.1 us)
Async XLA Ops:
  2.5 20.6 %collective-permute-start = (bf16[1040,128]{1,0:T(8,128)(2,1)S(1)}, bf16[1040,128]{1,0:T(8,128)(2,1)S(1)}, u32[]{:S(2)}, u32[]{:S(2)}) collective-permute-start(bf16[1040,128]{1,0:T(8,128)(2,1)S(1)} %shard_map.87), channel_id=1, source_target_pairs={{0,1},{1,0},{2,3},{3,2},{4,5},{5,4},{6,7},{7,6},{8,9},{9,8},{10,11... | collective-permute-start | bytes 798728 | tf_op jit(solution)/shard_map/ppermute | solution.py:257
  3.4 25.6 %collective-permute-start.1 = (bf16[1040,128]{1,0:T(8,128)(2,1)S(1)}, bf16[1040,128]{1,0:T(8,128)(2,1)S(1)}, u32[]{:S(2)}, u32[]{:S(2)}) collective-permute-start(bf16[1040,128]{1,0:T(8,128)(2,1)S(1)} %shard_map.88), channel_id=1, source_target_pairs={{0,2},{1,3},{2,0},{3,1},{4,6},{5,7},{6,4},{7,5},{8,10},{9,11},{10,... | collective-permute-start | bytes 798728 | tf_op jit(solution)/shard_map/ppermute | solution.py:257
  6.2 23.8 %collective-permute-start.10 = (bf16[1040,128]{1,0:T(8,128)(2,1)S(1)}, bf16[1040,128]{1,0:T(8,128)(2,1)S(1)}, u32[]{:S(2)}, u32[]{:S(2)}) collective-permute-start(bf16[1040,128]{1,0:T(8,128)(2,1)S(1)} %shard_map.97), channel_id=1, source_target_pairs={{0,3},{1,2},{2,1},{3,0},{4,7},{5,6},{6,5},{7,4},{8,11},{9,10},{10,... | collective-permute-start | bytes 798728 | tf_op jit(solution)/shard_map/ppermute | solution.py:257
  6.4 2.0 %collective-permute-start.2 = (bf16[128,128]{1,0:T(8,128)(2,1)S(1)}, bf16[128,128]{1,0:T(8,128)(2,1)S(1)}, u32[]{:S(2)}, u32[]{:S(2)}) collective-permute-start(bf16[128,128]{1,0:T(8,128)(2,1)S(1)} %get-tuple-element.48), channel_id=1, source_target_pairs={{0,1},{1,0},{2,3},{3,2},{4,5},{5,4},{6,7},{7,6},{8,9},{9,8},{10,11... | collective-permute-start | bytes 98312 | tf_op jit(solution)/shard_map/ppermute | solution.py:257
  6.5 13.0 %collective-permute-start.3 = (bf16[128,128]{1,0:T(8,128)(2,1)S(1)}, bf16[128,128]{1,0:T(8,128)(2,1)S(1)}, u32[]{:S(2)}, u32[]{:S(2)}) collective-permute-start(bf16[128,128]{1,0:T(8,128)(2,1)S(1)} %get-tuple-element.49), channel_id=1, source_target_pairs={{0,2},{1,3},{2,0},{3,1},{4,6},{5,7},{6,4},{7,5},{8,10},{9,11},{10,... | collective-permute-start | bytes 98312 | tf_op jit(solution)/shard_map/ppermute | solution.py:257
  8.4 11.4 %collective-permute-start.4 = (bf16[128,128]{1,0:T(8,128)(2,1)S(1)}, bf16[128,128]{1,0:T(8,128)(2,1)S(1)}, u32[]{:S(2)}, u32[]{:S(2)}) collective-permute-start(bf16[128,128]{1,0:T(8,128)(2,1)S(1)} %get-tuple-element.50), channel_id=1, source_target_pairs={{0,3},{1,2},{2,1},{3,0},{4,7},{5,6},{6,5},{7,4},{8,11},{9,10},{10,... | collective-permute-start | bytes 98312 | tf_op jit(solution)/shard_map/ppermute | solution.py:257
  19.9 7.2 %collective-permute-start.7 = (bf16[512,128]{1,0:T(8,128)(2,1)S(1)}, bf16[512,128]{1,0:T(8,128)(2,1)S(1)}, u32[]{:S(2)}, u32[]{:S(2)}) collective-permute-start(bf16[512,128]{1,0:T(8,128)(2,1)S(1)} %shard_map.89.refs_2_), channel_id=1, source_target_pairs={{0,4},{1,9},{2,6},{3,11},{4,0},{5,13},{6,2},{7,15},{8,12},{9,1},{1... | collective-permute-start | bytes 393224 | tf_op jit(solution)/shard_map/ppermute | solution.py:253
  21.5 6.4 %collective-permute-start.6 = (bf16[512,128]{1,0:T(8,128)(2,1)S(1)}, bf16[512,128]{1,0:T(8,128)(2,1)S(1)}, u32[]{:S(2)}, u32[]{:S(2)}) collective-permute-start(bf16[512,128]{1,0:T(8,128)(2,1)S(1)} %shard_map.89.refs_2_), channel_id=1, source_target_pairs={{0,8},{1,17},{2,10},{3,19},{4,12},{5,21},{6,14},{7,23},{8,0},{9,25... | collective-permute-start | bytes 393224 | tf_op jit(solution)/shard_map/ppermute | solution.py:253
  23.1 7.9 %collective-permute-start.5 = (bf16[512,128]{1,0:T(8,128)(2,1)S(1)}, bf16[512,128]{1,0:T(8,128)(2,1)S(1)}, u32[]{:S(2)}, u32[]{:S(2)}) collective-permute-start(bf16[512,128]{1,0:T(8,128)(2,1)S(1)} %shard_map.89.refs_2_), channel_id=1, source_target_pairs={{0,16},{1,5},{2,18},{3,7},{4,20},{5,1},{6,22},{7,3},{8,24},{9,13},... | collective-permute-start | bytes 393224 | tf_op jit(solution)/shard_map/ppermute | solution.py:253
  32.8 9.7 %collective-permute-start.14 = (bf16[512,128]{1,0:T(8,128)(2,1)S(1)}, bf16[512,128]{1,0:T(8,128)(2,1)S(1)}, u32[]{:S(2)}, u32[]{:S(2)}) collective-permute-start(bf16[512,128]{1,0:T(8,128)(2,1)S(1)} %get-tuple-element.76), channel_id=1, source_target_pairs={{0,16},{1,5},{2,18},{3,7},{4,20},{5,1},{6,22},{7,3},{8,24},{9,13},... | collective-permute-start | bytes 393224 | tf_op jit(solution)/shard_map/ppermute | solution.py:253
  34.5 9.6 %collective-permute-start.13 = (bf16[512,128]{1,0:T(8,128)(2,1)S(1)}, bf16[512,128]{1,0:T(8,128)(2,1)S(1)}, u32[]{:S(2)}, u32[]{:S(2)}) collective-permute-start(bf16[512,128]{1,0:T(8,128)(2,1)S(1)} %get-tuple-element.75), channel_id=1, source_target_pairs={{0,8},{1,17},{2,10},{3,19},{4,12},{5,21},{6,14},{7,23},{8,0},{9,25... | collective-permute-start | bytes 393224 | tf_op jit(solution)/shard_map/ppermute | solution.py:253
  36.6 7.5 %collective-permute-start.12 = (bf16[512,128]{1,0:T(8,128)(2,1)S(1)}, bf16[512,128]{1,0:T(8,128)(2,1)S(1)}, u32[]{:S(2)}, u32[]{:S(2)}) collective-permute-start(bf16[512,128]{1,0:T(8,128)(2,1)S(1)} %get-tuple-element.74), channel_id=1, source_target_pairs={{0,4},{1,9},{2,6},{3,11},{4,0},{5,13},{6,2},{7,15},{8,12},{9,1},{1... | collective-permute-start | bytes 393224 | tf_op jit(solution)/shard_map/ppermute | solution.py:253
  38.3 6.5 %collective-permute-start.11 = (bf16[512,128]{1,0:T(8,128)(2,1)S(1)}, bf16[512,128]{1,0:T(8,128)(2,1)S(1)}, u32[]{:S(2)}, u32[]{:S(2)}) collective-permute-start(bf16[512,128]{1,0:T(8,128)(2,1)S(1)} %get-tuple-element.72), channel_id=1, source_target_pairs={{0,3},{1,2},{2,1},{3,0},{4,7},{5,6},{6,5},{7,4},{8,11},{9,10},{10,... | collective-permute-start | bytes 393224 | tf_op jit(solution)/shard_map/ppermute | solution.py:257
  38.5 8.3 %collective-permute-start.8 = (bf16[512,128]{1,0:T(8,128)(2,1)S(1)}, bf16[512,128]{1,0:T(8,128)(2,1)S(1)}, u32[]{:S(2)}, u32[]{:S(2)}) collective-permute-start(bf16[512,128]{1,0:T(8,128)(2,1)S(1)} %get-tuple-element.63), channel_id=1, source_target_pairs={{0,1},{1,0},{2,3},{3,2},{4,5},{5,4},{6,7},{7,6},{8,9},{9,8},{10,11... | collective-permute-start | bytes 393224 | tf_op jit(solution)/shard_map/ppermute | solution.py:257
  42.6 5.2 %collective-permute-start.9 = (bf16[512,128]{1,0:T(8,128)(2,1)S(1)}, bf16[512,128]{1,0:T(8,128)(2,1)S(1)}, u32[]{:S(2)}, u32[]{:S(2)}) collective-permute-start(bf16[512,128]{1,0:T(8,128)(2,1)S(1)} %get-tuple-element.64), channel_id=1, source_target_pairs={{0,2},{1,3},{2,0},{3,1},{4,6},{5,7},{6,4},{7,5},{8,10},{9,11},{10,... | collective-permute-start | bytes 393224 | tf_op jit(solution)/shard_map/ppermute | solution.py:257
  44.1 4.5 %collective-permute-start.15 = (bf16[128,128]{1,0:T(8,128)(2,1)S(1)}, bf16[128,128]{1,0:T(8,128)(2,1)S(1)}, u32[]{:S(2)}, u32[]{:S(2)}) collective-permute-start(bf16[128,128]{1,0:T(8,128)(2,1)S(1)} %get-tuple-element.78), channel_id=1, source_target_pairs={{0,1},{1,0},{2,3},{3,2},{4,5},{5,4},{6,7},{7,6},{8,9},{9,8},{10,11... | collective-permute-start | bytes 98312 | tf_op jit(solution)/shard_map/ppermute | solution.py:257
  44.2 4.5 %collective-permute-start.16 = (bf16[128,128]{1,0:T(8,128)(2,1)S(1)}, bf16[128,128]{1,0:T(8,128)(2,1)S(1)}, u32[]{:S(2)}, u32[]{:S(2)}) collective-permute-start(bf16[128,128]{1,0:T(8,128)(2,1)S(1)} %get-tuple-element.79), channel_id=1, source_target_pairs={{0,2},{1,3},{2,0},{3,1},{4,6},{5,7},{6,4},{7,5},{8,10},{9,11},{10,... | collective-permute-start | bytes 98312 | tf_op jit(solution)/shard_map/ppermute | solution.py:257
  44.8 3.9 %collective-permute-start.17 = (bf16[128,128]{1,0:T(8,128)(2,1)S(1)}, bf16[128,128]{1,0:T(8,128)(2,1)S(1)}, u32[]{:S(2)}, u32[]{:S(2)}) collective-permute-start(bf16[128,128]{1,0:T(8,128)(2,1)S(1)} %get-tuple-element.80), channel_id=1, source_target_pairs={{0,3},{1,2},{2,1},{3,0},{4,7},{5,6},{6,5},{7,4},{8,11},{9,10},{10,... | collective-permute-start | bytes 98312 | tf_op jit(solution)/shard_map/ppermute | solution.py:257

commit v11 on v10

--- a/solution.py
+++ b/solution.py
@@ -28,10 +28,6 @@
 
 def dot_nn(a, b):
     return lax.dot_general(a, b, (((1,), (0,)), ((), ())), preferred_element_type=F32)
-
-
-def dot_tn(a, b):
-    return lax.dot_general(a, b, (((0,), (0,)), ((), ())), preferred_element_type=F32)
 
 
 def vmem(shape, dtype):
@@ -150,6 +146,7 @@
     block = kv_refs[0].shape[0] // 2
     dk = [acc_in[b][:block, :] if has_acc else None for b in range(blocks)]
     dv = [acc_in[b][block:, :] if has_acc else None for b in range(blocks)]
+    turned = [kv_refs[b][:block, :].T for b in range(blocks)]
     for i, m in enumerate(pieces):
         query = qg_refs[i][:span, :]
         grad = qg_refs[i][span : 2 * span, :]
@@ -165,7 +162,7 @@
             dscores = (probs * (dprobs - dots)).astype(BF16)
             part_v = dot_nn(probs.astype(BF16), grad)
             part_k = dot_nn(dscores, query)
-            part_q = dot_tn(keys, dscores)
+            part_q = dot_nn(turned[b], dscores)
             dv[b] = part_v if dv[b] is None else dv[b] + part_v
             dk[b] = part_k if dk[b] is None else dk[b] + part_k
             dq = part_q if dq is None else dq + part_q

time: 49.6 us -> 49.6 us (level)
  no operation moved by 1% of the time
where the time goes in v11:
time: 49.6 us; the launch traced here: 49.5 us
  starting transfers between devices  21.9 us (44%)
  waiting for transfers between devices  14.2 us (29%)
  Pallas kernels  12.6 us (25%)
  between operations  0.81 us (2%)
    pallas_call x20, Pallas kernels, call(): pl.pallas_call(kernel, out_shape=out_shapes, in_specs=specs, out_specs=[p...  12.6 us
    ppermute x12, waiting for transfers between devices, swap(): lax.ppermute(value, axis, [(i, i ^ distance) for i in range(lax.axis_size...  11.6 us
    ppermute x12, starting transfers between devices, swap(): lax.ppermute(value, axis, [(i, i ^ distance) for i in range(lax.axis_size...  11.1 us
    ppermute x6, starting transfers between devices, trade(): return lax.ppermute(value, ('ctx', 'head'), pairs)  10.8 us
    ppermute x6, waiting for transfers between devices, trade(): return lax.ppermute(value, ('ctx', 'head'), pairs)  2.6 us
  transfers between devices with their start and end apart: 18, of which 4 were waited for; matrix products, arithmetic and copies ran while one was open for 0% of the time, Pallas kernels for 16%

profile of v11, /device:TPU:0, one launch (start us, length us, event | category | flops | bytes accessed | tf_op | source)
XLA Modules:
  0.0 49.5 jit_solution(8840789621322753206)
XLA Ops:
  0.6 1.5 %shard_map.85 = (bf16[64,4096]{1,0:T(8,128)(2,1)S(1)}, bf16[64,4096]{1,0:T(8,128)(2,1)S(1)}, bf16[64,4096]{1,0:T(8,128)(2,1)S(1)}, bf16[128,128]{1,0:T(8,128)(2,...) custom-call(s32[1]{0:T(128)} %bitcast.place, ...), custom_call_target="tpu_custom_call" | custom-call | tf_op jit(solution)/shard_map/pallas_call | solution.py:50
  2.1 0.3 shard_map.87
  2.5 0.5 %collective-permute-start = (bf16[1040,128]{1,0:T(8,128)(2,1)S(1)}, bf16[1040,128]{1,0:T(8,128)(2,1)S(1)}, u32[]{:S(2)}, u32[]{:S(2)}) collective-permute-start(bf16[1040,128]{1,0:T(8,128)(2,1)S(1)} %shard_map.87), channel_id=1, source_target_pairs={{0,1},{1,0},{2,3},{3,2},{4,5},{5,4},{6,7},{7,6},{8,9},{9,8},{10,11... | collective-permute-start | bytes 798728 | tf_op jit(solution)/shard_map/ppermute | solution.py:254
  3.4 2.5 %collective-permute-start.1 = (bf16[1040,128]{1,0:T(8,128)(2,1)S(1)}, bf16[1040,128]{1,0:T(8,128)(2,1)S(1)}, u32[]{:S(2)}, u32[]{:S(2)}) collective-permute-start(bf16[1040,128]{1,0:T(8,128)(2,1)S(1)} %shard_map.88), channel_id=1, source_target_pairs={{0,2},{1,3},{2,0},{3,1},{4,6},{5,7},{6,4},{7,5},{8,10},{9,11},{10,... | collective-permute-start | bytes 798728 | tf_op jit(solution)/shard_map/ppermute | solution.py:254
  6.5 1.9 %collective-permute-start.3 = (bf16[128,128]{1,0:T(8,128)(2,1)S(1)}, bf16[128,128]{1,0:T(8,128)(2,1)S(1)}, u32[]{:S(2)}, u32[]{:S(2)}) collective-permute-start(bf16[128,128]{1,0:T(8,128)(2,1)S(1)} %get-tuple-element.49), channel_id=1, source_target_pairs={{0,2},{1,3},{2,0},{3,1},{4,6},{5,7},{6,4},{7,5},{8,10},{9,11},{10,... | collective-permute-start | bytes 98312 | tf_op jit(solution)/shard_map/ppermute | solution.py:254
  8.4 0.8 %collective-permute-start.4 = (bf16[128,128]{1,0:T(8,128)(2,1)S(1)}, bf16[128,128]{1,0:T(8,128)(2,1)S(1)}, u32[]{:S(2)}, u32[]{:S(2)}) collective-permute-start(bf16[128,128]{1,0:T(8,128)(2,1)S(1)} %get-tuple-element.50), channel_id=1, source_target_pairs={{0,3},{1,2},{2,1},{3,0},{4,7},{5,6},{6,5},{7,4},{8,11},{9,10},{10,... | collective-permute-start | bytes 98312 | tf_op jit(solution)/shard_map/ppermute | solution.py:254
  9.2 10.3 %collective-permute-done.3.refs_2_ = bf16[128,128]{1,0:T(8,128)(2,1)S(1)} collective-permute-done((bf16[128,128]{1,0:T(8,128)(2,1)S(1)}, bf16[128,128]{1,0:T(8,128)(2,1)S(1)}, u32[]{:S(2)}, u32[]{:S(2)}) %collective-permute-start.3) | collective-permute-done | bytes 32800 | tf_op jit(solution)/shard_map/ppermute | solution.py:254
  19.9 1.7 %collective-permute-start.7 = (bf16[512,128]{1,0:T(8,128)(2,1)S(1)}, bf16[512,128]{1,0:T(8,128)(2,1)S(1)}, u32[]{:S(2)}, u32[]{:S(2)}) collective-permute-start(bf16[512,128]{1,0:T(8,128)(2,1)S(1)} %shard_map.89.refs_2_), channel_id=1, source_target_pairs={{0,4},{1,9},{2,6},{3,11},{4,0},{5,13},{6,2},{7,15},{8,12},{9,1},{1... | collective-permute-start | bytes 393224 | tf_op jit(solution)/shard_map/ppermute | solution.py:250
  21.5 1.6 %collective-permute-start.6 = (bf16[512,128]{1,0:T(8,128)(2,1)S(1)}, bf16[512,128]{1,0:T(8,128)(2,1)S(1)}, u32[]{:S(2)}, u32[]{:S(2)}) collective-permute-start(bf16[512,128]{1,0:T(8,128)(2,1)S(1)} %shard_map.89.refs_2_), channel_id=1, source_target_pairs={{0,8},{1,17},{2,10},{3,19},{4,12},{5,21},{6,14},{7,23},{8,0},{9,25... | collective-permute-start | bytes 393224 | tf_op jit(solution)/shard_map/ppermute | solution.py:250
  23.1 2.6 %collective-permute-start.5 = (bf16[512,128]{1,0:T(8,128)(2,1)S(1)}, bf16[512,128]{1,0:T(8,128)(2,1)S(1)}, u32[]{:S(2)}, u32[]{:S(2)}) collective-permute-start(bf16[512,128]{1,0:T(8,128)(2,1)S(1)} %shard_map.89.refs_2_), channel_id=1, source_target_pairs={{0,16},{1,5},{2,18},{3,7},{4,20},{5,1},{6,22},{7,3},{8,24},{9,13},... | collective-permute-start | bytes 393224 | tf_op jit(solution)/shard_map/ppermute | solution.py:250
  26.0 0.5 shard_map.90
  26.5 0.5 shard_map.91
  27.0 0.9 %shard_map.92 = (f32[128,512]{1,0:T(8,128)S(1)}, f32[128,512]{1,0:T(8,128)S(1)}, f32[512,128]{1,0:T(8,128)S(1)}) custom-call(s32[1]{0:T(128)} %bitcast.place, bf16[1040,128]{1,0:T(8,128)(2,1)S(1)} %shard_map.86.refs_0_, bf16[1040,128]{1,0:T(8,128)(2,1)S(1)} %collective-permute-done.refs_0_.refs_1_, f32[32,128]{1,0:T(8,128)S(1)} %get-tuple-element.46.refs_1_.refs_2_.refs_3_, ...), custom_call_target="tpu_custom_call" | custom-call | tf_op jit(solution)/shard_map/pallas_call | solution.py:50
  28.0 0.9 %shard_map.93 = (f32[128,512]{1,0:T(8,128)S(1)}, f32[128,512]{1,0:T(8,128)S(1)}, f32[512,128]{1,0:T(8,128)S(1)}) custom-call(s32[1]{0:T(128)} %bitcast.place, bf16[1040,128]{1,0:T(8,128)(2,1)S(1)} %shard_map.86.refs_0_, bf16[1040,128]{1,0:T(8,128)(2,1)S(1)} %collective-permute-done.refs_0_.refs_1_, f32[32,128]{1,0:T(8,128)S(1)} %get-tuple-element.46.refs_1_.refs_2_.refs_3_, ...), custom_call_target="tpu_custom_call" | custom-call | tf_op jit(solution)/shard_map/pallas_call | solution.py:50
  28.9 1.1 %shard_map.94 = (f32[128,512]{1,0:T(8,128)S(1)}, f32[512,128]{1,0:T(8,128)S(1)}, f32[512,128]{1,0:T(8,128)S(1)}, f32[512,128]{1,0:T(8,128)S(1)}) custom-call(s32[1]{0:T(128)} %bitcast.place, bf16[1040,128]{1,0:T(8,128)(2,1)S(1)} %collective-permute-done.1.refs_0_.refs_2_, f32[32,128]{1,0:T(8,128)S(1)} %get-tuple-element.46.refs_1_.refs_2_.refs_3_, ...), custom_call_target="tpu_custom_call" | custom-call | tf_op jit(solution)/shard_map/pallas_call | solution.py:50
  30.0 0.5 shard_map.98
  30.5 0.5 shard_map.99
  31.0 1.3 %shard_map.95 = (f32[512,128]{1,0:T(8,128)S(1)}, bf16[512,128]{1,0:T(8,128)(2,1)S(1)}, bf16[512,128]{1,0:T(8,128)(2,1)S(1)}, f32[512,128]{1,0:T(8,128)S(1)}) custom-call(s32[1]{0:T(128)} %bitcast.place, bf16[1040,128]{1,0:T(8,128)(2,1)S(1)} %shard_map.86.refs_0_, bf16[1040,128]{1,0:T(8,128)(2,1)S(1)} %collective-permute-done.refs_0_.refs_1_, ...), custom_call_target="tpu_custom_call" | custom-call | tf_op jit(solution)/shard_map/pallas_call | solution.py:50
  32.4 0.5 shard_map.100
  32.8 1.7 %collective-permute-start.14 = (bf16[512,128]{1,0:T(8,128)(2,1)S(1)}, bf16[512,128]{1,0:T(8,128)(2,1)S(1)}, u32[]{:S(2)}, u32[]{:S(2)}) collective-permute-start(bf16[512,128]{1,0:T(8,128)(2,1)S(1)} %get-tuple-element.76), channel_id=1, source_target_pairs={{0,16},{1,5},{2,18},{3,7},{4,20},{5,1},{6,22},{7,3},{8,24},{9,13},... | collective-permute-start | bytes 393224 | tf_op jit(solution)/shard_map/ppermute | solution.py:250
  34.5 2.1 %collective-permute-start.13 = (bf16[512,128]{1,0:T(8,128)(2,1)S(1)}, bf16[512,128]{1,0:T(8,128)(2,1)S(1)}, u32[]{:S(2)}, u32[]{:S(2)}) collective-permute-start(bf16[512,128]{1,0:T(8,128)(2,1)S(1)} %get-tuple-element.75), channel_id=1, source_target_pairs={{0,8},{1,17},{2,10},{3,19},{4,12},{5,21},{6,14},{7,23},{8,0},{9,25... | collective-permute-start | bytes 393224 | tf_op jit(solution)/shard_map/ppermute | solution.py:250
  36.6 1.1 %collective-permute-start.12 = (bf16[512,128]{1,0:T(8,128)(2,1)S(1)}, bf16[512,128]{1,0:T(8,128)(2,1)S(1)}, u32[]{:S(2)}, u32[]{:S(2)}) collective-permute-start(bf16[512,128]{1,0:T(8,128)(2,1)S(1)} %get-tuple-element.74), channel_id=1, source_target_pairs={{0,4},{1,9},{2,6},{3,11},{4,0},{5,13},{6,2},{7,15},{8,12},{9,1},{1... | collective-permute-start | bytes 393224 | tf_op jit(solution)/shard_map/ppermute | solution.py:250
  37.8 0.6 %shard_map.101 = (bf16[512,128]{1,0:T(8,128)(2,1)S(1)}, f32[512,128]{1,0:T(8,128)S(1)}) custom-call(s32[1]{0:T(128)} %bitcast.place, bf16[1040,128]{1,0:T(8,128)(2,1)S(1)} %collective-permute-done.10.refs_0_, f32[32,128]{1,0:T(8,128)S(1)} %get-tuple-element.46.refs_1_.refs_2_.refs_3_, bf16[512,128]{1,0:T(8,128)(2,1)S(1)} %shard_map.89.refs_2_, ...), custom_call_target="tpu_custom_call" | custom-call | tf_op jit(solution)/shard_map/pallas_call | solution.py:50
  38.5 1.5 %collective-permute-start.8 = (bf16[512,128]{1,0:T(8,128)(2,1)S(1)}, bf16[512,128]{1,0:T(8,128)(2,1)S(1)}, u32[]{:S(2)}, u32[]{:S(2)}) collective-permute-start(bf16[512,128]{1,0:T(8,128)(2,1)S(1)} %get-tuple-element.63), channel_id=1, source_target_pairs={{0,1},{1,0},{2,3},{3,2},{4,5},{5,4},{6,7},{7,6},{8,9},{9,8},{10,11... | collective-permute-start | bytes 393224 | tf_op jit(solution)/shard_map/ppermute | solution.py:254
  40.0 2.5 %collective-permute-done.14.refs_3_ = bf16[512,128]{1,0:T(8,128)(2,1)S(1)} collective-permute-done((bf16[512,128]{1,0:T(8,128)(2,1)S(1)}, bf16[512,128]{1,0:T(8,128)(2,1)S(1)}, u32[]{:S(2)}, u32[]{:S(2)}) %collective-permute-start.14) | collective-permute-done | bytes 131104 | tf_op jit(solution)/shard_map/ppermute | solution.py:250
  42.6 1.5 %collective-permute-start.9 = (bf16[512,128]{1,0:T(8,128)(2,1)S(1)}, bf16[512,128]{1,0:T(8,128)(2,1)S(1)}, u32[]{:S(2)}, u32[]{:S(2)}) collective-permute-start(bf16[512,128]{1,0:T(8,128)(2,1)S(1)} %get-tuple-element.64), channel_id=1, source_target_pairs={{0,2},{1,3},{2,0},{3,1},{4,6},{5,7},{6,4},{7,5},{8,10},{9,11},{10,... | collective-permute-start | bytes 393224 | tf_op jit(solution)/shard_map/ppermute | solution.py:254
  44.2 0.6 %collective-permute-start.16 = (bf16[128,128]{1,0:T(8,128)(2,1)S(1)}, bf16[128,128]{1,0:T(8,128)(2,1)S(1)}, u32[]{:S(2)}, u32[]{:S(2)}) collective-permute-start(bf16[128,128]{1,0:T(8,128)(2,1)S(1)} %get-tuple-element.79), channel_id=1, source_target_pairs={{0,2},{1,3},{2,0},{3,1},{4,6},{5,7},{6,4},{7,5},{8,10},{9,11},{10,... | collective-permute-start | bytes 98312 | tf_op jit(solution)/shard_map/ppermute | solution.py:254
  44.8 1.2 %collective-permute-start.17 = (bf16[128,128]{1,0:T(8,128)(2,1)S(1)}, bf16[128,128]{1,0:T(8,128)(2,1)S(1)}, u32[]{:S(2)}, u32[]{:S(2)}) collective-permute-start(bf16[128,128]{1,0:T(8,128)(2,1)S(1)} %get-tuple-element.80), channel_id=1, source_target_pairs={{0,3},{1,2},{2,1},{3,0},{4,7},{5,6},{6,5},{7,4},{8,11},{9,10},{10,... | collective-permute-start | bytes 98312 | tf_op jit(solution)/shard_map/ppermute | solution.py:254
  46.1 0.7 %shard_map.96.filled = f32[64,4096]{1,0:T(8,128)} custom-call(s32[1]{0:T(128)} %bitcast.place, f32[512,128]{1,0:T(8,128)S(1)} %get-tuple-element.62.refs_0_), custom_call_target="tpu_custom_call" | custom-call | tf_op jit(solution)/shard_map/pallas_call | solution.py:50
  46.8 0.9 %collective-permute-done.9.refs_1_ = bf16[512,128]{1,0:T(8,128)(2,1)S(1)} collective-permute-done((bf16[512,128]{1,0:T(8,128)(2,1)S(1)}, bf16[512,128]{1,0:T(8,128)(2,1)S(1)}, u32[]{:S(2)}, u32[]{:S(2)}) %collective-permute-start.9) | collective-permute-done | bytes 131104 | tf_op jit(solution)/shard_map/ppermute | solution.py:254
  47.8 0.9 %shard_map.102 = f32[64,4096]{1,0:T(8,128)} custom-call(s32[1]{0:T(128)} %bitcast.place, f32[64,4096]{1,0:T(8,128)} %shard_map.96.filled, bf16[512,128]{1,0:T(8,128)(2,1)S(1)} %collective-permute-done.8.refs_0_, bf16[512,128]{1,0:T(8,128)(2,1)S(1)} %collective-permute-done.9.refs_1_, ...), custom_call_target="tpu_custom_call", output_to_operand_aliasing={{}: (1, {})} | custom-call | tf_op jit(solution)/shard_map/pallas_call | solution.py:50
  48.7 0.7 %shard_map.104 = (f32[64,512]{1,0:T(8,128)}, f32[64,512]{1,0:T(8,128)}) custom-call(s32[1]{0:T(128)} %bitcast.place, f32[128,128]{1,0:T(8,128)S(1)} %get-tuple-element.77.refs_0_, bf16[128,128]{1,0:T(8,128)(2,1)S(1)} %collective-permute-done.15.refs_1_, bf16[128,128]{1,0:T(8,128)(2,1)S(1)} %collective-permute-done.16.refs_2_, ...), custom_call_target="tpu_custom_call" | custom-call | tf_op jit(solution)/shard_map/pallas_call | solution.py:50
  (24 shorter events, 2.1 us)
Async XLA Ops:
  2.5 20.6 %collective-permute-start = (bf16[1040,128]{1,0:T(8,128)(2,1)S(1)}, bf16[1040,128]{1,0:T(8,128)(2,1)S(1)}, u32[]{:S(2)}, u32[]{:S(2)}) collective-permute-start(bf16[1040,128]{1,0:T(8,128)(2,1)S(1)} %shard_map.87), channel_id=1, source_target_pairs={{0,1},{1,0},{2,3},{3,2},{4,5},{5,4},{6,7},{7,6},{8,9},{9,8},{10,11... | collective-permute-start | bytes 798728 | tf_op jit(solution)/shard_map/ppermute | solution.py:254
  3.4 25.6 %collective-permute-start.1 = (bf16[1040,128]{1,0:T(8,128)(2,1)S(1)}, bf16[1040,128]{1,0:T(8,128)(2,1)S(1)}, u32[]{:S(2)}, u32[]{:S(2)}) collective-permute-start(bf16[1040,128]{1,0:T(8,128)(2,1)S(1)} %shard_map.88), channel_id=1, source_target_pairs={{0,2},{1,3},{2,0},{3,1},{4,6},{5,7},{6,4},{7,5},{8,10},{9,11},{10,... | collective-permute-start | bytes 798728 | tf_op jit(solution)/shard_map/ppermute | solution.py:254
  6.2 23.8 %collective-permute-start.10 = (bf16[1040,128]{1,0:T(8,128)(2,1)S(1)}, bf16[1040,128]{1,0:T(8,128)(2,1)S(1)}, u32[]{:S(2)}, u32[]{:S(2)}) collective-permute-start(bf16[1040,128]{1,0:T(8,128)(2,1)S(1)} %shard_map.97), channel_id=1, source_target_pairs={{0,3},{1,2},{2,1},{3,0},{4,7},{5,6},{6,5},{7,4},{8,11},{9,10},{10,... | collective-permute-start | bytes 798728 | tf_op jit(solution)/shard_map/ppermute | solution.py:254
  6.4 2.0 %collective-permute-start.2 = (bf16[128,128]{1,0:T(8,128)(2,1)S(1)}, bf16[128,128]{1,0:T(8,128)(2,1)S(1)}, u32[]{:S(2)}, u32[]{:S(2)}) collective-permute-start(bf16[128,128]{1,0:T(8,128)(2,1)S(1)} %get-tuple-element.48), channel_id=1, source_target_pairs={{0,1},{1,0},{2,3},{3,2},{4,5},{5,4},{6,7},{7,6},{8,9},{9,8},{10,11... | collective-permute-start | bytes 98312 | tf_op jit(solution)/shard_map/ppermute | solution.py:254
  6.5 13.0 %collective-permute-start.3 = (bf16[128,128]{1,0:T(8,128)(2,1)S(1)}, bf16[128,128]{1,0:T(8,128)(2,1)S(1)}, u32[]{:S(2)}, u32[]{:S(2)}) collective-permute-start(bf16[128,128]{1,0:T(8,128)(2,1)S(1)} %get-tuple-element.49), channel_id=1, source_target_pairs={{0,2},{1,3},{2,0},{3,1},{4,6},{5,7},{6,4},{7,5},{8,10},{9,11},{10,... | collective-permute-start | bytes 98312 | tf_op jit(solution)/shard_map/ppermute | solution.py:254
  8.4 11.4 %collective-permute-start.4 = (bf16[128,128]{1,0:T(8,128)(2,1)S(1)}, bf16[128,128]{1,0:T(8,128)(2,1)S(1)}, u32[]{:S(2)}, u32[]{:S(2)}) collective-permute-start(bf16[128,128]{1,0:T(8,128)(2,1)S(1)} %get-tuple-element.50), channel_id=1, source_target_pairs={{0,3},{1,2},{2,1},{3,0},{4,7},{5,6},{6,5},{7,4},{8,11},{9,10},{10,... | collective-permute-start | bytes 98312 | tf_op jit(solution)/shard_map/ppermute | solution.py:254
  19.9 7.2 %collective-permute-start.7 = (bf16[512,128]{1,0:T(8,128)(2,1)S(1)}, bf16[512,128]{1,0:T(8,128)(2,1)S(1)}, u32[]{:S(2)}, u32[]{:S(2)}) collective-permute-start(bf16[512,128]{1,0:T(8,128)(2,1)S(1)} %shard_map.89.refs_2_), channel_id=1, source_target_pairs={{0,4},{1,9},{2,6},{3,11},{4,0},{5,13},{6,2},{7,15},{8,12},{9,1},{1... | collective-permute-start | bytes 393224 | tf_op jit(solution)/shard_map/ppermute | solution.py:250
  21.5 6.4 %collective-permute-start.6 = (bf16[512,128]{1,0:T(8,128)(2,1)S(1)}, bf16[512,128]{1,0:T(8,128)(2,1)S(1)}, u32[]{:S(2)}, u32[]{:S(2)}) collective-permute-start(bf16[512,128]{1,0:T(8,128)(2,1)S(1)} %shard_map.89.refs_2_), channel_id=1, source_target_pairs={{0,8},{1,17},{2,10},{3,19},{4,12},{5,21},{6,14},{7,23},{8,0},{9,25... | collective-permute-start | bytes 393224 | tf_op jit(solution)/shard_map/ppermute | solution.py:250
  23.1 7.9 %collective-permute-start.5 = (bf16[512,128]{1,0:T(8,128)(2,1)S(1)}, bf16[512,128]{1,0:T(8,128)(2,1)S(1)}, u32[]{:S(2)}, u32[]{:S(2)}) collective-permute-start(bf16[512,128]{1,0:T(8,128)(2,1)S(1)} %shard_map.89.refs_2_), channel_id=1, source_target_pairs={{0,16},{1,5},{2,18},{3,7},{4,20},{5,1},{6,22},{7,3},{8,24},{9,13},... | collective-permute-start | bytes 393224 | tf_op jit(solution)/shard_map/ppermute | solution.py:250
  32.8 9.7 %collective-permute-start.14 = (bf16[512,128]{1,0:T(8,128)(2,1)S(1)}, bf16[512,128]{1,0:T(8,128)(2,1)S(1)}, u32[]{:S(2)}, u32[]{:S(2)}) collective-permute-start(bf16[512,128]{1,0:T(8,128)(2,1)S(1)} %get-tuple-element.76), channel_id=1, source_target_pairs={{0,16},{1,5},{2,18},{3,7},{4,20},{5,1},{6,22},{7,3},{8,24},{9,13},... | collective-permute-start | bytes 393224 | tf_op jit(solution)/shard_map/ppermute | solution.py:250
  34.5 9.6 %collective-permute-start.13 = (bf16[512,128]{1,0:T(8,128)(2,1)S(1)}, bf16[512,128]{1,0:T(8,128)(2,1)S(1)}, u32[]{:S(2)}, u32[]{:S(2)}) collective-permute-start(bf16[512,128]{1,0:T(8,128)(2,1)S(1)} %get-tuple-element.75), channel_id=1, source_target_pairs={{0,8},{1,17},{2,10},{3,19},{4,12},{5,21},{6,14},{7,23},{8,0},{9,25... | collective-permute-start | bytes 393224 | tf_op jit(solution)/shard_map/ppermute | solution.py:250
  36.6 7.5 %collective-permute-start.12 = (bf16[512,128]{1,0:T(8,128)(2,1)S(1)}, bf16[512,128]{1,0:T(8,128)(2,1)S(1)}, u32[]{:S(2)}, u32[]{:S(2)}) collective-permute-start(bf16[512,128]{1,0:T(8,128)(2,1)S(1)} %get-tuple-element.74), channel_id=1, source_target_pairs={{0,4},{1,9},{2,6},{3,11},{4,0},{5,13},{6,2},{7,15},{8,12},{9,1},{1... | collective-permute-start | bytes 393224 | tf_op jit(solution)/shard_map/ppermute | solution.py:250
  38.3 6.5 %collective-permute-start.11 = (bf16[512,128]{1,0:T(8,128)(2,1)S(1)}, bf16[512,128]{1,0:T(8,128)(2,1)S(1)}, u32[]{:S(2)}, u32[]{:S(2)}) collective-permute-start(bf16[512,128]{1,0:T(8,128)(2,1)S(1)} %get-tuple-element.72), channel_id=1, source_target_pairs={{0,3},{1,2},{2,1},{3,0},{4,7},{5,6},{6,5},{7,4},{8,11},{9,10},{10,... | collective-permute-start | bytes 393224 | tf_op jit(solution)/shard_map/ppermute | solution.py:254
  38.5 8.3 %collective-permute-start.8 = (bf16[512,128]{1,0:T(8,128)(2,1)S(1)}, bf16[512,128]{1,0:T(8,128)(2,1)S(1)}, u32[]{:S(2)}, u32[]{:S(2)}) collective-permute-start(bf16[512,128]{1,0:T(8,128)(2,1)S(1)} %get-tuple-element.63), channel_id=1, source_target_pairs={{0,1},{1,0},{2,3},{3,2},{4,5},{5,4},{6,7},{7,6},{8,9},{9,8},{10,11... | collective-permute-start | bytes 393224 | tf_op jit(solution)/shard_map/ppermute | solution.py:254
  42.6 5.2 %collective-permute-start.9 = (bf16[512,128]{1,0:T(8,128)(2,1)S(1)}, bf16[512,128]{1,0:T(8,128)(2,1)S(1)}, u32[]{:S(2)}, u32[]{:S(2)}) collective-permute-start(bf16[512,128]{1,0:T(8,128)(2,1)S(1)} %get-tuple-element.64), channel_id=1, source_target_pairs={{0,2},{1,3},{2,0},{3,1},{4,6},{5,7},{6,4},{7,5},{8,10},{9,11},{10,... | collective-permute-start | bytes 393224 | tf_op jit(solution)/shard_map/ppermute | solution.py:254
  44.1 4.6 %collective-permute-start.15 = (bf16[128,128]{1,0:T(8,128)(2,1)S(1)}, bf16[128,128]{1,0:T(8,128)(2,1)S(1)}, u32[]{:S(2)}, u32[]{:S(2)}) collective-permute-start(bf16[128,128]{1,0:T(8,128)(2,1)S(1)} %get-tuple-element.78), channel_id=1, source_target_pairs={{0,1},{1,0},{2,3},{3,2},{4,5},{5,4},{6,7},{7,6},{8,9},{9,8},{10,11... | collective-permute-start | bytes 98312 | tf_op jit(solution)/shard_map/ppermute | solution.py:254
  44.2 4.5 %collective-permute-start.16 = (bf16[128,128]{1,0:T(8,128)(2,1)S(1)}, bf16[128,128]{1,0:T(8,128)(2,1)S(1)}, u32[]{:S(2)}, u32[]{:S(2)}) collective-permute-start(bf16[128,128]{1,0:T(8,128)(2,1)S(1)} %get-tuple-element.79), channel_id=1, source_target_pairs={{0,2},{1,3},{2,0},{3,1},{4,6},{5,7},{6,4},{7,5},{8,10},{9,11},{10,... | collective-permute-start | bytes 98312 | tf_op jit(solution)/shard_map/ppermute | solution.py:254
  44.8 3.9 %collective-permute-start.17 = (bf16[128,128]{1,0:T(8,128)(2,1)S(1)}, bf16[128,128]{1,0:T(8,128)(2,1)S(1)}, u32[]{:S(2)}, u32[]{:S(2)}) collective-permute-start(bf16[128,128]{1,0:T(8,128)(2,1)S(1)} %get-tuple-element.80), channel_id=1, source_target_pairs={{0,3},{1,2},{2,1},{3,0},{4,7},{5,6},{6,5},{7,4},{8,11},{9,10},{10,... | collective-permute-start | bytes 98312 | tf_op jit(solution)/shard_map/ppermute | solution.py:254
